TPU v7x, 32 devices: a whole 2x2x4 slice. The times are simulated.
32 devices in a mesh: seq: 8 (over z, x), fsdp: 4 (over y, core).
Axes of the slice: x: 2, y: 2, z: 4, core: 2. Of those that a mesh axis runs over, the one named last changes fastest.
Arguments:
- layer_in: bfloat16 [4, 2048, 1024], P('fsdp', 'seq'), may hold values from -6 to 6
- encoder: bfloat16 [4, 512, 1024], P('fsdp', 'seq'), may hold values from -6 to 6
- decoder_ids: int32 [4, 2048], P('fsdp', 'seq'), may hold values from 0 to 3, never falling along the last dimension, each value on 1 to 1024 neighbouring positions
- encoder_ids: int32 [4, 512], P('fsdp', 'seq'), may hold values from 0 to 3, never falling along the last dimension, each value on 1 to 256 neighbouring positions
- rel_buckets: int32 [2048], replicated, may hold values from 0 to 31, as said below
- norm_self: bfloat16 [1024], P('fsdp'), may hold values from 0.5 to 1.5
- self_qkv: bfloat16 [1024, 16, 192], P('fsdp'), may hold values from -0.0625 to 0.0625
- self_out: bfloat16 [1024, 1024], P('fsdp'), may hold values from -1.5 to 1.5
- rel_table: bfloat16 [32, 16], P(None, 'fsdp'), may hold values from -4 to 4
- norm_cross: bfloat16 [1024], P('fsdp'), may hold values from 0.5 to 1.5
- cross_q: bfloat16 [1024, 1024], P('fsdp'), may hold values from -0.0625 to 0.0625
- cross_kv: bfloat16 [1024, 16, 128], P('fsdp'), may hold values from -0.0625 to 0.0625
- cross_out: bfloat16 [1024, 1024], P('fsdp'), may hold values from -1.5 to 1.5
- norm_ff: bfloat16 [1024], P('fsdp'), may hold values from 0.5 to 1.5
- ff_in: bfloat16 [1024, 5632], P('fsdp'), may hold values from -0.1875 to 0.1875
- ff_out: bfloat16 [2816, 1024], P('fsdp'), may hold values from -0.109375 to 0.109375
- cotangent: bfloat16 [4, 2048, 1024], P('fsdp', 'seq'), may hold values from -6 to 6
Outputs:
- layer_out: bfloat16 [4, 2048, 1024], P('fsdp', 'seq')
- grad_layer_in: float32 [4, 2048, 1024], P('fsdp', 'seq')
- grad_encoder: float32 [4, 512, 1024], P('fsdp', 'seq')
- grad_norm_self: float32 [1024], P('fsdp')
- grad_self_qkv: float32 [1024, 16, 192], P('fsdp')
- grad_self_out: float32 [1024, 1024], P('fsdp')
- grad_rel_table: float32 [32, 16], P(None, 'fsdp')
- grad_norm_cross: float32 [1024], P('fsdp')
- grad_cross_q: float32 [1024, 1024], P('fsdp')
- grad_cross_kv: float32 [1024, 16, 128], P('fsdp')
- grad_cross_out: float32 [1024, 1024], P('fsdp')
- grad_norm_ff: float32 [1024], P('fsdp')
- grad_ff_in: float32 [1024, 5632], P('fsdp')
- grad_ff_out: float32 [2816, 1024], P('fsdp')
Inputs may be any that keep to these rules, and one draw needn't show every extreme that they name: `rel_buckets`: the bucket of a query-key distance, in tokens, in the self-attention. Never falls along a sequence; every number from 0 to 3 occurs in each sequence, in decoder_ids and encoder_ids alike. `encoder_ids`: never falls along a sequence; every number from 0 to 3 occurs in each sequence.
All inputs are finite; a program needn't handle non-finite values.
Results may differ from a plain program's by a relative error of at most 0.024.
Values may be sent and summed in bfloat16 or wider, within the bound.
A program may use at most 192 MiB of HBM per device.

v0:
```python
import jax
import jax.numpy as jnp
from jax import lax
from jax.sharding import PartitionSpec as P

EPS = 1e-06
HIGH = lax.Precision.HIGHEST
MASKED = -1e30


def norm_apply(value, gain):
    return value * lax.rsqrt(jnp.mean(value * value, axis=-1, keepdims=True) + EPS) * gain


def norm_back(value, gain, grad):
    _, pull = jax.vjp(norm_apply, value, gain)
    return pull(grad)


def gate_mix(gate_up):
    inner = gate_up.shape[1] // 2
    return jax.nn.gelu(gate_up[:, :inner], approximate=True) * gate_up[:, inner:]


def bias_block(distance_bias, start, block):
    groups, length = distance_bias.shape
    period = length + block
    offsets = jnp.arange(period, dtype=jnp.int32)
    places = jnp.minimum(jnp.remainder(start - offsets, period), length - 1)
    circle = jnp.take(distance_bias, places, axis=1)
    tiled = jnp.tile(circle, (1, block + 1))[:, : block * (period - 1)]
    return tiled.reshape(groups, block, period - 1)[:, :, :length]


def bias_grad_block(grid, start):
    groups, block, length = grid.shape
    period = length + block
    padded = jnp.concatenate([grid, jnp.zeros((groups, block, block - 1), jnp.float32)], axis=2)
    flat = padded.reshape(groups, block * (period - 1))
    flat = jnp.concatenate([flat, jnp.zeros((groups, block), jnp.float32)], axis=1)
    folded = jnp.sum(flat.reshape(groups, block, period), axis=1)
    places = jnp.remainder(start - jnp.arange(length, dtype=jnp.int32), period)
    return jnp.take(folded, places, axis=1)


def score_rows(query, key, ids_query, ids_key, bias, which, start, block):
    query_rows = lax.dynamic_slice_in_dim(
        lax.dynamic_index_in_dim(query, which, 0, False), start, block, 0
    )
    key_rows = lax.dynamic_index_in_dim(key, which, 0, False)
    ids_rows = lax.dynamic_slice_in_dim(
        lax.dynamic_index_in_dim(ids_query, which, 0, False), start, block, 0
    )
    ids_cols = lax.dynamic_index_in_dim(ids_key, which, 0, False)
    score = jnp.einsum("qge,kge->gqk", query_rows, key_rows, preferred_element_type=jnp.float32)
    allowed = ids_rows[:, None] == ids_cols[None, :]
    if bias is not None:
        position = start + jnp.arange(block, dtype=jnp.int32)
        column = jnp.arange(key_rows.shape[0], dtype=jnp.int32)
        allowed = allowed & (column[None, :] <= position[:, None])
        score = score + bias_block(bias, start, block)
    return (query_rows, key_rows, jnp.where(allowed[None], score, MASKED))


def attend_forward(query, key, value, ids_query, ids_key, bias):
    seqs, length, groups, width = query.shape
    block = min(512, length)
    count = length // block

    def one(index):
        which = index // count
        start = index % count * block
        _, _, score = score_rows(query, key, ids_query, ids_key, bias, which, start, block)
        maximum = jnp.max(score, axis=-1, keepdims=True)
        exponent = jnp.exp(score - maximum)
        total = jnp.sum(exponent, axis=-1, keepdims=True)
        probability = (exponent / total).astype(jnp.bfloat16)
        value_rows = lax.dynamic_index_in_dim(value, which, 0, False)
        result = jnp.einsum(
            "gqk,kge->qge", probability, value_rows, preferred_element_type=jnp.float32
        )
        return (result.astype(jnp.bfloat16), (maximum + jnp.log(total))[..., 0])

    results, log_total = lax.map(one, jnp.arange(seqs * count, dtype=jnp.int32))
    return (results.reshape(seqs, length, groups, width), log_total)


def attend_backward(query, key, value, ids_query, ids_key, bias, log_total, grad_out):
    seqs, length, groups, width = query.shape
    keys = key.shape[1]
    block = min(512, length)
    count = length // block

    def per_sequence(which):
        value_rows = lax.dynamic_index_in_dim(value, which, 0, False)
        grad_seq = lax.dynamic_index_in_dim(grad_out, which, 0, False)

        def per_block(carry, step):
            grad_key, grad_value, grad_bias = carry
            start = step * block
            query_rows, key_rows, score = score_rows(
                query, key, ids_query, ids_key, bias, which, start, block
            )
            probability = jnp.exp(score - log_total[which * count + step][..., None])
            grad_rows = lax.dynamic_slice_in_dim(grad_seq, start, block, 0)
            grad_prob = jnp.einsum(
                "qge,kge->gqk", grad_rows, value_rows, preferred_element_type=jnp.float32
            )
            delta = jnp.sum(probability * grad_prob, axis=-1, keepdims=True)
            grad_score = (probability * (grad_prob - delta)).astype(jnp.bfloat16)
            grad_value = grad_value + jnp.einsum(
                "gqk,qge->kge",
                probability.astype(jnp.bfloat16),
                grad_rows,
                preferred_element_type=jnp.float32,
            )
            grad_key = grad_key + jnp.einsum(
                "gqk,qge->kge", grad_score, query_rows, preferred_element_type=jnp.float32
            )
            query_grad = jnp.einsum(
                "gqk,kge->qge", grad_score, key_rows, preferred_element_type=jnp.float32
            ).astype(jnp.bfloat16)
            if bias is not None:
                grad_bias = grad_bias + bias_grad_block(grad_score.astype(jnp.float32), start)
            return ((grad_key, grad_value, grad_bias), query_grad)

        empty = jnp.zeros((keys, groups, width), jnp.float32)
        if bias is not None:
            bias_start = jnp.zeros((groups, length), jnp.float32)
        else:
            bias_start = jnp.zeros((1,), jnp.float32)
        (grad_key, grad_value, grad_bias), query_grads = lax.scan(
            per_block, (empty, empty, bias_start), jnp.arange(count, dtype=jnp.int32)
        )
        return (
            grad_key.astype(jnp.bfloat16),
            grad_value.astype(jnp.bfloat16),
            grad_bias,
            query_grads.reshape(length, groups, width),
        )

    grad_key, grad_value, grad_bias, query_grads = lax.map(
        per_sequence, jnp.arange(seqs, dtype=jnp.int32)
    )
    return (query_grads, grad_key, grad_value, jnp.sum(grad_bias, axis=0))


def shards(
    layer_in,
    encoder,
    decoder_ids,
    encoder_ids,
    rel_buckets,
    norm_self,
    self_qkv,
    self_out,
    rel_table,
    norm_cross,
    cross_q,
    cross_kv,
    cross_out,
    norm_ff,
    ff_in,
    ff_out,
    cotangent,
):
    seqs, local_len, width = layer_in.shape
    enc_local = encoder.shape[1]
    parts = lax.axis_size("seq")
    heads = self_qkv.shape[1]
    head_dim = self_qkv.shape[2] // 3
    own_heads = heads // parts
    rows = seqs * local_len
    enc_rows = seqs * enc_local
    bucket_count = rel_table.shape[0]
    (
        gain_first,
        qkv_full,
        mix_self,
        table_full,
        gain_second,
        query_full,
        pairs_full,
        mix_cross,
        gain_third,
        inner_full,
        outer_full,
    ) = (
        lax.all_gather(norm_self, "fsdp", axis=0, tiled=True),
        lax.all_gather(self_qkv, "fsdp", axis=0, tiled=True),
        lax.all_gather(self_out, "fsdp", axis=0, tiled=True),
        lax.all_gather(rel_table, "fsdp", axis=1, tiled=True),
        lax.all_gather(norm_cross, "fsdp", axis=0, tiled=True),
        lax.all_gather(cross_q, "fsdp", axis=0, tiled=True),
        lax.all_gather(cross_kv, "fsdp", axis=0, tiled=True),
        lax.all_gather(cross_out, "fsdp", axis=0, tiled=True),
        lax.all_gather(norm_ff, "fsdp", axis=0, tiled=True),
        lax.all_gather(ff_in, "fsdp", axis=0, tiled=True),
        lax.all_gather(ff_out, "fsdp", axis=0, tiled=True),
    )
    ids_full, enc_ids_full = (
        lax.all_gather(decoder_ids, "seq", axis=1, tiled=True),
        lax.all_gather(encoder_ids, "seq", axis=1, tiled=True),
    )
    stream = layer_in.astype(jnp.float32).reshape(rows, width)
    normed_first = norm_apply(stream, gain_first.astype(jnp.float32)).astype(jnp.bfloat16)
    qkv_tok = (
        jnp.einsum("td,dhe->the", normed_first, qkv_full, preferred_element_type=jnp.float32)
        .astype(jnp.bfloat16)
        .reshape(seqs, local_len, heads, 3 * head_dim)
    )
    qkv_heads = lax.all_to_all(qkv_tok, "seq", split_axis=2, concat_axis=1, tiled=True)
    query_self = qkv_heads[..., :head_dim]
    key_self = qkv_heads[..., head_dim : 2 * head_dim]
    value_self = qkv_heads[..., 2 * head_dim :]
    first_head = lax.axis_index("seq") * own_heads
    table_own = lax.dynamic_slice_in_dim(table_full.astype(jnp.float32), first_head, own_heads, 1)
    onehot = (rel_buckets[:, None] == jnp.arange(bucket_count, dtype=jnp.int32)[None, :]).astype(
        jnp.float32
    )
    bias = jnp.einsum("ln,ng->gl", onehot, table_own, precision=HIGH)
    out_self, total_self = attend_forward(
        query_self, key_self, value_self, ids_full, ids_full, bias
    )
    self_tok = lax.all_to_all(out_self, "seq", split_axis=1, concat_axis=2, tiled=True).reshape(
        rows, width
    )
    after_self = stream + jnp.dot(self_tok, mix_self, preferred_element_type=jnp.float32)
    normed_second = norm_apply(after_self, gain_second.astype(jnp.float32)).astype(jnp.bfloat16)
    query_tok = (
        jnp.dot(normed_second, query_full, preferred_element_type=jnp.float32)
        .astype(jnp.bfloat16)
        .reshape(seqs, local_len, heads, head_dim)
    )
    enc_flat = encoder.reshape(enc_rows, width)
    pairs_tok = (
        jnp.einsum("td,dhe->the", enc_flat, pairs_full, preferred_element_type=jnp.float32)
        .astype(jnp.bfloat16)
        .reshape(seqs, enc_local, heads, 2 * head_dim)
    )
    query_cross, pairs_cross = (
        lax.all_to_all(query_tok, "seq", split_axis=2, concat_axis=1, tiled=True),
        lax.all_to_all(pairs_tok, "seq", split_axis=2, concat_axis=1, tiled=True),
    )
    key_cross = pairs_cross[..., :head_dim]
    value_cross = pairs_cross[..., head_dim:]
    out_cross, total_cross = attend_forward(
        query_cross, key_cross, value_cross, ids_full, enc_ids_full, None
    )
    cross_tok = lax.all_to_all(out_cross, "seq", split_axis=1, concat_axis=2, tiled=True).reshape(
        rows, width
    )
    after_cross = after_self + jnp.dot(cross_tok, mix_cross, preferred_element_type=jnp.float32)
    normed_third = norm_apply(after_cross, gain_third.astype(jnp.float32)).astype(jnp.bfloat16)
    gate_up = jnp.dot(normed_third, inner_full, preferred_element_type=jnp.float32)
    hidden = gate_mix(gate_up).astype(jnp.bfloat16)
    layer_out = (
        (after_cross + jnp.dot(hidden, outer_full, preferred_element_type=jnp.float32))
        .astype(jnp.bfloat16)
        .reshape(seqs, local_len, width)
    )
    (
        gain_first,
        qkv_full,
        mix_self,
        table_full,
        gain_second,
        query_full,
        pairs_full,
        mix_cross,
        gain_third,
        inner_full,
        outer_full,
    ) = (
        lax.all_gather(norm_self, "fsdp", axis=0, tiled=True),
        lax.all_gather(self_qkv, "fsdp", axis=0, tiled=True),
        lax.all_gather(self_out, "fsdp", axis=0, tiled=True),
        lax.all_gather(rel_table, "fsdp", axis=1, tiled=True),
        lax.all_gather(norm_cross, "fsdp", axis=0, tiled=True),
        lax.all_gather(cross_q, "fsdp", axis=0, tiled=True),
        lax.all_gather(cross_kv, "fsdp", axis=0, tiled=True),
        lax.all_gather(cross_out, "fsdp", axis=0, tiled=True),
        lax.all_gather(norm_ff, "fsdp", axis=0, tiled=True),
        lax.all_gather(ff_in, "fsdp", axis=0, tiled=True),
        lax.all_gather(ff_out, "fsdp", axis=0, tiled=True),
    )
    grad_low = cotangent.reshape(rows, width)
    grad_outer = jnp.einsum("tf,td->fd", hidden, grad_low, preferred_element_type=jnp.float32)
    grad_hidden = jnp.einsum("td,fd->tf", grad_low, outer_full, preferred_element_type=jnp.float32)
    _, pull_mix = jax.vjp(gate_mix, gate_up)
    grad_gate_up = pull_mix(grad_hidden)[0].astype(jnp.bfloat16)
    grad_inner = jnp.einsum(
        "td,tf->df", normed_third, grad_gate_up, preferred_element_type=jnp.float32
    )
    grad_third_in = jnp.einsum(
        "tf,df->td", grad_gate_up, inner_full, preferred_element_type=jnp.float32
    )
    grad_from_third, grad_gain_third = norm_back(
        after_cross, gain_third.astype(jnp.float32), grad_third_in
    )
    grad_middle = grad_low.astype(jnp.float32) + grad_from_third
    middle_low = grad_middle.astype(jnp.bfloat16)
    grad_mix_cross = jnp.einsum(
        "te,td->ed", cross_tok, middle_low, preferred_element_type=jnp.float32
    )
    grad_cross_tok = (
        jnp.einsum("td,ed->te", middle_low, mix_cross, preferred_element_type=jnp.float32)
        .astype(jnp.bfloat16)
        .reshape(seqs, local_len, heads, head_dim)
    )
    grad_cross_heads = lax.all_to_all(
        grad_cross_tok, "seq", split_axis=2, concat_axis=1, tiled=True
    )
    grad_query_cross, grad_key_cross, grad_value_cross, _ = attend_backward(
        query_cross,
        key_cross,
        value_cross,
        ids_full,
        enc_ids_full,
        None,
        total_cross,
        grad_cross_heads,
    )
    grad_query_tok, grad_pairs_tok = (
        lax.all_to_all(grad_query_cross, "seq", split_axis=1, concat_axis=2, tiled=True),
        lax.all_to_all(
            jnp.concatenate([grad_key_cross, grad_value_cross], axis=-1),
            "seq",
            split_axis=1,
            concat_axis=2,
            tiled=True,
        ),
    )
    grad_query_tok = grad_query_tok.reshape(rows, width)
    grad_pairs_tok = grad_pairs_tok.reshape(enc_rows, heads, 2 * head_dim)
    grad_query_w = jnp.einsum(
        "td,te->de", normed_second, grad_query_tok, preferred_element_type=jnp.float32
    )
    grad_second_in = jnp.einsum(
        "te,de->td", grad_query_tok, query_full, preferred_element_type=jnp.float32
    )
    grad_pairs_w = jnp.einsum(
        "td,the->dhe", enc_flat, grad_pairs_tok, preferred_element_type=jnp.float32
    )
    grad_encoder = jnp.einsum(
        "the,dhe->td", grad_pairs_tok, pairs_full, preferred_element_type=jnp.float32
    ).reshape(seqs, enc_local, width)
    grad_from_second, grad_gain_second = norm_back(
        after_self, gain_second.astype(jnp.float32), grad_second_in
    )
    grad_upper = grad_middle + grad_from_second
    upper_low = grad_upper.astype(jnp.bfloat16)
    grad_mix_self = jnp.einsum("te,td->ed", self_tok, upper_low, preferred_element_type=jnp.float32)
    grad_self_tok = (
        jnp.einsum("td,ed->te", upper_low, mix_self, preferred_element_type=jnp.float32)
        .astype(jnp.bfloat16)
        .reshape(seqs, local_len, heads, head_dim)
    )
    grad_self_heads = lax.all_to_all(grad_self_tok, "seq", split_axis=2, concat_axis=1, tiled=True)
    grad_query_self, grad_key_self, grad_value_self, grad_bias = attend_backward(
        query_self, key_self, value_self, ids_full, ids_full, bias, total_self, grad_self_heads
    )
    grad_qkv_tok = lax.all_to_all(
        jnp.concatenate([grad_query_self, grad_key_self, grad_value_self], axis=-1),
        "seq",
        split_axis=1,
        concat_axis=2,
        tiled=True,
    ).reshape(rows, heads, 3 * head_dim)
    grad_qkv_w = jnp.einsum(
        "td,the->dhe", normed_first, grad_qkv_tok, preferred_element_type=jnp.float32
    )
    grad_first_in = jnp.einsum(
        "the,dhe->td", grad_qkv_tok, qkv_full, preferred_element_type=jnp.float32
    )
    grad_from_first, grad_gain_first = norm_back(
        stream, gain_first.astype(jnp.float32), grad_first_in
    )
    grad_layer_in = (grad_upper + grad_from_first).reshape(seqs, local_len, width)
    by_bucket = jnp.einsum("ln,gl->ng", onehot, grad_bias, precision=HIGH)
    grad_table = lax.dynamic_update_slice_in_dim(
        jnp.zeros((bucket_count, heads), jnp.float32), by_bucket, first_head, 1
    )
    (
        part_gain_first,
        part_qkv,
        part_mix_self,
        part_table,
        part_gain_second,
        part_query,
        part_pairs,
        part_mix_cross,
        part_gain_third,
        part_inner,
        part_outer,
    ) = (
        lax.psum_scatter(
            grad_gain_first.astype(jnp.bfloat16), "fsdp", scatter_dimension=0, tiled=True
        ).astype(jnp.float32),
        lax.psum_scatter(
            grad_qkv_w.astype(jnp.bfloat16), "fsdp", scatter_dimension=0, tiled=True
        ).astype(jnp.float32),
        lax.psum_scatter(
            grad_mix_self.astype(jnp.bfloat16), "fsdp", scatter_dimension=0, tiled=True
        ).astype(jnp.float32),
        lax.psum_scatter(
            grad_table.astype(jnp.bfloat16), "fsdp", scatter_dimension=1, tiled=True
        ).astype(jnp.float32),
        lax.psum_scatter(
            grad_gain_second.astype(jnp.bfloat16), "fsdp", scatter_dimension=0, tiled=True
        ).astype(jnp.float32),
        lax.psum_scatter(
            grad_query_w.astype(jnp.bfloat16), "fsdp", scatter_dimension=0, tiled=True
        ).astype(jnp.float32),
        lax.psum_scatter(
            grad_pairs_w.astype(jnp.bfloat16), "fsdp", scatter_dimension=0, tiled=True
        ).astype(jnp.float32),
        lax.psum_scatter(
            grad_mix_cross.astype(jnp.bfloat16), "fsdp", scatter_dimension=0, tiled=True
        ).astype(jnp.float32),
        lax.psum_scatter(
            grad_gain_third.astype(jnp.bfloat16), "fsdp", scatter_dimension=0, tiled=True
        ).astype(jnp.float32),
        lax.psum_scatter(
            grad_inner.astype(jnp.bfloat16), "fsdp", scatter_dimension=0, tiled=True
        ).astype(jnp.float32),
        lax.psum_scatter(
            grad_outer.astype(jnp.bfloat16), "fsdp", scatter_dimension=0, tiled=True
        ).astype(jnp.float32),
    )
    (
        total_gain_first,
        total_qkv,
        total_mix_self,
        total_table,
        total_gain_second,
        total_query,
        total_pairs,
        total_mix_cross,
        total_gain_third,
        total_inner,
        total_outer,
    ) = (
        lax.psum(part_gain_first.astype(jnp.bfloat16), "seq").astype(jnp.float32),
        lax.psum(part_qkv.astype(jnp.bfloat16), "seq").astype(jnp.float32),
        lax.psum(part_mix_self.astype(jnp.bfloat16), "seq").astype(jnp.float32),
        lax.psum(part_table.astype(jnp.bfloat16), "seq").astype(jnp.float32),
        lax.psum(part_gain_second.astype(jnp.bfloat16), "seq").astype(jnp.float32),
        lax.psum(part_query.astype(jnp.bfloat16), "seq").astype(jnp.float32),
        lax.psum(part_pairs.astype(jnp.bfloat16), "seq").astype(jnp.float32),
        lax.psum(part_mix_cross.astype(jnp.bfloat16), "seq").astype(jnp.float32),
        lax.psum(part_gain_third.astype(jnp.bfloat16), "seq").astype(jnp.float32),
        lax.psum(part_inner.astype(jnp.bfloat16), "seq").astype(jnp.float32),
        lax.psum(part_outer.astype(jnp.bfloat16), "seq").astype(jnp.float32),
    )
    return (
        layer_out,
        grad_layer_in,
        grad_encoder,
        total_gain_first,
        total_qkv,
        total_mix_self,
        total_table,
        total_gain_second,
        total_query,
        total_pairs,
        total_mix_cross,
        total_gain_third,
        total_inner,
        total_outer,
    )


def solution(mesh):
    in_specs = (
        P("fsdp", "seq", None),
        P("fsdp", "seq", None),
        P("fsdp", "seq"),
        P("fsdp", "seq"),
        P(),
        P("fsdp"),
        P("fsdp", None, None),
        P("fsdp", None),
        P(None, "fsdp"),
        P("fsdp"),
        P("fsdp", None),
        P("fsdp", None, None),
        P("fsdp", None),
        P("fsdp"),
        P("fsdp", None),
        P("fsdp", None),
        P("fsdp", "seq", None),
    )
    out_specs = (
        P("fsdp", "seq", None),
        P("fsdp", "seq", None),
        P("fsdp", "seq", None),
        P("fsdp"),
        P("fsdp", None, None),
        P("fsdp", None),
        P(None, "fsdp"),
        P("fsdp"),
        P("fsdp", None),
        P("fsdp", None, None),
        P("fsdp", None),
        P("fsdp"),
        P("fsdp", None),
        P("fsdp", None),
    )
    return jax.shard_map(shards, mesh=mesh, in_specs=in_specs, out_specs=out_specs, check_vma=False)
```

profile of v0, /device:TPU:1, one launch (start us, length us, event | category | flops | bytes accessed | tf_op | source)
XLA Modules:
  0.0 1955.8 jit_solution(13596493134065745694)
XLA Ops:
  19.1 40.3 %all-gather.12.cloned.1.call-done = bf16[1024,16,192]{0,2,1:T(8,128)(2,1)} async-done(((bf16[256,16,192]{0,2,1:T(8,128)(2,1)}), bf16[1024,16,192]{0,2,1:T(8,128)(2,1)}) %all-gather.12.cloned.1.call-update) | async-done | bytes 6291472 | tf_op jit(solution)/shard_map/all_gather | solution.py:190
  76.9 32.3 %all_gather.49 = s32[1,2048]{1,0:T(1,128)S(1)} all-gather(s32[1,256]{1,0:T(1,128)S(1)} %copy-done.68), channel_id=1, replica_groups=mesh['seq'=8,'fsdp'=4] {'seq'}, dimensions={1}, use_global_device_ids=true | all-gather | bytes 9216 | tf_op jit(solution)/shard_map/all_gather | solution.py:202
  113.0 364.7 %while.91 = (s32[]{:T(128)}, bf16[4,512,2,64]{1,3,2,0:T(8,128)(2,1)}, f32[4,2,512]{2,1,0:T(2,128)S(1)}, s32[4]{0:T(128)S(1)}, s32[1,2048]{1,0:T(1,128)S(1)}, /*i...) while((s32[]{:T(128)}, ...), condition=%wide.region_4.6_spmd, body=%wide.region_1.5_spmd.sunk | while | flops 556931072 | bytes 133711200 | solution.py:84
  139.6 22.5 %copy.197 = f32[1,2,513,2560]{3,1,2,0:T(2,128)S(1)} copy(f32[1,2,513,2560]{3,2,1,0:T(8,128)S(1)} %broadcast_bitcast_fusion.4) | data formatting | bytes 21012480 | tf_op jit(solution)/shard_map/while
  166.4 25.6 %reshape.658 = f32[2620416]{0:T(1024)} reshape(f32[2,1310208]{1,0:T(2,128)} %slice.113) | data formatting | bytes 20963328 | tf_op jit(solution)/shard_map/while
  227.8 22.5 %copy.197 = f32[1,2,513,2560]{3,1,2,0:T(2,128)S(1)} copy(f32[1,2,513,2560]{3,2,1,0:T(8,128)S(1)} %broadcast_bitcast_fusion.4) | data formatting | bytes 21012480 | tf_op jit(solution)/shard_map/while
  254.6 24.3 %reshape.658 = f32[2620416]{0:T(1024)} reshape(f32[2,1310208]{1,0:T(2,128)} %slice.113) | data formatting | bytes 20963328 | tf_op jit(solution)/shard_map/while
  314.6 22.5 %copy.197 = f32[1,2,513,2560]{3,1,2,0:T(2,128)S(1)} copy(f32[1,2,513,2560]{3,2,1,0:T(8,128)S(1)} %broadcast_bitcast_fusion.4) | data formatting | bytes 21012480 | tf_op jit(solution)/shard_map/while
  341.4 24.3 %reshape.658 = f32[2620416]{0:T(1024)} reshape(f32[2,1310208]{1,0:T(2,128)} %slice.113) | data formatting | bytes 20963328 | tf_op jit(solution)/shard_map/while
  401.5 22.5 %copy.197 = f32[1,2,513,2560]{3,1,2,0:T(2,128)S(1)} copy(f32[1,2,513,2560]{3,2,1,0:T(8,128)S(1)} %broadcast_bitcast_fusion.4) | data formatting | bytes 21012480 | tf_op jit(solution)/shard_map/while
  428.3 24.3 %reshape.658 = f32[2620416]{0:T(1024)} reshape(f32[2,1310208]{1,0:T(2,128)} %slice.113) | data formatting | bytes 20963328 | tf_op jit(solution)/shard_map/while
  537.5 24.2 %while.92 = (s32[]{:T(128)}, bf16[4,512,2,64]{1,3,2,0:T(8,128)(2,1)S(1)}, f32[4,2,512]{2,1,0:T(2,128)}, s32[4]{0:T(128)S(1)}, s32[1,2048]{1,0:T(1,128)S(1)}, /*i...) while((s32[]{:T(128)}, ...), condition=%wide.region_9.11_spmd, body=%wide.region_6.10_spmd.sunk | while | flops 139262992 | bytes 7905612 | solution.py:84
  639.4 58.1 %while.93 = (s32[]{:T(128)}, f32[512,2,64]{0,2,1:T(8,128)}, f32[512,2,64]{0,2,1:T(8,128)}, bf16[4,512,2,64]{1,3,2,0:T(8,128)(2,1)}, s32[4]{0:T(128)S(1)}, /*inde...) while((s32[]{:T(128)}, f32[512,2,64]{0,2,1:T(8,128)}, ...), condition=%wide.region_14.16_spmd.clone, body=%wide.region_12.15_spmd.clone.sunk | while | flops 340327424 | bytes 26767868 | solution.py:132
  701.4 17.8 all_to_all.159
  775.0 643.0 %while.94 = (s32[]{:T(128)}, f32[2048,2,64]{0,2,1:T(8,128)S(1)}, f32[2048,2,64]{0,2,1:T(8,128)}, f32[2,2048]{0,1:T(8,128)}, bf16[4,512,2,64]{1,3,2,0:T(8,128)(2,...) while((s32[]{:T(128)}, f32[2048,2,64]{0,2,1:T(8,128)S(1)}, ...), condition=%wide.region_19.21_spmd.clone, body=%wide.region_16.20_spmd.clone.sunk | while | flops 1370682368 | bytes 294168032 | solution.py:132
  795.1 22.5 %copy.200 = f32[1,2,513,2560]{3,1,2,0:T(2,128)S(1)} copy(f32[1,2,513,2560]{3,2,1,0:T(8,128)S(1)} %broadcast_bitcast_fusion.5) | data formatting | bytes 21012480 | tf_op jit(solution)/shard_map/while/body/eval_jaxpr/while
  822.1 24.3 %reshape.665 = f32[2620416]{0:T(1024)} reshape(f32[2,1310208]{1,0:T(2,128)} %slice.116) | data formatting | bytes 20963328 | tf_op jit(solution)/shard_map/while/body/eval_jaxpr/while
  846.4 15.1 reshape.666
  954.0 22.5 %copy.200 = f32[1,2,513,2560]{3,1,2,0:T(2,128)S(1)} copy(f32[1,2,513,2560]{3,2,1,0:T(8,128)S(1)} %broadcast_bitcast_fusion.5) | data formatting | bytes 21012480 | tf_op jit(solution)/shard_map/while/body/eval_jaxpr/while
  981.0 24.2 %reshape.665 = f32[2620416]{0:T(1024)} reshape(f32[2,1310208]{1,0:T(2,128)} %slice.116) | data formatting | bytes 20963328 | tf_op jit(solution)/shard_map/while/body/eval_jaxpr/while
  1005.3 15.1 reshape.666
  1112.2 22.5 %copy.200 = f32[1,2,513,2560]{3,1,2,0:T(2,128)S(1)} copy(f32[1,2,513,2560]{3,2,1,0:T(8,128)S(1)} %broadcast_bitcast_fusion.5) | data formatting | bytes 21012480 | tf_op jit(solution)/shard_map/while/body/eval_jaxpr/while
  1139.2 24.2 %reshape.665 = f32[2620416]{0:T(1024)} reshape(f32[2,1310208]{1,0:T(2,128)} %slice.116) | data formatting | bytes 20963328 | tf_op jit(solution)/shard_map/while/body/eval_jaxpr/while
  1163.4 15.3 reshape.666
  1270.3 22.5 %copy.200 = f32[1,2,513,2560]{3,1,2,0:T(2,128)S(1)} copy(f32[1,2,513,2560]{3,2,1,0:T(8,128)S(1)} %broadcast_bitcast_fusion.5) | data formatting | bytes 21012480 | tf_op jit(solution)/shard_map/while/body/eval_jaxpr/while
  1297.6 24.2 %reshape.665 = f32[2620416]{0:T(1024)} reshape(f32[2,1310208]{1,0:T(2,128)} %slice.116) | data formatting | bytes 20963328 | tf_op jit(solution)/shard_map/while/body/eval_jaxpr/while
  1321.8 15.0 reshape.666
  1427.2 50.4 %all_to_all.161 = bf16[1,2048,2,192]{3,2,0,1:T(2,128)(2,1)} all-to-all(bf16[1,2048,2,192]{3,2,0,1:T(2,128)(2,1)S(1)} %copy.161), channel_id=1, replica_groups=mesh['seq'=8,'fsdp'=4] {'seq'}, dimensions={1} | all-to-all | bytes 3145728 | tf_op jit(solution)/shard_map/all_to_all | solution.py:363
  1509.0 46.9 %reduce-scatter.8.cloned.1.call-done = bf16[256,16,192]{0,2,1:T(8,128)(2,1)} async-done(((bf16[1024,16,192]{0,2,1:T(8,128)(2,1)}), bf16[256,16,192]{0,2,1:T(8,128)(2,1)}) %reduce-scatter.8.cloned.1.call-update) | async-done | bytes 1572880 | tf_op jit(solution)/shard_map/reduce_scatter | solution.py:400
  1556.0 94.6 %reduce-scatter.18.cloned.1.call-done = bf16[256,5632]{1,0:T(8,128)(2,1)} async-done(((bf16[1024,5632]{1,0:T(8,128)(2,1)}), bf16[256,5632]{1,0:T(8,128)(2,1)}) %reduce-scatter.18.cloned.1.call-update) | async-done | bytes 2883600 | tf_op jit(solution)/shard_map/reduce_scatter | solution.py:424
  1675.9 18.9 all-reduce.9
  1699.8 234.4 %all-reduce.14.cloned.1.call-done = (bf16[256,16,128]{0,2,1:T(8,128)(2,1)}, bf16[256,16,192]{0,2,1:T(8,128)(2,1)}, bf16[256,1024]{1,0:T(8,128)(2,1)}, bf16[256,1...) async-done(((bf16[256,16,128]{0,2,1:T(8,128)(2,1)}, bf16[256,16,192]{0,2,1:T(8,128)(2,1)}, ...) | async-done | bytes 8519696 | tf_op jit(solution)/shard_map/psum | solution.py:450
  (657 shorter events, 902.9 us)
Async XLA Ops:
  7.2 491.2 %copy-start = (bf16[1,64,1024]{2,1,0:T(8,128)(2,1)S(1)}, bf16[1,64,1024]{2,1,0:T(8,128)(2,1)}, u32[]{:S(2)}) copy-start(bf16[1,64,1024]{2,1,0:T(8,128)(2,1)} %param.28) | copy-start | bytes 393220
  7.2 52.1 %all-gather.12.cloned.1.call-start = ((), (), s32[]{:S(2)}) async-start(), calls=%async_computation.17 | async-start | bytes 7864320 | tf_op jit(solution)/shard_map/all_gather | solution.py:190
  8.0 490.5 %all-gather.18.cloned.1.call-start = ((), (), s32[]{:S(2)}) async-start(), calls=%async_computation.20 | async-start | bytes 5242880 | tf_op jit(solution)/shard_map/all_gather | solution.py:195
  10.5 499.0 %all-gather.14.cloned.1.call-start = ((), (), s32[]{:S(2)}) async-start(), calls=%async_computation.18 | async-start | bytes 2621440 | tf_op jit(solution)/shard_map/all_gather | solution.py:191
  11.2 501.0 %all-gather.16.cloned.1.call-start = ((), (), s32[]{:S(2)}) async-start(), calls=%async_computation.19 | async-start | bytes 2621440 | tf_op jit(solution)/shard_map/all_gather | solution.py:194
  11.8 568.9 %all-gather.20.cloned.1.call-start = ((), (), s32[]{:S(2)}) async-start(), calls=%async_computation.21 | async-start | bytes 2621440 | tf_op jit(solution)/shard_map/all_gather | solution.py:196
  18.3 45.8 %copy-start.50 = (f32[4,1,256]{2,1,0:T(1,128)}, f32[4,1,256]{2,1,0:T(1,128)S(1)}, u32[]{:S(2)}) copy-start(f32[4,1,256]{2,1,0:T(1,128)S(1)} %convert_element_type.303) | copy-start | bytes 12292
  19.1 45.1 %copy-start.57 = (f32[256]{0:T(256)}, f32[256]{0:T(256)S(1)}, u32[]{:S(2)}) copy-start(f32[256]{0:T(256)S(1)} %fusion.128) | copy-start | bytes 3076
  65.5 43.7 %copy-start.59 = (s32[2048]{0:T(1024)S(1)}, s32[2048]{0:T(1024)}, u32[]{:S(2)}) copy-start(s32[2048]{0:T(1024)} %param.31) | copy-start | bytes 24580
  65.5 45.1 %all-to-all-start = ((bf16[1,256,16,192]{1,3,0,2:T(8,128)(2,1)}), bf16[1,256,16,192]{1,3,0,2:T(8,128)(2,1)S(1)}, u32[]{:S(2)}, u32[]{:S(2)}) async-start(bf16[1,256,16,192]{1,3,0,2:T(8,128)(2,1)} %convert_bitcast_fusion.1), calls=%async_computation | async-start | bytes 3145728 | tf_op jit(solution)/shard_map/all_to_all | solution.py:212
  70.9 512.3 %all-gather.22.cloned.1.call-start = ((), (), s32[]{:S(2)}) async-start(), calls=%async_computation.22 | async-start | bytes 14417920 | tf_op jit(solution)/shard_map/all_gather | solution.py:198
  481.7 20.4 %all-to-all-start.1 = ((bf16[8,2,16384]{2,1,0:T(2,128)(2,1)}), bf16[8,2,16384]{2,1,0:T(2,128)(2,1)S(1)}, u32[]{:S(2)}, u32[]{:S(2)}) async-start(bf16[8,2,16384]{2,1,0:T(2,128)(2,1)} %reshape.637), calls=%async_computation.1 | async-start | bytes 1048576 | tf_op jit(solution)/shard_map/all_to_all | solution.py:225
  502.2 13.8 all-to-all-start.3
  512.1 68.5 %copy-start.8 = (f32[256,1024]{1,0:T(8,128)}, f32[256,1024]{1,0:T(8,128)S(1)}, u32[]{:S(2)}) copy-start(f32[256,1024]{1,0:T(8,128)S(1)} %get-tuple-element.1167) | copy-start | bytes 3145732
  516.0 20.0 %all-to-all-start.2 = ((bf16[1,256,16,64]{1,3,0,2:T(8,128)(2,1)}), bf16[1,256,16,64]{1,3,0,2:T(8,128)(2,1)S(1)}, u32[]{:S(2)}, u32[]{:S(2)}) async-start(bf16[1,256,16,64]{1,3,0,2:T(8,128)(2,1)} %bitcast.39), calls=%async_computation.2 | async-start | bytes 1048576 | tf_op jit(solution)/shard_map/all_to_all | solution.py:242
  521.4 71.5 %all-gather.24.cloned.1.call-start = ((), (), s32[]{:S(2)}) async-start(), calls=%async_computation.23 | async-start | bytes 7208960 | tf_op jit(solution)/shard_map/all_gather | solution.py:199
  563.9 15.1 all-to-all-start.4
  575.1 38.7 %copy-start.48 = (f32[4,1,256]{2,1,0:T(1,128)}, f32[4,1,256]{2,1,0:T(1,128)S(1)}, u32[]{:S(2)}) copy-start(f32[4,1,256]{2,1,0:T(1,128)S(1)} %convert_element_type.305) | copy-start | bytes 12292
  583.1 30.7 %copy-start.18 = (f32[256,1024]{1,0:T(8,128)}, f32[256,1024]{1,0:T(8,128)S(1)}, u32[]{:S(2)}) copy-start(f32[256,1024]{1,0:T(8,128)S(1)} %get-tuple-element.1169) | copy-start | bytes 3145732
  583.1 30.7 %copy-start.55 = (f32[256]{0:T(256)}, f32[256]{0:T(256)S(1)}, u32[]{:S(2)}) copy-start(f32[256]{0:T(256)S(1)} %fusion.130) | copy-start | bytes 3076
  617.5 19.7 %all-to-all-start.5 = ((bf16[1,256,16,64]{1,3,0,2:T(8,128)(2,1)}), bf16[1,256,16,64]{1,3,0,2:T(8,128)(2,1)S(1)}, u32[]{:S(2)}, u32[]{:S(2)}) async-start(bf16[1,256,16,64]{1,3,0,2:T(8,128)(2,1)} %bitcast.57), calls=%async_computation.5 | async-start | bytes 1048576 | tf_op jit(solution)/shard_map/all_to_all | solution.py:311
  623.9 885.0 %reduce-scatter.16.cloned.1.call-start = ((), (), s32[]{:S(2)}) async-start(), calls=%async_computation.28 | async-start | bytes 2621440 | tf_op jit(solution)/shard_map/reduce_scatter | solution.py:418
  626.2 882.8 %reduce-scatter.10.cloned.1.call-start = ((), (), s32[]{:S(2)}) async-start(), calls=%async_computation.25 | async-start | bytes 2621440 | tf_op jit(solution)/shard_map/reduce_scatter | solution.py:403
  701.4 26.1 %copy-start.54 = (f32[256]{0:T(256)S(1)}, f32[256]{0:T(256)}, u32[]{:S(2)}) copy-start(f32[256]{0:T(256)} %copy-done.53) | copy-start | bytes 3076
  732.0 776.9 %reduce-scatter.12.cloned.1.call-start = ((), (), s32[]{:S(2)}) async-start(), calls=%async_computation.26 | async-start | bytes 2621440 | tf_op jit(solution)/shard_map/reduce_scatter | solution.py:412
  734.3 774.7 %reduce-scatter.14.cloned.1.call-start = ((), (), s32[]{:S(2)}) async-start(), calls=%async_computation.27 | async-start | bytes 5242880 | tf_op jit(solution)/shard_map/reduce_scatter | solution.py:415
  754.3 18.2 all-to-all-start.7
  759.1 749.9 %reduce-scatter.20.cloned.1.call-start = ((), (), s32[]{:S(2)}) async-start(), calls=%async_computation.30 | async-start | bytes 7208960 | tf_op jit(solution)/shard_map/reduce_scatter | solution.py:427
  763.4 792.5 %reduce-scatter.8.cloned.1.call-start = ((), (), s32[]{:S(2)}) async-start(), calls=%async_computation.24 | async-start | bytes 7864320 | tf_op jit(solution)/shard_map/reduce_scatter | solution.py:400
  1497.1 153.5 %reduce-scatter.18.cloned.1.call-start = ((), (), s32[]{:S(2)}) async-start(), calls=%async_computation.29 | async-start | bytes 14417920 | tf_op jit(solution)/shard_map/reduce_scatter | solution.py:424
  1508.9 425.4 %all-reduce.14.cloned.1.call-start = ((), (), s32[]{:S(2)}) async-start(), calls=%async_computation.31 | async-start | bytes 17039360 | tf_op jit(solution)/shard_map/psum | solution.py:450
  1662.5 34.5 %copy-start.62 = (f32[256]{0:T(256)S(1)}, f32[256]{0:T(256)}, u32[]{:S(2)}) copy-start(f32[256]{0:T(256)} %copy-done.61) | copy-start | bytes 3076
  (99 other events, 587.6 us)
Sparse Core Ops, SparseCore 0:
  9.6 49.7 all-gather.11
  61.5 34.4 all-gather.17
  97.6 22.5 all-gather.13
  121.6 22.5 all-gather.15
  145.7 22.5 all-gather.19
  169.7 76.1 all-gather.21
  523.8 45.5 all-gather.23
  627.3 32.8 reduce-scatter.15
  732.1 30.9 reduce-scatter.9
  765.5 31.4 reduce-scatter.11
  799.6 44.5 reduce-scatter.13
  847.1 54.8 reduce-scatter.19
  1497.2 58.6 reduce-scatter.7
  1558.4 92.1 reduce-scatter.17
  1655.9 278.3 all-reduce.13
where the time goes:
time: 1970 us; the launch traced here: 1960 us
  local copies, waits for them, and re-layouts  796 us (40%)
  waiting for transfers between devices  444 us (23%)
  matrix products  268 us (14%)
  blocking collectives  179 us (9%)
  other arithmetic  146 us (7%)
  loops' own time  64.3 us (3%)
  starting transfers between devices  41.1 us (2%)
    while x108, local copies, waits for them, and re-layouts  448 us
    psum x1, waiting for transfers between devices, shards(): lax.psum(part_pairs.astype(jnp.bfloat16), 'seq').astype(jnp.float32)  234 us
    reshape x8, local copies, waits for them, and re-layouts, bias_block(): return tiled.reshape(groups, block, period - 1)[:, :, :length]  120 us
    reduce_scatter x1, waiting for transfers between devices, shards(): lax.psum_scatter(grad_inner.astype(jnp.bfloat16), 'fsdp', scatter_dimensi...  94.6 us
    dot_general x16, matrix products, score_rows(): jnp.einsum('qge,kge->gqk', query_rows, key_rows, preferred_element_type=j...  71.7 us
    all_to_all x1, blocking collectives, shards(): lax.all_to_all(jnp.concatenate([grad_query_self, grad_key_self, grad_valu...  50.4 us
    gather x8, local copies, waits for them, and re-layouts, bias_block(): circle = jnp.take(distance_bias, places, axis=1)  48.9 us
    reduce_scatter x1, waiting for transfers between devices, shards(): lax.psum_scatter(grad_qkv_w.astype(jnp.bfloat16), 'fsdp', scatter_dimensi...  46.9 us
  transfers between devices with their start and end apart: 22, of which 7 were waited for; matrix products, arithmetic and copies ran while one was open for 59% of the time, Pallas kernels for 0%

commit v1 on v0

v1 whole, which is shorter than its diff:
```python
import functools

import jax
import jax.numpy as jnp
from jax import lax
from jax.experimental import pallas as pl
from jax.experimental.pallas import tpu as pltpu
from jax.sharding import PartitionSpec as P

EPS = 1e-06
HIGH = lax.Precision.HIGHEST
MASKED = -1e30
DOCS = 4

BQ = 256
REACH = 1024


def blk(index, size):
    return pl.ds(pl.multiple_of(index * size, size), size)


def turn(value):
    return jnp.transpose(value.astype(jnp.float32), (1, 0))


def bias_tiles(ext_ref, tile_ref, own, bk):
    span = BQ + bk
    for h in range(own):
        for t in range(tile_ref.shape[1]):
            first = t * bk
            line = jnp.broadcast_to(ext_ref[h : h + 1, first : first + span], (bk, span))
            tile_ref[h, t] = pltpu.roll(line, 0, 1, stride=1, stride_axis=0)[:, bk:]


def tile_count(bk):
    return BQ // bk + REACH // bk


def unpack(ref, own, width, picks, flips, base):
    block = 256

    def one(b, _):
        rows = blk(b, block)
        value = ref[rows, :]
        if flips:
            flat = turn(value).astype(jnp.bfloat16)
            for target, piece in flips:
                for h in range(own):
                    at = h * width + piece * 64
                    target[base + h, :, rows] = flat[at : at + 64]
        for target, piece in picks:
            for h in range(own):
                at = h * width + piece * 64
                target[base + h, rows, :] = value[:, at : at + 64]
        return 0

    lax.fori_loop(0, ref.shape[0] // block, one, 0)


def dot(a, b):
    return jnp.dot(a, b, preferred_element_type=jnp.float32)


def score(own_index, key_tile, query_t, tile_ref, t, low, high, first_key):
    value = dot(key_tile, query_t)
    place = lax.broadcasted_iota(jnp.int32, value.shape, 0)
    keep = place >= low - first_key
    if high is not None:
        keep = keep & (place < high - first_key)
    else:
        value = value + tile_ref[own_index, t]
    return jnp.where(keep, value, MASKED)


def forward_body(own, bk, causal, lim_ref, rows_ref, q_t, k_rows, v_t, tile_ref, o_ref, ot_ref, lse_ref):
    length = o_ref.shape[0]

    def q_block(i, _):
        cols = blk(i, BQ)
        queries = [q_t[h, :, cols] for h in range(own)]
        low = rows_ref[0:1, cols]
        high = None if causal else rows_ref[1:2, cols]

        def k_block(j, carry):
            keys = blk(j, bk)
            t = i * (BQ // bk) - j + (BQ // bk - 1)
            out = []
            for h in range(own):
                top, total, acc = carry[h]
                s = score(h, k_rows[h, keys, :], queries[h], tile_ref, t, low, high, j * bk)
                new_top = jnp.maximum(top, jnp.max(s, axis=0, keepdims=True))
                p = jnp.exp(s - new_top)
                scale = jnp.exp(top - new_top)
                total = total * scale + jnp.sum(p, axis=0, keepdims=True)
                acc = acc * scale + dot(v_t[h, :, keys], p.astype(jnp.bfloat16))
                out.append((new_top, total, acc))
            return tuple(out)

        start = tuple(
            (
                jnp.full((1, BQ), MASKED, jnp.float32),
                jnp.zeros((1, BQ), jnp.float32),
                jnp.zeros((64, BQ), jnp.float32),
            )
            for _ in range(own)
        )
        ends = lax.fori_loop(lim_ref[0, i], lim_ref[1, i], k_block, start)
        for h in range(own):
            top, total, acc = ends[h]
            ot_ref[h * 64 : h * 64 + 64, cols] = acc / total
            lse_ref[h : h + 1, cols] = top + jnp.log(total)
        o_ref[cols, :] = turn(ot_ref[:, cols]).astype(jnp.bfloat16)
        return 0

    lax.fori_loop(0, length // BQ, q_block, 0)


def self_forward_kernel(own, bk, lim_ref, rows_ref, ext_ref, x_ref, o_ref, ot_ref, lse_ref, q_t, k_rows, v_t, tile_ref):
    bias_tiles(ext_ref, tile_ref, own, bk)
    unpack(x_ref, own, 192, [(k_rows, 1)], [(q_t, 0), (v_t, 2)], 0)
    forward_body(own, bk, True, lim_ref, rows_ref, q_t, k_rows, v_t, tile_ref, o_ref, ot_ref, lse_ref)


def cross_forward_kernel(own, bk, lim_ref, rows_ref, q_ref, kv_ref, o_ref, ot_ref, lse_ref, q_t, k_rows, v_t):
    unpack(q_ref, own, 64, [], [(q_t, 0)], 0)
    unpack(kv_ref, own, 128, [(k_rows, 0)], [(v_t, 1)], 0)
    forward_body(own, bk, False, lim_ref, rows_ref, q_t, k_rows, v_t, None, o_ref, ot_ref, lse_ref)


def backward_body(
    own, bk, causal, lim_ref, rows_ref, do_ref, ot_ref, lse_ref,
    q_t, q_rows, k_t, k_rows, v_rows, do_t, do_rows, tile_ref, sum_ref, dq_t, dk, dv,
):
    length = do_ref.shape[0]
    dk[...] = jnp.zeros_like(dk)
    dv[...] = jnp.zeros_like(dv)
    if causal:
        sum_ref[...] = jnp.zeros_like(sum_ref)

    def q_block(i, _):
        cols = blk(i, BQ)
        low = rows_ref[0:1, cols]
        high = None if causal else rows_ref[1:2, cols]
        per_head = []
        for h in range(own):
            grad_t = do_t[h, :, cols]
            delta = jnp.sum(
                grad_t.astype(jnp.float32) * ot_ref[h * 64 : h * 64 + 64, cols], axis=0, keepdims=True
            )
            per_head.append((q_t[h, :, cols], grad_t, delta, lse_ref[h : h + 1, cols]))

        def k_block(j, carry):
            keys = blk(j, bk)
            t = i * (BQ // bk) - j + (BQ // bk - 1)
            out = []
            for h in range(own):
                query_t, grad_t, delta, lse = per_head[h]
                s = score(h, k_rows[h, keys, :], query_t, tile_ref, t, low, high, j * bk)
                p = jnp.exp(s - lse)
                dp = dot(v_rows[h, keys, :], grad_t)
                ds = (p * (dp - delta)).astype(jnp.bfloat16)
                dv[h, keys, :] += dot(p.astype(jnp.bfloat16), do_rows[h, cols, :])
                dk[h, keys, :] += dot(ds, q_rows[h, cols, :])
                if causal:
                    sum_ref[h, t] += ds.astype(jnp.float32)
                out.append(carry[h] + dot(k_t[h, :, keys], ds))
            return tuple(out)

        ends = lax.fori_loop(
            lim_ref[0, i],
            lim_ref[1, i],
            k_block,
            tuple(jnp.zeros((64, BQ), jnp.float32) for _ in range(own)),
        )
        for h in range(own):
            dq_t[h * 64 : h * 64 + 64, cols] = ends[h]
        return 0

    lax.fori_loop(0, length // BQ, q_block, 0)


def diagonal_sums(sum_ref, u_ref, own, bk):
    flip = (
        lax.broadcasted_iota(jnp.int32, (bk, bk), 0) + lax.broadcasted_iota(jnp.int32, (bk, bk), 1) == bk - 1
    ).astype(jnp.float32)
    for h in range(own):
        for t in range(sum_ref.shape[1]):
            upside = jnp.dot(flip, sum_ref[h, t], precision=HIGH, preferred_element_type=jnp.float32)
            wide = jnp.concatenate([upside, jnp.zeros((bk, bk), jnp.float32)], axis=1)
            aligned = pltpu.roll(wide, 0, 1, stride=1, stride_axis=0)
            u_ref[h, t : t + 1, :] = jnp.sum(aligned, axis=0, keepdims=True)


def self_backward_kernel(
    own, bk, lim_ref, rows_ref, ext_ref, x_ref, do_ref, ot_ref, lse_ref, dx_ref, u_ref,
    q_t, q_rows, k_t, k_rows, v_rows, do_t, do_rows, tile_ref, sum_ref, dq_t, dk, dv,
):
    bias_tiles(ext_ref, tile_ref, own, bk)
    unpack(x_ref, own, 192, [(q_rows, 0), (k_rows, 1), (v_rows, 2)], [(q_t, 0), (k_t, 1)], 0)
    unpack(do_ref, own, 64, [(do_rows, 0)], [(do_t, 0)], 0)
    backward_body(
        own, bk, True, lim_ref, rows_ref, do_ref, ot_ref, lse_ref,
        q_t, q_rows, k_t, k_rows, v_rows, do_t, do_rows, tile_ref, sum_ref, dq_t, dk, dv,
    )
    diagonal_sums(sum_ref, u_ref, own, bk)

    def pack(b, _):
        rows = blk(b, 256)
        dq = turn(dq_t[:, rows])
        pieces = []
        for h in range(own):
            pieces += [dq[:, h * 64 : h * 64 + 64], dk[h, rows, :], dv[h, rows, :]]
        dx_ref[rows, :] = jnp.concatenate(pieces, axis=1).astype(jnp.bfloat16)
        return 0

    lax.fori_loop(0, x_ref.shape[0] // 256, pack, 0)


def cross_backward_kernel(
    own, bk, lim_ref, rows_ref, q_ref, kv_ref, do_ref, ot_ref, lse_ref, dq_ref, dkv_ref,
    q_t, q_rows, k_t, k_rows, v_rows, do_t, do_rows, dq_t, dk, dv,
):
    unpack(q_ref, own, 64, [(q_rows, 0)], [(q_t, 0)], 0)
    unpack(kv_ref, own, 128, [(k_rows, 0), (v_rows, 1)], [(k_t, 0)], 0)
    unpack(do_ref, own, 64, [(do_rows, 0)], [(do_t, 0)], 0)
    backward_body(
        own, bk, False, lim_ref, rows_ref, do_ref, ot_ref, lse_ref,
        q_t, q_rows, k_t, k_rows, v_rows, do_t, do_rows, None, None, dq_t, dk, dv,
    )

    def pack_q(b, _):
        rows = blk(b, 256)
        dq_ref[rows, :] = turn(dq_t[:, rows]).astype(jnp.bfloat16)
        return 0

    def pack_kv(b, _):
        rows = blk(b, 256)
        pieces = []
        for h in range(own):
            pieces += [dk[h, rows, :], dv[h, rows, :]]
        dkv_ref[rows, :] = jnp.concatenate(pieces, axis=1).astype(jnp.bfloat16)
        return 0

    lax.fori_loop(0, q_ref.shape[0] // 256, pack_q, 0)
    lax.fori_loop(0, kv_ref.shape[0] // 256, pack_kv, 0)


SMEM = pl.BlockSpec(memory_space=pltpu.SMEM)
VMEM = pl.BlockSpec(memory_space=pltpu.VMEM)
bf16, f32 = jnp.bfloat16, jnp.float32


def call(body, name, operands, outs, scratch, flops):
    size = sum(v.size * v.dtype.itemsize for v in operands)
    return pl.pallas_call(
        body,
        name=name,
        out_shape=[jax.ShapeDtypeStruct(s, d) for s, d in outs],
        in_specs=[SMEM] + [VMEM] * (len(operands) - 1),
        out_specs=[VMEM] * len(outs),
        scratch_shapes=[pltpu.VMEM(s, d) for s, d in scratch],
        compiler_params=pltpu.CompilerParams(vmem_limit_bytes=40 << 20),
        cost_estimate=pl.CostEstimate(flops=flops, bytes_accessed=2 * size, transcendentals=flops // 256),
    )(*operands)


def self_forward(limits, rows, ext, x, bk=256):
    length, own = x.shape[0], x.shape[1] // 192
    return call(
        functools.partial(self_forward_kernel, own, bk),
        "self_forward",
        [limits, rows, ext, x],
        [((length, own * 64), bf16), ((own * 64, length), f32), ((own, length), f32)],
        [
            ((own, 64, length), bf16),
            ((own, length, 64), bf16),
            ((own, 64, length), bf16),
            ((own, tile_count(bk), bk, BQ), f32),
        ],
        length * length * own * 64,
    )


def cross_forward(limits, rows, q, kv, bk=256):
    length, own, keys = q.shape[0], q.shape[1] // 64, kv.shape[0]
    return call(
        functools.partial(cross_forward_kernel, own, bk),
        "cross_forward",
        [limits, rows, q, kv],
        [((length, own * 64), bf16), ((own * 64, length), f32), ((own, length), f32)],
        [((own, 64, length), bf16), ((own, keys, 64), bf16), ((own, 64, keys), bf16)],
        length * keys * own * 128,
    )


def self_backward(limits, rows, ext, x, grad, o_t, lse, bk=256):
    length, own = x.shape[0], x.shape[1] // 192
    return call(
        functools.partial(self_backward_kernel, own, bk),
        "self_backward",
        [limits, rows, ext, x, grad, o_t, lse],
        [((length, own * 192), bf16), ((own, tile_count(bk), BQ + bk), f32)],
        [
            ((own, 64, length), bf16),
            ((own, length, 64), bf16),
            ((own, 64, length), bf16),
            ((own, length, 64), bf16),
            ((own, length, 64), bf16),
            ((own, 64, length), bf16),
            ((own, length, 64), bf16),
            ((own, tile_count(bk), bk, BQ), f32),
            ((own, tile_count(bk), bk, BQ), f32),
            ((own * 64, length), f32),
            ((own, length, 64), f32),
            ((own, length, 64), f32),
        ],
        length * length * own * 160,
    )


def cross_backward(limits, rows, q, kv, grad, o_t, lse, bk=256):
    length, own, keys = q.shape[0], q.shape[1] // 64, kv.shape[0]
    return call(
        functools.partial(cross_backward_kernel, own, bk),
        "cross_backward",
        [limits, rows, q, kv, grad, o_t, lse],
        [((length, own * 64), bf16), ((keys, own * 128), bf16)],
        [
            ((own, 64, length), bf16),
            ((own, length, 64), bf16),
            ((own, 64, keys), bf16),
            ((own, keys, 64), bf16),
            ((own, keys, 64), bf16),
            ((own, 64, length), bf16),
            ((own, length, 64), bf16),
            ((own * 64, length), f32),
            ((own, keys, 64), f32),
            ((own, keys, 64), f32),
        ],
        length * keys * own * 320,
    )


def norm_apply(value, gain):
    return value * lax.rsqrt(jnp.mean(value * value, axis=-1, keepdims=True) + EPS) * gain


def norm_back(value, gain, grad):
    _, pull = jax.vjp(norm_apply, value, gain)
    return pull(grad)


def gate_mix(gate_up):
    inner = gate_up.shape[1] // 2
    return jax.nn.gelu(gate_up[:, :inner], approximate=True) * gate_up[:, inner:]


def counts_below(ids, values):
    total = jnp.zeros_like(values)
    for doc in range(DOCS):
        total = total + jnp.where(values > doc, jnp.sum((ids == doc).astype(jnp.int32)), 0)
    return total


def swap(blocks):
    return lax.all_to_all(blocks, "seq", split_axis=0, concat_axis=0, tiled=True)


def shards(
    layer_in, encoder, decoder_ids, encoder_ids, rel_buckets,
    norm_self, self_qkv, self_out, rel_table, norm_cross, cross_q, cross_kv, cross_out, norm_ff, ff_in, ff_out,
    cotangent,
):
    seqs, local, width = layer_in.shape
    enc_local = encoder.shape[1]
    parts = lax.axis_size("seq")
    heads = self_qkv.shape[1]
    dh = self_qkv.shape[2] // 3
    own = heads // parts
    rows = seqs * local
    buckets, table_own = rel_table.shape
    length, keys = local * parts, enc_local * parts
    gather = lambda v: lax.all_gather(v, "fsdp", axis=0, tiled=True)

    qkv_w = gather(self_qkv).reshape(width, parts, own * 3 * dh)
    pairs_w = gather(cross_kv).reshape(width, parts, own * 2 * dh)
    mix_self = gather(self_out).reshape(parts, own * dh, width)
    query_w = gather(cross_q).reshape(width, parts, own * dh)
    mix_cross = gather(cross_out).reshape(parts, own * dh, width)
    inner_w = gather(ff_in)
    outer_w = gather(ff_out)
    small = jnp.concatenate([norm_self, norm_cross, norm_ff, rel_table.reshape(-1)])
    small = lax.all_gather(small, "fsdp", axis=0, tiled=False)
    part = norm_self.shape[0]
    gain_first, gain_second, gain_third = (
        small[:, i * part : (i + 1) * part].reshape(width).astype(f32) for i in range(3)
    )
    table = jnp.transpose(small[:, 3 * part :].reshape(-1, buckets, table_own), (1, 0, 2)).reshape(buckets, heads)
    both_ids = jnp.concatenate([decoder_ids.reshape(-1), encoder_ids.reshape(-1)])
    both_ids = lax.all_gather(both_ids, "seq", axis=0, tiled=False)
    ids = both_ids[:, :local].reshape(length)
    enc_ids = both_ids[:, local:].reshape(keys)

    first_seen = counts_below(ids, ids)
    enc_first = counts_below(enc_ids, ids)
    enc_last = counts_below(enc_ids, ids + 1)
    blocks = length // BQ
    bk = 256
    self_rows = jnp.broadcast_to(first_seen[None], (8, length))
    cross_rows = jnp.concatenate([enc_first[None], enc_last[None], jnp.zeros((6, length), jnp.int32)])
    self_limits = jnp.stack(
        [first_seen[::BQ] // bk, (jnp.arange(blocks, dtype=jnp.int32) + 1) * (BQ // bk)]
    )
    cross_limits = jnp.stack([enc_first[::BQ] // bk, (enc_last[BQ - 1 :: BQ] + bk - 1) // bk])

    first_head = lax.axis_index("seq") * own
    table_mine = lax.dynamic_slice_in_dim(table.astype(f32), first_head, own, 1)
    near = rel_buckets[:REACH]
    onehot = (near[:, None] == jnp.arange(buckets, dtype=jnp.int32)[None, :]).astype(f32)
    bias = jnp.einsum("ln,ng->gl", onehot, table_mine, precision=HIGH)
    ext = jnp.concatenate(
        [jnp.full((own, BQ), MASKED, f32), bias, jnp.zeros((own, BQ), f32)], axis=1
    )

    stream = layer_in.astype(f32).reshape(rows, width)
    normed_first = norm_apply(stream, gain_first).astype(bf16)
    qkv_tok = jnp.einsum("td,dge->gte", normed_first, qkv_w, preferred_element_type=f32).astype(bf16)
    qkv = swap(qkv_tok).reshape(length, own * 3 * dh)
    out_self, self_t, self_lse = self_forward(self_limits, self_rows, ext, qkv)
    self_tok = swap(out_self.reshape(parts, local, own * dh))
    after_self = stream + jnp.einsum("gtc,gcd->td", self_tok, mix_self, preferred_element_type=f32)
    normed_second = norm_apply(after_self, gain_second).astype(bf16)
    query_tok = jnp.einsum("td,dgc->gtc", normed_second, query_w, preferred_element_type=f32).astype(bf16)
    enc_flat = encoder.reshape(seqs * enc_local, width)
    pairs_tok = jnp.einsum("td,dge->gte", enc_flat, pairs_w, preferred_element_type=f32).astype(bf16)
    query_cross = swap(query_tok).reshape(length, own * dh)
    pairs = swap(pairs_tok).reshape(keys, own * 2 * dh)
    out_cross, cross_t, cross_lse = cross_forward(cross_limits, cross_rows, query_cross, pairs)
    cross_tok = swap(out_cross.reshape(parts, local, own * dh))
    after_cross = after_self + jnp.einsum("gtc,gcd->td", cross_tok, mix_cross, preferred_element_type=f32)
    normed_third = norm_apply(after_cross, gain_third).astype(bf16)
    gate_up = jnp.dot(normed_third, inner_w, preferred_element_type=f32)
    hidden = gate_mix(gate_up).astype(bf16)
    layer_out = (
        (after_cross + jnp.dot(hidden, outer_w, preferred_element_type=f32)).astype(bf16).reshape(seqs, local, width)
    )

    grad_low = cotangent.reshape(rows, width)
    grad_outer = jnp.einsum("tf,td->fd", hidden, grad_low, preferred_element_type=f32)
    grad_hidden = jnp.einsum("td,fd->tf", grad_low, outer_w, preferred_element_type=f32)
    _, pull_mix = jax.vjp(gate_mix, gate_up)
    grad_gate_up = pull_mix(grad_hidden)[0].astype(bf16)
    grad_inner = jnp.einsum("td,tf->df", normed_third, grad_gate_up, preferred_element_type=f32)
    grad_third_in = jnp.einsum("tf,df->td", grad_gate_up, inner_w, preferred_element_type=f32)
    grad_from_third, grad_gain_third = norm_back(after_cross, gain_third, grad_third_in)
    grad_middle = grad_low.astype(f32) + grad_from_third
    middle_low = grad_middle.astype(bf16)
    grad_mix_cross = jnp.einsum("gtc,td->gcd", cross_tok, middle_low, preferred_element_type=f32)
    grad_cross_tok = jnp.einsum("td,gcd->gtc", middle_low, mix_cross, preferred_element_type=f32).astype(bf16)
    grad_cross = swap(grad_cross_tok).reshape(length, own * dh)
    grad_query, grad_pairs = cross_backward(
        cross_limits, cross_rows, query_cross, pairs, grad_cross, cross_t, cross_lse
    )
    grad_query_tok = swap(grad_query.reshape(parts, local, own * dh))
    grad_pairs_tok = swap(grad_pairs.reshape(parts, enc_local, own * 2 * dh))
    grad_query_w = jnp.einsum("td,gtc->dgc", normed_second, grad_query_tok, preferred_element_type=f32)
    grad_second_in = jnp.einsum("gtc,dgc->td", grad_query_tok, query_w, preferred_element_type=f32)
    grad_pairs_w = jnp.einsum("td,gte->dge", enc_flat, grad_pairs_tok, preferred_element_type=f32)
    grad_encoder = jnp.einsum("gte,dge->td", grad_pairs_tok, pairs_w, preferred_element_type=f32).reshape(
        seqs, enc_local, width
    )
    grad_from_second, grad_gain_second = norm_back(after_self, gain_second, grad_second_in)
    grad_upper = grad_middle + grad_from_second
    upper_low = grad_upper.astype(bf16)
    grad_mix_self = jnp.einsum("gtc,td->gcd", self_tok, upper_low, preferred_element_type=f32)
    grad_self_tok = jnp.einsum("td,gcd->gtc", upper_low, mix_self, preferred_element_type=f32).astype(bf16)
    grad_self = swap(grad_self_tok).reshape(length, own * dh)
    grad_qkv, tile_sums = self_backward(self_limits, self_rows, ext, qkv, grad_self, self_t, self_lse)
    grad_qkv_tok = swap(grad_qkv.reshape(parts, local, own * 3 * dh))
    grad_qkv_w = jnp.einsum("td,gte->dge", normed_first, grad_qkv_tok, preferred_element_type=f32)
    grad_first_in = jnp.einsum("gte,dge->td", grad_qkv_tok, qkv_w, preferred_element_type=f32)
    grad_from_first, grad_gain_first = norm_back(stream, gain_first, grad_first_in)
    grad_layer_in = (grad_upper + grad_from_first).reshape(seqs, local, width)

    bucket_line = jnp.concatenate(
        [jnp.full((BQ,), -1, jnp.int32), near, jnp.full((BQ + bk,), -1, jnp.int32)]
    )
    by_tile = jnp.stack([bucket_line[t * bk + 1 : t * bk + 1 + BQ + bk] for t in range(tile_count(bk))])
    in_bucket = (by_tile[:, :, None] == jnp.arange(buckets, dtype=jnp.int32)).astype(f32)
    by_bucket = jnp.einsum("twn,gtw->ng", in_bucket, tile_sums, precision=HIGH)
    grad_table = lax.dynamic_update_slice_in_dim(jnp.zeros((buckets, heads), f32), by_bucket, first_head, 1)

    def reduce(grad):
        mine = lax.psum_scatter(grad.astype(bf16), "fsdp", scatter_dimension=0, tiled=True)
        return lax.psum(mine, "seq").astype(f32)

    total_qkv = reduce(grad_qkv_w.reshape(width, heads, 3 * dh))
    total_pairs = reduce(grad_pairs_w.reshape(width, heads, 2 * dh))
    total_mix_self = reduce(grad_mix_self.reshape(width, width))
    total_query = reduce(grad_query_w.reshape(width, width))
    total_mix_cross = reduce(grad_mix_cross.reshape(width, width))
    total_inner = reduce(grad_inner)
    total_outer = reduce(grad_outer)
    gains = jnp.concatenate(
        [g.reshape(-1, part) for g in (grad_gain_first, grad_gain_second, grad_gain_third)], axis=1
    )
    tables = jnp.transpose(grad_table.reshape(buckets, -1, table_own), (1, 0, 2)).reshape(-1, buckets * table_own)
    small_grads = jnp.concatenate([gains, tables], axis=1).astype(bf16)
    small_total = lax.psum(small_grads, ("seq", "fsdp")).astype(f32)
    mine = lax.dynamic_index_in_dim(small_total, lax.axis_index("fsdp"), 0, False)
    total_gain_first, total_gain_second, total_gain_third = (mine[i * part : (i + 1) * part] for i in range(3))
    total_table = mine[3 * part :].reshape(buckets, table_own)
    return (
        layer_out, grad_layer_in, grad_encoder, total_gain_first, total_qkv, total_mix_self, total_table,
        total_gain_second, total_query, total_pairs, total_mix_cross, total_gain_third, total_inner, total_outer,
    )


def solution(mesh):
    in_specs = (
        P("fsdp", "seq", None), P("fsdp", "seq", None), P("fsdp", "seq"), P("fsdp", "seq"), P(),
        P("fsdp"), P("fsdp", None, None), P("fsdp", None), P(None, "fsdp"), P("fsdp"), P("fsdp", None),
        P("fsdp", None, None), P("fsdp", None), P("fsdp"), P("fsdp", None), P("fsdp", None),
        P("fsdp", "seq", None),
    )
    out_specs = (
        P("fsdp", "seq", None), P("fsdp", "seq", None), P("fsdp", "seq", None), P("fsdp"), P("fsdp", None, None),
        P("fsdp", None), P(None, "fsdp"), P("fsdp"), P("fsdp", None), P("fsdp", None, None), P("fsdp", None),
        P("fsdp"), P("fsdp", None), P("fsdp", None),
    )
    return jax.shard_map(shards, mesh=mesh, in_specs=in_specs, out_specs=out_specs, check_vma=False)
```

time: 1970 us -> 1010 us (0.51)
  local copies, waits for them, and re-layouts: 796 us -> 27.9 us
  matrix products: 268 us -> 99.5 us
  other arithmetic: 146 us -> 27.8 us
  waiting for transfers between devices: 444 us -> 539 us
  loops' own time: 64.3 us -> 0 us
  Pallas kernels: 0 us -> 63 us
  blocking collectives: 179 us -> 209 us
  starting transfers between devices: 41.1 us -> 21.1 us
    while x111 -> x0, local copies, waits for them, and re-layouts: 449 us -> none
    dot_general x76 -> x21, matrix products: 246 us -> 88.3 us  [the longest x1 10.4 us: shards(): gate_up = jnp.dot(normed_third, inner_w, preferred_element_type=f32)]
    reshape x14 -> x7, local copies, waits for them, and re-layouts: 149 us -> 0.49 us  [the longest x1 0.13 us: shards(): jnp.transpose(grad_table.reshape(buckets, -1, table_own), (1, 0, 2))]
    gather x12 -> x0, local copies, waits for them, and re-layouts: 79.4 us -> none  [the longest x8 48.9 us: bias_block(): circle = jnp.take(distance_bias, places, axis=1)]
    another operation x4 -> x0, loops' own time: 64.3 us -> none  [the longest x2 32.3 us: per_sequence(): lax.scan(per_block, (empty, empty, bias_start), jnp.arange(count, dtype=j...]
    pallas_call x0 -> x4, Pallas kernels: none -> 63 us  [call(): pl.pallas_call(body, name=name, out_shape=[jax.ShapeDtypeStruct(s, d) for...]
    all_gather x7, waiting for transfers between devices: 40.4 us -> 100 us  [shards(): gather = lambda v: lax.all_gather(v, 'fsdp', axis=0, tiled=True)]
    all_gather x5 -> x1, blocking collectives: 58.8 us -> 6.06 us  [shards(): small = lax.all_gather(small, 'fsdp', axis=0, tiled=False)]
  transfers between devices with their start and end apart: 22 -> 20, of which waited for: 7 -> 11; matrix products, arithmetic and copies ran while one was open for 59% -> 11% of each run, Pallas kernels for 0% -> 6%
where the time goes in v1:
time: 1010 us; the launch traced here: 1000 us
  waiting for transfers between devices  539 us (53%)
  blocking collectives  209 us (21%)
  matrix products  99.5 us (10%)
  Pallas kernels  63 us (6%)
  local copies, waits for them, and re-layouts  27.9 us (3%)
  other arithmetic  27.8 us (3%)
  starting transfers between devices  21.1 us (2%)
  between operations  15.7 us (2%)
    psum x1, waiting for transfers between devices, reduce(): return lax.psum(mine, 'seq').astype(f32)  224 us
    reduce_scatter x7, waiting for transfers between devices, reduce(): lax.psum_scatter(grad.astype(bf16), 'fsdp', scatter_dimension=0, tiled=True)  188 us
    all_to_all x5, blocking collectives, swap(): lax.all_to_all(blocks, 'seq', split_axis=0, concat_axis=0, tiled=True)  107 us
    all_gather x7, waiting for transfers between devices, shards(): gather = lambda v: lax.all_gather(v, 'fsdp', axis=0, tiled=True)  100 us
    pallas_call x4, Pallas kernels, call(): pl.pallas_call(body, name=name, out_shape=[jax.ShapeDtypeStruct(s, d) for...  63 us
    unnamed x1, blocking collectives  52.8 us
    psum x1, blocking collectives, shards(): small_total = lax.psum(small_grads, ('seq', 'fsdp')).astype(f32)  43.1 us
    all_to_all x5, waiting for transfers between devices, swap(): lax.all_to_all(blocks, 'seq', split_axis=0, concat_axis=0, tiled=True)  23.1 us
  transfers between devices with their start and end apart: 20, of which 11 were waited for; matrix products, arithmetic and copies ran while one was open for 11% of the time, Pallas kernels for 6%

profile of v1, /device:TPU:1, one launch (start us, length us, event | category | flops | bytes accessed | tf_op | source)
XLA Modules:
  0.0 1002.9 jit_solution(12798151143222557978)
XLA Ops:
  14.5 6.1 all-gather.2
  20.8 38.6 %all-gather.11.cloned.1.call-done = bf16[1024,16,192]{0,2,1:T(8,128)(2,1)} async-done(((bf16[256,16,192]{0,2,1:T(8,128)(2,1)}), bf16[1024,16,192]{0,2,1:T(8,128)(2,1)}) %all-gather.11.cloned.1.call-update) | async-done | bytes 6291472 | tf_op jit(solution)/shard_map/all_gather | solution.py:384
  59.3 5.8 fusion.6
  65.2 5.4 all-to-all-start
  72.0 52.8 %all-reduce.3 = s32[2560]{0:T(1024)S(1)} all-reduce(s32[2560]{0:T(1024)S(1)} %add_dynamic-update-slice_fusion), channel_id=2, replica_groups=mesh['seq'=8,'fsdp'=4] {'seq'}, use_global_device_ids=true, to_apply=%add.3 | all-reduce | flops 2560 | bytes 20480
  128.8 5.2 fusion.54
  134.8 19.1 %self_forward.1 = (bf16[2048,128]{1,0:T(8,128)(2,1)}, f32[128,2048]{1,0:T(8,128)S(1)}, f32[2,2048]{1,0:T(2,128)S(1)}) custom-call(s32[2,8]{1,0:T(2,128)S(1)} %pad_add_fusion.lim_ref, s32[8,2048]{1,0:T(8,128)S(1)} %broadcast_in_dim.93.rows_ref, f32[2,1536]{1,0:T(2,128)S(1)} %maximum_maximum_fusion.ext_ref, bf16[2048,384]{1,0:T(8,128)(2,1)S(1)} %bitcast.195), custom_call_target="tpu_custom_call" | custom-call | flops 536870912 | bytes 3301504 | tf_op jit(solution)/shard_map/self_forward/pallas_call | solution.py:256
  183.6 8.7 all-to-all-done.2
  192.4 10.7 %cross_forward.1 = (bf16[2048,128]{1,0:T(8,128)(2,1)}, f32[128,2048]{1,0:T(8,128)S(1)}, f32[2,2048]{1,0:T(2,128)S(1)}) custom-call(s32[2,8]{1,0:T(2,128)S(1)} %pad_add_fusion.1.lim_ref, s32[8,2048]{1,0:T(8,128)S(1)} %add_add_fusion.3.rows_ref, bf16[2048,128]{1,0:T(8,128)(2,1)S(1)} %bitcast.198, bf16[512,256]{1,0:T(8,128)(2,1)S(1)} %bitcast.203), custom_call_target="tpu_custom_call" | custom-call | flops 268435456 | bytes 1704064 | tf_op jit(solution)/shard_map/cross_forward/pallas_call | solution.py:256
  207.8 8.8 all-to-all-done.4
  220.2 27.1 %all-gather.21.cloned.1.call-done = bf16[1024,5632]{1,0:T(8,128)(2,1)} async-done(((bf16[256,5632]{1,0:T(8,128)(2,1)}), bf16[1024,5632]{1,0:T(8,128)(2,1)}) %all-gather.21.cloned.1.call-update) | async-done | bytes 11534352 | tf_op jit(solution)/shard_map/all_gather | solution.py:384
  247.2 10.4 %fusion.66 = f32[256,5632]{1,0:T(8,128)} fusion(bf16[1024,5632]{1,0:T(8,128)(2,1)} %all-gather.21.cloned.1.call-done, f32[256,1024]{1,0:T(8,128)} %get-tuple-element.127, f32[1024]{0:T(1024)S(1)} %bitcast.222, f32[256]{0:T(256)S(1)} %fusion.59), kind=kOutput, calls=%fused_computation.152 | convolution fusion | flops 2953576448 | bytes 18355200 | tf_op jit(solution)/shard_map/dot_general | solution.py:443
  257.7 34.5 %all-gather.23.cloned.1.call-done = bf16[2816,1024]{1,0:T(8,128)(2,1)} async-done(((bf16[704,1024]{1,0:T(8,128)(2,1)}), bf16[2816,1024]{1,0:T(8,128)(2,1)}) %all-gather.23.cloned.1.call-update) | async-done | bytes 5767184 | tf_op jit(solution)/shard_map/all_gather | solution.py:384
  292.2 10.2 %fusion.30 = (f32[256,2816]{1,0:T(8,128)S(1)}, f32[256,2816]{1,0:T(8,128)}, bf16[256,2816]{1,0:T(8,128)(2,1)}) fusion(f32[256,5632]{1,0:T(8,128)} %fusion.66, bf16[2816,1024]{1,0:T(8,128)(2,1)} %all-gather.23.cloned.1.call-done, bf16[1,256,1024]{2,1,0:T(8,128)(2,1)} %param.33), kind=kOutput, calls=%fused_computation.66 | convolution fusion | flops 1493696512 | bytes 19267584 | tf_op jit(solution)/shard_map/td,fd->tf/dot_general | solution.py:451
  302.5 10.4 %multiply_reduce_fusion = (bf16[1024]{0:T(1024)(128)(2,1)S(1)}, f32[256]{0:T(256)S(1)}, f32[256,1024]{1,0:T(8,128)}) fusion(f32[256,1024]{1,0:T(8,128)S(1)} %copy-done.8, f32[256]{0:T(256)S(1)} %fusion.59, f32[1024]{0:T(1024)S(1)} %bitcast.223, bf16[1024,5632]{1,0:T(8,128)(2,1)} %all-gather.21.cloned.1.call-done, f32[256,2816]{1,0:T(8,128)} %get-tuple-element.103, ...), kind=kOutput, calls=%fused_computation.58 | convolution fusion | flops 2957245184 | bytes 19406848 | tf_op jit(solution)/shard_map/tf,df->td/dot_general | solution.py:455
  320.3 18.7 %all_to_all.50 = bf16[8,256,128]{2,1,0:T(8,128)(2,1)S(1)} all-to-all(bf16[8,256,128]{2,1,0:T(8,128)(2,1)S(1)} %fusion.15), channel_id=1, replica_groups=mesh['seq'=8,'fsdp'=4] {'seq'}, dimensions={0} | all-to-all | bytes 1048576 | tf_op jit(solution)/shard_map/all_to_all | solution.py:367
  339.1 11.2 %cross_backward.1 = (bf16[2048,128]{1,0:T(8,128)(2,1)S(1)}, bf16[512,256]{1,0:T(8,128)(2,1)S(1)}) custom-call(s32[2,8]{1,0:T(2,128)S(1)} %pad_add_fusion.1.lim_ref, s32[8,2048]{1,0:T(8,128)S(1)} %add_add_fusion.3.rows_ref, bf16[2048,128]{1,0:T(8,128)(2,1)S(1)} %bitcast.199, bf16[512,256]{1,0:T(8,128)(2,1)S(1)} %bitcast.204, bf16[2048,128]{1,0:T(8,128)(2,1)S(1)} %bitcast.200, ...), custom_call_target="tpu_custom_call" | custom-call | flops 671088640 | bytes 4882560 | tf_op jit(solution)/shard_map/cross_backward/pallas_call | solution.py:256
  350.3 19.1 %all_to_all.51 = bf16[8,256,128]{2,1,0:T(8,128)(2,1)S(1)} all-to-all(bf16[8,256,128]{2,1,0:T(8,128)(2,1)S(1)} %bitcast.202), channel_id=1, replica_groups=mesh['seq'=8,'fsdp'=4] {'seq'}, dimensions={0} | all-to-all | bytes 1048576 | tf_op jit(solution)/shard_map/all_to_all | solution.py:367
  381.8 10.9 %all_to_all.52 = bf16[8,64,256]{2,1,0:T(8,128)(2,1)S(1)} all-to-all(bf16[8,64,256]{2,1,0:T(8,128)(2,1)S(1)} %bitcast.205), channel_id=1, replica_groups=mesh['seq'=8,'fsdp'=4] {'seq'}, dimensions={0} | all-to-all | bytes 524288 | tf_op jit(solution)/shard_map/all_to_all | solution.py:367
  396.0 6.9 copy.74
  404.3 5.3 convolution_convert_fusion.1
  412.4 17.8 %all_to_all.53 = bf16[8,256,128]{2,1,0:T(8,128)(2,1)S(1)} all-to-all(bf16[8,256,128]{2,1,0:T(8,128)(2,1)S(1)} %fusion.16), channel_id=1, replica_groups=mesh['seq'=8,'fsdp'=4] {'seq'}, dimensions={0} | all-to-all | bytes 1048576 | tf_op jit(solution)/shard_map/all_to_all | solution.py:367
  430.2 22.1 %self_backward.1 = (bf16[2048,384]{1,0:T(8,128)(2,1)S(1)}, f32[2,5,512]{2,1,0:T(8,128)S(1)}) custom-call(s32[2,8]{1,0:T(2,128)S(1)} %pad_add_fusion.lim_ref, s32[8,2048]{1,0:T(8,128)S(1)} %broadcast_in_dim.93.rows_ref, f32[2,1536]{1,0:T(2,128)S(1)} %maximum_maximum_fusion.ext_ref, bf16[2048,384]{1,0:T(8,128)(2,1)S(1)} %bitcast.196, ...), custom_call_target="tpu_custom_call" | custom-call | flops 1342177280 | bytes 6480000 | tf_op jit(solution)/shard_map/self_backward/pallas_call | solution.py:256
  452.3 40.4 %all_to_all.54 = bf16[8,256,384]{2,1,0:T(8,128)(2,1)} all-to-all(bf16[8,256,384]{2,1,0:T(8,128)(2,1)S(1)} %bitcast.197), channel_id=1, replica_groups=mesh['seq'=8,'fsdp'=4] {'seq'}, dimensions={0} | all-to-all | bytes 3145728 | tf_op jit(solution)/shard_map/all_to_all | solution.py:367
  500.9 9.1 convolution_convert_fusion
  510.2 32.0 %reduce-scatter.20.cloned.1.call-done = bf16[704,1024]{1,0:T(8,128)(2,1)} async-done(((bf16[2816,1024]{1,0:T(8,128)(2,1)}), bf16[704,1024]{1,0:T(8,128)(2,1)}) %reduce-scatter.20.cloned.1.call-update) | async-done | bytes 1441808 | tf_op jit(solution)/shard_map/reduce_scatter | solution.py:495
  542.2 61.1 %reduce-scatter.8.cloned.1.call-done = bf16[256,16,192]{0,2,1:T(8,128)(2,1)} async-done(((bf16[1024,16,192]{0,2,1:T(8,128)(2,1)}), bf16[256,16,192]{0,2,1:T(8,128)(2,1)}) %reduce-scatter.8.cloned.1.call-update) | async-done | bytes 1572880 | tf_op jit(solution)/shard_map/reduce_scatter | solution.py:495
  603.3 94.6 %reduce-scatter.18.cloned.1.call-done = bf16[256,5632]{1,0:T(8,128)(2,1)} async-done(((bf16[1024,5632]{1,0:T(8,128)(2,1)}), bf16[256,5632]{1,0:T(8,128)(2,1)}) %reduce-scatter.18.cloned.1.call-update) | async-done | bytes 2883600 | tf_op jit(solution)/shard_map/reduce_scatter | solution.py:495
  698.8 5.7 fusion.17
  706.5 5.8 fusion.23
  712.4 43.1 %psum.56 = bf16[4,896]{1,0:T(4,128)(2,1)S(1)} all-reduce(bf16[4,896]{1,0:T(4,128)(2,1)S(1)} %pad_maximum_fusion), channel_id=1, replica_groups=mesh['seq'=8,'fsdp'=4] {'seq','fsdp'}, use_global_device_ids=true, to_apply=%region_17.18 | all-reduce | flops 3584 | bytes 14336 | tf_op jit(solution)/shard_map/psum | solution.py:510
  758.1 224.3 %all-reduce.7.cloned.1.call-done = (bf16[256,16,192]{0,2,1:T(8,128)(2,1)}, bf16[256,1024]{1,0:T(8,128)(2,1)}, bf16[256,1024]{1,0:T(8,128)(2,1)}, bf16[256,16,128...) async-done(((bf16[256,16,192]{0,2,1:T(8,128)(2,1)}, bf16[256,1024]{1,0:T(8,128)(2,1)}, ...) | async-done | bytes 8519696 | tf_op jit(solution)/shard_map/psum | solution.py:496
  (219 shorter events, 105.1 us)
Async XLA Ops:
  7.2 151.2 %copy-start = (bf16[1,64,1024]{2,1,0:T(8,128)(2,1)S(1)}, bf16[1,64,1024]{2,1,0:T(8,128)(2,1)}, u32[]{:S(2)}) copy-start(bf16[1,64,1024]{2,1,0:T(8,128)(2,1)} %param.18) | copy-start | bytes 393220
  7.2 52.1 %all-gather.11.cloned.1.call-start = ((), (), s32[]{:S(2)}) async-start(), calls=%async_computation.17 | async-start | bytes 7864320 | tf_op jit(solution)/shard_map/all_gather | solution.py:384
  7.9 150.4 %all-gather.17.cloned.1.call-start = ((), (), s32[]{:S(2)}) async-start(), calls=%async_computation.20 | async-start | bytes 5242880 | tf_op jit(solution)/shard_map/all_gather | solution.py:384
  10.4 161.2 %all-gather.13.cloned.1.call-start = ((), (), s32[]{:S(2)}) async-start(), calls=%async_computation.18 | async-start | bytes 2621440 | tf_op jit(solution)/shard_map/all_gather | solution.py:384
  11.2 163.2 %all-gather.15.cloned.1.call-start = ((), (), s32[]{:S(2)}) async-start(), calls=%async_computation.19 | async-start | bytes 2621440 | tf_op jit(solution)/shard_map/all_gather | solution.py:384
  12.3 195.5 %all-gather.19.cloned.1.call-start = ((), (), s32[]{:S(2)}) async-start(), calls=%async_computation.21 | async-start | bytes 2621440 | tf_op jit(solution)/shard_map/all_gather | solution.py:384
  12.9 234.4 %all-gather.21.cloned.1.call-start = ((), (), s32[]{:S(2)}) async-start(), calls=%async_computation.22 | async-start | bytes 14417920 | tf_op jit(solution)/shard_map/all_gather | solution.py:384
  13.4 278.8 %all-gather.23.cloned.1.call-start = ((), (), s32[]{:S(2)}) async-start(), calls=%async_computation.23 | async-start | bytes 7208960 | tf_op jit(solution)/shard_map/all_gather | solution.py:384
  65.2 68.9 %copy-start.30 = (s32[2048]{0:T(1024)S(1)}, s32[2048]{0:T(1024)}, u32[]{:S(2)}) copy-start(s32[2048]{0:T(1024)} %param.21) | copy-start | bytes 24580
  65.2 69.6 %all-to-all-start = ((bf16[8,256,384]{2,1,0:T(8,128)(2,1)}), bf16[8,256,384]{2,1,0:T(8,128)(2,1)S(1)}, u32[]{:S(2)}, u32[]{:S(2)}) async-start(bf16[8,256,384]{2,1,0:T(8,128)(2,1)} %fusion.6), calls=%async_computation | async-start | bytes 3145728 | tf_op jit(solution)/shard_map/all_to_all | solution.py:367
  154.9 12.6 %all-to-all-start.1 = ((bf16[8,256,128]{2,1,0:T(8,128)(2,1)}), bf16[8,256,128]{2,1,0:T(8,128)(2,1)S(1)}, u32[]{:S(2)}, u32[]{:S(2)}) async-start(bf16[8,256,128]{2,1,0:T(8,128)(2,1)} %bitcast.12), calls=%async_computation.1 | async-start | bytes 1048576 | tf_op jit(solution)/shard_map/all_to_all | solution.py:367
  168.2 10.5 %all-to-all-start.3 = ((bf16[8,64,256]{2,1,0:T(8,128)(2,1)}), bf16[8,64,256]{2,1,0:T(8,128)(2,1)S(1)}, u32[]{:S(2)}, u32[]{:S(2)}) async-start(bf16[8,64,256]{2,1,0:T(8,128)(2,1)} %fusion.18), calls=%async_computation.3 | async-start | bytes 524288 | tf_op jit(solution)/shard_map/all_to_all | solution.py:367
  178.7 13.7 %all-to-all-start.2 = ((bf16[8,256,128]{2,1,0:T(8,128)(2,1)}), bf16[8,256,128]{2,1,0:T(8,128)(2,1)S(1)}, u32[]{:S(2)}, u32[]{:S(2)}) async-start(bf16[8,256,128]{2,1,0:T(8,128)(2,1)} %fusion.14), calls=%async_computation.2 | async-start | bytes 1048576 | tf_op jit(solution)/shard_map/all_to_all | solution.py:367
  204.0 12.6 %all-to-all-start.4 = ((bf16[8,256,128]{2,1,0:T(8,128)(2,1)}), bf16[8,256,128]{2,1,0:T(8,128)(2,1)S(1)}, u32[]{:S(2)}, u32[]{:S(2)}) async-start(bf16[8,256,128]{2,1,0:T(8,128)(2,1)} %bitcast.26), calls=%async_computation.4 | async-start | bytes 1048576 | tf_op jit(solution)/shard_map/all_to_all | solution.py:367
  207.5 302.5 %reduce-scatter.16.cloned.1.call-start = ((), (), s32[]{:S(2)}) async-start(), calls=%async_computation.28 | async-start | bytes 2621440 | tf_op jit(solution)/shard_map/reduce_scatter | solution.py:495
  292.2 10.2 %copy-start.8 = (f32[256,1024]{1,0:T(8,128)S(1)}, f32[256,1024]{1,0:T(8,128)}, u32[]{:S(2)}) copy-start(f32[256,1024]{1,0:T(8,128)} %get-tuple-element.127) | copy-start | bytes 3145732
  302.4 10.4 %copy-start.22 = (f32[256,2816]{1,0:T(8,128)}, f32[256,2816]{1,0:T(8,128)S(1)}, u32[]{:S(2)}) copy-start(f32[256,2816]{1,0:T(8,128)S(1)} %get-tuple-element.102) | copy-start | bytes 8650756
  302.4 10.4 %copy-start.23 = (bf16[1,256,1024]{2,1,0:T(8,128)(2,1)S(1)}, bf16[1,256,1024]{2,1,0:T(8,128)(2,1)}, u32[]{:S(2)}) copy-start(bf16[1,256,1024]{2,1,0:T(8,128)(2,1)} %param.33) | copy-start | bytes 1572868
  317.5 192.6 %reduce-scatter.10.cloned.1.call-start = ((), (), s32[]{:S(2)}) async-start(), calls=%async_computation.25 | async-start | bytes 2621440 | tf_op jit(solution)/shard_map/reduce_scatter | solution.py:495
  317.6 21.5 %copy-start.3 = (f32[128,2048]{1,0:T(8,128)S(1)}, f32[128,2048]{1,0:T(8,128)}, u32[]{:S(2)}) copy-start(f32[128,2048]{1,0:T(8,128)} %copy-done.2) | copy-start | bytes 3145732
  339.1 30.3 %copy-start.7 = (f32[256,1024]{1,0:T(8,128)S(1)}, f32[256,1024]{1,0:T(8,128)}, u32[]{:S(2)}) copy-start(f32[256,1024]{1,0:T(8,128)} %copy-done.6) | copy-start | bytes 3145732
  339.1 30.3 %copy-start.15 = (bf16[1024,1024]{0,1:T(8,128)(2,1)S(1)}, bf16[1024,1024]{0,1:T(8,128)(2,1)}, u32[]{:S(2)}) copy-start(bf16[1024,1024]{0,1:T(8,128)(2,1)} %all-gather.15.cloned.1.call-done) | copy-start | bytes 6291460
  350.3 20.1 %copy-start.13 = (f32[256,1024]{1,0:T(8,128)S(1)}, f32[256,1024]{1,0:T(8,128)}, u32[]{:S(2)}) copy-start(f32[256,1024]{1,0:T(8,128)} %copy-done.12) | copy-start | bytes 3145732
  373.7 136.4 %reduce-scatter.12.cloned.1.call-start = ((), (), s32[]{:S(2)}) async-start(), calls=%async_computation.26 | async-start | bytes 2621440 | tf_op jit(solution)/shard_map/reduce_scatter | solution.py:495
  381.7 128.4 %reduce-scatter.14.cloned.1.call-start = ((), (), s32[]{:S(2)}) async-start(), calls=%async_computation.27 | async-start | bytes 5242880 | tf_op jit(solution)/shard_map/reduce_scatter | solution.py:495
  402.9 139.3 %reduce-scatter.20.cloned.1.call-start = ((), (), s32[]{:S(2)}) async-start(), calls=%async_computation.30 | async-start | bytes 7208960 | tf_op jit(solution)/shard_map/reduce_scatter | solution.py:495
  409.6 20.7 %copy-start.5 = (f32[128,2048]{1,0:T(8,128)S(1)}, f32[128,2048]{1,0:T(8,128)}, u32[]{:S(2)}) copy-start(f32[128,2048]{1,0:T(8,128)} %copy-done.4) | copy-start | bytes 3145732
  409.6 193.7 %reduce-scatter.8.cloned.1.call-start = ((), (), s32[]{:S(2)}) async-start(), calls=%async_computation.24 | async-start | bytes 7864320 | tf_op jit(solution)/shard_map/reduce_scatter | solution.py:495
  452.3 42.5 %copy-start.17 = (bf16[1,256,1024]{2,1,0:T(8,128)(2,1)S(1)}, bf16[1,256,1024]{2,1,0:T(8,128)(2,1)}, u32[]{:S(2)}) copy-start(bf16[1,256,1024]{2,1,0:T(8,128)(2,1)} %param.17) | copy-start | bytes 1572868
  499.6 198.3 %reduce-scatter.18.cloned.1.call-start = ((), (), s32[]{:S(2)}) async-start(), calls=%async_computation.29 | async-start | bytes 14417920 | tf_op jit(solution)/shard_map/reduce_scatter | solution.py:495
  510.0 472.5 %all-reduce.7.cloned.1.call-start = ((), (), s32[]{:S(2)}) async-start(), calls=%async_computation.31 | async-start | bytes 17039360 | tf_op jit(solution)/shard_map/psum | solution.py:496
  706.5 50.3 %copy-start.11 = (f32[256,1024]{1,0:T(8,128)S(1)}, f32[256,1024]{1,0:T(8,128)}, u32[]{:S(2)}) copy-start(f32[256,1024]{1,0:T(8,128)} %copy-done.10) | copy-start | bytes 3145732
  (27 other events, 88.6 us)
Sparse Core Ops, SparseCore 0:
  9.6 49.7 all-gather.10
  61.5 35.0 all-gather.16
  98.1 22.5 all-gather.12
  122.7 22.8 all-gather.14
  147.0 22.6 all-gather.18
  171.1 76.1 all-gather.20
  248.8 43.3 all-gather.22
  317.6 31.0 reduce-scatter.15
  373.8 29.4 reduce-scatter.9
  405.7 31.4 reduce-scatter.11
  439.8 44.4 reduce-scatter.13
  487.3 54.8 reduce-scatter.19
  544.9 58.3 reduce-scatter.7
  605.8 92.1 reduce-scatter.17
  703.3 279.1 all-reduce.6

commit v2 on v1

--- a/solution.py
+++ b/solution.py
@@ -342,6 +342,111 @@
     )
 
 
+MESH = pl.DeviceIdType.MESH
+
+
+def ring_place(index, n):
+    z, x = index // 2, index % 2
+    return z + x * (n - 1 - 2 * z)
+
+
+def ring_index(place, n):
+    x = place // (n // 2)
+    z = place + x * (n - 1 - 2 * place)
+    return 2 * z + x
+
+
+def ring_kernel(n, splits, *refs):
+    count = len(splits)
+    x_refs, y_refs, slots = refs[:count], refs[count : 2 * count], refs[2 * count : 3 * count]
+    send_sem, recv_sem = refs[3 * count :]
+    place = ring_place(lax.axis_index("seq"), n)
+    right = ring_index((place + 1) % n, n)
+    left = ring_index((place + n - 1) % n, n)
+    barrier = pltpu.get_barrier_semaphore()
+    for neighbour in (left, right):
+        pl.semaphore_signal(barrier, inc=1, device_id={"seq": neighbour}, device_id_type=MESH)
+    pl.semaphore_wait(barrier, 2)
+
+    streams = []
+    for k in range(count):
+        for piece in range(splits[k]):
+            streams.append((k, piece, piece % 2))
+
+    def view(ref, k, piece, chunk):
+        rows = x_refs[k].shape[0] // n
+        cols = x_refs[k].shape[1] // splits[k]
+        return ref.at[pl.ds(pl.multiple_of(chunk * rows, 8), rows), pl.ds(piece * cols, cols)]
+
+    def slot(k, piece, step):
+        rows = x_refs[k].shape[0] // n
+        cols = x_refs[k].shape[1] // splits[k]
+        return slots[k].at[pl.ds(step * rows, rows), pl.ds(piece * cols, cols)]
+
+    def copy(number, step, src, dst, down):
+        return pltpu.make_async_remote_copy(
+            src_ref=src,
+            dst_ref=dst,
+            send_sem=send_sem.at[number, step],
+            recv_sem=recv_sem.at[number, step],
+            device_id={"seq": left if down else right},
+            device_id_type=MESH,
+        )
+
+    def chunk_at(down, step):
+        return (place + 1 + step) % n if down else (place + 2 * n - 1 - step) % n
+
+    copies = {}
+
+    def start(number, step, src, dst, down):
+        copies[number, step] = copy(number, step, src, dst, down)
+        copies[number, step].start()
+
+    for number, (k, piece, down) in enumerate(streams):
+        start(number, 0, view(x_refs[k], k, piece, place), slot(k, piece, 0), down)
+    for step in range(n - 1):
+        for number, (k, piece, down) in enumerate(streams):
+            copies[number, step].wait_recv()
+            chunk = chunk_at(down, step)
+            mine = view(x_refs[k], k, piece, chunk)
+            landed = slot(k, piece, step)
+            total = landed[...].astype(jnp.float32) + mine[...].astype(jnp.float32)
+            if step < n - 2:
+                landed[...] = total.astype(jnp.bfloat16)
+                start(number, step + 1, landed, slot(k, piece, step + 1), down)
+            else:
+                done = view(y_refs[k], k, piece, chunk)
+                done[...] = total.astype(jnp.bfloat16)
+                start(number, n - 1, done, done, down)
+    for step in range(n - 1):
+        for number, (k, piece, down) in enumerate(streams):
+            copies[number, n - 1 + step].wait_recv()
+            if step < n - 2:
+                chunk = chunk_at(down, n - 1 + step)
+                done = view(y_refs[k], k, piece, chunk)
+                start(number, n + step, done, done, down)
+    for one in copies.values():
+        one.wait_send()
+
+
+def ring_total(arrays, splits, ident):
+    n = lax.axis_size("seq")
+    size = sum(v.size * 2 for v in arrays)
+    return pl.pallas_call(
+        functools.partial(ring_kernel, n, splits),
+        name="ring_total",
+        out_shape=[jax.ShapeDtypeStruct(v.shape, jnp.bfloat16) for v in arrays],
+        in_specs=[pl.BlockSpec(memory_space=pltpu.VMEM)] * len(arrays),
+        out_specs=[pl.BlockSpec(memory_space=pltpu.VMEM)] * len(arrays),
+        scratch_shapes=[pltpu.VMEM((v.shape[0] // n * (n - 1), v.shape[1]), jnp.bfloat16) for v in arrays]
+        + [pltpu.SemaphoreType.DMA((sum(splits), 2 * n - 2)), pltpu.SemaphoreType.DMA((sum(splits), 2 * n - 2))],
+        compiler_params=pltpu.CompilerParams(
+            collective_id=ident, has_side_effects=True, vmem_limit_bytes=48 << 20
+        ),
+        cost_estimate=pl.CostEstimate(flops=size, bytes_accessed=60 * size, transcendentals=0),
+    )(*arrays)
+
+
 def norm_apply(value, gain):
     return value * lax.rsqrt(jnp.mean(value * value, axis=-1, keepdims=True) + EPS) * gain
 
@@ -365,6 +470,17 @@
 
 def swap(blocks):
     return lax.all_to_all(blocks, "seq", split_axis=0, concat_axis=0, tiled=True)
+
+
+def scatter(grad):
+    return lax.psum_scatter(grad, "fsdp", scatter_dimension=0, tiled=True)
+
+
+def over_seq(arrays, splits, ident):
+    n = lax.axis_size("seq")
+    if all(v.shape[0] % (8 * n) == 0 and v.shape[1] % (128 * s) == 0 for v, s in zip(arrays, splits)):
+        return ring_total(arrays, splits, ident)
+    return [lax.psum(v, "seq") for v in arrays]
 
 
 def shards(
@@ -384,10 +500,11 @@
     gather = lambda v: lax.all_gather(v, "fsdp", axis=0, tiled=True)
 
     qkv_w = gather(self_qkv).reshape(width, parts, own * 3 * dh)
+    middle = gather(jnp.concatenate([self_out, cross_q, cross_out], axis=1))
     pairs_w = gather(cross_kv).reshape(width, parts, own * 2 * dh)
-    mix_self = gather(self_out).reshape(parts, own * dh, width)
-    query_w = gather(cross_q).reshape(width, parts, own * dh)
-    mix_cross = gather(cross_out).reshape(parts, own * dh, width)
+    mix_self = middle[:, :width].reshape(parts, own * dh, width)
+    query_w = middle[:, width : 2 * width].reshape(width, parts, own * dh)
+    mix_cross = middle[:, 2 * width :].reshape(parts, own * dh, width)
     inner_w = gather(ff_in)
     outer_w = gather(ff_out)
     small = jnp.concatenate([norm_self, norm_cross, norm_ff, rel_table.reshape(-1)])
@@ -455,7 +572,10 @@
     grad_third_in = jnp.einsum("tf,df->td", grad_gate_up, inner_w, preferred_element_type=f32)
     grad_from_third, grad_gain_third = norm_back(after_cross, gain_third, grad_third_in)
     grad_middle = grad_low.astype(f32) + grad_from_third
-    middle_low = grad_middle.astype(bf16)
+    middle_low, grad_inner, grad_outer = lax.optimization_barrier(
+        (grad_middle.astype(bf16), grad_inner.astype(bf16), grad_outer.astype(bf16))
+    )
+    part_inner, part_outer = scatter(grad_inner), scatter(grad_outer)
     grad_mix_cross = jnp.einsum("gtc,td->gcd", cross_tok, middle_low, preferred_element_type=f32)
     grad_cross_tok = jnp.einsum("td,gcd->gtc", middle_low, mix_cross, preferred_element_type=f32).astype(bf16)
     grad_cross = swap(grad_cross_tok).reshape(length, own * dh)
@@ -491,24 +611,39 @@
     by_bucket = jnp.einsum("twn,gtw->ng", in_bucket, tile_sums, precision=HIGH)
     grad_table = lax.dynamic_update_slice_in_dim(jnp.zeros((buckets, heads), f32), by_bucket, first_head, 1)
 
-    def reduce(grad):
-        mine = lax.psum_scatter(grad.astype(bf16), "fsdp", scatter_dimension=0, tiled=True)
-        return lax.psum(mine, "seq").astype(f32)
-
-    total_qkv = reduce(grad_qkv_w.reshape(width, heads, 3 * dh))
-    total_pairs = reduce(grad_pairs_w.reshape(width, heads, 2 * dh))
-    total_mix_self = reduce(grad_mix_self.reshape(width, width))
-    total_query = reduce(grad_query_w.reshape(width, width))
-    total_mix_cross = reduce(grad_mix_cross.reshape(width, width))
-    total_inner = reduce(grad_inner)
-    total_outer = reduce(grad_outer)
+    grad_mid = jnp.concatenate(
+        [
+            grad_mix_self.reshape(width, width).astype(bf16),
+            grad_query_w.reshape(width, width).astype(bf16),
+            grad_pairs_w.reshape(width, 2 * width).astype(bf16),
+            grad_mix_cross.reshape(width, width).astype(bf16),
+        ],
+        axis=1,
+    )
+    part_mid = scatter(grad_mid)
     gains = jnp.concatenate(
         [g.reshape(-1, part) for g in (grad_gain_first, grad_gain_second, grad_gain_third)], axis=1
     )
     tables = jnp.transpose(grad_table.reshape(buckets, -1, table_own), (1, 0, 2)).reshape(-1, buckets * table_own)
-    small_grads = jnp.concatenate([gains, tables], axis=1).astype(bf16)
-    small_total = lax.psum(small_grads, ("seq", "fsdp")).astype(f32)
-    mine = lax.dynamic_index_in_dim(small_total, lax.axis_index("fsdp"), 0, False)
+    small_grads = lax.psum(jnp.concatenate([gains, tables], axis=1).astype(bf16), "fsdp")
+    small_grads = lax.dynamic_index_in_dim(small_grads, lax.axis_index("fsdp"), 0, False)
+    small_size = small_grads.shape[0]
+    small_grads = jnp.pad(small_grads, (0, parts * 1024 - small_size)).reshape(parts * 8, 128)
+    grad_qkv_w, part_inner, part_outer = lax.optimization_barrier(
+        (grad_qkv_w.reshape(width, 3 * width).astype(bf16), part_inner, part_outer)
+    )
+    part_qkv = scatter(grad_qkv_w)
+    total_inner, total_outer = over_seq([part_inner, part_outer], (2, 2), 0)
+    total_inner, part_mid = lax.optimization_barrier((total_inner, part_mid))
+    (total_mid,) = over_seq([part_mid], (4,), 1)
+    part_qkv, small_grads, total_mid = lax.optimization_barrier((part_qkv, small_grads, total_mid))
+    total_qkv, small_total = over_seq([part_qkv, small_grads], (4, 1), 2)
+    total_qkv = total_qkv.astype(f32).reshape(-1, heads, 3 * dh)
+    total_inner, total_outer, total_mid = (v.astype(f32) for v in (total_inner, total_outer, total_mid))
+    total_mix_self, total_query = total_mid[:, :width], total_mid[:, width : 2 * width]
+    total_pairs = total_mid[:, 2 * width : 4 * width].reshape(-1, heads, 2 * dh)
+    total_mix_cross = total_mid[:, 4 * width :]
+    mine = small_total.reshape(-1)[:small_size].astype(f32)
     total_gain_first, total_gain_second, total_gain_third = (mine[i * part : (i + 1) * part] for i in range(3))
     total_table = mine[3 * part :].reshape(buckets, table_own)
     return (

time: 1010 us -> 751 us (0.74)
  the two profiles are of different devices: /device:TPU:1 before, /device:TPU:0 now
where the time goes in v2:
time: 751 us; the launch traced here: 740 us
  Pallas kernels  260 us (35%)
  blocking collectives  163 us (22%)
  matrix products  98.5 us (13%)
  waiting for transfers between devices  84.9 us (11%)
  local copies, waits for them, and re-layouts  57.5 us (8%)
  other arithmetic  33.5 us (4%)
  starting transfers between devices  27.7 us (4%)
  between operations  15.5 us (2%)
    pallas_call x3, Pallas kernels, ring_total(): pl.pallas_call(functools.partial(ring_kernel, n, splits), name='ring_tota...  199 us
    all_to_all x4, blocking collectives, swap(): lax.all_to_all(blocks, 'seq', split_axis=0, concat_axis=0, tiled=True)  87.6 us
    pallas_call x4, Pallas kernels, call(): pl.pallas_call(body, name=name, out_shape=[jax.ShapeDtypeStruct(s, d) for...  61.2 us
    unnamed x1, blocking collectives  59.2 us
    all_gather x5, waiting for transfers between devices, shards(): gather = lambda v: lax.all_gather(v, 'fsdp', axis=0, tiled=True)  57.8 us
    all_to_all x6, starting transfers between devices, swap(): lax.all_to_all(blocks, 'seq', split_axis=0, concat_axis=0, tiled=True)  26.9 us
    all_to_all x6, waiting for transfers between devices, swap(): lax.all_to_all(blocks, 'seq', split_axis=0, concat_axis=0, tiled=True)  24.5 us
    unnamed x111, local copies, waits for them, and re-layouts  23.2 us
  transfers between devices with their start and end apart: 15, of which 6 were waited for; matrix products, arithmetic and copies ran while one was open for 17% of the time, Pallas kernels for 28%

profile of v2, /device:TPU:0, one launch (start us, length us, event | category | flops | bytes accessed | tf_op | source)
XLA Modules:
  0.0 740.2 jit_solution(15982942297375437542)
XLA Ops:
  13.8 6.2 all-gather.2
  20.2 39.4 %all-gather.9.cloned.1.call-done = bf16[1024,16,192]{0,2,1:T(8,128)(2,1)} async-done(((bf16[256,16,192]{0,2,1:T(8,128)(2,1)}), bf16[1024,16,192]{0,2,1:T(8,128)(2,1)}) %all-gather.9.cloned.1.call-update) | async-done | bytes 6291472 | tf_op jit(solution)/shard_map/all_gather | solution.py:500
  59.5 5.8 fusion.6
  65.4 5.7 all-to-all-start
  72.4 59.2 %all-reduce.4 = s32[2560]{0:T(1024)S(1)} all-reduce(s32[2560]{0:T(1024)S(1)} %add_dynamic-update-slice_fusion), channel_id=2, replica_groups=mesh['seq'=8,'fsdp'=4] {'seq'}, use_global_device_ids=true, to_apply=%add.4 | all-reduce | flops 2560 | bytes 20480
  141.7 18.4 %self_forward.1 = (bf16[2048,128]{1,0:T(8,128)(2,1)}, f32[128,2048]{1,0:T(8,128)S(1)}, f32[2,2048]{1,0:T(2,128)S(1)}) custom-call(s32[2,8]{1,0:T(2,128)S(1)} %pad_add_fusion.lim_ref, s32[8,2048]{1,0:T(8,128)S(1)} %broadcast_in_dim.93.rows_ref, f32[2,1536]{1,0:T(2,128)S(1)} %maximum_maximum_fusion.ext_ref, bf16[2048,384]{1,0:T(8,128)(2,1)S(1)} %bitcast.209), custom_call_target="tpu_custom_call" | custom-call | flops 536870912 | bytes 3301504 | tf_op jit(solution)/shard_map/self_forward/pallas_call | solution.py:256
  164.6 5.7 fusion.67
  180.0 5.4 all-to-all-start.2
  190.0 7.6 %all-to-all-done.2 = bf16[8,256,128]{1,2,0:T(8,128)(2,1)} async-done(((bf16[8,256,128]{1,2,0:T(8,128)(2,1)}), bf16[8,256,128]{1,2,0:T(8,128)(2,1)}, u32[]{:S(2)}, u32[]{:S(2)}) %all-to-all-start.2) | async-done | bytes 524320 | tf_op jit(solution)/shard_map/all_to_all | solution.py:472
  203.8 6.7 all-to-all-done.3
  210.5 10.0 %cross_forward.1 = (bf16[2048,128]{1,0:T(8,128)(2,1)}, f32[128,2048]{1,0:T(8,128)S(1)}, f32[2,2048]{1,0:T(2,128)S(1)}) custom-call(s32[2,8]{1,0:T(2,128)S(1)} %pad_add_fusion.1.lim_ref, s32[8,2048]{1,0:T(8,128)S(1)} %add_add_fusion.3.rows_ref, bf16[2048,128]{1,0:T(8,128)(2,1)S(1)} %bitcast.212, bf16[512,256]{1,0:T(8,128)(2,1)S(1)} %bitcast.216), custom_call_target="tpu_custom_call" | custom-call | flops 268435456 | bytes 1704064 | tf_op jit(solution)/shard_map/cross_forward/pallas_call | solution.py:256
  225.6 9.7 %all-to-all-done.4 = bf16[8,256,128]{2,1,0:T(8,128)(2,1)S(1)} async-done(((bf16[8,256,128]{2,1,0:T(8,128)(2,1)}), bf16[8,256,128]{2,1,0:T(8,128)(2,1)S(1)}, u32[]{:S(2)}, u32[]{:S(2)}) %all-to-all-start.4) | async-done | bytes 524320 | tf_op jit(solution)/shard_map/all_to_all | solution.py:472
  239.0 10.4 %fusion.65 = f32[256,5632]{1,0:T(8,128)} fusion(bf16[1024,5632]{1,0:T(8,128)(2,1)} %all-gather.15.cloned.1.call-done, f32[256,1024]{1,0:T(8,128)} %get-tuple-element.170, f32[1024]{0:T(1024)S(1)} %bitcast.237, f32[256]{0:T(256)S(1)} %fusion.58), kind=kOutput, calls=%fused_computation.159 | convolution fusion | flops 2953576448 | bytes 18355200 | tf_op jit(solution)/shard_map/dot_general | solution.py:560
  249.4 18.4 %all-gather.17.cloned.1.call-done = bf16[2816,1024]{1,0:T(8,128)(2,1)} async-done(((bf16[704,1024]{1,0:T(8,128)(2,1)}), bf16[2816,1024]{1,0:T(8,128)(2,1)}) %all-gather.17.cloned.1.call-update) | async-done | bytes 5767184 | tf_op jit(solution)/shard_map/all_gather | solution.py:500
  267.8 10.2 %fusion.30 = (f32[256,2816]{1,0:T(8,128)S(1)}, f32[256,2816]{1,0:T(8,128)}, bf16[256,2816]{1,0:T(8,128)(2,1)}) fusion(f32[256,5632]{1,0:T(8,128)} %fusion.65, bf16[2816,1024]{1,0:T(8,128)(2,1)} %all-gather.17.cloned.1.call-done, bf16[1,256,1024]{2,1,0:T(8,128)(2,1)} %param.33), kind=kOutput, calls=%fused_computation.69 | convolution fusion | flops 1493696512 | bytes 19267584 | tf_op jit(solution)/shard_map/td,fd->tf/dot_general | solution.py:568
  279.6 7.9 %convolution_convert_fusion = bf16[1024,5632]{1,0:T(8,128)(2,1)} fusion(f32[256,2816]{1,0:T(8,128)} %get-tuple-element.140, f32[256,2816]{1,0:T(8,128)S(1)} %get-tuple-element.139, f32[256,1024]{1,0:T(8,128)S(1)} %copy-done.12, f32[1024]{0:T(1024)S(1)} %bitcast.238, f32[256]{0:T(256)S(1)} %fusion.58), kind=kOutput, calls=%fused_computation | convolution fusion | flops 2962227200 | bytes 18355200 | tf_op jit(solution)/shard_map/td,tf->df/dot_general | solution.py:571
  287.5 10.5 %multiply_reduce_fusion = (bf16[1024]{0:T(1024)(128)(2,1)S(1)}, f32[256]{0:T(256)S(1)}, f32[256,1024]{1,0:T(8,128)}) fusion(f32[256,1024]{1,0:T(8,128)} %get-tuple-element.170, f32[256]{0:T(256)S(1)} %fusion.58, f32[1024]{0:T(1024)S(1)} %bitcast.239, bf16[1024,5632]{1,0:T(8,128)(2,1)} %all-gather.15.cloned.1.call-done, f32[256,2816]{1,0:T(8,128)} %get-tuple-element.140, ...), kind=kOutput, calls=%fused_computation.61 | convolution fusion | flops 2957245184 | bytes 19406848 | tf_op jit(solution)/shard_map/tf,df->td/dot_general | solution.py:572
  308.4 20.3 %all_to_all.50 = bf16[8,256,128]{1,2,0:T(8,128)(2,1)} all-to-all(bf16[8,256,128]{1,2,0:T(8,128)(2,1)S(1)} %fusion.15), channel_id=1, replica_groups=mesh['seq'=8,'fsdp'=4] {'seq'}, dimensions={0} | all-to-all | bytes 1048576 | tf_op jit(solution)/shard_map/all_to_all | solution.py:472
  331.3 11.3 %cross_backward.1 = (bf16[2048,128]{1,0:T(8,128)(2,1)}, bf16[512,256]{1,0:T(8,128)(2,1)S(1)}) custom-call(s32[2,8]{1,0:T(2,128)S(1)} %pad_add_fusion.1.lim_ref, s32[8,2048]{1,0:T(8,128)S(1)} %add_add_fusion.3.rows_ref, bf16[2048,128]{1,0:T(8,128)(2,1)S(1)} %bitcast.213, bf16[512,256]{1,0:T(8,128)(2,1)S(1)} %bitcast.217, bf16[2048,128]{1,0:T(8,128)(2,1)S(1)} %bitcast.214, ...), custom_call_target="tpu_custom_call" | custom-call | flops 671088640 | bytes 4882560 | tf_op jit(solution)/shard_map/cross_backward/pallas_call | solution.py:256
  342.5 11.7 %all_to_all.51 = bf16[8,64,256]{2,1,0:T(8,128)(2,1)S(1)} all-to-all(bf16[8,64,256]{2,1,0:T(8,128)(2,1)S(1)} %bitcast.218), channel_id=1, replica_groups=mesh['seq'=8,'fsdp'=4] {'seq'}, dimensions={0} | all-to-all | bytes 524288 | tf_op jit(solution)/shard_map/all_to_all | solution.py:472
  364.9 6.8 copy.118
  389.0 5.8 pad_maximum_fusion
  398.3 17.9 %all_to_all.52 = bf16[8,256,128]{1,2,0:T(8,128)(2,1)S(1)} all-to-all(bf16[8,256,128]{1,2,0:T(8,128)(2,1)S(1)} %fusion.16), channel_id=1, replica_groups=mesh['seq'=8,'fsdp'=4] {'seq'}, dimensions={0} | all-to-all | bytes 1048576 | tf_op jit(solution)/shard_map/all_to_all | solution.py:472
  417.8 21.4 %self_backward.1 = (bf16[2048,384]{1,0:T(8,128)(2,1)S(1)}, f32[2,5,512]{2,1,0:T(8,128)S(1)}) custom-call(s32[2,8]{1,0:T(2,128)S(1)} %pad_add_fusion.lim_ref, s32[8,2048]{1,0:T(8,128)S(1)} %broadcast_in_dim.93.rows_ref, f32[2,1536]{1,0:T(2,128)S(1)} %maximum_maximum_fusion.ext_ref, bf16[2048,384]{1,0:T(8,128)(2,1)S(1)} %bitcast.210, ...), custom_call_target="tpu_custom_call" | custom-call | flops 1342177280 | bytes 6480000 | tf_op jit(solution)/shard_map/self_backward/pallas_call | solution.py:256
  439.2 37.6 %all_to_all.53 = bf16[8,256,384]{2,1,0:T(8,128)(2,1)S(1)} all-to-all(bf16[8,256,384]{2,1,0:T(8,128)(2,1)S(1)} %bitcast.211), channel_id=1, replica_groups=mesh['seq'=8,'fsdp'=4] {'seq'}, dimensions={0} | all-to-all | bytes 3145728 | tf_op jit(solution)/shard_map/all_to_all | solution.py:472
  478.5 6.4 convolution_convert_fusion.1
  486.1 5.7 fusion.17
  493.9 5.8 fusion.23
  499.8 9.8 %psum.7 = bf16[4,896]{1,0:T(4,128)(2,1)S(1)} all-reduce(bf16[4,896]{1,0:T(4,128)(2,1)S(1)} %pad_maximum_fusion.2), channel_id=1, replica_groups=mesh['seq'=8,'fsdp'=4] {'fsdp'}, use_global_device_ids=true, to_apply=%region_20.21 | all-reduce | flops 3584 | bytes 14336 | tf_op jit(solution)/shard_map/psum | solution.py:628
  513.5 89.6 %ring_total.3 = (bf16[256,5632]{1,0:T(8,128)(2,1)S(1)}, bf16[704,1024]{1,0:T(8,128)(2,1)S(1)}) custom-call(bf16[256,5632]{1,0:T(8,128)(2,1)} %reduce-scatter.5.cloned.1.call-done.refs_0_, bf16[704,1024]{1,0:T(8,128)(2,1)S(1)} %copy-done.5), custom_call_target="tpu_custom_call" | custom-call | flops 4325376 | bytes 259522560 | tf_op jit(solution)/shard_map/ring_total/pallas_call | solution.py:435
  610.1 59.6 %ring_total.4 = bf16[256,5120]{1,0:T(8,128)(2,1)S(1)} custom-call(bf16[256,5120]{1,0:T(8,128)(2,1)S(1)} %copy-done.2), custom_call_target="tpu_custom_call" | custom-call | flops 2621440 | bytes 157286400 | tf_op jit(solution)/shard_map/ring_total/pallas_call | solution.py:435
  671.2 49.3 %ring_total.5 = (bf16[256,3072]{1,0:T(8,128)(2,1)S(1)}, bf16[64,128]{1,0:T(8,128)(2,1)S(1)}) custom-call(bf16[256,3072]{1,0:T(8,128)(2,1)S(1)} %copy-done.3, bf16[64,128]{1,0:T(8,128)(2,1)S(1)} %pad_bitcast_fusion.refs_1_), custom_call_target="tpu_custom_call" | custom-call | flops 1589248 | bytes 95354880 | tf_op jit(solution)/shard_map/ring_total/pallas_call | solution.py:435
  (229 shorter events, 128.2 us)
Async XLA Ops:
  7.2 178.5 %copy-start = (bf16[1,64,1024]{2,1,0:T(8,128)(2,1)S(1)}, bf16[1,64,1024]{2,1,0:T(8,128)(2,1)}, u32[]{:S(2)}) copy-start(bf16[1,64,1024]{2,1,0:T(8,128)(2,1)} %param.18) | copy-start | bytes 393220
  7.2 52.3 %all-gather.9.cloned.1.call-start = ((), (), s32[]{:S(2)}) async-start(), calls=%async_computation.14 | async-start | bytes 7864320 | tf_op jit(solution)/shard_map/all_gather | solution.py:500
  7.9 156.7 %all-gather.11.cloned.1.call-start = ((), (), s32[]{:S(2)}) async-start(), calls=%async_computation.15 | async-start | bytes 7864320 | tf_op jit(solution)/shard_map/all_gather | solution.py:500
  10.6 175.0 %all-gather.13.cloned.1.call-start = ((), (), s32[]{:S(2)}) async-start(), calls=%async_computation.16 | async-start | bytes 5242880 | tf_op jit(solution)/shard_map/all_gather | solution.py:500
  12.3 7.7 %copy-start.23 = (bf16[1,256,1024]{2,1,0:T(8,128)(2,1)S(1)}, bf16[1,256,1024]{2,1,0:T(8,128)(2,1)}, u32[]{:S(2)}) copy-start(bf16[1,256,1024]{2,1,0:T(8,128)(2,1)} %param.17) | copy-start | bytes 1572868
  12.3 226.7 %all-gather.15.cloned.1.call-start = ((), (), s32[]{:S(2)}) async-start(), calls=%async_computation.17 | async-start | bytes 14417920 | tf_op jit(solution)/shard_map/all_gather | solution.py:500
  12.9 254.9 %all-gather.17.cloned.1.call-start = ((), (), s32[]{:S(2)}) async-start(), calls=%async_computation.18 | async-start | bytes 7208960 | tf_op jit(solution)/shard_map/all_gather | solution.py:500
  65.4 5.7 copy-start.46
  65.4 6.9 copy-start.41
  65.4 6.9 copy-start.45
  65.4 75.6 %copy-start.38 = (s32[2048]{0:T(1024)S(1)}, s32[2048]{0:T(1024)}, u32[]{:S(2)}) copy-start(s32[2048]{0:T(1024)} %param.21) | copy-start | bytes 24580
  65.4 76.3 %all-to-all-start = ((bf16[8,256,384]{2,1,0:T(8,128)(2,1)}), bf16[8,256,384]{2,1,0:T(8,128)(2,1)S(1)}, u32[]{:S(2)}, u32[]{:S(2)}) async-start(bf16[8,256,384]{2,1,0:T(8,128)(2,1)} %fusion.6), calls=%async_computation | async-start | bytes 3145728 | tf_op jit(solution)/shard_map/all_to_all | solution.py:472
  161.1 13.7 %all-to-all-start.1 = ((bf16[8,256,128]{2,1,0:T(8,128)(2,1)}), bf16[8,256,128]{2,1,0:T(8,128)(2,1)S(1)}, u32[]{:S(2)}, u32[]{:S(2)}) async-start(bf16[8,256,128]{2,1,0:T(8,128)(2,1)} %bitcast.12), calls=%async_computation.1 | async-start | bytes 1048576 | tf_op jit(solution)/shard_map/all_to_all | solution.py:472
  178.4 24.1 %copy-start.15 = (f32[256,1024]{1,0:T(8,128)}, f32[256,1024]{1,0:T(8,128)S(1)}, u32[]{:S(2)}) copy-start(f32[256,1024]{1,0:T(8,128)S(1)} %get-tuple-element.168) | copy-start | bytes 3145732
  180.0 17.6 %all-to-all-start.2 = ((bf16[8,256,128]{1,2,0:T(8,128)(2,1)}), bf16[8,256,128]{1,2,0:T(8,128)(2,1)}, u32[]{:S(2)}, u32[]{:S(2)}) async-start(bf16[8,256,128]{1,2,0:T(8,128)(2,1)} %fusion.14), calls=%async_computation.2 | async-start | bytes 1048576 | tf_op jit(solution)/shard_map/all_to_all | solution.py:472
  197.6 12.9 %all-to-all-start.3 = ((bf16[8,64,256]{2,1,0:T(8,128)(2,1)}), bf16[8,64,256]{2,1,0:T(8,128)(2,1)S(1)}, u32[]{:S(2)}, u32[]{:S(2)}) async-start(bf16[8,64,256]{2,1,0:T(8,128)(2,1)} %fusion.18), calls=%async_computation.3 | async-start | bytes 524288 | tf_op jit(solution)/shard_map/all_to_all | solution.py:472
  221.5 13.7 %all-to-all-start.4 = ((bf16[8,256,128]{2,1,0:T(8,128)(2,1)}), bf16[8,256,128]{2,1,0:T(8,128)(2,1)S(1)}, u32[]{:S(2)}, u32[]{:S(2)}) async-start(bf16[8,256,128]{2,1,0:T(8,128)(2,1)} %bitcast.26), calls=%async_computation.4 | async-start | bytes 1048576 | tf_op jit(solution)/shard_map/all_to_all | solution.py:472
  225.0 259.8 %reduce-scatter.7.cloned.1.call-start = ((), (), s32[]{:S(2)}) async-start(), calls=%async_computation.20 | async-start | bytes 7208960 | tf_op jit(solution)/shard_map/reduce_scatter | solution.py:476
  235.2 14.2 %copy-start.30 = (bf16[8,256,128]{2,1,0:T(8,128)(2,1)}, bf16[8,256,128]{2,1,0:T(8,128)(2,1)S(1)}, u32[]{:S(2)}) copy-start(bf16[8,256,128]{2,1,0:T(8,128)(2,1)S(1)} %all-to-all-done.4) | copy-start | bytes 1572868
  267.8 11.8 %copy-start.12 = (f32[256,1024]{1,0:T(8,128)S(1)}, f32[256,1024]{1,0:T(8,128)}, u32[]{:S(2)}) copy-start(f32[256,1024]{1,0:T(8,128)} %get-tuple-element.170) | copy-start | bytes 3145732
  287.5 10.6 %copy-start.31 = (bf16[1,256,1024]{2,1,0:T(8,128)(2,1)S(1)}, bf16[1,256,1024]{2,1,0:T(8,128)(2,1)}, u32[]{:S(2)}) copy-start(bf16[1,256,1024]{2,1,0:T(8,128)(2,1)} %param.33) | copy-start | bytes 1572868
  287.5 10.6 %copy-start.34 = (bf16[256,2816]{1,0:T(8,128)(2,1)S(1)}, bf16[256,2816]{1,0:T(8,128)(2,1)}, u32[]{:S(2)}) copy-start(bf16[256,2816]{1,0:T(8,128)(2,1)} %get-tuple-element.144) | copy-start | bytes 4325380
  305.0 179.9 %reduce-scatter.5.cloned.1.call-start = ((), (), s32[]{:S(2)}) async-start(), calls=%async_computation.19 | async-start | bytes 14417920 | tf_op jit(solution)/shard_map/reduce_scatter | solution.py:476
  354.2 17.5 %all-to-all-start.6 = ((bf16[8,256,128]{2,1,0:T(8,128)(2,1)}), bf16[8,256,128]{2,1,0:T(8,128)(2,1)}, u32[]{:S(2)}, u32[]{:S(2)}) async-start(bf16[8,256,128]{2,1,0:T(8,128)(2,1)} %bitcast.34), calls=%async_computation.6 | async-start | bytes 1048576 | tf_op jit(solution)/shard_map/all_to_all | solution.py:472
  358.4 245.8 %reduce-scatter.11.cloned.1.call-start = ((), (), s32[]{:S(2)}) async-start(), calls=%async_computation.22 | async-start | bytes 13107200 | tf_op jit(solution)/shard_map/reduce_scatter | solution.py:476
  364.9 9.1 %copy-start.16 = (f32[256,1024]{1,0:T(8,128)S(1)}, f32[256,1024]{1,0:T(8,128)}, u32[]{:S(2)}) copy-start(f32[256,1024]{1,0:T(8,128)} %copy-done.15) | copy-start | bytes 3145732
  381.7 4.7 copy-start.29
  394.8 275.0 %reduce-scatter.9.cloned.1.call-start = ((), (), s32[]{:S(2)}) async-start(), calls=%async_computation.21 | async-start | bytes 7864320 | tf_op jit(solution)/shard_map/reduce_scatter | solution.py:476
  439.2 39.2 %copy-start.24 = (bf16[1,256,1024]{2,1,0:T(8,128)(2,1)S(1)}, bf16[1,256,1024]{2,1,0:T(8,128)(2,1)}, u32[]{:S(2)}) copy-start(bf16[1,256,1024]{2,1,0:T(8,128)(2,1)} %param.17) | copy-start | bytes 1572868
  486.1 5.7 copy-start.22
  493.9 15.8 %copy-start.21 = (f32[256,1024]{1,0:T(8,128)S(1)}, f32[256,1024]{1,0:T(8,128)}, u32[]{:S(2)}) copy-start(f32[256,1024]{1,0:T(8,128)} %copy-done.19) | copy-start | bytes 3145732
  720.5 5.0 copy-start.4
  (30 other events, 58.9 us)
Sparse Core Ops, SparseCore 0:
  9.6 49.9 all-gather.8
  61.7 46.3 all-gather.10
  110.2 35.0 all-gather.12
  146.7 76.1 all-gather.14
  224.3 43.4 all-gather.16
  305.1 54.8 reduce-scatter.6
  362.8 92.1 reduce-scatter.4
  457.8 85.5 reduce-scatter.10
  546.1 58.3 reduce-scatter.8

commit v3 on v2

--- a/solution.py
+++ b/solution.py
@@ -356,6 +356,11 @@
     return 2 * z + x
 
 
+def ring_cut(shape, split, n):
+    rows, cols = shape[0] // n, shape[1]
+    return (rows, cols // split) if split > 0 else (rows // -split, cols)
+
+
 def ring_kernel(n, splits, *refs):
     count = len(splits)
     x_refs, y_refs, slots = refs[:count], refs[count : 2 * count], refs[2 * count : 3 * count]
@@ -370,18 +375,15 @@
 
     streams = []
     for k in range(count):
-        for piece in range(splits[k]):
+        for piece in range(abs(splits[k])):
             streams.append((k, piece, piece % 2))
 
-    def view(ref, k, piece, chunk):
-        rows = x_refs[k].shape[0] // n
-        cols = x_refs[k].shape[1] // splits[k]
-        return ref.at[pl.ds(pl.multiple_of(chunk * rows, 8), rows), pl.ds(piece * cols, cols)]
-
-    def slot(k, piece, step):
-        rows = x_refs[k].shape[0] // n
-        cols = x_refs[k].shape[1] // splits[k]
-        return slots[k].at[pl.ds(step * rows, rows), pl.ds(piece * cols, cols)]
+    def window(ref, k, piece, chunk):
+        whole = x_refs[k].shape[0] // n
+        rows, cols = ring_cut(x_refs[k].shape, splits[k], n)
+        if splits[k] > 0:
+            return ref.at[pl.ds(chunk * whole, rows), pl.ds(piece * cols, cols)]
+        return ref.at[pl.ds(chunk * whole + piece * rows, rows), :]
 
     def copy(number, step, src, dst, down):
         return pltpu.make_async_remote_copy(
@@ -403,19 +405,19 @@
         copies[number, step].start()
 
     for number, (k, piece, down) in enumerate(streams):
-        start(number, 0, view(x_refs[k], k, piece, place), slot(k, piece, 0), down)
+        start(number, 0, window(x_refs[k], k, piece, place), window(slots[k], k, piece, 0), down)
     for step in range(n - 1):
         for number, (k, piece, down) in enumerate(streams):
             copies[number, step].wait_recv()
             chunk = chunk_at(down, step)
-            mine = view(x_refs[k], k, piece, chunk)
-            landed = slot(k, piece, step)
+            mine = window(x_refs[k], k, piece, chunk)
+            landed = window(slots[k], k, piece, step)
             total = landed[...].astype(jnp.float32) + mine[...].astype(jnp.float32)
             if step < n - 2:
                 landed[...] = total.astype(jnp.bfloat16)
-                start(number, step + 1, landed, slot(k, piece, step + 1), down)
+                start(number, step + 1, landed, window(slots[k], k, piece, step + 1), down)
             else:
-                done = view(y_refs[k], k, piece, chunk)
+                done = window(y_refs[k], k, piece, chunk)
                 done[...] = total.astype(jnp.bfloat16)
                 start(number, n - 1, done, done, down)
     for step in range(n - 1):
@@ -423,7 +425,7 @@
             copies[number, n - 1 + step].wait_recv()
             if step < n - 2:
                 chunk = chunk_at(down, n - 1 + step)
-                done = view(y_refs[k], k, piece, chunk)
+                done = window(y_refs[k], k, piece, chunk)
                 start(number, n + step, done, done, down)
     for one in copies.values():
         one.wait_send()
@@ -432,6 +434,7 @@
 def ring_total(arrays, splits, ident):
     n = lax.axis_size("seq")
     size = sum(v.size * 2 for v in arrays)
+    streams = sum(abs(s) for s in splits)
     return pl.pallas_call(
         functools.partial(ring_kernel, n, splits),
         name="ring_total",
@@ -439,7 +442,7 @@
         in_specs=[pl.BlockSpec(memory_space=pltpu.VMEM)] * len(arrays),
         out_specs=[pl.BlockSpec(memory_space=pltpu.VMEM)] * len(arrays),
         scratch_shapes=[pltpu.VMEM((v.shape[0] // n * (n - 1), v.shape[1]), jnp.bfloat16) for v in arrays]
-        + [pltpu.SemaphoreType.DMA((sum(splits), 2 * n - 2)), pltpu.SemaphoreType.DMA((sum(splits), 2 * n - 2))],
+        + [pltpu.SemaphoreType.DMA((streams, 2 * n - 2)), pltpu.SemaphoreType.DMA((streams, 2 * n - 2))],
         compiler_params=pltpu.CompilerParams(
             collective_id=ident, has_side_effects=True, vmem_limit_bytes=48 << 20
         ),
@@ -447,6 +450,69 @@
     )(*arrays)
 
 
+def team(n):
+    s, f = lax.axis_index("seq"), lax.axis_index("fsdp")
+    half = s // (n // 2)
+    away = (half + f) % 2
+    return f // 2, half, (s + away * (n // 2)) % n
+
+
+def swap_kernel(n, count, *refs):
+    x_refs, y_refs = refs[:count], refs[count : 2 * count]
+    send_sem, recv_sem, own_sem = refs[2 * count :]
+    pair, half, rank = team(n)
+
+    def device(other):
+        away = (other // (n // 2) + half) % 2
+        return {"seq": (other + away * (n // 2)) % n, "fsdp": 2 * pair + (half + away) % 2}
+
+    barrier = pltpu.get_barrier_semaphore()
+    for j in range(1, n):
+        pl.semaphore_signal(barrier, inc=1, device_id=device((rank + j) % n), device_id_type=MESH)
+    pl.semaphore_wait(barrier, n - 1)
+    copies = []
+    for k in range(count):
+        for j in range(1, n):
+            other = (rank + j) % n
+            one = pltpu.make_async_remote_copy(
+                src_ref=x_refs[k].at[other],
+                dst_ref=y_refs[k].at[rank],
+                send_sem=send_sem.at[k, j],
+                recv_sem=recv_sem.at[k, j],
+                device_id=device(other),
+                device_id_type=MESH,
+            )
+            one.start()
+            copies.append(one)
+    own = [
+        pltpu.make_async_copy(x_refs[k].at[rank], y_refs[k].at[rank], own_sem.at[k]) for k in range(count)
+    ]
+    for one in own:
+        one.start()
+    for one in copies + own:
+        one.wait()
+
+
+def swap(arrays, ident):
+    n = lax.axis_size("seq")
+    count = len(arrays)
+    size = sum(v.size * 2 for v in arrays)
+    return pl.pallas_call(
+        functools.partial(swap_kernel, n, count),
+        name="swap",
+        out_shape=[jax.ShapeDtypeStruct(v.shape, v.dtype) for v in arrays],
+        in_specs=[pl.BlockSpec(memory_space=pl.ANY)] * count,
+        out_specs=[pl.BlockSpec(memory_space=pl.ANY)] * count,
+        scratch_shapes=[
+            pltpu.SemaphoreType.DMA((count, n)),
+            pltpu.SemaphoreType.DMA((count, n)),
+            pltpu.SemaphoreType.DMA((count,)),
+        ],
+        compiler_params=pltpu.CompilerParams(collective_id=ident, has_side_effects=True),
+        cost_estimate=pl.CostEstimate(flops=0, bytes_accessed=30 * size, transcendentals=0),
+    )(*arrays)
+
+
 def norm_apply(value, gain):
     return value * lax.rsqrt(jnp.mean(value * value, axis=-1, keepdims=True) + EPS) * gain
 
@@ -456,9 +522,8 @@
     return pull(grad)
 
 
-def gate_mix(gate_up):
-    inner = gate_up.shape[1] // 2
-    return jax.nn.gelu(gate_up[:, :inner], approximate=True) * gate_up[:, inner:]
+def gate_mix(gate, up):
+    return jax.nn.gelu(gate, approximate=True) * up
 
 
 def counts_below(ids, values):
@@ -468,8 +533,19 @@
     return total
 
 
-def swap(blocks):
-    return lax.all_to_all(blocks, "seq", split_axis=0, concat_axis=0, tiled=True)
+def change_home(value):
+    n, fan = lax.axis_size("seq"), lax.axis_size("fsdp")
+    pairs = []
+    for s in range(n):
+        for f in range(fan):
+            away = (s // (n // 2) + f) % 2
+            target = ((s + n // 2) % n, f ^ 1) if away else (s, f)
+            pairs.append((s * fan + f, target[0] * fan + target[1]))
+    return lax.ppermute(value, ("seq", "fsdp"), pairs)
+
+
+def spread(blocks):
+    return lax.all_to_all(blocks, "fsdp", split_axis=0, concat_axis=0, tiled=True)
 
 
 def scatter(grad):
@@ -502,11 +578,13 @@
     qkv_w = gather(self_qkv).reshape(width, parts, own * 3 * dh)
     middle = gather(jnp.concatenate([self_out, cross_q, cross_out], axis=1))
     pairs_w = gather(cross_kv).reshape(width, parts, own * 2 * dh)
+    fan = lax.axis_size("fsdp")
+    units = ff_in.shape[1] // (2 * fan)
+    inner_mine = spread(jnp.transpose(ff_in.reshape(-1, 2, fan, units), (2, 1, 0, 3)))
+    gate_w, up_w = (inner_mine[:, i].reshape(width, units) for i in range(2))
     mix_self = middle[:, :width].reshape(parts, own * dh, width)
     query_w = middle[:, width : 2 * width].reshape(width, parts, own * dh)
     mix_cross = middle[:, 2 * width :].reshape(parts, own * dh, width)
-    inner_w = gather(ff_in)
-    outer_w = gather(ff_out)
     small = jnp.concatenate([norm_self, norm_cross, norm_ff, rel_table.reshape(-1)])
     small = lax.all_gather(small, "fsdp", axis=0, tiled=False)
     part = norm_self.shape[0]
@@ -515,7 +593,10 @@
     )
     table = jnp.transpose(small[:, 3 * part :].reshape(-1, buckets, table_own), (1, 0, 2)).reshape(buckets, heads)
     both_ids = jnp.concatenate([decoder_ids.reshape(-1), encoder_ids.reshape(-1)])
-    both_ids = lax.all_gather(both_ids, "seq", axis=0, tiled=False)
+    both_ids = lax.all_gather(both_ids, ("seq", "fsdp"), axis=0, tiled=False).reshape(parts, fan, -1)
+    pair, half, rank = team(parts)
+    both_ids = lax.dynamic_index_in_dim(both_ids, 2 * pair + half, 1, False)
+    qkv_w, both_ids, small = lax.optimization_barrier((qkv_w, both_ids, small))
     ids = both_ids[:, :local].reshape(length)
     enc_ids = both_ids[:, local:].reshape(keys)
 
@@ -531,7 +612,7 @@
     )
     cross_limits = jnp.stack([enc_first[::BQ] // bk, (enc_last[BQ - 1 :: BQ] + bk - 1) // bk])
 
-    first_head = lax.axis_index("seq") * own
+    first_head = rank * own
     table_mine = lax.dynamic_slice_in_dim(table.astype(f32), first_head, own, 1)
     near = rel_buckets[:REACH]
     onehot = (near[:, None] == jnp.arange(buckets, dtype=jnp.int32)[None, :]).astype(f32)
@@ -540,68 +621,83 @@
         [jnp.full((own, BQ), MASKED, f32), bias, jnp.zeros((own, BQ), f32)], axis=1
     )
 
-    stream = layer_in.astype(f32).reshape(rows, width)
+    stream = change_home(layer_in.reshape(rows, width)).astype(f32)
+    others = change_home(jnp.concatenate([cotangent.reshape(rows, width), encoder.reshape(-1, width)]))
+    grad_low, enc_flat = others[:rows], others[rows:]
     normed_first = norm_apply(stream, gain_first).astype(bf16)
     qkv_tok = jnp.einsum("td,dge->gte", normed_first, qkv_w, preferred_element_type=f32).astype(bf16)
-    qkv = swap(qkv_tok).reshape(length, own * 3 * dh)
+    (qkv,) = swap([qkv_tok], 10)
+    qkv = qkv.reshape(length, own * 3 * dh)
     out_self, self_t, self_lse = self_forward(self_limits, self_rows, ext, qkv)
-    self_tok = swap(out_self.reshape(parts, local, own * dh))
+    (self_tok,) = swap([out_self.reshape(parts, local, own * dh)], 11)
     after_self = stream + jnp.einsum("gtc,gcd->td", self_tok, mix_self, preferred_element_type=f32)
     normed_second = norm_apply(after_self, gain_second).astype(bf16)
     query_tok = jnp.einsum("td,dgc->gtc", normed_second, query_w, preferred_element_type=f32).astype(bf16)
-    enc_flat = encoder.reshape(seqs * enc_local, width)
     pairs_tok = jnp.einsum("td,dge->gte", enc_flat, pairs_w, preferred_element_type=f32).astype(bf16)
-    query_cross = swap(query_tok).reshape(length, own * dh)
-    pairs = swap(pairs_tok).reshape(keys, own * 2 * dh)
+    query_cross, pairs = swap([query_tok, pairs_tok], 12)
+    query_cross, pairs = query_cross.reshape(length, own * dh), pairs.reshape(keys, own * 2 * dh)
     out_cross, cross_t, cross_lse = cross_forward(cross_limits, cross_rows, query_cross, pairs)
-    cross_tok = swap(out_cross.reshape(parts, local, own * dh))
+    (cross_tok,) = swap([out_cross.reshape(parts, local, own * dh)], 11)
     after_cross = after_self + jnp.einsum("gtc,gcd->td", cross_tok, mix_cross, preferred_element_type=f32)
     normed_third = norm_apply(after_cross, gain_third).astype(bf16)
-    gate_up = jnp.dot(normed_third, inner_w, preferred_element_type=f32)
-    hidden = gate_mix(gate_up).astype(bf16)
-    layer_out = (
-        (after_cross + jnp.dot(hidden, outer_w, preferred_element_type=f32)).astype(bf16).reshape(seqs, local, width)
-    )
-
-    grad_low = cotangent.reshape(rows, width)
-    grad_outer = jnp.einsum("tf,td->fd", hidden, grad_low, preferred_element_type=f32)
-    grad_hidden = jnp.einsum("td,fd->tf", grad_low, outer_w, preferred_element_type=f32)
-    _, pull_mix = jax.vjp(gate_mix, gate_up)
-    grad_gate_up = pull_mix(grad_hidden)[0].astype(bf16)
-    grad_inner = jnp.einsum("td,tf->df", normed_third, grad_gate_up, preferred_element_type=f32)
-    grad_third_in = jnp.einsum("tf,df->td", grad_gate_up, inner_w, preferred_element_type=f32)
+    normed_group = gather(normed_third)
+    gate = jnp.dot(normed_group, gate_w, preferred_element_type=f32)
+    up = jnp.dot(normed_group, up_w, preferred_element_type=f32)
+    hidden = gate_mix(gate, up).astype(bf16)
+    outer_part = jnp.dot(hidden, ff_out, preferred_element_type=f32).astype(bf16)
+    layer_out = (after_cross + scatter(outer_part).astype(f32)).astype(bf16)
+    layer_out = change_home(layer_out).reshape(seqs, local, width)
+
+    grad_group = gather(grad_low)
+    part_outer = jnp.einsum("tf,td->fd", hidden, grad_group, preferred_element_type=f32).astype(bf16)
+    grad_hidden = jnp.einsum("td,fd->tf", grad_group, ff_out, preferred_element_type=f32)
+    _, pull_mix = jax.vjp(gate_mix, gate, up)
+    grad_gate, grad_up = (g.astype(bf16) for g in pull_mix(grad_hidden))
+    grad_third_in = jnp.einsum("tf,df->td", grad_gate, gate_w, preferred_element_type=f32) + jnp.einsum(
+        "tf,df->td", grad_up, up_w, preferred_element_type=f32
+    )
+    grad_third_in = scatter(grad_third_in.astype(bf16))
+    grad_inner = [
+        jnp.einsum("td,tf->df", normed_group, g, preferred_element_type=f32).astype(bf16).reshape(fan, -1, units)
+        for g in (grad_gate, grad_up)
+    ]
+    grad_third_in, grad_inner, part_outer = lax.optimization_barrier(
+        (grad_third_in, jnp.stack(grad_inner, axis=1), part_outer)
+    )
+    part_inner = jnp.transpose(spread(grad_inner), (2, 1, 0, 3)).reshape(-1, 2 * fan * units)
+    grad_third_in = grad_third_in.astype(f32)
     grad_from_third, grad_gain_third = norm_back(after_cross, gain_third, grad_third_in)
     grad_middle = grad_low.astype(f32) + grad_from_third
-    middle_low, grad_inner, grad_outer = lax.optimization_barrier(
-        (grad_middle.astype(bf16), grad_inner.astype(bf16), grad_outer.astype(bf16))
-    )
-    part_inner, part_outer = scatter(grad_inner), scatter(grad_outer)
+    middle_low = grad_middle.astype(bf16)
     grad_mix_cross = jnp.einsum("gtc,td->gcd", cross_tok, middle_low, preferred_element_type=f32)
     grad_cross_tok = jnp.einsum("td,gcd->gtc", middle_low, mix_cross, preferred_element_type=f32).astype(bf16)
-    grad_cross = swap(grad_cross_tok).reshape(length, own * dh)
+    (grad_cross,) = swap([grad_cross_tok], 11)
+    grad_cross = grad_cross.reshape(length, own * dh)
     grad_query, grad_pairs = cross_backward(
         cross_limits, cross_rows, query_cross, pairs, grad_cross, cross_t, cross_lse
     )
-    grad_query_tok = swap(grad_query.reshape(parts, local, own * dh))
-    grad_pairs_tok = swap(grad_pairs.reshape(parts, enc_local, own * 2 * dh))
+    grad_query_tok, grad_pairs_tok = swap(
+        [grad_query.reshape(parts, local, own * dh), grad_pairs.reshape(parts, enc_local, own * 2 * dh)], 12
+    )
     grad_query_w = jnp.einsum("td,gtc->dgc", normed_second, grad_query_tok, preferred_element_type=f32)
     grad_second_in = jnp.einsum("gtc,dgc->td", grad_query_tok, query_w, preferred_element_type=f32)
     grad_pairs_w = jnp.einsum("td,gte->dge", enc_flat, grad_pairs_tok, preferred_element_type=f32)
-    grad_encoder = jnp.einsum("gte,dge->td", grad_pairs_tok, pairs_w, preferred_element_type=f32).reshape(
-        seqs, enc_local, width
-    )
+    grad_encoder = jnp.einsum("gte,dge->td", grad_pairs_tok, pairs_w, preferred_element_type=f32)
+    grad_encoder = change_home(grad_encoder.astype(bf16)).astype(f32).reshape(seqs, enc_local, width)
     grad_from_second, grad_gain_second = norm_back(after_self, gain_second, grad_second_in)
     grad_upper = grad_middle + grad_from_second
     upper_low = grad_upper.astype(bf16)
     grad_mix_self = jnp.einsum("gtc,td->gcd", self_tok, upper_low, preferred_element_type=f32)
     grad_self_tok = jnp.einsum("td,gcd->gtc", upper_low, mix_self, preferred_element_type=f32).astype(bf16)
-    grad_self = swap(grad_self_tok).reshape(length, own * dh)
+    (grad_self,) = swap([grad_self_tok], 11)
+    grad_self = grad_self.reshape(length, own * dh)
     grad_qkv, tile_sums = self_backward(self_limits, self_rows, ext, qkv, grad_self, self_t, self_lse)
-    grad_qkv_tok = swap(grad_qkv.reshape(parts, local, own * 3 * dh))
+    (grad_qkv_tok,) = swap([grad_qkv.reshape(parts, local, own * 3 * dh)], 10)
     grad_qkv_w = jnp.einsum("td,gte->dge", normed_first, grad_qkv_tok, preferred_element_type=f32)
     grad_first_in = jnp.einsum("gte,dge->td", grad_qkv_tok, qkv_w, preferred_element_type=f32)
     grad_from_first, grad_gain_first = norm_back(stream, gain_first, grad_first_in)
-    grad_layer_in = (grad_upper + grad_from_first).reshape(seqs, local, width)
+    grad_layer_in = change_home((grad_upper + grad_from_first).astype(bf16)).astype(f32)
+    grad_layer_in = grad_layer_in.reshape(seqs, local, width)
 
     bucket_line = jnp.concatenate(
         [jnp.full((BQ,), -1, jnp.int32), near, jnp.full((BQ + bk,), -1, jnp.int32)]

time: 751 us -> 810 us (1.079)
  Pallas kernels: 260 us -> 370 us
  blocking collectives: 163 us -> 61.5 us
  local copies, waits for them, and re-layouts: 57.5 us -> 104 us
  waiting for transfers between devices: 84.9 us -> 108 us
  matrix products: 98.5 us -> 81.5 us
    pallas_call x0 -> x8, Pallas kernels: none -> 107 us  [swap(): pl.pallas_call(functools.partial(swap_kernel, n, count), name='swap', out...]
    all_to_all x4 -> x0, blocking collectives: 87.6 us -> none  [swap(): lax.all_to_all(blocks, 'seq', split_axis=0, concat_axis=0, tiled=True)]
    reduce_scatter x4, waiting for transfers between devices: 0.04 us -> 39.6 us  [scatter(): return lax.psum_scatter(grad, 'fsdp', scatter_dimension=0, tiled=True)]
    all_gather x5, waiting for transfers between devices: 57.8 us -> 20.9 us  [shards(): gather = lambda v: lax.all_gather(v, 'fsdp', axis=0, tiled=True)]
    unnamed x111 -> x155, local copies, waits for them, and re-layouts: 23.2 us -> 45.2 us
    all_to_all x6 -> x2, waiting for transfers between devices: 24.5 us -> 46.5 us  [spread(): lax.all_to_all(blocks, 'fsdp', split_axis=0, concat_axis=0, tiled=True)]
    all_to_all x6 -> x2, starting transfers between devices: 26.9 us -> 9.35 us  [spread(): lax.all_to_all(blocks, 'fsdp', split_axis=0, concat_axis=0, tiled=True)]
    dot_general x6 -> x9, matrix products: 49 us -> 33.6 us  [the longest x2 7.55 us: shards(): jnp.einsum('td,tf->df', normed_group, g, preferred_element_type=f32)]
  transfers between devices with their start and end apart: 15 -> 16, of which waited for: 6 -> 4; matrix products, arithmetic and copies ran while one was open for 17% -> 14% of each run, Pallas kernels for 28% -> 32%
where the time goes in v3:
time: 810 us; the launch traced here: 802 us
  Pallas kernels  370 us (46%)
  waiting for transfers between devices  108 us (13%)
  local copies, waits for them, and re-layouts  104 us (13%)
  matrix products  81.5 us (10%)
  blocking collectives  61.5 us (8%)
  other arithmetic  40.8 us (5%)
  starting transfers between devices  21.7 us (3%)
  between operations  15.2 us (2%)
    pallas_call x3, Pallas kernels, ring_total(): pl.pallas_call(functools.partial(ring_kernel, n, splits), name='ring_tota...  205 us
    pallas_call x8, Pallas kernels, swap(): pl.pallas_call(functools.partial(swap_kernel, n, count), name='swap', out...  107 us
    pallas_call x4, Pallas kernels, call(): pl.pallas_call(body, name=name, out_shape=[jax.ShapeDtypeStruct(s, d) for...  58.9 us
    unnamed x1, blocking collectives  48 us
    all_to_all x2, waiting for transfers between devices, spread(): lax.all_to_all(blocks, 'fsdp', split_axis=0, concat_axis=0, tiled=True)  46.5 us
    unnamed x155, local copies, waits for them, and re-layouts  45.2 us
    reduce_scatter x4, waiting for transfers between devices, scatter(): return lax.psum_scatter(grad, 'fsdp', scatter_dimension=0, tiled=True)  39.6 us
    all_gather x5, waiting for transfers between devices, shards(): gather = lambda v: lax.all_gather(v, 'fsdp', axis=0, tiled=True)  20.9 us
  transfers between devices with their start and end apart: 16, of which 4 were waited for; matrix products, arithmetic and copies ran while one was open for 14% of the time, Pallas kernels for 32%

profile of v3, /device:TPU:0, one launch (start us, length us, event | category | flops | bytes accessed | tf_op | source)
XLA Modules:
  0.0 802.4 jit_solution(12839667045505558434)
XLA Ops:
  17.5 48.0 %all-reduce.3 = s32[8,4,320]{2,1,0:T(4,128)S(1)} all-reduce(s32[8,4,320]{2,1,0:T(4,128)S(1)} %reshape.495), channel_id=2, replica_groups=mesh['seq'=8,'fsdp'=4] {'seq','fsdp'}, use_global_device_ids=true, to_apply=%add.2 | all-reduce | flops 10240 | bytes 81920
  65.9 5.8 all-gather.2
  77.2 20.9 %all-gather.9.cloned.1.call-done = bf16[1024,16,192]{0,2,1:T(8,128)(2,1)} async-done(((bf16[256,16,192]{0,2,1:T(8,128)(2,1)}), bf16[1024,16,192]{0,2,1:T(8,128)(2,1)}) %all-gather.9.cloned.1.call-update) | async-done | bytes 6291472 | tf_op jit(solution)/shard_map/all_gather | solution.py:576
  107.3 6.8 fusion.7.refs_0_
  114.1 20.8 %swap.8 = bf16[8,256,384]{2,1,0:T(8,128)(2,1)} custom-call(bf16[8,256,384]{2,1,0:T(8,128)(2,1)} %fusion.7.refs_0_), custom_call_target="tpu_custom_call" | custom-call | bytes 47185920 | tf_op jit(solution)/shard_map/swap/pallas_call | solution.py:500
  136.4 17.6 %self_forward.1 = (bf16[2048,128]{1,0:T(8,128)(2,1)S(1)}, f32[128,2048]{1,0:T(8,128)S(1)}, f32[2,2048]{1,0:T(2,128)S(1)}) custom-call(s32[2,8]{1,0:T(2,128)S(1)} %pad_add_fusion.lim_ref, s32[8,2048]{1,0:T(8,128)S(1)} %broadcast_in_dim.93.rows_ref, f32[2,1536]{1,0:T(2,128)S(1)} %maximum_maximum_fusion.ext_ref, bf16[2048,384]{1,0:T(8,128)(2,1)S(1)} %bitcast.205), custom_call_target="tpu_custom_call" | custom-call | flops 536870912 | bytes 3301504 | tf_op jit(solution)/shard_map/self_forward/pallas_call | solution.py:256
  155.8 9.5 %swap.9 = bf16[8,256,128]{2,1,0:T(8,128)(2,1)} custom-call(bf16[8,256,128]{2,1,0:T(8,128)(2,1)} %bitcast.211), custom_call_target="tpu_custom_call" | custom-call | bytes 15728640 | tf_op jit(solution)/shard_map/swap/pallas_call | solution.py:500
  165.6 5.8 fusion.56
  179.8 13.4 %swap.10 = (bf16[8,256,128]{2,1,0:T(8,128)(2,1)}, bf16[8,64,256]{2,1,0:T(8,128)(2,1)}) custom-call(bf16[8,256,128]{2,1,0:T(8,128)(2,1)} %fusion.13.refs_0_, bf16[8,64,256]{2,1,0:T(8,128)(2,1)} %fusion.16.refs_1_), custom_call_target="tpu_custom_call" | custom-call | bytes 23592960 | tf_op jit(solution)/shard_map/swap/pallas_call | solution.py:500
  195.3 9.2 %cross_forward.1 = (bf16[2048,128]{1,0:T(8,128)(2,1)S(1)}, f32[128,2048]{1,0:T(8,128)S(1)}, f32[2,2048]{1,0:T(2,128)S(1)}) custom-call(s32[2,8]{1,0:T(2,128)S(1)} %pad_add_fusion.1.lim_ref, s32[8,2048]{1,0:T(8,128)S(1)} %add_add_fusion.3.rows_ref, bf16[2048,128]{1,0:T(8,128)(2,1)S(1)} %bitcast.214, bf16[512,256]{1,0:T(8,128)(2,1)S(1)} %bitcast.216), custom_call_target="tpu_custom_call" | custom-call | flops 268435456 | bytes 1704064 | tf_op jit(solution)/shard_map/cross_forward/pallas_call | solution.py:256
  206.3 9.4 %swap.11 = bf16[8,256,128]{2,1,0:T(8,128)(2,1)} custom-call(bf16[8,256,128]{2,1,0:T(8,128)(2,1)} %bitcast.212), custom_call_target="tpu_custom_call" | custom-call | bytes 15728640 | tf_op jit(solution)/shard_map/swap/pallas_call | solution.py:500
  234.7 46.5 %all-to-all-done = bf16[4,2,256,704]{2,3,1,0:T(8,128)(2,1)} async-done(((bf16[4,2,256,704]{2,3,1,0:T(8,128)(2,1)}), bf16[4,2,256,704]{2,3,1,0:T(8,128)(2,1)}, u32[]{:S(2)}, u32[]{:S(2)}) %all-to-all-start) | async-done | bytes 2883616 | tf_op jit(solution)/shard_map/all_to_all | solution.py:548
  288.3 5.4 fusion.61
  297.0 7.4 multiply_convert_fusion
  334.8 6.8 reduce-scatter.7.cloned.1.call-done
  343.0 32.8 %reduce-scatter.5.cloned.1.call-done = bf16[256,1024]{1,0:T(8,128)(2,1)} async-done(((bf16[1024,1024]{1,0:T(8,128)(2,1)}), bf16[256,1024]{1,0:T(8,128)(2,1)}) %reduce-scatter.5.cloned.1.call-update) | async-done | bytes 524304 | tf_op jit(solution)/shard_map/reduce_scatter | solution.py:552
  382.1 10.0 %swap.12 = bf16[8,256,128]{2,1,0:T(8,128)(2,1)} custom-call(bf16[8,256,128]{2,1,0:T(8,128)(2,1)} %fusion.14.refs_0_), custom_call_target="tpu_custom_call" | custom-call | bytes 15728640 | tf_op jit(solution)/shard_map/swap/pallas_call | solution.py:500
  394.4 10.6 %cross_backward.1 = (bf16[2048,128]{1,0:T(8,128)(2,1)S(1)}, bf16[512,256]{1,0:T(8,128)(2,1)S(1)}) custom-call(s32[2,8]{1,0:T(2,128)S(1)} %pad_add_fusion.1.lim_ref, s32[8,2048]{1,0:T(8,128)S(1)} %add_add_fusion.3.rows_ref, bf16[2048,128]{1,0:T(8,128)(2,1)S(1)} %bitcast.215, bf16[512,256]{1,0:T(8,128)(2,1)S(1)} %bitcast.217, bf16[2048,128]{1,0:T(8,128)(2,1)S(1)} %bitcast.209, ...), custom_call_target="tpu_custom_call" | custom-call | flops 671088640 | bytes 4882560 | tf_op jit(solution)/shard_map/cross_backward/pallas_call | solution.py:256
  406.5 12.6 %swap.13 = (bf16[8,256,128]{2,1,0:T(8,128)(2,1)}, bf16[8,64,256]{2,1,0:T(8,128)(2,1)}) custom-call(bf16[8,256,128]{2,1,0:T(8,128)(2,1)} %bitcast.208, bf16[8,64,256]{2,1,0:T(8,128)(2,1)} %bitcast.213), custom_call_target="tpu_custom_call" | custom-call | bytes 23592960 | tf_op jit(solution)/shard_map/swap/pallas_call | solution.py:500
  427.4 6.6 copy.152
  445.1 6.6 pad_maximum_fusion
  460.0 9.9 %swap.14 = bf16[8,256,128]{2,1,0:T(8,128)(2,1)} custom-call(bf16[8,256,128]{2,1,0:T(8,128)(2,1)} %fusion.15.refs_0_), custom_call_target="tpu_custom_call" | custom-call | bytes 15728640 | tf_op jit(solution)/shard_map/swap/pallas_call | solution.py:500
  472.1 21.5 %self_backward.1 = (bf16[2048,384]{1,0:T(8,128)(2,1)S(1)}, f32[2,5,512]{2,1,0:T(8,128)S(1)}) custom-call(s32[2,8]{1,0:T(2,128)S(1)} %pad_add_fusion.lim_ref, s32[8,2048]{1,0:T(8,128)S(1)} %broadcast_in_dim.93.rows_ref, f32[2,1536]{1,0:T(2,128)S(1)} %maximum_maximum_fusion.ext_ref, bf16[2048,384]{1,0:T(8,128)(2,1)S(1)} %bitcast.206, ...), custom_call_target="tpu_custom_call" | custom-call | flops 1342177280 | bytes 6480000 | tf_op jit(solution)/shard_map/self_backward/pallas_call | solution.py:256
  494.8 20.9 %swap.15 = bf16[8,256,384]{2,1,0:T(8,128)(2,1)} custom-call(bf16[8,256,384]{2,1,0:T(8,128)(2,1)} %bitcast.207), custom_call_target="tpu_custom_call" | custom-call | bytes 47185920 | tf_op jit(solution)/shard_map/swap/pallas_call | solution.py:500
  515.6 6.0 convolution_convert_fusion
  521.6 8.6 %copy.150 = bf16[1024,3072]{1,0:T(8,128)(2,1)} copy(bf16[1024,3072]{0,1:T(8,128)(2,1)} %bitcast.218) | data formatting | bytes 12582912 | tf_op jit(solution)/shard_map/convert_element_type | solution.py:729
  534.7 5.7 collective-permute-start.2
  540.4 5.4 fusion.20
  550.9 7.7 psum.7
  565.0 95.7 %ring_total.3 = (bf16[256,5632]{1,0:T(8,128)(2,1)S(1)}, bf16[704,1024]{1,0:T(8,128)(2,1)S(1)}) custom-call(bf16[256,5632]{1,0:T(8,128)(2,1)} %copy.131.refs_0_, bf16[704,1024]{1,0:T(8,128)(2,1)S(1)} %convolution_convert_fusion.8.refs_1_), custom_call_target="tpu_custom_call" | custom-call | flops 4325376 | bytes 259522560 | tf_op jit(solution)/shard_map/ring_total/pallas_call | solution.py:438
  666.1 60.6 %ring_total.4 = bf16[256,5120]{1,0:T(8,128)(2,1)S(1)} custom-call(bf16[256,5120]{1,0:T(8,128)(2,1)S(1)} %copy-done.4), custom_call_target="tpu_custom_call" | custom-call | flops 2621440 | bytes 157286400 | tf_op jit(solution)/shard_map/ring_total/pallas_call | solution.py:438
  728.1 48.6 %ring_total.5 = (bf16[256,3072]{1,0:T(8,128)(2,1)S(1)}, bf16[64,128]{1,0:T(8,128)(2,1)S(1)}) custom-call(bf16[256,3072]{1,0:T(8,128)(2,1)S(1)} %copy-done.7, bf16[64,128]{1,0:T(8,128)(2,1)S(1)} %pad_bitcast_fusion.refs_1_), custom_call_target="tpu_custom_call" | custom-call | flops 1589248 | bytes 95354880 | tf_op jit(solution)/shard_map/ring_total/pallas_call | solution.py:438
  (297 shorter events, 184.1 us)
Async XLA Ops:
  7.2 289.8 %copy-start = (bf16[704,1024]{1,0:T(8,128)(2,1)S(1)}, bf16[704,1024]{1,0:T(8,128)(2,1)}, u32[]{:S(2)}) copy-start(bf16[704,1024]{1,0:T(8,128)(2,1)} %param.32) | copy-start | bytes 4325380
  7.2 65.4 %all-gather.13.cloned.1.call-start = ((), (), s32[]{:S(2)}) async-start(), calls=%async_computation.8 | async-start | bytes 5242880 | tf_op jit(solution)/shard_map/all_gather | solution.py:576
  9.9 88.2 %all-gather.9.cloned.1.call-start = ((), (), s32[]{:S(2)}) async-start(), calls=%async_computation.6 | async-start | bytes 7864320 | tf_op jit(solution)/shard_map/all_gather | solution.py:576
  10.6 155.0 %all-gather.11.cloned.1.call-start = ((), (), s32[]{:S(2)}) async-start(), calls=%async_computation.7 | async-start | bytes 7864320 | tf_op jit(solution)/shard_map/all_gather | solution.py:576
  12.0 53.7 %copy-start.53 = (bf16[32,4]{0,1:T(4,128)(2,1)S(1)}, bf16[32,4]{0,1:T(4,128)(2,1)}, u32[]{:S(2)}) copy-start(bf16[32,4]{0,1:T(4,128)(2,1)} %param.25) | copy-start | bytes 772
  12.0 53.9 %copy-start.56 = (bf16[256]{0:T(256)(128)(2,1)S(1)}, bf16[256]{0:T(256)(128)(2,1)}, u32[]{:S(2)}) copy-start(bf16[256]{0:T(256)(128)(2,1)} %param.30) | copy-start | bytes 1540
  12.0 53.9 %copy-start.57 = (bf16[256]{0:T(256)(128)(2,1)S(1)}, bf16[256]{0:T(256)(128)(2,1)}, u32[]{:S(2)}) copy-start(bf16[256]{0:T(256)(128)(2,1)} %param.26) | copy-start | bytes 1540
  12.0 53.9 %copy-start.58 = (bf16[256]{0:T(256)(128)(2,1)S(1)}, bf16[256]{0:T(256)(128)(2,1)}, u32[]{:S(2)}) copy-start(bf16[256]{0:T(256)(128)(2,1)} %param.22) | copy-start | bytes 1540
  12.0 59.7 %copy-start.51 = (s32[2048]{0:T(1024)S(1)}, s32[2048]{0:T(1024)}, u32[]{:S(2)}) copy-start(s32[2048]{0:T(1024)} %param.21) | copy-start | bytes 24580
  12.0 276.3 %all-gather.15.cloned.1.call-start = ((), (), s32[]{:S(2)}) async-start(), calls=%async_computation.9 | async-start | bytes 2621440 | tf_op jit(solution)/shard_map/all_gather | solution.py:576
  12.1 60.3 %collective-permute-start = (bf16[256,1024]{1,0:T(8,128)(2,1)}, bf16[256,1024]{1,0:T(8,128)(2,1)S(1)}, u32[]{:S(2)}, u32[]{:S(2)}) collective-permute-start(bf16[256,1024]{1,0:T(8,128)(2,1)} %bitcast.278), channel_id=1, source_target_pairs={{0,0},{1,16},{2,2},{3,18},{4,4},{5,20},{6,6},{7,22},{8,8},{9,24},{... | collective-permute-start | bytes 1572872 | tf_op jit(solution)/shard_map/ppermute | solution.py:544
  15.6 57.1 %collective-permute-start.1 = (bf16[320,1024]{1,0:T(8,128)(2,1)}, bf16[320,1024]{1,0:T(8,128)(2,1)S(1)}, u32[]{:S(2)}, u32[]{:S(2)}) collective-permute-start(bf16[320,1024]{1,0:T(8,128)(2,1)} %pad_maximum_fusion.3), channel_id=1, source_target_pairs={{0,0},{1,16},{2,2},{3,18},{4,4},{5,20},{6,6},{7,22},{8,8},{9,24},{... | collective-permute-start | bytes 1966088 | tf_op jit(solution)/shard_map/ppermute | solution.py:544
  72.4 34.9 %copy-start.35 = (bf16[256,1024]{1,0:T(8,128)(2,1)}, bf16[256,1024]{1,0:T(8,128)(2,1)S(1)}, u32[]{:S(2)}) copy-start(bf16[256,1024]{1,0:T(8,128)(2,1)S(1)} %collective-permute-done) | copy-start | bytes 1572868
  178.1 42.1 %copy-start.24 = (f32[256,1024]{1,0:T(8,128)}, f32[256,1024]{1,0:T(8,128)S(1)}, u32[]{:S(2)}) copy-start(f32[256,1024]{1,0:T(8,128)S(1)} %get-tuple-element.184) | copy-start | bytes 3145732
  228.5 52.6 %all-to-all-start = ((bf16[4,2,256,704]{2,3,1,0:T(8,128)(2,1)}), bf16[4,2,256,704]{2,3,1,0:T(8,128)(2,1)}, u32[]{:S(2)}, u32[]{:S(2)}) async-start(bf16[4,2,256,704]{2,3,1,0:T(8,128)(2,1)} %copy.116), calls=%async_computation | async-start | bytes 5767168 | tf_op jit(solution)/shard_map/all_to_all | solution.py:548
  233.3 63.7 %all-gather.17.cloned.1.call-start = ((), (), s32[]{:S(2)}) async-start(), calls=%async_computation.11 | async-start | bytes 2621440 | tf_op jit(solution)/shard_map/all_gather | solution.py:576
  234.2 107.4 %reduce-scatter.7.cloned.1.call-start = ((), (), s32[]{:S(2)}) async-start(), calls=%async_computation.12 | async-start | bytes 2621440 | tf_op jit(solution)/shard_map/reduce_scatter | solution.py:552
  297.0 7.4 copy-start.43
  310.1 65.7 %reduce-scatter.5.cloned.1.call-start = ((), (), s32[]{:S(2)}) async-start(), calls=%async_computation.10 | async-start | bytes 2621440 | tf_op jit(solution)/shard_map/reduce_scatter | solution.py:552
  314.6 349.7 %reduce-scatter.11.cloned.1.call-start = ((), (), s32[]{:S(2)}) async-start(), calls=%async_computation.14 | async-start | bytes 13107200 | tf_op jit(solution)/shard_map/reduce_scatter | solution.py:552
  333.2 8.5 %copy-start.32 = (f32[256,1024]{1,0:T(8,128)S(1)}, f32[256,1024]{1,0:T(8,128)}, u32[]{:S(2)}) copy-start(f32[256,1024]{1,0:T(8,128)} %copy-done.31) | copy-start | bytes 3145732
  380.0 12.1 %copy-start.17 = (bf16[8,256,128]{2,1,0:T(8,128)(2,1)S(1)}, bf16[8,256,128]{2,1,0:T(8,128)(2,1)}, u32[]{:S(2)}) copy-start(bf16[8,256,128]{2,1,0:T(8,128)(2,1)} %get-tuple-element.48) | copy-start | bytes 1572868
  380.0 12.1 %copy-start.19 = (bf16[8,64,256]{2,1,0:T(8,128)(2,1)S(1)}, bf16[8,64,256]{2,1,0:T(8,128)(2,1)}, u32[]{:S(2)}) copy-start(bf16[8,64,256]{2,1,0:T(8,128)(2,1)} %get-tuple-element.49) | copy-start | bytes 786436
  451.7 78.5 %all-to-all-start.1 = ((bf16[4,2,256,704]{2,3,1,0:T(8,128)(2,1)}), bf16[4,2,256,704]{2,3,1,0:T(8,128)(2,1)}, u32[]{:S(2)}, u32[]{:S(2)}) async-start(bf16[4,2,256,704]{2,3,1,0:T(8,128)(2,1)} %pad_maximum_fusion.1), calls=%async_computation.3 | async-start | bytes 5767168 | tf_op jit(solution)/shard_map/all_to_all | solution.py:548
  456.4 13.5 %copy-start.6 = (bf16[8,256,384]{2,1,0:T(8,128)(2,1)S(1)}, bf16[8,256,384]{2,1,0:T(8,128)(2,1)}, u32[]{:S(2)}) copy-start(bf16[8,256,384]{2,1,0:T(8,128)(2,1)} %swap.8) | copy-start | bytes 4718596
  456.4 270.3 %reduce-scatter.9.cloned.1.call-start = ((), (), s32[]{:S(2)}) async-start(), calls=%async_computation.13 | async-start | bytes 7864320 | tf_op jit(solution)/shard_map/reduce_scatter | solution.py:552
  494.8 20.9 %copy-start.36 = (bf16[256,1024]{1,0:T(8,128)(2,1)S(1)}, bf16[256,1024]{1,0:T(8,128)(2,1)}, u32[]{:S(2)}) copy-start(bf16[256,1024]{1,0:T(8,128)(2,1)} %copy-done.35) | copy-start | bytes 1572868
  534.7 11.2 %copy-start.29 = (f32[256,1024]{1,0:T(8,128)S(1)}, f32[256,1024]{1,0:T(8,128)}, u32[]{:S(2)}) copy-start(f32[256,1024]{1,0:T(8,128)} %copy-done.28) | copy-start | bytes 3145732
  534.7 24.7 %collective-permute-start.2 = (bf16[256,1024]{1,0:T(8,128)(2,1)}, bf16[256,1024]{1,0:T(8,128)(2,1)}, u32[]{:S(2)}, u32[]{:S(2)}) collective-permute-start(bf16[256,1024]{1,0:T(8,128)(2,1)} %get-tuple-element.163), channel_id=1, source_target_pairs={{0,0},{1,16},{2,2},{3,18},{4,4},{5,20},{6,6},{7,22},{8,8},{9,24},{... | collective-permute-start | bytes 1572872 | tf_op jit(solution)/shard_map/ppermute | solution.py:544
  540.4 8.3 %copy-start.33 = (bf16[1024,16,128]{0,2,1:T(8,128)(2,1)S(1)}, bf16[1024,16,128]{0,2,1:T(8,128)(2,1)}, u32[]{:S(2)}) copy-start(bf16[1024,16,128]{0,2,1:T(8,128)(2,1)} %all-gather.13.cloned.1.call-done) | copy-start | bytes 12582916
  547.0 12.4 %collective-permute-start.3 = (bf16[256,1024]{1,0:T(8,128)(2,1)}, bf16[256,1024]{1,0:T(8,128)(2,1)S(1)}, u32[]{:S(2)}, u32[]{:S(2)}) collective-permute-start(bf16[256,1024]{1,0:T(8,128)(2,1)} %fusion.26), channel_id=1, source_target_pairs={{0,0},{1,16},{2,2},{3,18},{4,4},{5,20},{6,6},{7,22},{8,8},{9,24},{... | collective-permute-start | bytes 1572872 | tf_op jit(solution)/shard_map/ppermute | solution.py:544
  549.6 9.0 %collective-permute-start.4 = (bf16[64,1024]{1,0:T(8,128)(2,1)S(1)}, bf16[64,1024]{1,0:T(8,128)(2,1)S(1)}, u32[]{:S(2)}, u32[]{:S(2)}) collective-permute-start(bf16[64,1024]{1,0:T(8,128)(2,1)S(1)} %fusion.17), channel_id=1, source_target_pairs={{0,0},{1,16},{2,2},{3,18},{4,4},{5,20},{6,6},{7,22},{8,8},{9,24},{... | collective-permute-start | bytes 393224 | tf_op jit(solution)/shard_map/ppermute | solution.py:544
  (51 other events, 130.5 us)
Sparse Core Ops, SparseCore 0:
  10.2 38.4 all-gather.12
  50.2 47.8 all-gather.8
  100.2 46.2 all-gather.10
  220.4 23.9 all-gather.14
  245.8 37.4 all-gather.16
  310.2 31.3 reduce-scatter.6
  344.3 31.4 reduce-scatter.4
  451.9 96.2 reduce-scatter.10
  550.7 56.5 reduce-scatter.8

commit v4 on v3

--- a/solution.py
+++ b/solution.py
@@ -4,6 +4,7 @@
 import jax.numpy as jnp
 from jax import lax
 from jax.experimental import pallas as pl
+from jax.experimental.layout import Layout, with_layout_constraint
 from jax.experimental.pallas import tpu as pltpu
 from jax.sharding import PartitionSpec as P
 
@@ -545,7 +546,21 @@
 
 
 def spread(blocks):
-    return lax.all_to_all(blocks, "fsdp", split_axis=0, concat_axis=0, tiled=True)
+    fan, me = lax.axis_size("fsdp"), lax.axis_index("fsdp")
+    result = blocks
+    for far in range(1, fan):
+        block = lax.dynamic_index_in_dim(blocks, (me + far) % fan, 0, True)
+        block = lax.ppermute(block, "fsdp", [(f, (f + far) % fan) for f in range(fan)])
+        result = lax.dynamic_update_slice_in_dim(result, block, (me - far) % fan, 0)
+    return result
+
+
+def flat(blocks):
+    return jnp.transpose(blocks, (1, 0, 2)).reshape(blocks.shape[1], -1)
+
+
+def by_rows(value):
+    return with_layout_constraint(value, Layout(major_to_minor=tuple(range(value.ndim))))
 
 
 def scatter(grad):
@@ -554,7 +569,12 @@
 
 def over_seq(arrays, splits, ident):
     n = lax.axis_size("seq")
-    if all(v.shape[0] % (8 * n) == 0 and v.shape[1] % (128 * s) == 0 for v, s in zip(arrays, splits)):
+    if all(
+        v.shape[0] % (8 * n) == 0
+        and ring_cut(v.shape, s, n)[0] % 8 == 0
+        and v.shape[1] % (128 * max(s, 1)) == 0
+        for v, s in zip(arrays, splits)
+    ):
         return ring_total(arrays, splits, ident)
     return [lax.psum(v, "seq") for v in arrays]
 
@@ -575,30 +595,38 @@
     length, keys = local * parts, enc_local * parts
     gather = lambda v: lax.all_gather(v, "fsdp", axis=0, tiled=True)
 
-    qkv_w = gather(self_qkv).reshape(width, parts, own * 3 * dh)
-    middle = gather(jnp.concatenate([self_out, cross_q, cross_out], axis=1))
-    pairs_w = gather(cross_kv).reshape(width, parts, own * 2 * dh)
     fan = lax.axis_size("fsdp")
     units = ff_in.shape[1] // (2 * fan)
-    inner_mine = spread(jnp.transpose(ff_in.reshape(-1, 2, fan, units), (2, 1, 0, 3)))
-    gate_w, up_w = (inner_mine[:, i].reshape(width, units) for i in range(2))
-    mix_self = middle[:, :width].reshape(parts, own * dh, width)
-    query_w = middle[:, width : 2 * width].reshape(width, parts, own * dh)
-    mix_cross = middle[:, 2 * width :].reshape(parts, own * dh, width)
+    part = norm_self.shape[0]
+    pair, half, rank = team(parts)
+
+    qkv_w = gather(self_qkv)
     small = jnp.concatenate([norm_self, norm_cross, norm_ff, rel_table.reshape(-1)])
     small = lax.all_gather(small, "fsdp", axis=0, tiled=False)
-    part = norm_self.shape[0]
+    qkv_w, small, first_batch, cross_out = lax.optimization_barrier(
+        (qkv_w, small, jnp.concatenate([self_out, cross_q, cross_kv.reshape(-1, 2 * width)], axis=1), cross_out)
+    )
+    qkv_w = qkv_w.reshape(width, parts, own * 3 * dh)
+    first_batch = by_rows(gather(by_rows(first_batch)))
+    inner_t = jnp.transpose(ff_in.T.reshape(2, fan, units, -1), (1, 0, 2, 3))
+    first_batch, cross_out, inner_t = lax.optimization_barrier((first_batch, cross_out, inner_t))
+    mix_self = first_batch[:, :width].reshape(parts, own * dh, width)
+    query_w = first_batch[:, width : 2 * width].reshape(width, parts, own * dh)
+    pairs_w = first_batch[:, 2 * width :].reshape(width, parts, own * 2 * dh)
+    mix_cross = gather(cross_out)
+    inner_t = spread(inner_t)
+    gate_t, up_t = (jnp.transpose(inner_t[:, i], (1, 0, 2)).reshape(units, width) for i in range(2))
+
     gain_first, gain_second, gain_third = (
         small[:, i * part : (i + 1) * part].reshape(width).astype(f32) for i in range(3)
     )
     table = jnp.transpose(small[:, 3 * part :].reshape(-1, buckets, table_own), (1, 0, 2)).reshape(buckets, heads)
     both_ids = jnp.concatenate([decoder_ids.reshape(-1), encoder_ids.reshape(-1)])
-    both_ids = lax.all_gather(both_ids, ("seq", "fsdp"), axis=0, tiled=False).reshape(parts, fan, -1)
-    pair, half, rank = team(parts)
-    both_ids = lax.dynamic_index_in_dim(both_ids, 2 * pair + half, 1, False)
-    qkv_w, both_ids, small = lax.optimization_barrier((qkv_w, both_ids, small))
+    both_ids = change_home(jnp.pad(both_ids, (0, 1024 - local - enc_local)).reshape(8, 128))
+    (both_ids,) = swap([jnp.broadcast_to(both_ids[None], (parts, 8, 128))], 13)
+    both_ids = both_ids.reshape(parts, 1024)
     ids = both_ids[:, :local].reshape(length)
-    enc_ids = both_ids[:, local:].reshape(keys)
+    enc_ids = both_ids[:, local : local + enc_local].reshape(keys)
 
     first_seen = counts_below(ids, ids)
     enc_first = counts_below(enc_ids, ids)
@@ -624,6 +652,9 @@
     stream = change_home(layer_in.reshape(rows, width)).astype(f32)
     others = change_home(jnp.concatenate([cotangent.reshape(rows, width), encoder.reshape(-1, width)]))
     grad_low, enc_flat = others[:rows], others[rows:]
+    mix_cross, grad_low = lax.optimization_barrier((mix_cross, grad_low))
+    mix_cross = mix_cross.reshape(parts, own * dh, width)
+    grad_group = gather(grad_low)
     normed_first = norm_apply(stream, gain_first).astype(bf16)
     qkv_tok = jnp.einsum("td,dge->gte", normed_first, qkv_w, preferred_element_type=f32).astype(bf16)
     (qkv,) = swap([qkv_tok], 10)
@@ -641,30 +672,29 @@
     after_cross = after_self + jnp.einsum("gtc,gcd->td", cross_tok, mix_cross, preferred_element_type=f32)
     normed_third = norm_apply(after_cross, gain_third).astype(bf16)
     normed_group = gather(normed_third)
-    gate = jnp.dot(normed_group, gate_w, preferred_element_type=f32)
-    up = jnp.dot(normed_group, up_w, preferred_element_type=f32)
+    gate = jnp.einsum("td,fd->tf", normed_group, gate_t, preferred_element_type=f32)
+    up = jnp.einsum("td,fd->tf", normed_group, up_t, preferred_element_type=f32)
     hidden = gate_mix(gate, up).astype(bf16)
-    outer_part = jnp.dot(hidden, ff_out, preferred_element_type=f32).astype(bf16)
-    layer_out = (after_cross + scatter(outer_part).astype(f32)).astype(bf16)
-    layer_out = change_home(layer_out).reshape(seqs, local, width)
-
-    grad_group = gather(grad_low)
-    part_outer = jnp.einsum("tf,td->fd", hidden, grad_group, preferred_element_type=f32).astype(bf16)
+
     grad_hidden = jnp.einsum("td,fd->tf", grad_group, ff_out, preferred_element_type=f32)
     _, pull_mix = jax.vjp(gate_mix, gate, up)
     grad_gate, grad_up = (g.astype(bf16) for g in pull_mix(grad_hidden))
-    grad_third_in = jnp.einsum("tf,df->td", grad_gate, gate_w, preferred_element_type=f32) + jnp.einsum(
-        "tf,df->td", grad_up, up_w, preferred_element_type=f32
+    grad_third_in = jnp.dot(grad_gate, gate_t, preferred_element_type=f32) + jnp.dot(
+        grad_up, up_t, preferred_element_type=f32
     )
     grad_third_in = scatter(grad_third_in.astype(bf16))
+    outer_part = jnp.dot(hidden, ff_out, preferred_element_type=f32).astype(bf16)
+    part_outer = jnp.einsum("tf,td->fd", hidden, grad_group, preferred_element_type=f32).astype(bf16)
     grad_inner = [
-        jnp.einsum("td,tf->df", normed_group, g, preferred_element_type=f32).astype(bf16).reshape(fan, -1, units)
+        jnp.einsum("tf,td->fd", g, normed_group, preferred_element_type=f32).astype(bf16)
         for g in (grad_gate, grad_up)
     ]
-    grad_third_in, grad_inner, part_outer = lax.optimization_barrier(
-        (grad_third_in, jnp.stack(grad_inner, axis=1), part_outer)
-    )
-    part_inner = jnp.transpose(spread(grad_inner), (2, 1, 0, 3)).reshape(-1, 2 * fan * units)
+    grad_inner = jnp.transpose(jnp.stack(grad_inner).reshape(2, units, fan, -1), (2, 0, 1, 3))
+    grad_third_in, outer_part, part_outer, grad_inner = lax.optimization_barrier(
+        (grad_third_in, outer_part, part_outer, grad_inner)
+    )
+    outer_part = scatter(outer_part)
+    part_inner = spread(grad_inner).reshape(2 * fan * units, -1)
     grad_third_in = grad_third_in.astype(f32)
     grad_from_third, grad_gain_third = norm_back(after_cross, gain_third, grad_third_in)
     grad_middle = grad_low.astype(f32) + grad_from_third
@@ -679,22 +709,41 @@
     grad_query_tok, grad_pairs_tok = swap(
         [grad_query.reshape(parts, local, own * dh), grad_pairs.reshape(parts, enc_local, own * 2 * dh)], 12
     )
-    grad_query_w = jnp.einsum("td,gtc->dgc", normed_second, grad_query_tok, preferred_element_type=f32)
-    grad_second_in = jnp.einsum("gtc,dgc->td", grad_query_tok, query_w, preferred_element_type=f32)
-    grad_pairs_w = jnp.einsum("td,gte->dge", enc_flat, grad_pairs_tok, preferred_element_type=f32)
-    grad_encoder = jnp.einsum("gte,dge->td", grad_pairs_tok, pairs_w, preferred_element_type=f32)
+    grad_query_tok, grad_pairs_tok = flat(grad_query_tok), flat(grad_pairs_tok)
+    grad_query_w = jnp.einsum("td,te->de", normed_second, grad_query_tok, preferred_element_type=f32)
+    grad_second_in = jnp.einsum("te,de->td", grad_query_tok, query_w.reshape(width, -1), preferred_element_type=f32)
+    grad_pairs_w = jnp.einsum("td,te->de", enc_flat, grad_pairs_tok, preferred_element_type=f32)
+    grad_encoder = jnp.einsum("te,de->td", grad_pairs_tok, pairs_w.reshape(width, -1), preferred_element_type=f32)
     grad_encoder = change_home(grad_encoder.astype(bf16)).astype(f32).reshape(seqs, enc_local, width)
     grad_from_second, grad_gain_second = norm_back(after_self, gain_second, grad_second_in)
     grad_upper = grad_middle + grad_from_second
     upper_low = grad_upper.astype(bf16)
     grad_mix_self = jnp.einsum("gtc,td->gcd", self_tok, upper_low, preferred_element_type=f32)
     grad_self_tok = jnp.einsum("td,gcd->gtc", upper_low, mix_self, preferred_element_type=f32).astype(bf16)
+    grad_mid = jnp.concatenate(
+        [
+            grad_query_w.astype(bf16),
+            grad_pairs_w.astype(bf16),
+            grad_mix_cross.reshape(width, width).astype(bf16),
+        ],
+        axis=1,
+    )
+    grad_self_tok, grad_mid = lax.optimization_barrier((grad_self_tok, grad_mid))
+    part_mid = scatter(grad_mid)
     (grad_self,) = swap([grad_self_tok], 11)
     grad_self = grad_self.reshape(length, own * dh)
     grad_qkv, tile_sums = self_backward(self_limits, self_rows, ext, qkv, grad_self, self_t, self_lse)
     (grad_qkv_tok,) = swap([grad_qkv.reshape(parts, local, own * 3 * dh)], 10)
-    grad_qkv_w = jnp.einsum("td,gte->dge", normed_first, grad_qkv_tok, preferred_element_type=f32)
-    grad_first_in = jnp.einsum("gte,dge->td", grad_qkv_tok, qkv_w, preferred_element_type=f32)
+    grad_qkv_tok = flat(grad_qkv_tok)
+    grad_qkv_w = jnp.einsum("td,te->de", normed_first, grad_qkv_tok, preferred_element_type=f32)
+    grad_last = jnp.concatenate([grad_mix_self.reshape(width, width).astype(bf16), grad_qkv_w.astype(bf16)], axis=1)
+    grad_last, part_mid, part_inner, part_outer, outer_part = lax.optimization_barrier(
+        (grad_last, part_mid, part_inner, part_outer, outer_part)
+    )
+    part_last = scatter(grad_last)
+    layer_out = (after_cross + outer_part.astype(f32)).astype(bf16)
+    layer_out = change_home(layer_out).reshape(seqs, local, width)
+    grad_first_in = jnp.einsum("te,de->td", grad_qkv_tok, qkv_w.reshape(width, -1), preferred_element_type=f32)
     grad_from_first, grad_gain_first = norm_back(stream, gain_first, grad_first_in)
     grad_layer_in = change_home((grad_upper + grad_from_first).astype(bf16)).astype(f32)
     grad_layer_in = grad_layer_in.reshape(seqs, local, width)
@@ -707,16 +756,6 @@
     by_bucket = jnp.einsum("twn,gtw->ng", in_bucket, tile_sums, precision=HIGH)
     grad_table = lax.dynamic_update_slice_in_dim(jnp.zeros((buckets, heads), f32), by_bucket, first_head, 1)
 
-    grad_mid = jnp.concatenate(
-        [
-            grad_mix_self.reshape(width, width).astype(bf16),
-            grad_query_w.reshape(width, width).astype(bf16),
-            grad_pairs_w.reshape(width, 2 * width).astype(bf16),
-            grad_mix_cross.reshape(width, width).astype(bf16),
-        ],
-        axis=1,
-    )
-    part_mid = scatter(grad_mid)
     gains = jnp.concatenate(
         [g.reshape(-1, part) for g in (grad_gain_first, grad_gain_second, grad_gain_third)], axis=1
     )
@@ -725,20 +764,15 @@
     small_grads = lax.dynamic_index_in_dim(small_grads, lax.axis_index("fsdp"), 0, False)
     small_size = small_grads.shape[0]
     small_grads = jnp.pad(small_grads, (0, parts * 1024 - small_size)).reshape(parts * 8, 128)
-    grad_qkv_w, part_inner, part_outer = lax.optimization_barrier(
-        (grad_qkv_w.reshape(width, 3 * width).astype(bf16), part_inner, part_outer)
-    )
-    part_qkv = scatter(grad_qkv_w)
-    total_inner, total_outer = over_seq([part_inner, part_outer], (2, 2), 0)
-    total_inner, part_mid = lax.optimization_barrier((total_inner, part_mid))
-    (total_mid,) = over_seq([part_mid], (4,), 1)
-    part_qkv, small_grads, total_mid = lax.optimization_barrier((part_qkv, small_grads, total_mid))
-    total_qkv, small_total = over_seq([part_qkv, small_grads], (4, 1), 2)
-    total_qkv = total_qkv.astype(f32).reshape(-1, heads, 3 * dh)
-    total_inner, total_outer, total_mid = (v.astype(f32) for v in (total_inner, total_outer, total_mid))
-    total_mix_self, total_query = total_mid[:, :width], total_mid[:, width : 2 * width]
-    total_pairs = total_mid[:, 2 * width : 4 * width].reshape(-1, heads, 2 * dh)
-    total_mix_cross = total_mid[:, 4 * width :]
+    total_inner, total_outer = over_seq([part_inner, part_outer], (-2, 2), 0)
+    total_inner, part_mid, part_last = lax.optimization_barrier((total_inner, part_mid, part_last))
+    total_mid, total_last, small_total = over_seq([part_mid, part_last, small_grads], (2, 2, 1), 1)
+    total_outer, total_mid, total_last = (v.astype(f32) for v in (total_outer, total_mid, total_last))
+    total_inner = jnp.transpose(total_inner.reshape(fan, 2, units, -1), (3, 1, 0, 2)).reshape(-1, 2 * fan * units)
+    total_inner = total_inner.astype(f32)
+    total_query, total_mix_cross = total_mid[:, :width], total_mid[:, 3 * width :]
+    total_pairs = total_mid[:, width : 3 * width].reshape(-1, heads, 2 * dh)
+    total_mix_self, total_qkv = total_last[:, :width], total_last[:, width:].reshape(-1, heads, 3 * dh)
     mine = small_total.reshape(-1)[:small_size].astype(f32)
     total_gain_first, total_gain_second, total_gain_third = (mine[i * part : (i + 1) * part] for i in range(3))
     total_table = mine[3 * part :].reshape(buckets, table_own)

time: 810 us -> 785 us (0.969)
  the two profiles are of different devices: /device:TPU:0 before, /device:TPU:1 now
where the time goes in v4:
time: 785 us; the launch traced here: 769 us
  Pallas kernels  344 us (44%)
  waiting for transfers between devices  145 us (18%)
  local copies, waits for them, and re-layouts  98.4 us (13%)
  matrix products  81.5 us (10%)
  other arithmetic  41.6 us (5%)
  starting transfers between devices  32 us (4%)
  between operations  15.4 us (2%)
  blocking collectives  11.8 us (2%)
    pallas_call x2, Pallas kernels, ring_total(): pl.pallas_call(functools.partial(ring_kernel, n, splits), name='ring_tota...  173 us
    pallas_call x9, Pallas kernels, swap(): pl.pallas_call(functools.partial(swap_kernel, n, count), name='swap', out...  113 us
    all_gather x5, waiting for transfers between devices, shards(): gather = lambda v: lax.all_gather(v, 'fsdp', axis=0, tiled=True)  90.4 us
    pallas_call x4, Pallas kernels, call(): pl.pallas_call(body, name=name, out_shape=[jax.ShapeDtypeStruct(s, d) for...  57.6 us
    ppermute x6, waiting for transfers between devices, spread(): lax.ppermute(block, 'fsdp', [(f, (f + far) % fan) for f in range(fan)])  52 us
    unnamed x134, local copies, waits for them, and re-layouts  37.7 us
    ppermute x6, starting transfers between devices, change_home(): return lax.ppermute(value, ('seq', 'fsdp'), pairs)  19.4 us
  transfers between devices with their start and end apart: 21, of which 8 were waited for; matrix products, arithmetic and copies ran while one was open for 21% of the time, Pallas kernels for 34%

profile of v4, /device:TPU:1, one launch (start us, length us, event | category | flops | bytes accessed | tf_op | source)
XLA Modules:
  0.0 769.4 jit_solution(840086241880937877)
XLA Ops:
  9.6 6.1 all-gather.1
  18.1 41.3 %all-gather.8.cloned.1.call-done = bf16[1024,16,192]{0,2,1:T(8,128)(2,1)} async-done(((bf16[256,16,192]{0,2,1:T(8,128)(2,1)}), bf16[1024,16,192]{0,2,1:T(8,128)(2,1)}) %all-gather.8.cloned.1.call-update) | async-done | bytes 6291472 | tf_op jit(solution)/shard_map/all_gather | solution.py:596
  70.8 49.0 %all-gather.10.cloned.1.call-done = bf16[1024,4096]{1,0:T(8,128)(2,1)} async-done(((bf16[256,4096]{1,0:T(8,128)(2,1)}), bf16[1024,4096]{1,0:T(8,128)(2,1)}) %all-gather.10.cloned.1.call-update) | async-done | bytes 8388624 | tf_op jit(solution)/shard_map/all_gather | solution.py:596
  125.8 7.4 swap.9
  138.1 5.2 fusion.56
  145.0 5.8 fusion.10.refs_0_
  150.8 23.1 %swap.10 = bf16[8,256,384]{2,1,0:T(8,128)(2,1)} custom-call(bf16[8,256,384]{2,1,0:T(8,128)(2,1)} %fusion.10.refs_0_), custom_call_target="tpu_custom_call" | custom-call | bytes 47185920 | tf_op jit(solution)/shard_map/swap/pallas_call | solution.py:501
  175.8 17.6 %self_forward.1 = (bf16[2048,128]{1,0:T(8,128)(2,1)S(1)}, f32[128,2048]{1,0:T(8,128)S(1)}, f32[2,2048]{1,0:T(2,128)S(1)}) custom-call(s32[2,8]{1,0:T(2,128)S(1)} %get-tuple-element.213.lim_ref, s32[8,2048]{1,0:T(8,128)S(1)} %broadcast_in_dim.100.rows_ref, f32[2,1536]{1,0:T(2,128)S(1)} %maximum_maximum_fusion.ext_ref, bf16[2048,384]{1,0:T(8,128)(2,1)S(1)} %bitcast.213), custom_call_target="tpu_custom_call" | custom-call | flops 536870912 | bytes 3301504 | tf_op jit(solution)/shard_map/self_forward/pallas_call | solution.py:257
  195.2 8.3 %swap.11 = bf16[8,256,128]{2,1,0:T(8,128)(2,1)} custom-call(bf16[8,256,128]{2,1,0:T(8,128)(2,1)} %bitcast.219), custom_call_target="tpu_custom_call" | custom-call | bytes 15728640 | tf_op jit(solution)/shard_map/swap/pallas_call | solution.py:501
  220.8 13.5 %swap.12 = (bf16[8,256,128]{2,1,0:T(8,128)(2,1)}, bf16[8,64,256]{2,1,0:T(8,128)(2,1)}) custom-call(bf16[8,256,128]{2,1,0:T(8,128)(2,1)} %fusion.16.refs_0_, bf16[8,64,256]{2,1,0:T(8,128)(2,1)} %fusion.22.refs_1_), custom_call_target="tpu_custom_call" | custom-call | bytes 23592960 | tf_op jit(solution)/shard_map/swap/pallas_call | solution.py:501
  236.3 8.6 %cross_forward.1 = (bf16[2048,128]{1,0:T(8,128)(2,1)S(1)}, f32[128,2048]{1,0:T(8,128)S(1)}, f32[2,2048]{1,0:T(2,128)S(1)}) custom-call(s32[2,8]{1,0:T(2,128)S(1)} %get-tuple-element.214.lim_ref, s32[8,2048]{1,0:T(8,128)S(1)} %add_add_fusion.3.rows_ref, bf16[2048,128]{1,0:T(8,128)(2,1)S(1)} %bitcast.222, bf16[512,256]{1,0:T(8,128)(2,1)S(1)} %bitcast.224), custom_call_target="tpu_custom_call" | custom-call | flops 268435456 | bytes 1704064 | tf_op jit(solution)/shard_map/cross_forward/pallas_call | solution.py:257
  245.6 8.8 %swap.13 = bf16[8,256,128]{2,1,0:T(8,128)(2,1)} custom-call(bf16[8,256,128]{2,1,0:T(8,128)(2,1)} %bitcast.220), custom_call_target="tpu_custom_call" | custom-call | bytes 15728640 | tf_op jit(solution)/shard_map/swap/pallas_call | solution.py:501
  265.0 19.1 %collective-permute-done.3 = bf16[1,2,704,256]{3,2,0,1:T(8,128)(2,1)} collective-permute-done((bf16[1,2,704,256]{3,2,0,1:T(8,128)(2,1)}, bf16[1,2,704,256]{3,2,0,1:T(8,128)(2,1)}, u32[]{:S(2)}, u32[]{:S(2)}) %collective-permute-start.3) | collective-permute-done | bytes 720928 | tf_op jit(solution)/shard_map/ppermute | solution.py:553
  290.0 14.2 %collective-permute-done.4 = bf16[1,2,704,256]{3,2,0,1:T(8,128)(2,1)} collective-permute-done((bf16[1,2,704,256]{3,2,0,1:T(8,128)(2,1)}, bf16[1,2,704,256]{3,2,0,1:T(8,128)(2,1)}, u32[]{:S(2)}, u32[]{:S(2)}) %collective-permute-start.4) | collective-permute-done | bytes 720928 | tf_op jit(solution)/shard_map/ppermute | solution.py:553
  306.3 6.8 collective-permute-done.5
  319.7 4.9 fusion.73
  338.8 4.8 convolution_convert_fusion.7
  365.5 4.8 convolution_convert_fusion.9.refs_1_
  377.7 9.3 %swap.14 = bf16[8,256,128]{2,1,0:T(8,128)(2,1)} custom-call(bf16[8,256,128]{2,1,0:T(8,128)(2,1)} %fusion.17.refs_0_), custom_call_target="tpu_custom_call" | custom-call | bytes 15728640 | tf_op jit(solution)/shard_map/swap/pallas_call | solution.py:501
  388.1 9.9 %cross_backward.1 = (bf16[2048,128]{1,0:T(8,128)(2,1)S(1)}, bf16[512,256]{1,0:T(8,128)(2,1)S(1)}) custom-call(s32[2,8]{1,0:T(2,128)S(1)} %get-tuple-element.214.lim_ref, s32[8,2048]{1,0:T(8,128)S(1)} %add_add_fusion.3.rows_ref, bf16[2048,128]{1,0:T(8,128)(2,1)S(1)} %bitcast.223, bf16[512,256]{1,0:T(8,128)(2,1)S(1)} %bitcast.225, ...), custom_call_target="tpu_custom_call" | custom-call | flops 671088640 | bytes 4882560 | tf_op jit(solution)/shard_map/cross_backward/pallas_call | solution.py:257
  399.5 13.5 %swap.15 = (bf16[8,256,128]{2,1,0:T(8,128)(2,1)}, bf16[8,64,256]{2,1,0:T(8,128)(2,1)}) custom-call(bf16[8,256,128]{2,1,0:T(8,128)(2,1)} %bitcast.216, bf16[8,64,256]{2,1,0:T(8,128)(2,1)} %bitcast.221), custom_call_target="tpu_custom_call" | custom-call | bytes 23592960 | tf_op jit(solution)/shard_map/swap/pallas_call | solution.py:501
  434.3 8.1 %swap.16 = bf16[8,256,128]{2,1,0:T(8,128)(2,1)} custom-call(bf16[8,256,128]{2,1,0:T(8,128)(2,1)} %fusion.18.refs_0_), custom_call_target="tpu_custom_call" | custom-call | bytes 15728640 | tf_op jit(solution)/shard_map/swap/pallas_call | solution.py:501
  443.6 21.5 %self_backward.1 = (bf16[2048,384]{1,0:T(8,128)(2,1)S(1)}, f32[2,5,512]{2,1,0:T(8,128)S(1)}) custom-call(s32[2,8]{1,0:T(2,128)S(1)} %get-tuple-element.213.lim_ref, s32[8,2048]{1,0:T(8,128)S(1)} %broadcast_in_dim.100.rows_ref, f32[2,1536]{1,0:T(2,128)S(1)} %maximum_maximum_fusion.ext_ref, bf16[2048,384]{1,0:T(8,128)(2,1)S(1)} %bitcast.214, ...), custom_call_target="tpu_custom_call" | custom-call | flops 1342177280 | bytes 6480000 | tf_op jit(solution)/shard_map/self_backward/pallas_call | solution.py:257
  466.2 21.4 %swap.17 = bf16[8,256,384]{2,1,0:T(8,128)(2,1)} custom-call(bf16[8,256,384]{2,1,0:T(8,128)(2,1)} %bitcast.215), custom_call_target="tpu_custom_call" | custom-call | bytes 47185920 | tf_op jit(solution)/shard_map/swap/pallas_call | solution.py:501
  501.5 7.8 %pad_maximum_fusion.1 = bf16[1024,4096]{1,0:T(8,128)(2,1)} fusion(bf16[1024,3072]{1,0:T(8,128)(2,1)} %convolution_convert_fusion, bf16[1024,1024]{1,0:T(8,128)(2,1)} %bitcast.239), kind=kLoop, calls=%fused_computation.1 | loop fusion | flops 16777216 | bytes 16777216 | tf_op jit(solution)/shard_map/concatenate | solution.py:739
  509.2 5.0 collective-permute-done.7
  516.2 6.9 collective-permute-done.8
  532.5 7.0 fusion.27
  547.1 5.8 psum.7
  562.2 90.4 %ring_total.2 = (bf16[5632,256]{1,0:T(8,128)(2,1)S(1)}, bf16[704,1024]{1,0:T(8,128)(2,1)S(1)}) custom-call(bf16[5632,256]{1,0:T(8,128)(2,1)} %bitcast.52.refs_0_, bf16[704,1024]{1,0:T(8,128)(2,1)S(1)} %copy-done.5), custom_call_target="tpu_custom_call" | custom-call | flops 4325376 | bytes 259522560 | tf_op jit(solution)/shard_map/ring_total/pallas_call | solution.py:439
  654.6 82.3 %ring_total.3 = (bf16[256,4096]{1,0:T(8,128)(2,1)S(1)}, bf16[256,4096]{1,0:T(8,128)(2,1)S(1)}, bf16[64,128]{1,0:T(8,128)(2,1)S(1)}) custom-call(bf16[256,4096]{1,0:T(8,128)(2,1)} %reduce-scatter.7.cloned.1.call-done.refs_0_, bf16[256,4096]{1,0:T(8,128)(2,1)} %reduce-scatter.11.cloned.1.call-done.refs_1_, bf16[64,128]{1,0:T(8,128)(2,1)S(1)} %pad_bitcast_fusion.refs_2_), custom_call_target="tpu_custom_call" | custom-call | flops 4210688 | bytes 252641280 | tf_op jit(solution)/shard_map/ring_total/pallas_call | solution.py:439
  755.3 6.3 copy.120
  (293 shorter events, 209.8 us)
Async XLA Ops:
  7.2 312.5 %copy-start = (bf16[704,1024]{1,0:T(8,128)(2,1)S(1)}, bf16[704,1024]{1,0:T(8,128)(2,1)}, u32[]{:S(2)}) copy-start(bf16[704,1024]{1,0:T(8,128)(2,1)} %param.32) | copy-start | bytes 4325380
  7.2 52.1 %all-gather.8.cloned.1.call-start = ((), (), s32[]{:S(2)}) async-start(), calls=%async_computation.4 | async-start | bytes 7864320 | tf_op jit(solution)/shard_map/all_gather | solution.py:596
  8.0 111.9 %all-gather.10.cloned.1.call-start = ((), (), s32[]{:S(2)}) async-start(), calls=%async_computation.5 | async-start | bytes 10485760 | tf_op jit(solution)/shard_map/all_gather | solution.py:596
  18.1 41.4 %copy-start.49 = (s32[1,256]{1,0:T(1,128)S(1)}, s32[1,256]{1,0:T(1,128)}, u32[]{:S(2)}) copy-start(s32[1,256]{1,0:T(1,128)} %param.19) | copy-start | bytes 3076
  18.1 41.4 %copy-start.50 = (s32[1,64]{1,0:T(1,128)S(1)}, s32[1,64]{1,0:T(1,128)}, u32[]{:S(2)}) copy-start(s32[1,64]{1,0:T(1,128)} %param.20) | copy-start | bytes 772
  59.4 114.5 %all-gather.12.cloned.1.call-start = ((), (), s32[]{:S(2)}) async-start(), calls=%async_computation.6 | async-start | bytes 2621440 | tf_op jit(solution)/shard_map/all_gather | solution.py:596
  59.5 65.7 %collective-permute-start.1 = (s32[8,128]{1,0:T(8,128)S(1)}, s32[8,128]{1,0:T(8,128)S(1)}, u32[]{:S(2)}, u32[]{:S(2)}) collective-permute-start(s32[8,128]{1,0:T(8,128)S(1)} %pad_bitcast_fusion.1), channel_id=1, source_target_pairs={{0,0},{1,16},{2,2},{3,18},{4,4},{5,20},{6,6},{7,22},{8,8},{9,24},{... | collective-permute-start | bytes 12296 | tf_op jit(solution)/shard_map/ppermute | solution.py:545
  63.7 56.2 %copy-start.36 = (bf16[1,256,1024]{2,1,0:T(8,128)(2,1)S(1)}, bf16[1,256,1024]{2,1,0:T(8,128)(2,1)}, u32[]{:S(2)}) copy-start(bf16[1,256,1024]{2,1,0:T(8,128)(2,1)} %param.33) | copy-start | bytes 1572868
  63.7 56.2 %copy-start.39 = (bf16[1,64,1024]{2,1,0:T(8,128)(2,1)S(1)}, bf16[1,64,1024]{2,1,0:T(8,128)(2,1)}, u32[]{:S(2)}) copy-start(bf16[1,64,1024]{2,1,0:T(8,128)(2,1)} %param.18) | copy-start | bytes 393220
  63.7 61.4 %copy-start.40 = (s32[2048]{0:T(1024)S(1)}, s32[2048]{0:T(1024)}, u32[]{:S(2)}) copy-start(s32[2048]{0:T(1024)} %param.21) | copy-start | bytes 24580
  63.7 79.9 %collective-permute-start = (bf16[256,1024]{1,0:T(8,128)(2,1)}, bf16[256,1024]{1,0:T(8,128)(2,1)S(1)}, u32[]{:S(2)}, u32[]{:S(2)}) collective-permute-start(bf16[256,1024]{1,0:T(8,128)(2,1)} %bitcast), channel_id=1, source_target_pairs={{0,0},{1,16},{2,2},{3,18},{4,4},{5,20},{6,6},{7,22},{8,8},{9,24},{... | collective-permute-start | bytes 1572872 | tf_op jit(solution)/shard_map/ppermute | solution.py:545
  70.8 73.9 %copy-start.41 = (bf16[4,1,896]{2,0,1:T(4,128)(2,1)S(1)}, bf16[4,1,896]{2,0,1:T(4,128)(2,1)}, u32[]{:S(2)}) copy-start(bf16[4,1,896]{2,0,1:T(4,128)(2,1)} %copy.160) | copy-start | bytes 21508
  119.9 199.8 %all-gather.14.cloned.1.call-start = ((), (), s32[]{:S(2)}) async-start(), calls=%async_computation.7 | async-start | bytes 2621440 | tf_op jit(solution)/shard_map/all_gather | solution.py:596
  120.8 23.0 %collective-permute-start.2 = (bf16[320,1024]{1,0:T(8,128)(2,1)}, bf16[320,1024]{1,0:T(8,128)(2,1)S(1)}, u32[]{:S(2)}, u32[]{:S(2)}) collective-permute-start(bf16[320,1024]{1,0:T(8,128)(2,1)} %pad_maximum_fusion.3), channel_id=1, source_target_pairs={{0,0},{1,16},{2,2},{3,18},{4,4},{5,20},{6,6},{7,22},{8,8},{9,24},{... | collective-permute-start | bytes 1966088 | tf_op jit(solution)/shard_map/ppermute | solution.py:545
  125.1 48.9 %copy-start.42 = (s32[1024]{0:T(1024)}, s32[1024]{0:T(1024)S(1)}, u32[]{:S(2)}) copy-start(s32[1024]{0:T(1024)S(1)} %slice.126) | copy-start | bytes 12292
  174.0 150.6 %all-gather.16.cloned.1.call-start = ((), (), s32[]{:S(2)}) async-start(), calls=%async_computation.8 | async-start | bytes 2621440 | tf_op jit(solution)/shard_map/all_gather | solution.py:596
  259.2 111.2 %reduce-scatter.5.cloned.1.call-start = ((), (), s32[]{:S(2)}) async-start(), calls=%async_computation.9 | async-start | bytes 2621440 | tf_op jit(solution)/shard_map/reduce_scatter | solution.py:567
  261.2 22.9 %collective-permute-start.3 = (bf16[1,2,704,256]{3,2,0,1:T(8,128)(2,1)}, bf16[1,2,704,256]{3,2,0,1:T(8,128)(2,1)}, u32[]{:S(2)}, u32[]{:S(2)}) collective-permute-start(bf16[1,2,704,256]{3,2,0,1:T(8,128)(2,1)} %constant_dynamic-slice_fusion.6), channel_id=1, source_target_pairs={{0,1},{1,2},{2,3},{3,0},{4,5},{5,6},{6,7},{7,4},{8,9},{9,10},{10,1... | collective-permute-start | bytes 2162696 | tf_op jit(solution)/shard_map/ppermute | solution.py:553
  287.1 17.1 %collective-permute-start.4 = (bf16[1,2,704,256]{3,2,0,1:T(8,128)(2,1)}, bf16[1,2,704,256]{3,2,0,1:T(8,128)(2,1)}, u32[]{:S(2)}, u32[]{:S(2)}) collective-permute-start(bf16[1,2,704,256]{3,2,0,1:T(8,128)(2,1)} %get-tuple-element.184), channel_id=1, source_target_pairs={{0,2},{1,3},{2,0},{3,1},{4,6},{5,7},{6,4},{7,5},{8,10},{9,11},{10,... | collective-permute-start | bytes 2162696 | tf_op jit(solution)/shard_map/ppermute | solution.py:553
  287.1 25.9 %collective-permute-start.5 = (bf16[1,2,704,256]{3,2,0,1:T(8,128)(2,1)}, bf16[1,2,704,256]{3,2,0,1:T(8,128)(2,1)}, u32[]{:S(2)}, u32[]{:S(2)}) collective-permute-start(bf16[1,2,704,256]{3,2,0,1:T(8,128)(2,1)} %get-tuple-element.183), channel_id=1, source_target_pairs={{0,3},{1,0},{2,1},{3,2},{4,7},{5,4},{6,5},{7,6},{8,11},{9,8},{10,9... | collective-permute-start | bytes 2162696 | tf_op jit(solution)/shard_map/ppermute | solution.py:553
  338.4 186.7 %reduce-scatter.9.cloned.1.call-start = ((), (), s32[]{:S(2)}) async-start(), calls=%async_computation.11 | async-start | bytes 2621440 | tf_op jit(solution)/shard_map/reduce_scatter | solution.py:567
  370.3 154.8 %reduce-scatter.7.cloned.1.call-start = ((), (), s32[]{:S(2)}) async-start(), calls=%async_computation.10 | async-start | bytes 10485760 | tf_op jit(solution)/shard_map/reduce_scatter | solution.py:567
  399.5 15.8 %copy-start.23 = (f32[256,1024]{1,0:T(8,128)S(1)}, f32[256,1024]{1,0:T(8,128)}, u32[]{:S(2)}) copy-start(f32[256,1024]{1,0:T(8,128)} %copy-done.22) | copy-start | bytes 3145732
  429.2 13.1 %copy-start.17 = (f32[128,2048]{1,0:T(8,128)S(1)}, f32[128,2048]{1,0:T(8,128)}, u32[]{:S(2)}) copy-start(f32[128,2048]{1,0:T(8,128)} %copy-done.16) | copy-start | bytes 3145732
  429.3 225.3 %reduce-scatter.11.cloned.1.call-start = ((), (), s32[]{:S(2)}) async-start(), calls=%async_computation.12 | async-start | bytes 10485760 | tf_op jit(solution)/shard_map/reduce_scatter | solution.py:567
  431.5 62.6 %collective-permute-start.6 = (bf16[1,2,704,256]{3,2,1,0:T(8,128)(2,1)}, bf16[1,2,704,256]{3,2,1,0:T(8,128)(2,1)}, u32[]{:S(2)}, u32[]{:S(2)}) collective-permute-start(bf16[1,2,704,256]{3,2,1,0:T(8,128)(2,1)} %constant_dynamic-slice_fusion.3), channel_id=1, source_target_pairs={{0,1},{1,2},{2,3},{3,0},{4,5},{5,6},{6,7},{7,4},{8,9},{9,10},{10,1... | collective-permute-start | bytes 2162696 | tf_op jit(solution)/shard_map/ppermute | solution.py:553
  497.2 17.0 %collective-permute-start.7 = (bf16[1,2,704,256]{3,2,1,0:T(8,128)(2,1)}, bf16[1,2,704,256]{3,2,1,0:T(8,128)(2,1)}, u32[]{:S(2)}, u32[]{:S(2)}) collective-permute-start(bf16[1,2,704,256]{3,2,1,0:T(8,128)(2,1)} %get-tuple-element.179), channel_id=1, source_target_pairs={{0,2},{1,3},{2,0},{3,1},{4,6},{5,7},{6,4},{7,5},{8,10},{9,11},{10,... | collective-permute-start | bytes 2162696 | tf_op jit(solution)/shard_map/ppermute | solution.py:553
  500.3 22.8 %collective-permute-start.8 = (bf16[1,2,704,256]{3,2,1,0:T(8,128)(2,1)}, bf16[1,2,704,256]{3,2,1,0:T(8,128)(2,1)}, u32[]{:S(2)}, u32[]{:S(2)}) collective-permute-start(bf16[1,2,704,256]{3,2,1,0:T(8,128)(2,1)} %get-tuple-element.178), channel_id=1, source_target_pairs={{0,3},{1,0},{2,1},{3,2},{4,7},{5,4},{6,5},{7,6},{8,11},{9,8},{10,9... | collective-permute-start | bytes 2162696 | tf_op jit(solution)/shard_map/ppermute | solution.py:553
  530.3 25.7 %collective-permute-start.11 = (bf16[64,1024]{1,0:T(8,128)(2,1)}, bf16[64,1024]{1,0:T(8,128)(2,1)}, u32[]{:S(2)}, u32[]{:S(2)}) collective-permute-start(bf16[64,1024]{1,0:T(8,128)(2,1)} %convolution_convert_fusion.13), channel_id=1, source_target_pairs={{0,0},{1,16},{2,2},{3,18},{4,4},{5,20},{6,6},{7,22},{8,8},{9,24},{... | collective-permute-start | bytes 393224 | tf_op jit(solution)/shard_map/ppermute | solution.py:545
  539.6 13.4 %copy-start.20 = (f32[256,1024]{1,0:T(8,128)S(1)}, f32[256,1024]{1,0:T(8,128)}, u32[]{:S(2)}) copy-start(f32[256,1024]{1,0:T(8,128)} %copy-done.18) | copy-start | bytes 3145732
  542.5 17.3 %collective-permute-start.10 = (bf16[256,1024]{1,0:T(8,128)(2,1)}, bf16[256,1024]{1,0:T(8,128)(2,1)S(1)}, u32[]{:S(2)}, u32[]{:S(2)}) collective-permute-start(bf16[256,1024]{1,0:T(8,128)(2,1)} %fusion.33), channel_id=1, source_target_pairs={{0,0},{1,16},{2,2},{3,18},{4,4},{5,20},{6,6},{7,22},{8,8},{9,24},{... | collective-permute-start | bytes 1572872 | tf_op jit(solution)/shard_map/ppermute | solution.py:545
  554.1 100.5 %collective-permute-start.9 = (bf16[256,1024]{1,0:T(8,128)(2,1)S(1)}, bf16[256,1024]{1,0:T(8,128)(2,1)S(1)}, u32[]{:S(2)}, u32[]{:S(2)}) collective-permute-start(bf16[256,1024]{1,0:T(8,128)(2,1)S(1)} %add_convert_fusion.1), channel_id=1, source_target_pairs={{0,0},{1,16},{2,2},{3,18},{4,4},{5,20},{6,6},{7,22},{8,8},{9,24},{... | collective-permute-start | bytes 1572872 | tf_op jit(solution)/shard_map/ppermute | solution.py:545
  (47 other events, 166.2 us)
Sparse Core Ops, SparseCore 0:
  9.6 49.7 all-gather.7
  61.5 58.2 all-gather.9
  121.4 22.5 all-gather.11
  174.1 20.5 all-gather.13
  259.3 26.9 all-gather.15
  338.5 29.7 reduce-scatter.4
  371.5 31.3 reduce-scatter.8
  429.4 71.0 reduce-scatter.6
  525.3 70.6 reduce-scatter.10

commit v5 on v4

--- a/solution.py
+++ b/solution.py
@@ -262,7 +262,7 @@
         out_specs=[VMEM] * len(outs),
         scratch_shapes=[pltpu.VMEM(s, d) for s, d in scratch],
         compiler_params=pltpu.CompilerParams(vmem_limit_bytes=40 << 20),
-        cost_estimate=pl.CostEstimate(flops=flops, bytes_accessed=2 * size, transcendentals=flops // 256),
+        cost_estimate=pl.CostEstimate(flops=0, bytes_accessed=size, transcendentals=0),
     )(*operands)
 
 
@@ -357,37 +357,49 @@
     return 2 * z + x
 
 
-def ring_cut(shape, split, n):
-    rows, cols = shape[0] // n, shape[1]
-    return (rows, cols // split) if split > 0 else (rows // -split, cols)
-
-
-def ring_kernel(n, splits, *refs):
-    count = len(splits)
-    x_refs, y_refs, slots = refs[:count], refs[count : 2 * count], refs[2 * count : 3 * count]
-    send_sem, recv_sem = refs[3 * count :]
+def ring_greet(n, others):
     place = ring_place(lax.axis_index("seq"), n)
     right = ring_index((place + 1) % n, n)
     left = ring_index((place + n - 1) % n, n)
     barrier = pltpu.get_barrier_semaphore()
     for neighbour in (left, right):
         pl.semaphore_signal(barrier, inc=1, device_id={"seq": neighbour}, device_id_type=MESH)
-    pl.semaphore_wait(barrier, 2)
-
-    streams = []
-    for k in range(count):
-        for piece in range(abs(splits[k])):
-            streams.append((k, piece, piece % 2))
+    for other in others:
+        pl.semaphore_signal(barrier, inc=1, device_id={"fsdp": other}, device_id_type=MESH)
+    pl.semaphore_wait(barrier, 2 + len(others))
+    return place, right, left
+
+
+def ring_cut(shape, split, n):
+    rows, cols = shape[0] // n, shape[1]
+    return (rows, cols // split) if split > 0 else (rows // -split, cols)
+
+
+def ring_window(ref, shape, split, n, piece, chunk):
+    whole = shape[0] // n
+    rows, cols = ring_cut(shape, split, n)
+    if split > 0:
+        return ref.at[pl.ds(chunk * whole, rows), pl.ds(piece * cols, cols)]
+    return ref.at[pl.ds(chunk * whole + piece * rows, rows), :]
+
+
+def ring_kernel(n, splits, *refs):
+    count = len(splits)
+    x_refs, y_refs, slots = refs[:count], refs[count : 2 * count], refs[2 * count : 3 * count]
+    send_sem, recv_sem = refs[3 * count :]
+    place, right, left = ring_greet(n, [])
+    streams = [(k, piece, piece % 2) for k in range(count) for piece in range(abs(splits[k]))]
 
     def window(ref, k, piece, chunk):
-        whole = x_refs[k].shape[0] // n
-        rows, cols = ring_cut(x_refs[k].shape, splits[k], n)
-        if splits[k] > 0:
-            return ref.at[pl.ds(chunk * whole, rows), pl.ds(piece * cols, cols)]
-        return ref.at[pl.ds(chunk * whole + piece * rows, rows), :]
-
-    def copy(number, step, src, dst, down):
-        return pltpu.make_async_remote_copy(
+        return ring_window(ref, x_refs[k].shape, splits[k], n, piece, chunk)
+
+    def chunk_at(down, step):
+        return (place + 1 + step) % n if down else (place + 2 * n - 1 - step) % n
+
+    copies = {}
+
+    def start(number, step, src, dst, down):
+        copies[number, step] = pltpu.make_async_remote_copy(
             src_ref=src,
             dst_ref=dst,
             send_sem=send_sem.at[number, step],
@@ -395,14 +407,6 @@
             device_id={"seq": left if down else right},
             device_id_type=MESH,
         )
-
-    def chunk_at(down, step):
-        return (place + 1 + step) % n if down else (place + 2 * n - 1 - step) % n
-
-    copies = {}
-
-    def start(number, step, src, dst, down):
-        copies[number, step] = copy(number, step, src, dst, down)
         copies[number, step].start()
 
     for number, (k, piece, down) in enumerate(streams):
@@ -425,30 +429,117 @@
         for number, (k, piece, down) in enumerate(streams):
             copies[number, n - 1 + step].wait_recv()
             if step < n - 2:
-                chunk = chunk_at(down, n - 1 + step)
-                done = window(y_refs[k], k, piece, chunk)
+                done = window(y_refs[k], k, piece, chunk_at(down, n - 1 + step))
                 start(number, n + step, done, done, down)
     for one in copies.values():
         one.wait_send()
 
 
-def ring_total(arrays, splits, ident):
-    n = lax.axis_size("seq")
+def ring_call(body, name, arrays, outs, scratch, ident):
     size = sum(v.size * 2 for v in arrays)
-    streams = sum(abs(s) for s in splits)
     return pl.pallas_call(
-        functools.partial(ring_kernel, n, splits),
-        name="ring_total",
-        out_shape=[jax.ShapeDtypeStruct(v.shape, jnp.bfloat16) for v in arrays],
+        body,
+        name=name,
+        out_shape=[jax.ShapeDtypeStruct(s, jnp.bfloat16) for s in outs],
         in_specs=[pl.BlockSpec(memory_space=pltpu.VMEM)] * len(arrays),
-        out_specs=[pl.BlockSpec(memory_space=pltpu.VMEM)] * len(arrays),
-        scratch_shapes=[pltpu.VMEM((v.shape[0] // n * (n - 1), v.shape[1]), jnp.bfloat16) for v in arrays]
-        + [pltpu.SemaphoreType.DMA((streams, 2 * n - 2)), pltpu.SemaphoreType.DMA((streams, 2 * n - 2))],
+        out_specs=[pl.BlockSpec(memory_space=pltpu.VMEM)] * len(outs),
+        scratch_shapes=scratch,
         compiler_params=pltpu.CompilerParams(
             collective_id=ident, has_side_effects=True, vmem_limit_bytes=48 << 20
         ),
-        cost_estimate=pl.CostEstimate(flops=size, bytes_accessed=60 * size, transcendentals=0),
+        cost_estimate=pl.CostEstimate(flops=0, bytes_accessed=size, transcendentals=0),
     )(*arrays)
+
+
+def ring_total(arrays, splits, ident):
+    n = lax.axis_size("seq")
+    streams = sum(abs(s) for s in splits)
+    return ring_call(
+        functools.partial(ring_kernel, n, splits),
+        "ring_total",
+        arrays,
+        [v.shape for v in arrays],
+        [pltpu.VMEM((v.shape[0] // n * (n - 1), v.shape[1]), jnp.bfloat16) for v in arrays]
+        + [pltpu.SemaphoreType.DMA((streams, 2 * n - 2))] * 2,
+        ident,
+    )
+
+
+def units_kernel(n, fan, x_ref, inner_ref, outer_ref, swap_send, swap_recv, own_sem, send_sem, recv_sem):
+    s, me = lax.axis_index("seq"), lax.axis_index("fsdp")
+    rows, width = x_ref.shape[0] // 3, x_ref.shape[1]
+    cols = width // fan
+    block = 2 * fan * rows
+    place, right, left = ring_greet(n, [(me + far) % fan for far in range(1, fan)])
+    moves = []
+    for far in range(fan):
+        target = (me + far) % fan
+        for half in range(2):
+            src = x_ref.at[pl.ds(half * rows, rows), pl.ds(pl.multiple_of(target * cols, 128), cols)]
+            dst = inner_ref.at[pl.ds(s * block + (me * 2 + half) * rows, rows), :]
+            if far:
+                one = pltpu.make_async_remote_copy(
+                    src_ref=src,
+                    dst_ref=dst,
+                    send_sem=swap_send.at[far, half],
+                    recv_sem=swap_recv.at[far, half],
+                    device_id={"fsdp": target},
+                    device_id_type=MESH,
+                )
+            else:
+                one = pltpu.make_async_copy(src, dst, own_sem.at[half])
+            one.start()
+            moves.append(one)
+    mine = pltpu.make_async_copy(
+        x_ref.at[pl.ds(2 * rows, rows), :], outer_ref.at[pl.ds(s * rows, rows), :], own_sem.at[2]
+    )
+    mine.start()
+    copies = {}
+    outs = ((outer_ref, (n * rows, width), 2), (inner_ref, (n * block, cols), -2))
+
+    def start(k, piece, step):
+        ref, shape, split = outs[k]
+        chunk = ring_index((place + step) % n if piece else (place + n - step) % n, n)
+        view = ring_window(ref, shape, split, n, piece, chunk)
+        copies[k, piece, step] = pltpu.make_async_remote_copy(
+            src_ref=view,
+            dst_ref=view,
+            send_sem=send_sem.at[2 * k + piece, step],
+            recv_sem=recv_sem.at[2 * k + piece, step],
+            device_id={"seq": left if piece else right},
+            device_id_type=MESH,
+        )
+        copies[k, piece, step].start()
+
+    mine.wait()
+    start(0, 0, 0)
+    start(0, 1, 0)
+    for one in moves:
+        one.wait()
+    start(1, 0, 0)
+    start(1, 1, 0)
+    for step in range(n - 1):
+        for k in range(2):
+            for piece in range(2):
+                copies[k, piece, step].wait_recv()
+                if step < n - 2:
+                    start(k, piece, step + 1)
+    for one in copies.values():
+        one.wait_send()
+
+
+def units_total(part, ident):
+    n, fan = lax.axis_size("seq"), lax.axis_size("fsdp")
+    rows, width = part.shape[0] // 3, part.shape[1]
+    sems = lambda *shape: pltpu.SemaphoreType.DMA(shape)
+    return ring_call(
+        functools.partial(units_kernel, n, fan),
+        "units_total",
+        [part],
+        [(n * 2 * fan * rows, width // fan), (n * rows, width)],
+        [sems(fan, 2), sems(fan, 2), sems(3), sems(4, n - 1), sems(4, n - 1)],
+        ident,
+    )
 
 
 def team(n):
@@ -458,10 +549,13 @@
     return f // 2, half, (s + away * (n // 2)) % n
 
 
-def swap_kernel(n, count, *refs):
-    x_refs, y_refs = refs[:count], refs[count : 2 * count]
-    send_sem, recv_sem, own_sem = refs[2 * count :]
+def swap_kernel(n, fan, count, fars, fresh, *refs):
+    given = count + (len(fars) > 0) + (0 if fresh else 2)
+    x_refs, y_refs = refs[:count], refs[given : given + count]
+    sems = refs[given + count + (2 if fars else 0) :]
+    send_sem, recv_sem, own_sem = sems[:3]
     pair, half, rank = team(n)
+    me = lax.axis_index("fsdp")
 
     def device(other):
         away = (other // (n // 2) + half) % 2
@@ -470,7 +564,10 @@
     barrier = pltpu.get_barrier_semaphore()
     for j in range(1, n):
         pl.semaphore_signal(barrier, inc=1, device_id=device((rank + j) % n), device_id_type=MESH)
-    pl.semaphore_wait(barrier, n - 1)
+    travel = [far for far in fars if far]
+    for far in travel:
+        pl.semaphore_signal(barrier, inc=1, device_id={"fsdp": (me + fan - far) % fan}, device_id_type=MESH)
+    pl.semaphore_wait(barrier, n - 1 + len(travel))
     copies = []
     for k in range(count):
         for j in range(1, n):
@@ -485,33 +582,65 @@
             )
             one.start()
             copies.append(one)
-    own = [
-        pltpu.make_async_copy(x_refs[k].at[rank], y_refs[k].at[rank], own_sem.at[k]) for k in range(count)
-    ]
-    for one in own:
+    for k in range(count):
+        one = pltpu.make_async_copy(x_refs[k].at[rank], y_refs[k].at[rank], own_sem.at[k])
         one.start()
-    for one in copies + own:
+        copies.append(one)
+    if fars:
+        w_ref, halves = refs[count], refs[given + count : given + count + 2]
+        far_send, far_recv, far_own = sems[3:]
+        units, cols = halves[0].shape[0], w_ref.shape[1]
+        for i, far in enumerate(fars):
+            target = (me + far) % fan
+            for part in range(2):
+                src = w_ref.at[pl.ds((part * fan + target) * units, units), :]
+                dst = halves[part].at[:, pl.ds(pl.multiple_of(me * cols, 128), cols)]
+                if far:
+                    one = pltpu.make_async_remote_copy(
+                        src_ref=src,
+                        dst_ref=dst,
+                        send_sem=far_send.at[i, part],
+                        recv_sem=far_recv.at[i, part],
+                        device_id={"fsdp": target},
+                        device_id_type=MESH,
+                    )
+                else:
+                    one = pltpu.make_async_copy(src, dst, far_own.at[part])
+                one.start()
+                copies.append(one)
+    for one in copies:
         one.wait()
 
 
-def swap(arrays, ident):
-    n = lax.axis_size("seq")
+def swap(arrays, ident, fars=(), given=None, halves=None):
+    n, fan = lax.axis_size("seq"), lax.axis_size("fsdp")
     count = len(arrays)
     size = sum(v.size * 2 for v in arrays)
+    operands, outs, alias = list(arrays), [jax.ShapeDtypeStruct(v.shape, v.dtype) for v in arrays], {}
+    scratch = [
+        pltpu.SemaphoreType.DMA((count, n)),
+        pltpu.SemaphoreType.DMA((count, n)),
+        pltpu.SemaphoreType.DMA((count,)),
+    ]
+    if fars:
+        operands.append(given)
+        shape = (given.shape[0] // (2 * fan), given.shape[1] * fan)
+        outs += [jax.ShapeDtypeStruct(shape, given.dtype)] * 2
+        scratch += [pltpu.SemaphoreType.DMA((len(fars), 2))] * 2 + [pltpu.SemaphoreType.DMA((2,))]
+        if halves is not None:
+            operands += list(halves)
+            alias = {count + 1: count, count + 2: count + 1}
     return pl.pallas_call(
-        functools.partial(swap_kernel, n, count),
+        functools.partial(swap_kernel, n, fan, count, fars, not fars or halves is None),
         name="swap",
-        out_shape=[jax.ShapeDtypeStruct(v.shape, v.dtype) for v in arrays],
-        in_specs=[pl.BlockSpec(memory_space=pl.ANY)] * count,
-        out_specs=[pl.BlockSpec(memory_space=pl.ANY)] * count,
-        scratch_shapes=[
-            pltpu.SemaphoreType.DMA((count, n)),
-            pltpu.SemaphoreType.DMA((count, n)),
-            pltpu.SemaphoreType.DMA((count,)),
-        ],
+        out_shape=outs,
+        in_specs=[pl.BlockSpec(memory_space=pl.ANY)] * len(operands),
+        out_specs=[pl.BlockSpec(memory_space=pl.ANY)] * len(outs),
+        scratch_shapes=scratch,
+        input_output_aliases=alias,
         compiler_params=pltpu.CompilerParams(collective_id=ident, has_side_effects=True),
-        cost_estimate=pl.CostEstimate(flops=0, bytes_accessed=30 * size, transcendentals=0),
-    )(*arrays)
+        cost_estimate=pl.CostEstimate(flops=0, bytes_accessed=size, transcendentals=0),
+    )(*operands)
 
 
 def norm_apply(value, gain):
@@ -603,27 +732,24 @@
     qkv_w = gather(self_qkv)
     small = jnp.concatenate([norm_self, norm_cross, norm_ff, rel_table.reshape(-1)])
     small = lax.all_gather(small, "fsdp", axis=0, tiled=False)
-    qkv_w, small, first_batch, cross_out = lax.optimization_barrier(
-        (qkv_w, small, jnp.concatenate([self_out, cross_q, cross_kv.reshape(-1, 2 * width)], axis=1), cross_out)
-    )
-    qkv_w = qkv_w.reshape(width, parts, own * 3 * dh)
-    first_batch = by_rows(gather(by_rows(first_batch)))
-    inner_t = jnp.transpose(ff_in.T.reshape(2, fan, units, -1), (1, 0, 2, 3))
-    first_batch, cross_out, inner_t = lax.optimization_barrier((first_batch, cross_out, inner_t))
-    mix_self = first_batch[:, :width].reshape(parts, own * dh, width)
-    query_w = first_batch[:, width : 2 * width].reshape(width, parts, own * dh)
-    pairs_w = first_batch[:, 2 * width :].reshape(width, parts, own * 2 * dh)
-    mix_cross = gather(cross_out)
-    inner_t = spread(inner_t)
-    gate_t, up_t = (jnp.transpose(inner_t[:, i], (1, 0, 2)).reshape(units, width) for i in range(2))
-
-    gain_first, gain_second, gain_third = (
-        small[:, i * part : (i + 1) * part].reshape(width).astype(f32) for i in range(3)
-    )
-    table = jnp.transpose(small[:, 3 * part :].reshape(-1, buckets, table_own), (1, 0, 2)).reshape(buckets, heads)
+    early = jnp.stack([self_out, cross_q, *jnp.split(cross_kv.reshape(-1, 2 * width), 2, axis=1)])
+    small, early = lax.optimization_barrier((small, early))
+    early = lax.all_gather(early, "fsdp", axis=1, tiled=True)
     both_ids = jnp.concatenate([decoder_ids.reshape(-1), encoder_ids.reshape(-1)])
     both_ids = change_home(jnp.pad(both_ids, (0, 1024 - local - enc_local)).reshape(8, 128))
     (both_ids,) = swap([jnp.broadcast_to(both_ids[None], (parts, 8, 128))], 13)
+    home = change_home(layer_in.reshape(rows, width))
+    inner_t = ff_in.T
+    qkv_w, small, both_ids, home, inner_t = lax.optimization_barrier((qkv_w, small, both_ids, home, inner_t))
+    qkv_w = qkv_w.reshape(width, parts, own * 3 * dh)
+    mix_self = early[0].reshape(parts, own * dh, width)
+    query_w = early[1].reshape(width, parts, own * dh)
+    pairs_w = early[2:]
+
+    gain_first, gain_second, gain_third = (
+        small[:, i * part : (i + 1) * part].reshape(width).astype(f32) for i in range(3)
+    )
+    table = jnp.transpose(small[:, 3 * part :].reshape(-1, buckets, table_own), (1, 0, 2)).reshape(buckets, heads)
     both_ids = both_ids.reshape(parts, 1024)
     ids = both_ids[:, :local].reshape(length)
     enc_ids = both_ids[:, local : local + enc_local].reshape(keys)
@@ -649,26 +775,36 @@
         [jnp.full((own, BQ), MASKED, f32), bias, jnp.zeros((own, BQ), f32)], axis=1
     )
 
-    stream = change_home(layer_in.reshape(rows, width)).astype(f32)
+    stream = home.astype(f32)
+    normed_first = norm_apply(stream, gain_first).astype(bf16)
+    qkv_tok = jnp.einsum("td,dge->gte", normed_first, qkv_w, preferred_element_type=f32).astype(bf16)
+    qkv_tok, cross_out, cotangent, encoder = lax.optimization_barrier((qkv_tok, cross_out, cotangent, encoder))
+    mix_cross = gather(cross_out).reshape(parts, own * dh, width)
     others = change_home(jnp.concatenate([cotangent.reshape(rows, width), encoder.reshape(-1, width)]))
     grad_low, enc_flat = others[:rows], others[rows:]
-    mix_cross, grad_low = lax.optimization_barrier((mix_cross, grad_low))
-    mix_cross = mix_cross.reshape(parts, own * dh, width)
-    grad_group = gather(grad_low)
-    normed_first = norm_apply(stream, gain_first).astype(bf16)
-    qkv_tok = jnp.einsum("td,dge->gte", normed_first, qkv_w, preferred_element_type=f32).astype(bf16)
     (qkv,) = swap([qkv_tok], 10)
     qkv = qkv.reshape(length, own * 3 * dh)
     out_self, self_t, self_lse = self_forward(self_limits, self_rows, ext, qkv)
-    (self_tok,) = swap([out_self.reshape(parts, local, own * dh)], 11)
+    out_self, grad_low = lax.optimization_barrier((out_self, grad_low))
+    grad_group = gather(grad_low)
+    by_kernel = (width // fan) % 128 == 0
+    fars = [tuple(far for far in range(fan) if (far + 2) % 3 == i) if by_kernel else () for i in range(3)]
+    self_tok, *halves = swap([out_self.reshape(parts, local, own * dh)], 14, fars[0], inner_t)
     after_self = stream + jnp.einsum("gtc,gcd->td", self_tok, mix_self, preferred_element_type=f32)
     normed_second = norm_apply(after_self, gain_second).astype(bf16)
     query_tok = jnp.einsum("td,dgc->gtc", normed_second, query_w, preferred_element_type=f32).astype(bf16)
-    pairs_tok = jnp.einsum("td,dge->gte", enc_flat, pairs_w, preferred_element_type=f32).astype(bf16)
-    query_cross, pairs = swap([query_tok, pairs_tok], 12)
+    pairs_tok = jnp.einsum(
+        "td,sdge->sgte", enc_flat, pairs_w.reshape(2, width, parts // 2, -1), preferred_element_type=f32
+    )
+    pairs_tok = pairs_tok.astype(bf16).reshape(parts, enc_local, -1)
+    query_cross, pairs, *halves = swap([query_tok, pairs_tok], 15, fars[1], inner_t, halves)
     query_cross, pairs = query_cross.reshape(length, own * dh), pairs.reshape(keys, own * 2 * dh)
     out_cross, cross_t, cross_lse = cross_forward(cross_limits, cross_rows, query_cross, pairs)
-    (cross_tok,) = swap([out_cross.reshape(parts, local, own * dh)], 11)
+    cross_tok, *halves = swap([out_cross.reshape(parts, local, own * dh)], 16, fars[2], inner_t, halves)
+    if not by_kernel:
+        halves = spread(jnp.transpose(inner_t.reshape(2, fan, units, -1), (1, 0, 2, 3)))
+        halves = [jnp.transpose(halves[:, i], (1, 0, 2)).reshape(units, width) for i in range(2)]
+    gate_t, up_t = halves
     after_cross = after_self + jnp.einsum("gtc,gcd->td", cross_tok, mix_cross, preferred_element_type=f32)
     normed_third = norm_apply(after_cross, gain_third).astype(bf16)
     normed_group = gather(normed_third)
@@ -684,17 +820,16 @@
     )
     grad_third_in = scatter(grad_third_in.astype(bf16))
     outer_part = jnp.dot(hidden, ff_out, preferred_element_type=f32).astype(bf16)
-    part_outer = jnp.einsum("tf,td->fd", hidden, grad_group, preferred_element_type=f32).astype(bf16)
-    grad_inner = [
-        jnp.einsum("tf,td->fd", g, normed_group, preferred_element_type=f32).astype(bf16)
-        for g in (grad_gate, grad_up)
+    grad_units = [
+        jnp.einsum("tf,td->fd", g, y, preferred_element_type=f32).astype(bf16)
+        for g, y in ((grad_gate, normed_group), (grad_up, normed_group), (hidden, grad_group))
     ]
-    grad_inner = jnp.transpose(jnp.stack(grad_inner).reshape(2, units, fan, -1), (2, 0, 1, 3))
-    grad_third_in, outer_part, part_outer, grad_inner = lax.optimization_barrier(
-        (grad_third_in, outer_part, part_outer, grad_inner)
-    )
-    outer_part = scatter(outer_part)
-    part_inner = spread(grad_inner).reshape(2 * fan * units, -1)
+    grad_third_in, outer_part, grad_units = lax.optimization_barrier((grad_third_in, outer_part, grad_units))
+    if by_kernel:
+        grad_units = jnp.stack([g.reshape(parts, units // parts, width) for g in grad_units], axis=1)
+        part_units = lax.psum_scatter(
+            grad_units.reshape(3 * units, width), "seq", scatter_dimension=0, tiled=True
+        )
     grad_third_in = grad_third_in.astype(f32)
     grad_from_third, grad_gain_third = norm_back(after_cross, gain_third, grad_third_in)
     grad_middle = grad_low.astype(f32) + grad_from_third
@@ -713,7 +848,10 @@
     grad_query_w = jnp.einsum("td,te->de", normed_second, grad_query_tok, preferred_element_type=f32)
     grad_second_in = jnp.einsum("te,de->td", grad_query_tok, query_w.reshape(width, -1), preferred_element_type=f32)
     grad_pairs_w = jnp.einsum("td,te->de", enc_flat, grad_pairs_tok, preferred_element_type=f32)
-    grad_encoder = jnp.einsum("te,de->td", grad_pairs_tok, pairs_w.reshape(width, -1), preferred_element_type=f32)
+    grad_encoder = sum(
+        jnp.einsum("te,de->td", grad_pairs_tok[:, i * width : (i + 1) * width], pairs_w[i], preferred_element_type=f32)
+        for i in range(2)
+    )
     grad_encoder = change_home(grad_encoder.astype(bf16)).astype(f32).reshape(seqs, enc_local, width)
     grad_from_second, grad_gain_second = norm_back(after_self, gain_second, grad_second_in)
     grad_upper = grad_middle + grad_from_second
@@ -725,10 +863,12 @@
             grad_query_w.astype(bf16),
             grad_pairs_w.astype(bf16),
             grad_mix_cross.reshape(width, width).astype(bf16),
+            grad_mix_self.reshape(width, width).astype(bf16),
         ],
         axis=1,
     )
-    grad_self_tok, grad_mid = lax.optimization_barrier((grad_self_tok, grad_mid))
+    if by_kernel:
+        grad_self_tok, grad_mid, part_units = lax.optimization_barrier((grad_self_tok, grad_mid, part_units))
     part_mid = scatter(grad_mid)
     (grad_self,) = swap([grad_self_tok], 11)
     grad_self = grad_self.reshape(length, own * dh)
@@ -736,15 +876,12 @@
     (grad_qkv_tok,) = swap([grad_qkv.reshape(parts, local, own * 3 * dh)], 10)
     grad_qkv_tok = flat(grad_qkv_tok)
     grad_qkv_w = jnp.einsum("td,te->de", normed_first, grad_qkv_tok, preferred_element_type=f32)
-    grad_last = jnp.concatenate([grad_mix_self.reshape(width, width).astype(bf16), grad_qkv_w.astype(bf16)], axis=1)
-    grad_last, part_mid, part_inner, part_outer, outer_part = lax.optimization_barrier(
-        (grad_last, part_mid, part_inner, part_outer, outer_part)
-    )
+    grad_last, part_mid = lax.optimization_barrier((grad_qkv_w.astype(bf16), part_mid))
     part_last = scatter(grad_last)
-    layer_out = (after_cross + outer_part.astype(f32)).astype(bf16)
-    layer_out = change_home(layer_out).reshape(seqs, local, width)
     grad_first_in = jnp.einsum("te,de->td", grad_qkv_tok, qkv_w.reshape(width, -1), preferred_element_type=f32)
     grad_from_first, grad_gain_first = norm_back(stream, gain_first, grad_first_in)
+    grad_gain_first, outer_part = lax.optimization_barrier((grad_gain_first, outer_part))
+    outer_part = scatter(outer_part)
     grad_layer_in = change_home((grad_upper + grad_from_first).astype(bf16)).astype(f32)
     grad_layer_in = grad_layer_in.reshape(seqs, local, width)
 
@@ -764,15 +901,23 @@
     small_grads = lax.dynamic_index_in_dim(small_grads, lax.axis_index("fsdp"), 0, False)
     small_size = small_grads.shape[0]
     small_grads = jnp.pad(small_grads, (0, parts * 1024 - small_size)).reshape(parts * 8, 128)
-    total_inner, total_outer = over_seq([part_inner, part_outer], (-2, 2), 0)
-    total_inner, part_mid, part_last = lax.optimization_barrier((total_inner, part_mid, part_last))
-    total_mid, total_last, small_total = over_seq([part_mid, part_last, small_grads], (2, 2, 1), 1)
-    total_outer, total_mid, total_last = (v.astype(f32) for v in (total_outer, total_mid, total_last))
-    total_inner = jnp.transpose(total_inner.reshape(fan, 2, units, -1), (3, 1, 0, 2)).reshape(-1, 2 * fan * units)
-    total_inner = total_inner.astype(f32)
-    total_query, total_mix_cross = total_mid[:, :width], total_mid[:, 3 * width :]
+    grad_layer_in, small_grads, part_last = lax.optimization_barrier((grad_layer_in, small_grads, part_last))
+    if by_kernel:
+        total_inner, total_outer = units_total(part_units, 0)
+        total_inner = jnp.transpose(total_inner.reshape(parts, fan, 2, units // parts, -1), (4, 2, 1, 0, 3))
+    else:
+        grad_units = [lax.psum(g, "seq") for g in grad_units]
+        total_inner = spread(jnp.transpose(jnp.stack(grad_units[:2]).reshape(2, units, fan, -1), (2, 0, 1, 3)))
+        total_inner, total_outer = jnp.transpose(total_inner, (3, 1, 0, 2)), grad_units[2]
+    total_inner = total_inner.astype(f32).reshape(-1, 2 * fan * units)
+    total_outer, part_last = lax.optimization_barrier((total_outer, part_last))
+    total_mid, total_qkv, small_total = over_seq([part_mid, part_last, small_grads], (2, 2, 1), 1)
+    layer_out = (after_cross + outer_part.astype(f32)).astype(bf16)
+    layer_out = change_home(layer_out).reshape(seqs, local, width)
+    total_outer, total_mid, total_qkv = (v.astype(f32) for v in (total_outer, total_mid, total_qkv))
+    total_query, total_mix_cross = total_mid[:, :width], total_mid[:, 3 * width : 4 * width]
     total_pairs = total_mid[:, width : 3 * width].reshape(-1, heads, 2 * dh)
-    total_mix_self, total_qkv = total_last[:, :width], total_last[:, width:].reshape(-1, heads, 3 * dh)
+    total_mix_self, total_qkv = total_mid[:, 4 * width :], total_qkv.reshape(-1, heads, 3 * dh)
     mine = small_total.reshape(-1)[:small_size].astype(f32)
     total_gain_first, total_gain_second, total_gain_third = (mine[i * part : (i + 1) * part] for i in range(3))
     total_table = mine[3 * part :].reshape(buckets, table_own)

time: 785 us -> 723 us (0.921)
  waiting for transfers between devices: 145 us -> 116 us
  local copies, waits for them, and re-layouts: 98.4 us -> 75.4 us
  matrix products: 81.5 us -> 72.8 us
    all_gather x5 -> x4, waiting for transfers between devices: 90.4 us -> 30.6 us  [shards(): gather = lambda v: lax.all_gather(v, 'fsdp', axis=0, tiled=True)]
    reduce_scatter x4, waiting for transfers between devices: 0.01 us -> 53.9 us  [scatter(): return lax.psum_scatter(grad, 'fsdp', scatter_dimension=0, tiled=True)]
    ppermute x6 -> x0, waiting for transfers between devices: 52 us -> none  [spread(): lax.ppermute(block, 'fsdp', [(f, (f + far) % fan) for f in range(fan)])]
    reduce_scatter x0 -> x1, waiting for transfers between devices: none -> 22 us  [shards(): lax.psum_scatter(grad_units.reshape(3 * units, width), 'seq', scatter_dim...]
    another operation x4 -> x1, local copies, waits for them, and re-layouts: 12.6 us -> 0.07 us  [shards(): jnp.stack([self_out, cross_q, *jnp.split(cross_kv.reshape(-1, 2 * width),...]
    ppermute x6 -> x0, starting transfers between devices: 11.6 us -> none  [spread(): lax.ppermute(block, 'fsdp', [(f, (f + far) % fan) for f in range(fan)])]
    dynamic_slice x4 -> x0, local copies, waits for them, and re-layouts: 10.3 us -> none  [spread(): block = lax.dynamic_index_in_dim(blocks, (me + far) % fan, 0, True)]
    concatenate x2 -> x0, other arithmetic: 9.27 us -> none  [the longest x1 7.75 us: shards(): jnp.concatenate([grad_mix_self.reshape(width, width).astype(bf16), grad_q...]
  transfers between devices with their start and end apart: 21 -> 16, of which waited for: 8 -> 8; matrix products, arithmetic and copies ran while one was open for 21% -> 19% of each run, Pallas kernels for 34% -> 38%
where the time goes in v5:
time: 723 us; the launch traced here: 709 us
  Pallas kernels  350 us (48%)
  waiting for transfers between devices  116 us (16%)
  local copies, waits for them, and re-layouts  75.4 us (10%)
  matrix products  72.8 us (10%)
  other arithmetic  40.4 us (6%)
  starting transfers between devices  25.9 us (4%)
  between operations  15.6 us (2%)
  blocking collectives  13.2 us (2%)
    pallas_call x9, Pallas kernels, swap(): pl.pallas_call(functools.partial(swap_kernel, n, fan, count, fars, not fa...  162 us
    pallas_call x2, Pallas kernels, ring_call(): pl.pallas_call(body, name=name, out_shape=[jax.ShapeDtypeStruct(s, jnp.bf...  133 us
    pallas_call x4, Pallas kernels, call(): pl.pallas_call(body, name=name, out_shape=[jax.ShapeDtypeStruct(s, d) for...  55 us
    reduce_scatter x4, waiting for transfers between devices, scatter(): return lax.psum_scatter(grad, 'fsdp', scatter_dimension=0, tiled=True)  53.9 us
    unnamed x171, local copies, waits for them, and re-layouts  43.3 us
    all_gather x4, waiting for transfers between devices, shards(): gather = lambda v: lax.all_gather(v, 'fsdp', axis=0, tiled=True)  30.6 us
    ppermute x6, starting transfers between devices, change_home(): return lax.ppermute(value, ('seq', 'fsdp'), pairs)  23.9 us
    reduce_scatter x1, waiting for transfers between devices, shards(): lax.psum_scatter(grad_units.reshape(3 * units, width), 'seq', scatter_dim...  22 us
  transfers between devices with their start and end apart: 16, of which 8 were waited for; matrix products, arithmetic and copies ran while one was open for 19% of the time, Pallas kernels for 38%

profile of v5, /device:TPU:1, one launch (start us, length us, event | category | flops | bytes accessed | tf_op | source)
XLA Modules:
  0.0 709.1 jit_solution(9579219081999424655)
XLA Ops:
  9.6 6.1 all-gather.1
  21.6 4.7 collective-permute-start.1
  32.9 6.0 collective-permute-done
  39.5 5.0 swap.9
  44.6 14.8 %all-gather.8.cloned.1.call-done = bf16[1024,16,192]{0,2,1:T(8,128)(2,1)} async-done(((bf16[256,16,192]{0,2,1:T(8,128)(2,1)}), bf16[1024,16,192]{0,2,1:T(8,128)(2,1)}) %all-gather.8.cloned.1.call-update) | async-done | bytes 6291472 | tf_op jit(solution)/shard_map/all_gather | solution.py:725
  60.0 5.8 fusion.11.refs_0_
  74.3 5.3 fusion.55
  82.2 21.0 %swap.10 = bf16[8,256,384]{2,1,0:T(8,128)(2,1)} custom-call(bf16[8,256,384]{2,1,0:T(8,128)(2,1)} %fusion.11.refs_0_), custom_call_target="tpu_custom_call" | custom-call | bytes 1572864 | tf_op jit(solution)/shard_map/swap/pallas_call | solution.py:633
  112.5 15.6 %self_forward.1 = (bf16[2048,128]{1,0:T(8,128)(2,1)S(1)}, f32[128,2048]{1,0:T(8,128)S(1)}, f32[2,2048]{1,0:T(2,128)S(1)}) custom-call(s32[2,8]{1,0:T(2,128)S(1)} %pad_add_fusion.1.lim_ref, s32[8,2048]{1,0:T(8,128)S(1)} %broadcast_in_dim.100.rows_ref, f32[2,1536]{1,0:T(2,128)S(1)} %maximum_maximum_fusion.ext_ref, bf16[2048,384]{1,0:T(8,128)(2,1)S(1)} %bitcast.217), custom_call_target="tpu_custom_call" | custom-call | bytes 1650752 | tf_op jit(solution)/shard_map/self_forward/pallas_call | solution.py:257
  132.1 17.2 %swap.11 = (bf16[8,256,128]{2,1,0:T(8,128)(2,1)}, bf16[704,1024]{1,0:T(8,128)(2,1)}, bf16[704,1024]{1,0:T(8,128)(2,1)}) custom-call(bf16[8,256,128]{2,1,0:T(8,128)(2,1)} %bitcast.229, bf16[5632,256]{1,0:T(8,128)(2,1)} %bitcast.231), custom_call_target="tpu_custom_call" | custom-call | bytes 524288 | tf_op jit(solution)/shard_map/swap/pallas_call | solution.py:633
  165.8 21.8 %swap.12 = (bf16[8,256,128]{2,1,0:T(8,128)(2,1)}, bf16[8,64,256]{2,1,0:T(8,128)(2,1)}, bf16[704,1024]{1,0:T(8,128)(2,1)}, bf16[704,1024]{1,0:T(8,128)(2,1)}) custom-call(bf16[8,256,128]{2,1,0:T(8,128)(2,1)} %fusion.17.refs_0_, bf16[8,64,256]{2,1,0:T(8,128)(2,1)} %bitcast.259, ...), custom_call_target="tpu_custom_call", output_to_operand_aliasing={{2}: (3, {}), {3}: (4, {})} | custom-call | bytes 786432 | tf_op jit(solution)/shard_map/swap/pallas_call | solution.py:633
  189.6 9.2 %cross_forward.1 = (bf16[2048,128]{1,0:T(8,128)(2,1)S(1)}, f32[128,2048]{1,0:T(8,128)S(1)}, f32[2,2048]{1,0:T(2,128)S(1)}) custom-call(s32[2,8]{1,0:T(2,128)S(1)} %pad_add_fusion.2.lim_ref, s32[8,2048]{1,0:T(8,128)S(1)} %add_add_fusion.3.rows_ref, bf16[2048,128]{1,0:T(8,128)(2,1)S(1)} %bitcast.220, bf16[512,256]{1,0:T(8,128)(2,1)S(1)} %bitcast.225), custom_call_target="tpu_custom_call" | custom-call | bytes 852032 | tf_op jit(solution)/shard_map/cross_forward/pallas_call | solution.py:257
  200.6 27.9 %swap.13 = (bf16[8,256,128]{2,1,0:T(8,128)(2,1)}, bf16[704,1024]{1,0:T(8,128)(2,1)}, bf16[704,1024]{1,0:T(8,128)(2,1)}) custom-call(bf16[8,256,128]{2,1,0:T(8,128)(2,1)} %bitcast.227, bf16[5632,256]{1,0:T(8,128)(2,1)} %bitcast.233, bf16[704,1024]{1,0:T(8,128)(2,1)} %get-tuple-element.89.refs_2_, ...), custom_call_target="tpu_custom_call", output_to_operand_aliasing={{1}: (2, {}), {2}: (3, {})} | custom-call | bytes 524288 | tf_op jit(solution)/shard_map/swap/pallas_call | solution.py:633
  233.8 4.9 fusion.69
  238.6 15.8 %all-gather.16.cloned.1.call-done = bf16[1024,1024]{1,0:T(8,128)(2,1)} async-done(((bf16[256,1024]{1,0:T(8,128)(2,1)}), bf16[1024,1024]{1,0:T(8,128)(2,1)}) %all-gather.16.cloned.1.call-update) | async-done | bytes 2097168 | tf_op jit(solution)/shard_map/all_gather | solution.py:725
  282.9 16.5 %reduce-scatter.6.cloned.1.call-done = bf16[256,1024]{1,0:T(8,128)(2,1)} async-done(((bf16[1024,1024]{1,0:T(8,128)(2,1)}), bf16[256,1024]{1,0:T(8,128)(2,1)}) %reduce-scatter.6.cloned.1.call-update) | async-done | bytes 524304 | tf_op jit(solution)/shard_map/reduce_scatter | solution.py:696
  309.9 17.1 %swap.14 = bf16[8,256,128]{2,1,0:T(8,128)(2,1)} custom-call(bf16[8,256,128]{2,1,0:T(8,128)(2,1)} %fusion.18.refs_0_), custom_call_target="tpu_custom_call" | custom-call | bytes 524288 | tf_op jit(solution)/shard_map/swap/pallas_call | solution.py:633
  329.2 10.6 %cross_backward.1 = (bf16[2048,128]{1,0:T(8,128)(2,1)S(1)}, bf16[512,256]{1,0:T(8,128)(2,1)S(1)}) custom-call(s32[2,8]{1,0:T(2,128)S(1)} %pad_add_fusion.2.lim_ref, s32[8,2048]{1,0:T(8,128)S(1)} %add_add_fusion.3.rows_ref, bf16[2048,128]{1,0:T(8,128)(2,1)S(1)} %bitcast.221, bf16[512,256]{1,0:T(8,128)(2,1)S(1)} %bitcast.226, bf16[2048,128]{1,0:T(8,128)(2,1)S(1)} %bitcast.222, ...), custom_call_target="tpu_custom_call" | custom-call | bytes 2441280 | tf_op jit(solution)/shard_map/cross_backward/pallas_call | solution.py:257
  341.3 21.5 %swap.15 = (bf16[8,256,128]{2,1,0:T(8,128)(2,1)}, bf16[8,64,256]{2,1,0:T(8,128)(2,1)}) custom-call(bf16[8,256,128]{2,1,0:T(8,128)(2,1)} %bitcast.228, bf16[8,64,256]{2,1,0:T(8,128)(2,1)} %bitcast.230), custom_call_target="tpu_custom_call" | custom-call | bytes 786432 | tf_op jit(solution)/shard_map/swap/pallas_call | solution.py:633
  376.7 6.1 pad_maximum_fusion
  382.8 22.0 %reduce-scatter.8.cloned.1.call-done.x_ref = bf16[264,1024]{1,0:T(8,128)(2,1)} async-done(((bf16[2112,1024]{1,0:T(8,128)(2,1)}), bf16[264,1024]{1,0:T(8,128)(2,1)}) %reduce-scatter.8.cloned.1.call-update) | async-done | bytes 540688 | tf_op jit(solution)/shard_map/reduce_scatter | solution.py:830
  405.0 10.4 %swap.16 = bf16[8,256,128]{2,1,0:T(8,128)(2,1)} custom-call(bf16[8,256,128]{2,1,0:T(8,128)(2,1)} %fusion.19.refs_0_), custom_call_target="tpu_custom_call" | custom-call | bytes 524288 | tf_op jit(solution)/shard_map/swap/pallas_call | solution.py:633
  416.7 19.6 %self_backward.1 = (bf16[2048,384]{1,0:T(8,128)(2,1)S(1)}, f32[2,5,512]{2,1,0:T(8,128)S(1)}) custom-call(s32[2,8]{1,0:T(2,128)S(1)} %pad_add_fusion.1.lim_ref, s32[8,2048]{1,0:T(8,128)S(1)} %broadcast_in_dim.100.rows_ref, f32[2,1536]{1,0:T(2,128)S(1)} %maximum_maximum_fusion.ext_ref, bf16[2048,384]{1,0:T(8,128)(2,1)S(1)} %bitcast.218, ...), custom_call_target="tpu_custom_call" | custom-call | bytes 3240000 | tf_op jit(solution)/shard_map/self_backward/pallas_call | solution.py:257
  437.4 20.3 %swap.17 = bf16[8,256,384]{2,1,0:T(8,128)(2,1)} custom-call(bf16[8,256,384]{2,1,0:T(8,128)(2,1)} %bitcast.224), custom_call_target="tpu_custom_call" | custom-call | bytes 1572864 | tf_op jit(solution)/shard_map/swap/pallas_call | solution.py:633
  459.6 5.7 fusion.32
  470.0 22.4 %reduce-scatter.12.cloned.1.call-done.refs_0_ = bf16[256,5120]{1,0:T(8,128)(2,1)} async-done(((bf16[1024,5120]{1,0:T(8,128)(2,1)}), bf16[256,5120]{1,0:T(8,128)(2,1)}) %reduce-scatter.12.cloned.1.call-update) | async-done | bytes 2621456 | tf_op jit(solution)/shard_map/reduce_scatter | solution.py:696
  512.0 15.0 %reduce-scatter.10.cloned.1.call-done = bf16[256,1024]{1,0:T(8,128)(2,1)} async-done(((bf16[1024,1024]{1,0:T(8,128)(2,1)}), bf16[256,1024]{1,0:T(8,128)(2,1)}) %reduce-scatter.10.cloned.1.call-update) | async-done | bytes 524304 | tf_op jit(solution)/shard_map/reduce_scatter | solution.py:696
  528.2 4.8 collective-permute-start.3
  534.7 51.9 %units_total.1 = (bf16[5632,256]{1,0:T(8,128)(2,1)S(1)}, bf16[704,1024]{1,0:T(8,128)(2,1)S(1)}) custom-call(bf16[264,1024]{1,0:T(8,128)(2,1)S(1)} %copy-done.15), custom_call_target="tpu_custom_call" | custom-call | bytes 540672 | tf_op jit(solution)/shard_map/units_total/pallas_call | solution.py:440
  589.7 6.3 copy.131
  596.0 7.1 %psum.7 = bf16[4,896]{1,0:T(4,128)(2,1)S(1)} all-reduce(bf16[4,896]{1,0:T(4,128)(2,1)S(1)} %pad_maximum_fusion.4), channel_id=1, replica_groups=mesh['seq'=8,'fsdp'=4] {'fsdp'}, use_global_device_ids=true, to_apply=%region_20.21 | all-reduce | flops 3584 | bytes 14336 | tf_op jit(solution)/shard_map/psum | solution.py:900
  605.6 80.7 %ring_total.1 = (bf16[256,5120]{1,0:T(8,128)(2,1)S(1)}, bf16[256,3072]{1,0:T(8,128)(2,1)S(1)}, bf16[64,128]{1,0:T(8,128)(2,1)S(1)}) custom-call(bf16[256,5120]{1,0:T(8,128)(2,1)} %reduce-scatter.12.cloned.1.call-done.refs_0_, bf16[256,3072]{1,0:T(8,128)(2,1)S(1)} %copy-done.8, bf16[64,128]{1,0:T(8,128)(2,1)S(1)} %pad_bitcast_fusion.refs_2_), custom_call_target="tpu_custom_call" | custom-call | bytes 4210688 | tf_op jit(solution)/shard_map/ring_total/pallas_call | solution.py:440
  (306 shorter events, 174.5 us)
Async XLA Ops:
  7.2 226.6 %copy-start = (bf16[704,1024]{1,0:T(8,128)(2,1)S(1)}, bf16[704,1024]{1,0:T(8,128)(2,1)}, u32[]{:S(2)}) copy-start(bf16[704,1024]{1,0:T(8,128)(2,1)} %param.32) | copy-start | bytes 4325380
  7.2 52.1 %all-gather.8.cloned.1.call-start = ((), (), s32[]{:S(2)}) async-start(), calls=%async_computation.5 | async-start | bytes 7864320 | tf_op jit(solution)/shard_map/all_gather | solution.py:725
  7.9 141.4 %all-gather.10.cloned.1.call-start = ((), (), s32[]{:S(2)}) async-start(), calls=%async_computation.6 | async-start | bytes 10485760 | tf_op jit(solution)/shard_map/all_gather | solution.py:737
  20.5 208.1 %all-gather.12.cloned.1.call-start = ((), (), s32[]{:S(2)}) async-start(), calls=%async_computation.7 | async-start | bytes 2621440 | tf_op jit(solution)/shard_map/all_gather | solution.py:725
  21.6 22.9 %collective-permute-start.1 = (bf16[256,1024]{1,0:T(8,128)(2,1)S(1)}, bf16[256,1024]{1,0:T(8,128)(2,1)S(1)}, u32[]{:S(2)}, u32[]{:S(2)}) collective-permute-start(bf16[256,1024]{1,0:T(8,128)(2,1)S(1)} %bitcast.300), channel_id=1, source_target_pairs={{0,0},{1,16},{2,2},{3,18},{4,4},{5,20},{6,6},{7,22},{8,8},{9,24},{... | collective-permute-start | bytes 1572872 | tf_op jit(solution)/shard_map/ppermute | solution.py:674
  26.4 12.5 %collective-permute-start = (s32[8,128]{1,0:T(8,128)S(1)}, s32[8,128]{1,0:T(8,128)S(1)}, u32[]{:S(2)}, u32[]{:S(2)}) collective-permute-start(s32[8,128]{1,0:T(8,128)S(1)} %pad_bitcast_fusion.1), channel_id=1, source_target_pairs={{0,0},{1,16},{2,2},{3,18},{4,4},{5,20},{6,6},{7,22},{8,8},{9,24},{... | collective-permute-start | bytes 12296 | tf_op jit(solution)/shard_map/ppermute | solution.py:674
  44.6 21.2 %copy-start.31 = (bf16[256,1024]{1,0:T(8,128)(2,1)}, bf16[256,1024]{1,0:T(8,128)(2,1)S(1)}, u32[]{:S(2)}) copy-start(bf16[256,1024]{1,0:T(8,128)(2,1)S(1)} %collective-permute-done.1) | copy-start | bytes 1572868
  65.8 37.3 %copy-start.44 = (bf16[1,256,1024]{2,1,0:T(8,128)(2,1)S(1)}, bf16[1,256,1024]{2,1,0:T(8,128)(2,1)}, u32[]{:S(2)}) copy-start(bf16[1,256,1024]{2,1,0:T(8,128)(2,1)} %param.33) | copy-start | bytes 1572868
  65.8 167.9 %all-gather.14.cloned.1.call-start = ((), (), s32[]{:S(2)}) async-start(), calls=%async_computation.8 | async-start | bytes 2621440 | tf_op jit(solution)/shard_map/all_gather | solution.py:725
  104.2 27.8 %copy-start.65 = (s32[8]{0:T(128)S(1)}, s32[8]{0:T(128)}, u32[]{:S(2)}) copy-start(s32[8]{0:T(128)} %slice.137) | copy-start | bytes 100
  104.2 27.8 %copy-start.66 = (s32[8]{0:T(128)S(1)}, s32[8]{0:T(128)}, u32[]{:S(2)}) copy-start(s32[8]{0:T(128)} %slice.136) | copy-start | bytes 100
  104.2 27.8 %copy-start.48 = (s32[1,1,8,256]{3,1,2,0:T(1,128)S(1)}, s32[1,1,8,256]{3,1,2,0:T(1,128)}, u32[]{:S(2)}) copy-start(s32[1,1,8,256]{3,1,2,0:T(1,128)} %copy.148) | copy-start | bytes 24580
  104.2 27.8 %copy-start.63 = (s32[8]{0:T(128)S(1)}, s32[8]{0:T(128)}, u32[]{:S(2)}) copy-start(s32[8]{0:T(128)} %pad.26.clone) | copy-start | bytes 100
  104.3 25.7 %collective-permute-start.2 = (bf16[320,1024]{1,0:T(8,128)(2,1)S(1)}, bf16[320,1024]{1,0:T(8,128)(2,1)S(1)}, u32[]{:S(2)}, u32[]{:S(2)}) collective-permute-start(bf16[320,1024]{1,0:T(8,128)(2,1)S(1)} %pad_maximum_fusion.3), channel_id=1, source_target_pairs={{0,0},{1,16},{2,2},{3,18},{4,4},{5,20},{6,6},{7,22},{8,8},{9,24},{... | collective-permute-start | bytes 1966088 | tf_op jit(solution)/shard_map/ppermute | solution.py:674
  131.6 122.8 %all-gather.16.cloned.1.call-start = ((), (), s32[]{:S(2)}) async-start(), calls=%async_computation.9 | async-start | bytes 2621440 | tf_op jit(solution)/shard_map/all_gather | solution.py:725
  233.3 66.1 %reduce-scatter.6.cloned.1.call-start = ((), (), s32[]{:S(2)}) async-start(), calls=%async_computation.10 | async-start | bytes 2621440 | tf_op jit(solution)/shard_map/reduce_scatter | solution.py:696
  268.2 136.5 %reduce-scatter.8.cloned.1.call-start = ((), (), s32[]{:S(2)}) async-start(), calls=%async_computation.11 | async-start | bytes 4866048 | tf_op jit(solution)/shard_map/reduce_scatter | solution.py:830
  303.1 189.4 %reduce-scatter.12.cloned.1.call-start = ((), (), s32[]{:S(2)}) async-start(), calls=%async_computation.13 | async-start | bytes 13107200 | tf_op jit(solution)/shard_map/reduce_scatter | solution.py:696
  308.3 18.6 %copy-start.4 = (bf16[8,256,128]{2,1,0:T(8,128)(2,1)S(1)}, bf16[8,256,128]{2,1,0:T(8,128)(2,1)}, u32[]{:S(2)}) copy-start(bf16[8,256,128]{2,1,0:T(8,128)(2,1)} %get-tuple-element.86) | copy-start | bytes 1572868
  308.3 18.6 %copy-start.14 = (bf16[8,64,256]{2,1,0:T(8,128)(2,1)S(1)}, bf16[8,64,256]{2,1,0:T(8,128)(2,1)}, u32[]{:S(2)}) copy-start(bf16[8,64,256]{2,1,0:T(8,128)(2,1)} %get-tuple-element.87) | copy-start | bytes 786436
  341.3 24.5 %copy-start.21 = (f32[256,1024]{1,0:T(8,128)S(1)}, f32[256,1024]{1,0:T(8,128)}, u32[]{:S(2)}) copy-start(f32[256,1024]{1,0:T(8,128)} %copy-done.20) | copy-start | bytes 3145732
  382.8 32.7 %copy-start.10 = (f32[128,2048]{1,0:T(8,128)S(1)}, f32[128,2048]{1,0:T(8,128)}, u32[]{:S(2)}) copy-start(f32[128,2048]{1,0:T(8,128)} %copy-done.9) | copy-start | bytes 3145732
  404.8 122.2 %reduce-scatter.10.cloned.1.call-start = ((), (), s32[]{:S(2)}) async-start(), calls=%async_computation.12 | async-start | bytes 2621440 | tf_op jit(solution)/shard_map/reduce_scatter | solution.py:696
  465.3 138.9 %reduce-scatter.14.cloned.1.call-start = ((), (), s32[]{:S(2)}) async-start(), calls=%async_computation.14 | async-start | bytes 7864320 | tf_op jit(solution)/shard_map/reduce_scatter | solution.py:696
  470.0 22.4 %copy-start.51 = (s32[2048]{0:T(1024)S(1)}, s32[2048]{0:T(1024)}, u32[]{:S(2)}) copy-start(s32[2048]{0:T(1024)} %param.21) | copy-start | bytes 24580
  470.0 22.5 %copy-start.61 = (pred[1536]{0:T(1024)(128)(4,1)S(1)}, pred[1536]{0:T(1024)(128)(4,1)}, u32[]{:S(2)}) copy-start(pred[1536]{0:T(1024)(128)(4,1)} %constant.127.clone.1) | copy-start | bytes 4612
  494.7 11.7 %copy-start.28 = (f32[256,1024]{1,0:T(8,128)S(1)}, f32[256,1024]{1,0:T(8,128)}, u32[]{:S(2)}) copy-start(f32[256,1024]{1,0:T(8,128)} %copy-done.27) | copy-start | bytes 3145732
  496.8 30.2 %copy-start.24 = (f32[256,1024]{1,0:T(8,128)S(1)}, f32[256,1024]{1,0:T(8,128)}, u32[]{:S(2)}) copy-start(f32[256,1024]{1,0:T(8,128)} %copy-done.22) | copy-start | bytes 3145732
  496.8 8.8 %collective-permute-start.5 = (bf16[64,1024]{1,0:T(8,128)(2,1)S(1)}, bf16[64,1024]{1,0:T(8,128)(2,1)S(1)}, u32[]{:S(2)}, u32[]{:S(2)}) collective-permute-start(bf16[64,1024]{1,0:T(8,128)(2,1)S(1)} %fusion.21), channel_id=1, source_target_pairs={{0,0},{1,16},{2,2},{3,18},{4,4},{5,20},{6,6},{7,22},{8,8},{9,24},{... | collective-permute-start | bytes 393224 | tf_op jit(solution)/shard_map/ppermute | solution.py:674
  506.4 28.4 %copy-start.15 = (bf16[264,1024]{1,0:T(8,128)(2,1)S(1)}, bf16[264,1024]{1,0:T(8,128)(2,1)}, u32[]{:S(2)}) copy-start(bf16[264,1024]{1,0:T(8,128)(2,1)} %reduce-scatter.8.cloned.1.call-done.x_ref) | copy-start | bytes 1622020
  508.7 94.4 %collective-permute-start.4 = (bf16[256,1024]{1,0:T(8,128)(2,1)}, bf16[256,1024]{1,0:T(8,128)(2,1)S(1)}, u32[]{:S(2)}, u32[]{:S(2)}) collective-permute-start(bf16[256,1024]{1,0:T(8,128)(2,1)} %fusion.30), channel_id=1, source_target_pairs={{0,0},{1,16},{2,2},{3,18},{4,4},{5,20},{6,6},{7,22},{8,8},{9,24},{... | collective-permute-start | bytes 1572872 | tf_op jit(solution)/shard_map/ppermute | solution.py:674
  528.2 76.0 %collective-permute-start.3 = (bf16[256,1024]{1,0:T(8,128)(2,1)S(1)}, bf16[256,1024]{1,0:T(8,128)(2,1)S(1)}, u32[]{:S(2)}, u32[]{:S(2)}) collective-permute-start(bf16[256,1024]{1,0:T(8,128)(2,1)S(1)} %add_convert_fusion.1), channel_id=1, source_target_pairs={{0,0},{1,16},{2,2},{3,18},{4,4},{5,20},{6,6},{7,22},{8,8},{9,24},{... | collective-permute-start | bytes 1572872 | tf_op jit(solution)/shard_map/ppermute | solution.py:674
  (60 other events, 197.6 us)
Sparse Core Ops, SparseCore 0:
  9.6 49.7 all-gather.7
  61.5 59.4 all-gather.9
  122.5 25.6 all-gather.11
  150.2 23.6 all-gather.13
  233.5 20.8 all-gather.15
  268.4 31.0 reduce-scatter.5
  304.0 100.6 reduce-scatter.7
  407.4 85.0 reduce-scatter.11
  495.6 31.4 reduce-scatter.9
  529.5 58.3 reduce-scatter.13

commit v6 on v5

--- a/solution.py
+++ b/solution.py
@@ -440,14 +440,14 @@
     return pl.pallas_call(
         body,
         name=name,
-        out_shape=[jax.ShapeDtypeStruct(s, jnp.bfloat16) for s in outs],
+        out_shape=[jax.ShapeDtypeStruct(s, d) for s, d in outs],
         in_specs=[pl.BlockSpec(memory_space=pltpu.VMEM)] * len(arrays),
         out_specs=[pl.BlockSpec(memory_space=pltpu.VMEM)] * len(outs),
         scratch_shapes=scratch,
         compiler_params=pltpu.CompilerParams(
             collective_id=ident, has_side_effects=True, vmem_limit_bytes=48 << 20
         ),
-        cost_estimate=pl.CostEstimate(flops=0, bytes_accessed=size, transcendentals=0),
+        cost_estimate=pl.CostEstimate(flops=0, bytes_accessed=60 * size, transcendentals=0),
     )(*arrays)
 
 
@@ -458,14 +458,17 @@
         functools.partial(ring_kernel, n, splits),
         "ring_total",
         arrays,
-        [v.shape for v in arrays],
+        [(v.shape, jnp.bfloat16) for v in arrays],
         [pltpu.VMEM((v.shape[0] // n * (n - 1), v.shape[1]), jnp.bfloat16) for v in arrays]
         + [pltpu.SemaphoreType.DMA((streams, 2 * n - 2))] * 2,
         ident,
     )
 
 
-def units_kernel(n, fan, x_ref, inner_ref, outer_ref, swap_send, swap_recv, own_sem, send_sem, recv_sem):
+def units_kernel(
+    n, fan, x_ref, part_ref, inner_ref, outer_ref, sum_ref, landed,
+    swap_send, swap_recv, own_sem, send_sem, recv_sem, part_send, part_recv,
+):
     s, me = lax.axis_index("seq"), lax.axis_index("fsdp")
     rows, width = x_ref.shape[0] // 3, x_ref.shape[1]
     cols = width // fan
@@ -511,6 +514,20 @@
         )
         copies[k, piece, step].start()
 
+    tokens = sum_ref.shape[0]
+    parts = []
+    for far in range(1, fan):
+        target = (me + far) % fan
+        one = pltpu.make_async_remote_copy(
+            src_ref=part_ref.at[pl.ds(target * tokens, tokens), :],
+            dst_ref=landed.at[far],
+            send_sem=part_send.at[far],
+            recv_sem=part_recv.at[far],
+            device_id={"fsdp": target},
+            device_id_type=MESH,
+        )
+        one.start()
+        parts.append(one)
     mine.wait()
     start(0, 0, 0)
     start(0, 1, 0)
@@ -524,20 +541,31 @@
                 copies[k, piece, step].wait_recv()
                 if step < n - 2:
                     start(k, piece, step + 1)
+    total = part_ref[pl.ds(pl.multiple_of(me * tokens, tokens), tokens), :].astype(jnp.float32)
+    for far in range(1, fan):
+        parts[far - 1].wait()
+        total = total + landed[far].astype(jnp.float32)
+    sum_ref[...] = total
     for one in copies.values():
         one.wait_send()
 
 
-def units_total(part, ident):
+def units_total(grads, part, ident):
     n, fan = lax.axis_size("seq"), lax.axis_size("fsdp")
-    rows, width = part.shape[0] // 3, part.shape[1]
+    rows, width = grads.shape[0] // 3, grads.shape[1]
+    tokens = part.shape[0] // fan
     sems = lambda *shape: pltpu.SemaphoreType.DMA(shape)
     return ring_call(
         functools.partial(units_kernel, n, fan),
         "units_total",
-        [part],
-        [(n * 2 * fan * rows, width // fan), (n * rows, width)],
-        [sems(fan, 2), sems(fan, 2), sems(3), sems(4, n - 1), sems(4, n - 1)],
+        [grads, part],
+        [
+            ((n * 2 * fan * rows, width // fan), jnp.bfloat16),
+            ((n * rows, width), jnp.bfloat16),
+            ((tokens, part.shape[1]), jnp.float32),
+        ],
+        [pltpu.VMEM((fan, tokens, part.shape[1]), jnp.bfloat16), sems(fan, 2), sems(fan, 2), sems(3)]
+        + [sems(4, n - 1), sems(4, n - 1), sems(fan), sems(fan)],
         ident,
     )
 
@@ -588,7 +616,8 @@
         copies.append(one)
     if fars:
         w_ref, halves = refs[count], refs[given + count : given + count + 2]
-        far_send, far_recv, far_own = sems[3:]
+        far_send, far_recv, far_own, stage = sems[3:]
+        rest = []
         units, cols = halves[0].shape[0], w_ref.shape[1]
         for i, far in enumerate(fars):
             target = (me + far) % fan
@@ -605,9 +634,15 @@
                         device_id_type=MESH,
                     )
                 else:
-                    one = pltpu.make_async_copy(src, dst, far_own.at[part])
+                    one = pltpu.make_async_copy(src, stage.at[part], far_own.at[0, part])
+                    rest.append((one, pltpu.make_async_copy(stage.at[part], dst, far_own.at[1, part])))
                 one.start()
-                copies.append(one)
+                if far:
+                    copies.append(one)
+        for inward, outward in rest:
+            inward.wait()
+            outward.start()
+            copies.append(outward)
     for one in copies:
         one.wait()
 
@@ -626,7 +661,10 @@
         operands.append(given)
         shape = (given.shape[0] // (2 * fan), given.shape[1] * fan)
         outs += [jax.ShapeDtypeStruct(shape, given.dtype)] * 2
-        scratch += [pltpu.SemaphoreType.DMA((len(fars), 2))] * 2 + [pltpu.SemaphoreType.DMA((2,))]
+        scratch += [pltpu.SemaphoreType.DMA((len(fars), 2))] * 2 + [
+            pltpu.SemaphoreType.DMA((2, 2)),
+            pltpu.VMEM((2, given.shape[0] // (2 * fan), given.shape[1]), given.dtype),
+        ]
         if halves is not None:
             operands += list(halves)
             alias = {count + 1: count, count + 2: count + 1}
@@ -732,7 +770,7 @@
     qkv_w = gather(self_qkv)
     small = jnp.concatenate([norm_self, norm_cross, norm_ff, rel_table.reshape(-1)])
     small = lax.all_gather(small, "fsdp", axis=0, tiled=False)
-    early = jnp.stack([self_out, cross_q, *jnp.split(cross_kv.reshape(-1, 2 * width), 2, axis=1)])
+    early = by_rows(jnp.stack([self_out, cross_q, *jnp.split(cross_kv.reshape(-1, 2 * width), 2, axis=1)]))
     small, early = lax.optimization_barrier((small, early))
     early = lax.all_gather(early, "fsdp", axis=1, tiled=True)
     both_ids = jnp.concatenate([decoder_ids.reshape(-1), encoder_ids.reshape(-1)])
@@ -740,8 +778,7 @@
     (both_ids,) = swap([jnp.broadcast_to(both_ids[None], (parts, 8, 128))], 13)
     home = change_home(layer_in.reshape(rows, width))
     inner_t = ff_in.T
-    qkv_w, small, both_ids, home, inner_t = lax.optimization_barrier((qkv_w, small, both_ids, home, inner_t))
-    qkv_w = qkv_w.reshape(width, parts, own * 3 * dh)
+    early = by_rows(early)
     mix_self = early[0].reshape(parts, own * dh, width)
     query_w = early[1].reshape(width, parts, own * dh)
     pairs_w = early[2:]
@@ -774,6 +811,11 @@
     ext = jnp.concatenate(
         [jnp.full((own, BQ), MASKED, f32), bias, jnp.zeros((own, BQ), f32)], axis=1
     )
+
+    qkv_w, home, inner_t, ext, self_rows, cross_rows, self_limits, cross_limits = lax.optimization_barrier(
+        (qkv_w, home, inner_t, ext, self_rows, cross_rows, self_limits, cross_limits)
+    )
+    qkv_w = qkv_w.reshape(width, parts, own * 3 * dh)
 
     stream = home.astype(f32)
     normed_first = norm_apply(stream, gain_first).astype(bf16)
@@ -852,7 +894,6 @@
         jnp.einsum("te,de->td", grad_pairs_tok[:, i * width : (i + 1) * width], pairs_w[i], preferred_element_type=f32)
         for i in range(2)
     )
-    grad_encoder = change_home(grad_encoder.astype(bf16)).astype(f32).reshape(seqs, enc_local, width)
     grad_from_second, grad_gain_second = norm_back(after_self, gain_second, grad_second_in)
     grad_upper = grad_middle + grad_from_second
     upper_low = grad_upper.astype(bf16)
@@ -867,8 +908,7 @@
         ],
         axis=1,
     )
-    if by_kernel:
-        grad_self_tok, grad_mid, part_units = lax.optimization_barrier((grad_self_tok, grad_mid, part_units))
+    grad_self_tok, grad_mid = lax.optimization_barrier((grad_self_tok, grad_mid))
     part_mid = scatter(grad_mid)
     (grad_self,) = swap([grad_self_tok], 11)
     grad_self = grad_self.reshape(length, own * dh)
@@ -876,15 +916,11 @@
     (grad_qkv_tok,) = swap([grad_qkv.reshape(parts, local, own * 3 * dh)], 10)
     grad_qkv_tok = flat(grad_qkv_tok)
     grad_qkv_w = jnp.einsum("td,te->de", normed_first, grad_qkv_tok, preferred_element_type=f32)
-    grad_last, part_mid = lax.optimization_barrier((grad_qkv_w.astype(bf16), part_mid))
-    part_last = scatter(grad_last)
     grad_first_in = jnp.einsum("te,de->td", grad_qkv_tok, qkv_w.reshape(width, -1), preferred_element_type=f32)
     grad_from_first, grad_gain_first = norm_back(stream, gain_first, grad_first_in)
-    grad_gain_first, outer_part = lax.optimization_barrier((grad_gain_first, outer_part))
-    outer_part = scatter(outer_part)
-    grad_layer_in = change_home((grad_upper + grad_from_first).astype(bf16)).astype(f32)
-    grad_layer_in = grad_layer_in.reshape(seqs, local, width)
-
+    grad_layer_in = (grad_upper + grad_from_first).astype(bf16)
+    if not by_kernel:
+        part_units = grad_units
     bucket_line = jnp.concatenate(
         [jnp.full((BQ,), -1, jnp.int32), near, jnp.full((BQ + bk,), -1, jnp.int32)]
     )
@@ -901,19 +937,31 @@
     small_grads = lax.dynamic_index_in_dim(small_grads, lax.axis_index("fsdp"), 0, False)
     small_size = small_grads.shape[0]
     small_grads = jnp.pad(small_grads, (0, parts * 1024 - small_size)).reshape(parts * 8, 128)
-    grad_layer_in, small_grads, part_last = lax.optimization_barrier((grad_layer_in, small_grads, part_last))
+    going_home = jnp.concatenate([grad_layer_in, grad_encoder.astype(bf16)])
+    going_home, small_grads, grad_qkv_w, part_units, part_mid = lax.optimization_barrier(
+        (going_home, small_grads, grad_qkv_w.astype(bf16), part_units, part_mid)
+    )
+    part_last = scatter(grad_qkv_w)
+    going_home = change_home(going_home)
     if by_kernel:
-        total_inner, total_outer = units_total(part_units, 0)
-        total_inner = jnp.transpose(total_inner.reshape(parts, fan, 2, units // parts, -1), (4, 2, 1, 0, 3))
+        total_inner, total_outer, outer_sum = units_total(part_units, outer_part, 0)
     else:
         grad_units = [lax.psum(g, "seq") for g in grad_units]
         total_inner = spread(jnp.transpose(jnp.stack(grad_units[:2]).reshape(2, units, fan, -1), (2, 0, 1, 3)))
-        total_inner, total_outer = jnp.transpose(total_inner, (3, 1, 0, 2)), grad_units[2]
-    total_inner = total_inner.astype(f32).reshape(-1, 2 * fan * units)
-    total_outer, part_last = lax.optimization_barrier((total_outer, part_last))
+        total_outer, outer_sum = grad_units[2], scatter(outer_part).astype(f32)
     total_mid, total_qkv, small_total = over_seq([part_mid, part_last, small_grads], (2, 2, 1), 1)
-    layer_out = (after_cross + outer_part.astype(f32)).astype(bf16)
+    layer_out = (after_cross + outer_sum).astype(bf16)
+    layer_out, total_inner, total_outer, total_mid, total_qkv, going_home = lax.optimization_barrier(
+        (layer_out, total_inner, total_outer, total_mid, total_qkv, going_home)
+    )
     layer_out = change_home(layer_out).reshape(seqs, local, width)
+    grad_layer_in = going_home[:rows].astype(f32).reshape(seqs, local, width)
+    grad_encoder = going_home[rows:].astype(f32).reshape(seqs, enc_local, width)
+    if by_kernel:
+        total_inner = jnp.transpose(total_inner.reshape(parts, fan, 2, units // parts, -1), (4, 2, 1, 0, 3))
+    else:
+        total_inner = jnp.transpose(total_inner, (3, 1, 0, 2))
+    total_inner = total_inner.reshape(-1, 2 * fan * units).astype(f32)
     total_outer, total_mid, total_qkv = (v.astype(f32) for v in (total_outer, total_mid, total_qkv))
     total_query, total_mix_cross = total_mid[:, :width], total_mid[:, 3 * width : 4 * width]
     total_pairs = total_mid[:, width : 3 * width].reshape(-1, heads, 2 * dh)

time: 723 us -> 682 us (0.943)
  waiting for transfers between devices: 116 us -> 79.3 us
  Pallas kernels: 350 us -> 373 us
  local copies, waits for them, and re-layouts: 75.4 us -> 64.4 us
    reduce_scatter x1, waiting for transfers between devices: 22 us -> 0.01 us  [shards(): lax.psum_scatter(grad_units.reshape(3 * units, width), 'seq', scatter_dim...]
    pallas_call x2, Pallas kernels: 133 us -> 146 us  [ring_call(): pl.pallas_call(body, name=name, out_shape=[jax.ShapeDtypeStruct(s, d) for...]
    pallas_call x9, Pallas kernels: 162 us -> 172 us  [swap(): pl.pallas_call(functools.partial(swap_kernel, n, fan, count, fars, not fa...]
    reduce_scatter x4 -> x3, waiting for transfers between devices: 53.9 us -> 45.5 us  [scatter(): return lax.psum_scatter(grad, 'fsdp', scatter_dimension=0, tiled=True)]
    ppermute x6 -> x5, starting transfers between devices: 23.9 us -> 19.3 us  [change_home(): return lax.ppermute(value, ('seq', 'fsdp'), pairs)]
    unnamed x171 -> x155, local copies, waits for them, and re-layouts: 43.3 us -> 39.2 us
  transfers between devices with their start and end apart: 16 -> 14, of which waited for: 8 -> 6; matrix products, arithmetic and copies ran while one was open for 19% -> 19% of each run, Pallas kernels for 38% -> 55%
where the time goes in v6:
time: 682 us; the launch traced here: 673 us
  Pallas kernels  373 us (55%)
  waiting for transfers between devices  79.3 us (12%)
  matrix products  73.7 us (11%)
  local copies, waits for them, and re-layouts  64.4 us (9%)
  other arithmetic  34.5 us (5%)
  starting transfers between devices  21.2 us (3%)
  between operations  15.2 us (2%)
  blocking collectives  12.1 us (2%)
    pallas_call x9, Pallas kernels, swap(): pl.pallas_call(functools.partial(swap_kernel, n, fan, count, fars, not fa...  172 us
    pallas_call x2, Pallas kernels, ring_call(): pl.pallas_call(body, name=name, out_shape=[jax.ShapeDtypeStruct(s, d) for...  146 us
    pallas_call x4, Pallas kernels, call(): pl.pallas_call(body, name=name, out_shape=[jax.ShapeDtypeStruct(s, d) for...  55 us
    reduce_scatter x3, waiting for transfers between devices, scatter(): return lax.psum_scatter(grad, 'fsdp', scatter_dimension=0, tiled=True)  45.5 us
    unnamed x155, local copies, waits for them, and re-layouts  39.2 us
    all_gather x4, waiting for transfers between devices, shards(): gather = lambda v: lax.all_gather(v, 'fsdp', axis=0, tiled=True)  27.7 us
    ppermute x5, starting transfers between devices, change_home(): return lax.ppermute(value, ('seq', 'fsdp'), pairs)  19.3 us
  transfers between devices with their start and end apart: 14, of which 6 were waited for; matrix products, arithmetic and copies ran while one was open for 19% of the time, Pallas kernels for 55%

profile of v6, /device:TPU:1, one launch (start us, length us, event | category | flops | bytes accessed | tf_op | source)
XLA Modules:
  0.0 673.2 jit_solution(15842927594121075629)
XLA Ops:
  9.6 6.1 all-gather.1
  19.5 4.7 collective-permute-start
  31.6 5.2 collective-permute-done.1
  37.4 5.0 swap.9
  47.2 5.2 fusion.61
  52.8 6.5 all-gather.8.cloned.1.call-done
  59.6 5.9 fusion.14.refs_0_
  70.6 24.9 %swap.10 = bf16[8,256,384]{2,1,0:T(8,128)(2,1)} custom-call(bf16[8,256,384]{2,1,0:T(8,128)(2,1)} %fusion.14.refs_0_), custom_call_target="tpu_custom_call" | custom-call | bytes 1572864 | tf_op jit(solution)/shard_map/swap/pallas_call | solution.py:671
  97.0 15.6 %self_forward.1 = (bf16[2048,128]{1,0:T(8,128)(2,1)S(1)}, f32[128,2048]{1,0:T(8,128)S(1)}, f32[2,2048]{1,0:T(2,128)S(1)}) custom-call(s32[2,8]{1,0:T(2,128)S(1)} %pad_add_fusion.1.lim_ref, s32[8,2048]{1,0:T(8,128)S(1)} %broadcast_in_dim.102.rows_ref, f32[2,1536]{1,0:T(2,128)S(1)} %maximum_maximum_fusion.ext_ref, bf16[2048,384]{1,0:T(8,128)(2,1)S(1)} %bitcast.224), custom_call_target="tpu_custom_call" | custom-call | bytes 1650752 | tf_op jit(solution)/shard_map/self_forward/pallas_call | solution.py:257
  115.7 17.5 %swap.11 = (bf16[8,256,128]{2,1,0:T(8,128)(2,1)}, bf16[704,1024]{1,0:T(8,128)(2,1)}, bf16[704,1024]{1,0:T(8,128)(2,1)}) custom-call(bf16[8,256,128]{2,1,0:T(8,128)(2,1)} %bitcast.235, bf16[5632,256]{1,0:T(8,128)(2,1)} %bitcast.237), custom_call_target="tpu_custom_call" | custom-call | bytes 524288 | tf_op jit(solution)/shard_map/swap/pallas_call | solution.py:671
  133.2 4.7 fusion.71
  150.7 31.4 %swap.12 = (bf16[8,256,128]{2,1,0:T(8,128)(2,1)}, bf16[8,64,256]{2,1,0:T(8,128)(2,1)}, bf16[704,1024]{1,0:T(8,128)(2,1)}, bf16[704,1024]{1,0:T(8,128)(2,1)}) custom-call(bf16[8,256,128]{2,1,0:T(8,128)(2,1)} %fusion.20.refs_0_, bf16[8,64,256]{2,1,0:T(8,128)(2,1)} %bitcast.273, ...), custom_call_target="tpu_custom_call", output_to_operand_aliasing={{2}: (3, {}), {3}: (4, {})} | custom-call | bytes 786432 | tf_op jit(solution)/shard_map/swap/pallas_call | solution.py:671
  184.1 9.2 %cross_forward.1 = (bf16[2048,128]{1,0:T(8,128)(2,1)S(1)}, f32[128,2048]{1,0:T(8,128)S(1)}, f32[2,2048]{1,0:T(2,128)S(1)}) custom-call(s32[2,8]{1,0:T(2,128)S(1)} %pad_add_fusion.2.lim_ref, s32[8,2048]{1,0:T(8,128)S(1)} %add_add_fusion.3.rows_ref, bf16[2048,128]{1,0:T(8,128)(2,1)S(1)} %bitcast.226, bf16[512,256]{1,0:T(8,128)(2,1)S(1)} %bitcast.231), custom_call_target="tpu_custom_call" | custom-call | bytes 852032 | tf_op jit(solution)/shard_map/cross_forward/pallas_call | solution.py:257
  195.1 11.3 %swap.13 = (bf16[8,256,128]{2,1,0:T(8,128)(2,1)}, bf16[704,1024]{1,0:T(8,128)(2,1)}, bf16[704,1024]{1,0:T(8,128)(2,1)}) custom-call(bf16[8,256,128]{2,1,0:T(8,128)(2,1)} %bitcast.233, bf16[5632,256]{1,0:T(8,128)(2,1)} %bitcast.239, bf16[704,1024]{1,0:T(8,128)(2,1)} %get-tuple-element.97.refs_2_, ...), custom_call_target="tpu_custom_call", output_to_operand_aliasing={{1}: (2, {}), {2}: (3, {})} | custom-call | bytes 524288 | tf_op jit(solution)/shard_map/swap/pallas_call | solution.py:671
  211.6 4.9 fusion.75
  216.5 21.2 %all-gather.16.cloned.1.call-done = bf16[1024,1024]{1,0:T(8,128)(2,1)} async-done(((bf16[256,1024]{1,0:T(8,128)(2,1)}), bf16[1024,1024]{1,0:T(8,128)(2,1)}) %all-gather.16.cloned.1.call-update) | async-done | bytes 2097168 | tf_op jit(solution)/shard_map/all_gather | solution.py:763
  241.7 4.7 multiply_convert_fusion
  264.1 18.6 %reduce-scatter.5.cloned.1.call-done = bf16[256,1024]{1,0:T(8,128)(2,1)} async-done(((bf16[1024,1024]{1,0:T(8,128)(2,1)}), bf16[256,1024]{1,0:T(8,128)(2,1)}) %reduce-scatter.5.cloned.1.call-update) | async-done | bytes 524304 | tf_op jit(solution)/shard_map/reduce_scatter | solution.py:734
  293.0 16.6 %swap.14 = bf16[8,256,128]{2,1,0:T(8,128)(2,1)} custom-call(bf16[8,256,128]{2,1,0:T(8,128)(2,1)} %fusion.21.refs_0_), custom_call_target="tpu_custom_call" | custom-call | bytes 524288 | tf_op jit(solution)/shard_map/swap/pallas_call | solution.py:671
  310.7 10.6 %cross_backward.1 = (bf16[2048,128]{1,0:T(8,128)(2,1)S(1)}, bf16[512,256]{1,0:T(8,128)(2,1)S(1)}) custom-call(s32[2,8]{1,0:T(2,128)S(1)} %pad_add_fusion.2.lim_ref, s32[8,2048]{1,0:T(8,128)S(1)} %add_add_fusion.3.rows_ref, bf16[2048,128]{1,0:T(8,128)(2,1)S(1)} %bitcast.227, bf16[512,256]{1,0:T(8,128)(2,1)S(1)} %bitcast.232, bf16[2048,128]{1,0:T(8,128)(2,1)S(1)} %bitcast.228, ...), custom_call_target="tpu_custom_call" | custom-call | bytes 2441280 | tf_op jit(solution)/shard_map/cross_backward/pallas_call | solution.py:257
  322.8 23.1 %swap.15 = (bf16[8,256,128]{2,1,0:T(8,128)(2,1)}, bf16[8,64,256]{2,1,0:T(8,128)(2,1)}) custom-call(bf16[8,256,128]{2,1,0:T(8,128)(2,1)} %bitcast.234, bf16[8,64,256]{2,1,0:T(8,128)(2,1)} %bitcast.236), custom_call_target="tpu_custom_call" | custom-call | bytes 786432 | tf_op jit(solution)/shard_map/swap/pallas_call | solution.py:671
  360.8 6.1 pad_maximum_fusion
  367.7 18.2 %swap.16 = bf16[8,256,128]{2,1,0:T(8,128)(2,1)} custom-call(bf16[8,256,128]{2,1,0:T(8,128)(2,1)} %fusion.22.refs_0_), custom_call_target="tpu_custom_call" | custom-call | bytes 524288 | tf_op jit(solution)/shard_map/swap/pallas_call | solution.py:671
  386.9 19.6 %self_backward.1 = (bf16[2048,384]{1,0:T(8,128)(2,1)S(1)}, f32[2,5,512]{2,1,0:T(8,128)S(1)}) custom-call(s32[2,8]{1,0:T(2,128)S(1)} %pad_add_fusion.1.lim_ref, s32[8,2048]{1,0:T(8,128)S(1)} %broadcast_in_dim.102.rows_ref, f32[2,1536]{1,0:T(2,128)S(1)} %maximum_maximum_fusion.ext_ref, bf16[2048,384]{1,0:T(8,128)(2,1)S(1)} %bitcast.225, ...), custom_call_target="tpu_custom_call" | custom-call | bytes 3240000 | tf_op jit(solution)/shard_map/self_backward/pallas_call | solution.py:257
  407.6 23.5 %swap.17 = bf16[8,256,384]{2,1,0:T(8,128)(2,1)} custom-call(bf16[8,256,384]{2,1,0:T(8,128)(2,1)} %bitcast.230), custom_call_target="tpu_custom_call" | custom-call | bytes 1572864 | tf_op jit(solution)/shard_map/swap/pallas_call | solution.py:671
  433.6 5.7 fusion.30
  439.3 6.0 psum.7
  456.3 25.7 %reduce-scatter.9.cloned.1.call-done.refs_0_ = bf16[256,5120]{1,0:T(8,128)(2,1)} async-done(((bf16[1024,5120]{1,0:T(8,128)(2,1)}), bf16[256,5120]{1,0:T(8,128)(2,1)}) %reduce-scatter.9.cloned.1.call-update) | async-done | bytes 2621456 | tf_op jit(solution)/shard_map/reduce_scatter | solution.py:734
  482.1 5.0 collective-permute-start.3
  487.1 61.2 %units_total.1 = (bf16[5632,256]{1,0:T(8,128)(2,1)}, bf16[704,1024]{1,0:T(8,128)(2,1)S(1)}, f32[256,1024]{1,0:T(8,128)S(1)}) custom-call(bf16[264,1024]{1,0:T(8,128)(2,1)S(1)} %copy-done.20, bf16[1024,1024]{1,0:T(8,128)(2,1)S(1)} %copy-done.6), custom_call_target="tpu_custom_call" | custom-call | bytes 158269440 | tf_op jit(solution)/shard_map/units_total/pallas_call | solution.py:440
  553.0 84.9 %ring_total.1 = (bf16[256,5120]{1,0:T(8,128)(2,1)S(1)}, bf16[256,3072]{1,0:T(8,128)(2,1)S(1)}, bf16[64,128]{1,0:T(8,128)(2,1)S(1)}) custom-call(bf16[256,5120]{1,0:T(8,128)(2,1)} %reduce-scatter.9.cloned.1.call-done.refs_0_, bf16[256,3072]{1,0:T(8,128)(2,1)S(1)} %copy-done.12, bf16[64,128]{1,0:T(8,128)(2,1)S(1)} %pad_bitcast_fusion.refs_2_), custom_call_target="tpu_custom_call" | custom-call | bytes 252641280 | tf_op jit(solution)/shard_map/ring_total/pallas_call | solution.py:440
  654.7 6.3 copy.123
  (286 shorter events, 142.8 us)
Async XLA Ops:
  7.2 204.5 %copy-start = (bf16[704,1024]{1,0:T(8,128)(2,1)S(1)}, bf16[704,1024]{1,0:T(8,128)(2,1)}, u32[]{:S(2)}) copy-start(bf16[704,1024]{1,0:T(8,128)(2,1)} %param.32) | copy-start | bytes 4325380
  7.2 8.5 %copy-start.49 = (bf16[256,16,128]{2,1,0:T(8,128)(2,1)S(1)}, bf16[256,16,128]{2,1,0:T(8,128)(2,1)}, u32[]{:S(2)}) copy-start(bf16[256,16,128]{2,1,0:T(8,128)(2,1)} %param.28) | copy-start | bytes 3145732
  7.2 52.1 %all-gather.8.cloned.1.call-start = ((), (), s32[]{:S(2)}) async-start(), calls=%async_computation.4 | async-start | bytes 7864320 | tf_op jit(solution)/shard_map/all_gather | solution.py:763
  7.9 125.3 %all-gather.10.cloned.1.call-start = ((), (), s32[]{:S(2)}) async-start(), calls=%async_computation.5 | async-start | bytes 10485760 | tf_op jit(solution)/shard_map/all_gather | solution.py:775
  18.4 5.8 copy-start.57
  18.4 7.8 %copy-start.54 = (s32[2048]{0:T(1024)S(1)}, s32[2048]{0:T(1024)}, u32[]{:S(2)}) copy-start(s32[2048]{0:T(1024)} %param.21) | copy-start | bytes 24580
  18.5 188.0 %all-gather.12.cloned.1.call-start = ((), (), s32[]{:S(2)}) async-start(), calls=%async_computation.6 | async-start | bytes 2621440 | tf_op jit(solution)/shard_map/all_gather | solution.py:763
  19.5 33.3 %collective-permute-start = (bf16[256,1024]{1,0:T(8,128)(2,1)S(1)}, bf16[256,1024]{1,0:T(8,128)(2,1)S(1)}, u32[]{:S(2)}, u32[]{:S(2)}) collective-permute-start(bf16[256,1024]{1,0:T(8,128)(2,1)S(1)} %bitcast.308), channel_id=1, source_target_pairs={{0,0},{1,16},{2,2},{3,18},{4,4},{5,20},{6,6},{7,22},{8,8},{9,24},{... | collective-permute-start | bytes 1572872 | tf_op jit(solution)/shard_map/ppermute | solution.py:712
  24.3 12.5 %collective-permute-start.1 = (s32[8,128]{1,0:T(8,128)S(1)}, s32[8,128]{1,0:T(8,128)S(1)}, u32[]{:S(2)}, u32[]{:S(2)}) collective-permute-start(s32[8,128]{1,0:T(8,128)S(1)} %pad_bitcast_fusion.1), channel_id=1, source_target_pairs={{0,0},{1,16},{2,2},{3,18},{4,4},{5,20},{6,6},{7,22},{8,8},{9,24},{... | collective-permute-start | bytes 12296 | tf_op jit(solution)/shard_map/ppermute | solution.py:712
  52.8 12.6 %copy-start.34 = (bf16[256,1024]{1,0:T(8,128)(2,1)}, bf16[256,1024]{1,0:T(8,128)(2,1)S(1)}, u32[]{:S(2)}) copy-start(bf16[256,1024]{1,0:T(8,128)(2,1)S(1)} %collective-permute-done) | copy-start | bytes 1572868
  59.5 6.0 copy-start.50
  59.6 6.0 copy-start.53
  65.5 146.1 %all-gather.14.cloned.1.call-start = ((), (), s32[]{:S(2)}) async-start(), calls=%async_computation.7 | async-start | bytes 2621440 | tf_op jit(solution)/shard_map/all_gather | solution.py:763
  66.4 47.0 %collective-permute-start.2 = (bf16[320,1024]{1,0:T(8,128)(2,1)}, bf16[320,1024]{1,0:T(8,128)(2,1)}, u32[]{:S(2)}, u32[]{:S(2)}) collective-permute-start(bf16[320,1024]{1,0:T(8,128)(2,1)} %pad_maximum_fusion.3), channel_id=1, source_target_pairs={{0,0},{1,16},{2,2},{3,18},{4,4},{5,20},{6,6},{7,22},{8,8},{9,24},{... | collective-permute-start | bytes 1966088 | tf_op jit(solution)/shard_map/ppermute | solution.py:712
  115.3 122.4 %all-gather.16.cloned.1.call-start = ((), (), s32[]{:S(2)}) async-start(), calls=%async_computation.8 | async-start | bytes 2621440 | tf_op jit(solution)/shard_map/all_gather | solution.py:763
  211.2 71.5 %reduce-scatter.5.cloned.1.call-start = ((), (), s32[]{:S(2)}) async-start(), calls=%async_computation.9 | async-start | bytes 2621440 | tf_op jit(solution)/shard_map/reduce_scatter | solution.py:734
  251.5 204.8 %reduce-scatter.7.cloned.1.call-start = ((), (), s32[]{:S(2)}) async-start(), calls=%async_computation.10 | async-start | bytes 4866048 | tf_op jit(solution)/shard_map/reduce_scatter | solution.py:872
  286.4 195.7 %reduce-scatter.9.cloned.1.call-start = ((), (), s32[]{:S(2)}) async-start(), calls=%async_computation.11 | async-start | bytes 13107200 | tf_op jit(solution)/shard_map/reduce_scatter | solution.py:734
  291.4 18.2 %copy-start.8 = (bf16[8,256,128]{2,1,0:T(8,128)(2,1)S(1)}, bf16[8,256,128]{2,1,0:T(8,128)(2,1)}, u32[]{:S(2)}) copy-start(bf16[8,256,128]{2,1,0:T(8,128)(2,1)} %get-tuple-element.94) | copy-start | bytes 1572868
  291.4 18.2 %copy-start.17 = (f32[128,2048]{1,0:T(8,128)S(1)}, f32[128,2048]{1,0:T(8,128)}, u32[]{:S(2)}) copy-start(f32[128,2048]{1,0:T(8,128)} %copy-done.16) | copy-start | bytes 3145732
  291.4 18.2 %copy-start.19 = (bf16[8,64,256]{2,1,0:T(8,128)(2,1)S(1)}, bf16[8,64,256]{2,1,0:T(8,128)(2,1)}, u32[]{:S(2)}) copy-start(bf16[8,64,256]{2,1,0:T(8,128)(2,1)} %get-tuple-element.95) | copy-start | bytes 786436
  346.9 11.7 %copy-start.47 = (bf16[8,8,8,256]{3,2,0,1:T(8,128)(2,1)}, bf16[8,8,8,256]{3,2,0,1:T(8,128)(2,1)S(1)}, u32[]{:S(2)}) copy-start(bf16[8,8,8,256]{3,2,0,1:T(8,128)(2,1)S(1)} %copy.135) | copy-start | bytes 786436
  366.9 19.0 %copy-start.3 = (bf16[8,256,384]{2,1,0:T(8,128)(2,1)S(1)}, bf16[8,256,384]{2,1,0:T(8,128)(2,1)}, u32[]{:S(2)}) copy-start(bf16[8,256,384]{2,1,0:T(8,128)(2,1)} %swap.10) | copy-start | bytes 4718596
  366.9 184.7 %reduce-scatter.11.cloned.1.call-start = ((), (), s32[]{:S(2)}) async-start(), calls=%async_computation.12 | async-start | bytes 7864320 | tf_op jit(solution)/shard_map/reduce_scatter | solution.py:734
  433.6 11.8 %copy-start.48 = (bf16[8,8,8,256]{3,2,0,1:T(8,128)(2,1)S(1)}, bf16[8,8,8,256]{3,2,0,1:T(8,128)(2,1)}, u32[]{:S(2)}) copy-start(bf16[8,8,8,256]{3,2,0,1:T(8,128)(2,1)} %copy-done.47) | copy-start | bytes 786436
  456.3 30.7 %copy-start.6 = (bf16[1024,1024]{1,0:T(8,128)(2,1)S(1)}, bf16[1024,1024]{1,0:T(8,128)(2,1)}, u32[]{:S(2)}) copy-start(bf16[1024,1024]{1,0:T(8,128)(2,1)} %convolution_convert_fusion.5.part_ref) | copy-start | bytes 6291460
  456.3 30.7 %copy-start.20 = (bf16[264,1024]{1,0:T(8,128)(2,1)S(1)}, bf16[264,1024]{1,0:T(8,128)(2,1)}, u32[]{:S(2)}) copy-start(bf16[264,1024]{1,0:T(8,128)(2,1)} %reduce-scatter.7.cloned.1.call-done.x_ref) | copy-start | bytes 1622020
  482.1 67.3 %copy-start.27 = (f32[256,1024]{1,0:T(8,128)S(1)}, f32[256,1024]{1,0:T(8,128)}, u32[]{:S(2)}) copy-start(f32[256,1024]{1,0:T(8,128)} %copy-done.25) | copy-start | bytes 3145732
  482.1 157.0 %collective-permute-start.3 = (bf16[320,1024]{1,0:T(8,128)(2,1)}, bf16[320,1024]{1,0:T(8,128)(2,1)S(1)}, u32[]{:S(2)}, u32[]{:S(2)}) collective-permute-start(bf16[320,1024]{1,0:T(8,128)(2,1)} %pad_maximum_fusion.4), channel_id=1, source_target_pairs={{0,0},{1,16},{2,2},{3,18},{4,4},{5,20},{6,6},{7,22},{8,8},{9,24},{... | collective-permute-start | bytes 1966088 | tf_op jit(solution)/shard_map/ppermute | solution.py:712
  639.0 9.3 %copy-start.4 = (bf16[256,5120]{1,0:T(8,128)(2,1)}, bf16[256,5120]{1,0:T(8,128)(2,1)S(1)}, u32[]{:S(2)}) copy-start(bf16[256,5120]{1,0:T(8,128)(2,1)S(1)} %get-tuple-element.135) | copy-start | bytes 7864324
  641.0 24.6 %collective-permute-start.4 = (bf16[256,1024]{1,0:T(8,128)(2,1)}, bf16[256,1024]{1,0:T(8,128)(2,1)S(1)}, u32[]{:S(2)}, u32[]{:S(2)}) collective-permute-start(bf16[256,1024]{1,0:T(8,128)(2,1)} %add_convert_fusion.1), channel_id=1, source_target_pairs={{0,0},{1,16},{2,2},{3,18},{4,4},{5,20},{6,6},{7,22},{8,8},{9,24},{... | collective-permute-start | bytes 1572872 | tf_op jit(solution)/shard_map/ppermute | solution.py:712
  654.7 6.3 copy-start.15
  (51 other events, 114.2 us)
Sparse Core Ops, SparseCore 0:
  9.6 49.7 all-gather.7
  61.5 58.2 all-gather.9
  121.4 22.5 all-gather.11
  146.0 37.2 all-gather.13
  211.3 26.2 all-gather.15
  251.6 31.0 reduce-scatter.4
  287.3 106.3 reduce-scatter.6
  396.3 85.6 reduce-scatter.8
  484.6 66.9 reduce-scatter.10

commit v7 on v6

--- a/solution.py
+++ b/solution.py
@@ -447,7 +447,7 @@
         compiler_params=pltpu.CompilerParams(
             collective_id=ident, has_side_effects=True, vmem_limit_bytes=48 << 20
         ),
-        cost_estimate=pl.CostEstimate(flops=0, bytes_accessed=60 * size, transcendentals=0),
+        cost_estimate=pl.CostEstimate(flops=0, bytes_accessed=size, transcendentals=0),
     )(*arrays)
 
 
@@ -770,19 +770,15 @@
     qkv_w = gather(self_qkv)
     small = jnp.concatenate([norm_self, norm_cross, norm_ff, rel_table.reshape(-1)])
     small = lax.all_gather(small, "fsdp", axis=0, tiled=False)
-    early = by_rows(jnp.stack([self_out, cross_q, *jnp.split(cross_kv.reshape(-1, 2 * width), 2, axis=1)]))
-    small, early = lax.optimization_barrier((small, early))
-    early = lax.all_gather(early, "fsdp", axis=1, tiled=True)
+    small, self_out = lax.optimization_barrier((small, self_out))
+    mix_self = gather(self_out).reshape(parts, own * dh, width)
     both_ids = jnp.concatenate([decoder_ids.reshape(-1), encoder_ids.reshape(-1)])
     both_ids = change_home(jnp.pad(both_ids, (0, 1024 - local - enc_local)).reshape(8, 128))
     (both_ids,) = swap([jnp.broadcast_to(both_ids[None], (parts, 8, 128))], 13)
+    both_ids, cross_q = lax.optimization_barrier((both_ids, cross_q))
+    query_w = gather(cross_q)
     home = change_home(layer_in.reshape(rows, width))
     inner_t = ff_in.T
-    early = by_rows(early)
-    mix_self = early[0].reshape(parts, own * dh, width)
-    query_w = early[1].reshape(width, parts, own * dh)
-    pairs_w = early[2:]
-
     gain_first, gain_second, gain_third = (
         small[:, i * part : (i + 1) * part].reshape(width).astype(f32) for i in range(3)
     )
@@ -812,33 +808,36 @@
         [jnp.full((own, BQ), MASKED, f32), bias, jnp.zeros((own, BQ), f32)], axis=1
     )
 
-    qkv_w, home, inner_t, ext, self_rows, cross_rows, self_limits, cross_limits = lax.optimization_barrier(
-        (qkv_w, home, inner_t, ext, self_rows, cross_rows, self_limits, cross_limits)
+    pairs_t = jnp.transpose(cross_kv, (1, 2, 0))
+    qkv_w, home, inner_t, pairs_t, ext, self_rows, cross_rows, self_limits, cross_limits = lax.optimization_barrier(
+        (qkv_w, home, inner_t, pairs_t, ext, self_rows, cross_rows, self_limits, cross_limits)
     )
     qkv_w = qkv_w.reshape(width, parts, own * 3 * dh)
 
     stream = home.astype(f32)
     normed_first = norm_apply(stream, gain_first).astype(bf16)
     qkv_tok = jnp.einsum("td,dge->gte", normed_first, qkv_w, preferred_element_type=f32).astype(bf16)
-    qkv_tok, cross_out, cotangent, encoder = lax.optimization_barrier((qkv_tok, cross_out, cotangent, encoder))
-    mix_cross = gather(cross_out).reshape(parts, own * dh, width)
+    qkv_tok, pairs_t, cotangent, encoder = lax.optimization_barrier((qkv_tok, pairs_t, cotangent, encoder))
+    pairs_t = lax.all_gather(pairs_t, "fsdp", axis=2, tiled=True).reshape(parts, own * 2 * dh, width)
     others = change_home(jnp.concatenate([cotangent.reshape(rows, width), encoder.reshape(-1, width)]))
     grad_low, enc_flat = others[:rows], others[rows:]
     (qkv,) = swap([qkv_tok], 10)
+    qkv, cross_out, grad_low = lax.optimization_barrier((qkv, cross_out, grad_low))
+    if rows == cross_out.shape[0]:
+        mix_cross, grad_group = lax.all_gather(jnp.stack([cross_out, grad_low]), "fsdp", axis=1, tiled=True)
+    else:
+        mix_cross, grad_group = gather(cross_out), gather(grad_low)
+    mix_cross = mix_cross.reshape(parts, own * dh, width)
     qkv = qkv.reshape(length, own * 3 * dh)
     out_self, self_t, self_lse = self_forward(self_limits, self_rows, ext, qkv)
-    out_self, grad_low = lax.optimization_barrier((out_self, grad_low))
-    grad_group = gather(grad_low)
     by_kernel = (width // fan) % 128 == 0
     fars = [tuple(far for far in range(fan) if (far + 2) % 3 == i) if by_kernel else () for i in range(3)]
     self_tok, *halves = swap([out_self.reshape(parts, local, own * dh)], 14, fars[0], inner_t)
     after_self = stream + jnp.einsum("gtc,gcd->td", self_tok, mix_self, preferred_element_type=f32)
     normed_second = norm_apply(after_self, gain_second).astype(bf16)
-    query_tok = jnp.einsum("td,dgc->gtc", normed_second, query_w, preferred_element_type=f32).astype(bf16)
-    pairs_tok = jnp.einsum(
-        "td,sdge->sgte", enc_flat, pairs_w.reshape(2, width, parts // 2, -1), preferred_element_type=f32
-    )
-    pairs_tok = pairs_tok.astype(bf16).reshape(parts, enc_local, -1)
+    query_tok = jnp.dot(normed_second, query_w, preferred_element_type=f32).astype(bf16)
+    query_tok = jnp.transpose(query_tok.reshape(rows, parts, own * dh), (1, 0, 2))
+    pairs_tok = jnp.einsum("td,ged->gte", enc_flat, pairs_t, preferred_element_type=f32).astype(bf16)
     query_cross, pairs, *halves = swap([query_tok, pairs_tok], 15, fars[1], inner_t, halves)
     query_cross, pairs = query_cross.reshape(length, own * dh), pairs.reshape(keys, own * 2 * dh)
     out_cross, cross_t, cross_lse = cross_forward(cross_limits, cross_rows, query_cross, pairs)
@@ -888,12 +887,9 @@
     )
     grad_query_tok, grad_pairs_tok = flat(grad_query_tok), flat(grad_pairs_tok)
     grad_query_w = jnp.einsum("td,te->de", normed_second, grad_query_tok, preferred_element_type=f32)
-    grad_second_in = jnp.einsum("te,de->td", grad_query_tok, query_w.reshape(width, -1), preferred_element_type=f32)
+    grad_second_in = jnp.einsum("te,de->td", grad_query_tok, query_w, preferred_element_type=f32)
     grad_pairs_w = jnp.einsum("td,te->de", enc_flat, grad_pairs_tok, preferred_element_type=f32)
-    grad_encoder = sum(
-        jnp.einsum("te,de->td", grad_pairs_tok[:, i * width : (i + 1) * width], pairs_w[i], preferred_element_type=f32)
-        for i in range(2)
-    )
+    grad_encoder = jnp.dot(grad_pairs_tok, pairs_t.reshape(-1, width), preferred_element_type=f32)
     grad_from_second, grad_gain_second = norm_back(after_self, gain_second, grad_second_in)
     grad_upper = grad_middle + grad_from_second
     upper_low = grad_upper.astype(bf16)
@@ -938,8 +934,8 @@
     small_size = small_grads.shape[0]
     small_grads = jnp.pad(small_grads, (0, parts * 1024 - small_size)).reshape(parts * 8, 128)
     going_home = jnp.concatenate([grad_layer_in, grad_encoder.astype(bf16)])
-    going_home, small_grads, grad_qkv_w, part_units, part_mid = lax.optimization_barrier(
-        (going_home, small_grads, grad_qkv_w.astype(bf16), part_units, part_mid)
+    going_home, small_grads, grad_qkv_w, part_units = lax.optimization_barrier(
+        (going_home, small_grads, grad_qkv_w.astype(bf16), part_units)
     )
     part_last = scatter(grad_qkv_w)
     going_home = change_home(going_home)

time: 682 us -> 712 us (1.044)
  Pallas kernels: 373 us -> 383 us
  waiting for transfers between devices: 79.3 us -> 88.3 us
    unnamed x155 -> x210, local copies, waits for them, and re-layouts: 39.2 us -> 37.5 us
  transfers between devices with their start and end apart: 14 -> 15, of which waited for: 6 -> 5; matrix products, arithmetic and copies ran while one was open for 19% -> 16% of each run, Pallas kernels for 55% -> 54%
where the time goes in v7:
time: 712 us; the launch traced here: 703 us
  Pallas kernels  383 us (54%)
  waiting for transfers between devices  88.3 us (12%)
  matrix products  73.2 us (10%)
  local copies, waits for them, and re-layouts  66.9 us (9%)
  other arithmetic  39.6 us (6%)
  starting transfers between devices  24.9 us (3%)
  between operations  15.8 us (2%)
  blocking collectives  12 us (2%)
    pallas_call x9, Pallas kernels, swap(): pl.pallas_call(functools.partial(swap_kernel, n, fan, count, fars, not fa...  178 us
    pallas_call x2, Pallas kernels, ring_call(): pl.pallas_call(body, name=name, out_shape=[jax.ShapeDtypeStruct(s, d) for...  143 us
    pallas_call x4, Pallas kernels, call(): pl.pallas_call(body, name=name, out_shape=[jax.ShapeDtypeStruct(s, d) for...  61.5 us
    reduce_scatter x3, waiting for transfers between devices, scatter(): return lax.psum_scatter(grad, 'fsdp', scatter_dimension=0, tiled=True)  47.8 us
    unnamed x210, local copies, waits for them, and re-layouts  37.5 us
    all_gather x4, waiting for transfers between devices, shards(): gather = lambda v: lax.all_gather(v, 'fsdp', axis=0, tiled=True)  31.8 us
    ppermute x5, starting transfers between devices, change_home(): return lax.ppermute(value, ('seq', 'fsdp'), pairs)  22.9 us
  transfers between devices with their start and end apart: 15, of which 5 were waited for; matrix products, arithmetic and copies ran while one was open for 16% of the time, Pallas kernels for 54%

profile of v7, /device:TPU:1, one launch (start us, length us, event | category | flops | bytes accessed | tf_op | source)
XLA Modules:
  0.0 703.4 jit_solution(1323744719209412458)
XLA Ops:
  9.6 6.1 all-gather.1
  15.8 4.7 collective-permute-start.1
  28.4 5.1 swap.9
  38.4 5.2 fusion.55
  44.1 15.3 %all-gather.9.cloned.1.call-done = bf16[1024,16,192]{0,2,1:T(8,128)(2,1)} async-done(((bf16[256,16,192]{0,2,1:T(8,128)(2,1)}), bf16[1024,16,192]{0,2,1:T(8,128)(2,1)}) %all-gather.9.cloned.1.call-update) | async-done | bytes 6291472 | tf_op jit(solution)/shard_map/all_gather | solution.py:763
  60.2 5.9 fusion.13.refs_0_
  71.2 24.9 %swap.10 = bf16[8,256,384]{2,1,0:T(8,128)(2,1)} custom-call(bf16[8,256,384]{2,1,0:T(8,128)(2,1)} %fusion.13.refs_0_), custom_call_target="tpu_custom_call" | custom-call | bytes 1572864 | tf_op jit(solution)/shard_map/swap/pallas_call | solution.py:671
  101.2 18.3 %self_forward.1 = (bf16[2048,128]{1,0:T(8,128)(2,1)S(1)}, f32[128,2048]{1,0:T(8,128)S(1)}, f32[2,2048]{1,0:T(2,128)S(1)}) custom-call(s32[2,8]{1,0:T(2,128)S(1)} %pad_add_fusion.1.lim_ref, s32[8,2048]{1,0:T(8,128)S(1)} %broadcast_in_dim.102.rows_ref, f32[2,1536]{1,0:T(2,128)S(1)} %maximum_maximum_fusion.ext_ref, bf16[2048,384]{1,0:T(8,128)(2,1)S(1)} %bitcast.205), custom_call_target="tpu_custom_call" | custom-call | bytes 1650752 | tf_op jit(solution)/shard_map/self_forward/pallas_call | solution.py:257
  121.9 26.0 %swap.11 = (bf16[8,256,128]{2,1,0:T(8,128)(2,1)}, bf16[704,1024]{1,0:T(8,128)(2,1)}, bf16[704,1024]{1,0:T(8,128)(2,1)}) custom-call(bf16[8,256,128]{2,1,0:T(8,128)(2,1)} %bitcast.216, bf16[5632,256]{1,0:T(8,128)(2,1)} %bitcast.218), custom_call_target="tpu_custom_call" | custom-call | bytes 524288 | tf_op jit(solution)/shard_map/swap/pallas_call | solution.py:671
  159.1 6.7 copy.104
  170.1 30.4 %swap.12 = (bf16[8,256,128]{2,1,0:T(8,128)(2,1)}, bf16[8,64,256]{2,1,0:T(8,128)(2,1)}, bf16[704,1024]{1,0:T(8,128)(2,1)}, bf16[704,1024]{1,0:T(8,128)(2,1)}) custom-call(bf16[8,256,128]{2,1,0:T(8,128)(2,1)} %bitcast.241, bf16[8,64,256]{2,1,0:T(8,128)(2,1)} %fusion.21.refs_1_, ...), custom_call_target="tpu_custom_call", output_to_operand_aliasing={{2}: (3, {}), {3}: (4, {})} | custom-call | bytes 786432 | tf_op jit(solution)/shard_map/swap/pallas_call | solution.py:671
  202.5 9.9 %cross_forward.1 = (bf16[2048,128]{1,0:T(8,128)(2,1)S(1)}, f32[128,2048]{1,0:T(8,128)S(1)}, f32[2,2048]{1,0:T(2,128)S(1)}) custom-call(s32[2,8]{1,0:T(2,128)S(1)} %pad_add_fusion.2.lim_ref, s32[8,2048]{1,0:T(8,128)S(1)} %add_add_fusion.3.rows_ref, bf16[2048,128]{1,0:T(8,128)(2,1)S(1)} %bitcast.207, bf16[512,256]{1,0:T(8,128)(2,1)S(1)} %bitcast.212), custom_call_target="tpu_custom_call" | custom-call | bytes 852032 | tf_op jit(solution)/shard_map/cross_forward/pallas_call | solution.py:257
  214.2 12.1 %swap.13 = (bf16[8,256,128]{2,1,0:T(8,128)(2,1)}, bf16[704,1024]{1,0:T(8,128)(2,1)}, bf16[704,1024]{1,0:T(8,128)(2,1)}) custom-call(bf16[8,256,128]{2,1,0:T(8,128)(2,1)} %bitcast.214, bf16[5632,256]{1,0:T(8,128)(2,1)} %bitcast.220, bf16[704,1024]{1,0:T(8,128)(2,1)} %get-tuple-element.104.refs_2_, ...), custom_call_target="tpu_custom_call", output_to_operand_aliasing={{1}: (2, {}), {2}: (3, {})} | custom-call | bytes 524288 | tf_op jit(solution)/shard_map/swap/pallas_call | solution.py:671
  231.9 4.9 fusion.11
  236.7 16.4 %all-gather.19.cloned.1.call-done = bf16[1024,1024]{1,0:T(8,128)(2,1)} async-done(((bf16[256,1024]{1,0:T(8,128)(2,1)}), bf16[1024,1024]{1,0:T(8,128)(2,1)}) %all-gather.19.cloned.1.call-update) | async-done | bytes 2097168 | tf_op jit(solution)/shard_map/all_gather | solution.py:763
  280.0 18.2 %reduce-scatter.5.cloned.1.call-done = bf16[256,1024]{1,0:T(8,128)(2,1)} async-done(((bf16[1024,1024]{1,0:T(8,128)(2,1)}), bf16[256,1024]{1,0:T(8,128)(2,1)}) %reduce-scatter.5.cloned.1.call-update) | async-done | bytes 524304 | tf_op jit(solution)/shard_map/reduce_scatter | solution.py:734
  309.1 17.5 %swap.14 = bf16[8,256,128]{2,1,0:T(8,128)(2,1)} custom-call(bf16[8,256,128]{2,1,0:T(8,128)(2,1)} %fusion.19.refs_0_), custom_call_target="tpu_custom_call" | custom-call | bytes 524288 | tf_op jit(solution)/shard_map/swap/pallas_call | solution.py:671
  327.7 11.2 %cross_backward.1 = (bf16[2048,128]{1,0:T(8,128)(2,1)S(1)}, bf16[512,256]{1,0:T(8,128)(2,1)S(1)}) custom-call(s32[2,8]{1,0:T(2,128)S(1)} %pad_add_fusion.2.lim_ref, s32[8,2048]{1,0:T(8,128)S(1)} %copy-done.22, bf16[2048,128]{1,0:T(8,128)(2,1)S(1)} %bitcast.208, bf16[512,256]{1,0:T(8,128)(2,1)S(1)} %bitcast.213, bf16[2048,128]{1,0:T(8,128)(2,1)S(1)} %bitcast.209, ...), custom_call_target="tpu_custom_call" | custom-call | bytes 2441280 | tf_op jit(solution)/shard_map/cross_backward/pallas_call | solution.py:257
  340.4 21.2 %swap.15 = (bf16[8,256,128]{2,1,0:T(8,128)(2,1)}, bf16[8,64,256]{2,1,0:T(8,128)(2,1)}) custom-call(bf16[8,256,128]{2,1,0:T(8,128)(2,1)} %bitcast.215, bf16[8,64,256]{2,1,0:T(8,128)(2,1)} %bitcast.217), custom_call_target="tpu_custom_call" | custom-call | bytes 786432 | tf_op jit(solution)/shard_map/swap/pallas_call | solution.py:671
  375.0 6.2 pad_maximum_fusion
  382.7 17.5 %swap.16 = bf16[8,256,128]{2,1,0:T(8,128)(2,1)} custom-call(bf16[8,256,128]{2,1,0:T(8,128)(2,1)} %fusion.20.refs_0_), custom_call_target="tpu_custom_call" | custom-call | bytes 524288 | tf_op jit(solution)/shard_map/swap/pallas_call | solution.py:671
  401.3 22.1 %self_backward.1 = (bf16[2048,384]{1,0:T(8,128)(2,1)S(1)}, f32[2,5,512]{2,1,0:T(8,128)S(1)}) custom-call(s32[2,8]{1,0:T(2,128)S(1)} %copy-done.33, s32[8,2048]{1,0:T(8,128)S(1)} %copy-done.20, f32[2,1536]{1,0:T(2,128)S(1)} %maximum_maximum_fusion.ext_ref, bf16[2048,384]{1,0:T(8,128)(2,1)S(1)} %bitcast.206, bf16[2048,128]{1,0:T(8,128)(2,1)S(1)} %bitcast.210, ...), custom_call_target="tpu_custom_call" | custom-call | bytes 3240000 | tf_op jit(solution)/shard_map/self_backward/pallas_call | solution.py:257
  424.5 23.7 %swap.17 = bf16[8,256,384]{2,1,0:T(8,128)(2,1)} custom-call(bf16[8,256,384]{2,1,0:T(8,128)(2,1)} %bitcast.211), custom_call_target="tpu_custom_call" | custom-call | bytes 1572864 | tf_op jit(solution)/shard_map/swap/pallas_call | solution.py:671
  450.1 5.8 fusion.27
  456.5 5.9 psum.7
  473.2 6.4 collective-permute-start.3
  480.6 58.6 %units_total.1 = (bf16[5632,256]{1,0:T(8,128)(2,1)}, bf16[704,1024]{1,0:T(8,128)(2,1)S(1)}, f32[256,1024]{1,0:T(8,128)S(1)}) custom-call(bf16[264,1024]{1,0:T(8,128)(2,1)S(1)} %copy-done.23, bf16[1024,1024]{1,0:T(8,128)(2,1)S(1)} %copy-done.4), custom_call_target="tpu_custom_call" | custom-call | bytes 2637824 | tf_op jit(solution)/shard_map/units_total/pallas_call | solution.py:440
  540.5 29.6 %reduce-scatter.11.cloned.1.call-done.refs_1_ = bf16[256,3072]{1,0:T(8,128)(2,1)} async-done(((bf16[1024,3072]{1,0:T(8,128)(2,1)}), bf16[256,3072]{1,0:T(8,128)(2,1)}) %reduce-scatter.11.cloned.1.call-update) | async-done | bytes 1572880 | tf_op jit(solution)/shard_map/reduce_scatter | solution.py:734
  571.6 84.1 %ring_total.1 = (bf16[256,5120]{1,0:T(8,128)(2,1)S(1)}, bf16[256,3072]{1,0:T(8,128)(2,1)S(1)}, bf16[64,128]{1,0:T(8,128)(2,1)S(1)}) custom-call(bf16[256,5120]{1,0:T(8,128)(2,1)} %reduce-scatter.9.cloned.1.call-done.refs_0_, bf16[256,3072]{1,0:T(8,128)(2,1)S(1)} %copy-done.10, bf16[64,128]{1,0:T(8,128)(2,1)S(1)} %pad_bitcast_fusion.refs_2_), custom_call_target="tpu_custom_call" | custom-call | bytes 4210688 | tf_op jit(solution)/shard_map/ring_total/pallas_call | solution.py:440
  662.9 6.2 copy.121
  677.3 5.7 collective-permute-start.4
  687.6 7.9 %collective-permute-done.4 = bf16[256,1024]{1,0:T(8,128)(2,1)S(1)} collective-permute-done((bf16[256,1024]{1,0:T(8,128)(2,1)S(1)}, bf16[256,1024]{1,0:T(8,128)(2,1)S(1)}, u32[]{:S(2)}, u32[]{:S(2)}) %collective-permute-start.4) | collective-permute-done | bytes 524320 | tf_op jit(solution)/shard_map/ppermute | solution.py:712
  (342 shorter events, 147.9 us)
Async XLA Ops:
  7.2 224.7 %copy-start = (bf16[704,1024]{1,0:T(8,128)(2,1)S(1)}, bf16[704,1024]{1,0:T(8,128)(2,1)}, u32[]{:S(2)}) copy-start(bf16[704,1024]{1,0:T(8,128)(2,1)} %param.32) | copy-start | bytes 4325380
  7.2 52.1 %all-gather.9.cloned.1.call-start = ((), (), s32[]{:S(2)}) async-start(), calls=%async_computation.4 | async-start | bytes 7864320 | tf_op jit(solution)/shard_map/all_gather | solution.py:763
  8.0 139.9 %all-gather.11.cloned.1.call-start = ((), (), s32[]{:S(2)}) async-start(), calls=%async_computation.5 | async-start | bytes 2621440 | tf_op jit(solution)/shard_map/all_gather | solution.py:763
  15.7 135.7 %all-gather.13.cloned.1.call-start = ((), (), s32[]{:S(2)}) async-start(), calls=%async_computation.6 | async-start | bytes 2621440 | tf_op jit(solution)/shard_map/all_gather | solution.py:763
  15.8 12.0 %collective-permute-start.1 = (s32[8,128]{1,0:T(8,128)S(1)}, s32[8,128]{1,0:T(8,128)S(1)}, u32[]{:S(2)}, u32[]{:S(2)}) collective-permute-start(s32[8,128]{1,0:T(8,128)S(1)} %pad_bitcast_fusion.1), channel_id=1, source_target_pairs={{0,0},{1,16},{2,2},{3,18},{4,4},{5,20},{6,6},{7,22},{8,8},{9,24},{... | collective-permute-start | bytes 12296 | tf_op jit(solution)/shard_map/ppermute | solution.py:712
  20.5 23.5 %collective-permute-start = (bf16[256,1024]{1,0:T(8,128)(2,1)S(1)}, bf16[256,1024]{1,0:T(8,128)(2,1)S(1)}, u32[]{:S(2)}, u32[]{:S(2)}) collective-permute-start(bf16[256,1024]{1,0:T(8,128)(2,1)S(1)} %bitcast.288), channel_id=1, source_target_pairs={{0,0},{1,16},{2,2},{3,18},{4,4},{5,20},{6,6},{7,22},{8,8},{9,24},{... | collective-permute-start | bytes 1572872 | tf_op jit(solution)/shard_map/ppermute | solution.py:712
  27.8 38.3 %copy-start.59 = (f32[1,2,4,128]{3,1,2,0:T(2,128)}, f32[1,2,4,128]{3,1,2,0:T(2,128)S(1)}, u32[]{:S(2)}) copy-start(f32[1,2,4,128]{3,1,2,0:T(2,128)S(1)} %copy.136) | copy-start | bytes 12292
  33.6 125.5 %all-gather.15.cloned.1.call-start = ((), (), s32[]{:S(2)}) async-start(), calls=%async_computation.7 | async-start | bytes 5242880 | tf_op jit(solution)/shard_map/all_gather | solution.py:821
  43.9 57.3 %copy-start.32 = (s32[2,8]{1,0:T(2,128)}, s32[2,8]{1,0:T(2,128)S(1)}, u32[]{:S(2)}) copy-start(s32[2,8]{1,0:T(2,128)S(1)} %pad_add_fusion.1.lim_ref) | copy-start | bytes 196
  44.1 156.5 %copy-start.21 = (s32[8,2048]{1,0:T(8,128)}, s32[8,2048]{1,0:T(8,128)S(1)}, u32[]{:S(2)}) copy-start(s32[8,2048]{1,0:T(8,128)S(1)} %add_add_fusion.3.rows_ref) | copy-start | bytes 196612
  44.1 22.0 %copy-start.45 = (bf16[256,1024]{1,0:T(8,128)(2,1)}, bf16[256,1024]{1,0:T(8,128)(2,1)S(1)}, u32[]{:S(2)}) copy-start(bf16[256,1024]{1,0:T(8,128)(2,1)S(1)} %collective-permute-done) | copy-start | bytes 1572868
  59.4 41.8 %copy-start.19 = (s32[8,2048]{1,0:T(8,128)}, s32[8,2048]{1,0:T(8,128)S(1)}, u32[]{:S(2)}) copy-start(s32[8,2048]{1,0:T(8,128)S(1)} %broadcast_in_dim.102.rows_ref) | copy-start | bytes 196612
  66.1 160.2 %all-gather.17.cloned.1.call-start = ((), (), s32[]{:S(2)}) async-start(), calls=%async_computation.8 | async-start | bytes 5242880 | tf_op jit(solution)/shard_map/all_gather | solution.py:827
  67.0 29.1 %collective-permute-start.2 = (bf16[320,1024]{1,0:T(8,128)(2,1)}, bf16[320,1024]{1,0:T(8,128)(2,1)}, u32[]{:S(2)}, u32[]{:S(2)}) collective-permute-start(bf16[320,1024]{1,0:T(8,128)(2,1)} %pad_maximum_fusion.3), channel_id=1, source_target_pairs={{0,0},{1,16},{2,2},{3,18},{4,4},{5,20},{6,6},{7,22},{8,8},{9,24},{... | collective-permute-start | bytes 1966088 | tf_op jit(solution)/shard_map/ppermute | solution.py:712
  100.3 152.9 %all-gather.19.cloned.1.call-start = ((), (), s32[]{:S(2)}) async-start(), calls=%async_computation.9 | async-start | bytes 2621440 | tf_op jit(solution)/shard_map/all_gather | solution.py:763
  100.6 50.9 %copy-start.61 = (f32[1,2,4,128]{3,1,2,0:T(2,128)}, f32[1,2,4,128]{3,1,2,0:T(2,128)S(1)}, u32[]{:S(2)}) copy-start(f32[1,2,4,128]{3,1,2,0:T(2,128)S(1)} %copy.137) | copy-start | bytes 12292
  231.5 66.7 %reduce-scatter.5.cloned.1.call-start = ((), (), s32[]{:S(2)}) async-start(), calls=%async_computation.10 | async-start | bytes 2621440 | tf_op jit(solution)/shard_map/reduce_scatter | solution.py:734
  267.0 206.1 %reduce-scatter.7.cloned.1.call-start = ((), (), s32[]{:S(2)}) async-start(), calls=%async_computation.11 | async-start | bytes 4866048 | tf_op jit(solution)/shard_map/reduce_scatter | solution.py:871
  301.9 238.5 %reduce-scatter.9.cloned.1.call-start = ((), (), s32[]{:S(2)}) async-start(), calls=%async_computation.12 | async-start | bytes 13107200 | tf_op jit(solution)/shard_map/reduce_scatter | solution.py:734
  307.5 19.1 %copy-start.6 = (bf16[8,256,128]{2,1,0:T(8,128)(2,1)S(1)}, bf16[8,256,128]{2,1,0:T(8,128)(2,1)}, u32[]{:S(2)}) copy-start(bf16[8,256,128]{2,1,0:T(8,128)(2,1)} %get-tuple-element.101) | copy-start | bytes 1572868
  307.5 19.1 %copy-start.16 = (f32[128,2048]{1,0:T(8,128)S(1)}, f32[128,2048]{1,0:T(8,128)}, u32[]{:S(2)}) copy-start(f32[128,2048]{1,0:T(8,128)} %copy-done.15) | copy-start | bytes 3145732
  307.5 19.1 %copy-start.18 = (bf16[8,64,256]{2,1,0:T(8,128)(2,1)S(1)}, bf16[8,64,256]{2,1,0:T(8,128)(2,1)}, u32[]{:S(2)}) copy-start(bf16[8,64,256]{2,1,0:T(8,128)(2,1)} %get-tuple-element.102) | copy-start | bytes 786436
  307.5 19.1 %copy-start.22 = (s32[8,2048]{1,0:T(8,128)S(1)}, s32[8,2048]{1,0:T(8,128)}, u32[]{:S(2)}) copy-start(s32[8,2048]{1,0:T(8,128)} %copy-done.21) | copy-start | bytes 196612
  307.5 19.1 %copy-start.31 = (f32[2,2048]{1,0:T(2,128)S(1)}, f32[2,2048]{1,0:T(2,128)}, u32[]{:S(2)}) copy-start(f32[2,2048]{1,0:T(2,128)} %copy-done.30) | copy-start | bytes 49156
  327.7 36.1 %copy-start.62 = (f32[1,2,4,128]{3,1,2,0:T(2,128)S(1)}, f32[1,2,4,128]{3,1,2,0:T(2,128)}, u32[]{:S(2)}) copy-start(f32[1,2,4,128]{3,1,2,0:T(2,128)} %copy-done.61) | copy-start | bytes 12292
  327.7 36.1 %copy-start.67 = (f32[256]{0:T(256)S(1)}, f32[256]{0:T(256)}, u32[]{:S(2)}) copy-start(f32[256]{0:T(256)} %copy-done.66) | copy-start | bytes 3076
  340.4 23.5 %copy-start.35 = (f32[256,1024]{1,0:T(8,128)S(1)}, f32[256,1024]{1,0:T(8,128)}, u32[]{:S(2)}) copy-start(f32[256,1024]{1,0:T(8,128)} %get-tuple-element.245) | copy-start | bytes 3145732
  381.2 188.9 %reduce-scatter.11.cloned.1.call-start = ((), (), s32[]{:S(2)}) async-start(), calls=%async_computation.13 | async-start | bytes 7864320 | tf_op jit(solution)/shard_map/reduce_scatter | solution.py:734
  473.2 182.5 %collective-permute-start.3 = (bf16[320,1024]{1,0:T(8,128)(2,1)}, bf16[320,1024]{1,0:T(8,128)(2,1)}, u32[]{:S(2)}, u32[]{:S(2)}) collective-permute-start(bf16[320,1024]{1,0:T(8,128)(2,1)} %pad_maximum_fusion.4), channel_id=1, source_target_pairs={{0,0},{1,16},{2,2},{3,18},{4,4},{5,20},{6,6},{7,22},{8,8},{9,24},{... | collective-permute-start | bytes 1966088 | tf_op jit(solution)/shard_map/ppermute | solution.py:712
  480.6 58.7 %copy-start.38 = (f32[256,1024]{1,0:T(8,128)S(1)}, f32[256,1024]{1,0:T(8,128)}, u32[]{:S(2)}) copy-start(f32[256,1024]{1,0:T(8,128)} %copy-done.36) | copy-start | bytes 3145732
  571.6 88.3 %copy-start.52 = (bf16[5632,256]{1,0:T(8,128)(2,1)S(1)}, bf16[5632,256]{1,0:T(8,128)(2,1)}, u32[]{:S(2)}) copy-start(bf16[5632,256]{1,0:T(8,128)(2,1)} %get-tuple-element.142) | copy-start | bytes 8650756
  677.3 18.2 %collective-permute-start.4 = (bf16[256,1024]{1,0:T(8,128)(2,1)S(1)}, bf16[256,1024]{1,0:T(8,128)(2,1)S(1)}, u32[]{:S(2)}, u32[]{:S(2)}) collective-permute-start(bf16[256,1024]{1,0:T(8,128)(2,1)S(1)} %copy-done.57), channel_id=1, source_target_pairs={{0,0},{1,16},{2,2},{3,18},{4,4},{5,20},{6,6},{7,22},{8,8},{9,24},{... | collective-permute-start | bytes 1572872 | tf_op jit(solution)/shard_map/ppermute | solution.py:712
  (79 other events, 343.5 us)
Sparse Core Ops, SparseCore 0:
  9.6 49.7 all-gather.8
  60.9 22.5 all-gather.10
  85.1 22.6 all-gather.12
  109.2 42.1 all-gather.14
  153.4 41.2 all-gather.16
  231.6 21.5 all-gather.18
  267.1 31.0 reduce-scatter.4
  302.8 106.4 reduce-scatter.6
  411.9 96.0 reduce-scatter.8
  510.4 59.6 reduce-scatter.10

commit v8 on v6

--- a/solution.py
+++ b/solution.py
@@ -466,19 +466,67 @@
 
 
 def units_kernel(
-    n, fan, x_ref, part_ref, inner_ref, outer_ref, sum_ref, landed,
-    swap_send, swap_recv, own_sem, send_sem, recv_sem, part_send, part_recv,
+    n, fan, x_ref, part_ref, inner_ref, outer_ref, sum_ref, slots, acc, landed,
+    down_send, down_recv, swap_send, swap_recv, own_sem, send_sem, recv_sem, part_send, part_recv,
 ):
     s, me = lax.axis_index("seq"), lax.axis_index("fsdp")
-    rows, width = x_ref.shape[0] // 3, x_ref.shape[1]
+    rows, width = acc.shape[0] // 3, x_ref.shape[1]
     cols = width // fan
     block = 2 * fan * rows
     place, right, left = ring_greet(n, [(me + far) % fan for far in range(1, fan)])
+    tokens = sum_ref.shape[0]
+    parts = []
+    for far in range(1, fan):
+        target = (me + far) % fan
+        one = pltpu.make_async_remote_copy(
+            src_ref=part_ref.at[pl.ds(target * tokens, tokens), :],
+            dst_ref=landed.at[far],
+            send_sem=part_send.at[far],
+            recv_sem=part_recv.at[far],
+            device_id={"fsdp": target},
+            device_id_type=MESH,
+        )
+        one.start()
+        parts.append(one)
+
+    sums = {}
+
+    def piece_of(ref, at, piece):
+        return ref.at[pl.ds(at * 3 * rows, 3 * rows), pl.ds(piece * cols, cols)]
+
+    def send_sum(piece, step, src):
+        to = left if piece >= fan // 2 else right
+        sums[piece, step] = pltpu.make_async_remote_copy(
+            src_ref=src,
+            dst_ref=piece_of(slots, step, piece),
+            send_sem=down_send.at[piece, step],
+            recv_sem=down_recv.at[piece, step],
+            device_id={"seq": to},
+            device_id_type=MESH,
+        )
+        sums[piece, step].start()
+
+    def chunk(piece, step):
+        return ring_index((place + 1 + step) % n if piece >= fan // 2 else (place + 2 * n - 1 - step) % n, n)
+
+    for piece in range(fan):
+        send_sum(piece, 0, piece_of(x_ref, chunk(piece, 0), piece))
+    for step in range(n - 1):
+        for piece in range(fan):
+            sums[piece, step].wait_recv()
+            arrived = piece_of(slots, step, piece)
+            mine = piece_of(x_ref, chunk(piece, step + 1), piece)
+            total = (arrived[...].astype(jnp.float32) + mine[...].astype(jnp.float32)).astype(jnp.bfloat16)
+            if step < n - 2:
+                arrived[...] = total
+                send_sum(piece, step + 1, arrived)
+            else:
+                acc[:, piece * cols : (piece + 1) * cols] = total
     moves = []
     for far in range(fan):
         target = (me + far) % fan
         for half in range(2):
-            src = x_ref.at[pl.ds(half * rows, rows), pl.ds(pl.multiple_of(target * cols, 128), cols)]
+            src = acc.at[pl.ds(half * rows, rows), pl.ds(pl.multiple_of(target * cols, 128), cols)]
             dst = inner_ref.at[pl.ds(s * block + (me * 2 + half) * rows, rows), :]
             if far:
                 one = pltpu.make_async_remote_copy(
@@ -494,7 +542,7 @@
             one.start()
             moves.append(one)
     mine = pltpu.make_async_copy(
-        x_ref.at[pl.ds(2 * rows, rows), :], outer_ref.at[pl.ds(s * rows, rows), :], own_sem.at[2]
+        acc.at[pl.ds(2 * rows, rows), :], outer_ref.at[pl.ds(s * rows, rows), :], own_sem.at[2]
     )
     mine.start()
     copies = {}
@@ -514,20 +562,6 @@
         )
         copies[k, piece, step].start()
 
-    tokens = sum_ref.shape[0]
-    parts = []
-    for far in range(1, fan):
-        target = (me + far) % fan
-        one = pltpu.make_async_remote_copy(
-            src_ref=part_ref.at[pl.ds(target * tokens, tokens), :],
-            dst_ref=landed.at[far],
-            send_sem=part_send.at[far],
-            recv_sem=part_recv.at[far],
-            device_id={"fsdp": target},
-            device_id_type=MESH,
-        )
-        one.start()
-        parts.append(one)
     mine.wait()
     start(0, 0, 0)
     start(0, 1, 0)
@@ -546,13 +580,13 @@
         parts[far - 1].wait()
         total = total + landed[far].astype(jnp.float32)
     sum_ref[...] = total
-    for one in copies.values():
+    for one in [*copies.values(), *sums.values()]:
         one.wait_send()
 
 
 def units_total(grads, part, ident):
     n, fan = lax.axis_size("seq"), lax.axis_size("fsdp")
-    rows, width = grads.shape[0] // 3, grads.shape[1]
+    rows, width = grads.shape[0] // (3 * n), grads.shape[1]
     tokens = part.shape[0] // fan
     sems = lambda *shape: pltpu.SemaphoreType.DMA(shape)
     return ring_call(
@@ -564,7 +598,12 @@
             ((n * rows, width), jnp.bfloat16),
             ((tokens, part.shape[1]), jnp.float32),
         ],
-        [pltpu.VMEM((fan, tokens, part.shape[1]), jnp.bfloat16), sems(fan, 2), sems(fan, 2), sems(3)]
+        [
+            pltpu.VMEM(((n - 1) * 3 * rows, width), jnp.bfloat16),
+            pltpu.VMEM((3 * rows, width), jnp.bfloat16),
+            pltpu.VMEM((fan, tokens, part.shape[1]), jnp.bfloat16),
+        ]
+        + [sems(fan, n - 1), sems(fan, n - 1), sems(fan, 2), sems(fan, 2), sems(3)]
         + [sems(4, n - 1), sems(4, n - 1), sems(fan), sems(fan)],
         ident,
     )
@@ -775,9 +814,16 @@
     early = lax.all_gather(early, "fsdp", axis=1, tiled=True)
     both_ids = jnp.concatenate([decoder_ids.reshape(-1), encoder_ids.reshape(-1)])
     both_ids = change_home(jnp.pad(both_ids, (0, 1024 - local - enc_local)).reshape(8, 128))
-    (both_ids,) = swap([jnp.broadcast_to(both_ids[None], (parts, 8, 128))], 13)
+    inner_t = ff_in.T
+    by_kernel = (width // fan) % 128 == 0
+    both_ids, *halves = swap(
+        [jnp.broadcast_to(both_ids[None], (parts, 8, 128))], 13, tuple(range(fan)) if by_kernel else (), inner_t
+    )
+    if not by_kernel:
+        halves = spread(jnp.transpose(inner_t.reshape(2, fan, units, -1), (1, 0, 2, 3)))
+        halves = [jnp.transpose(halves[:, i], (1, 0, 2)).reshape(units, width) for i in range(2)]
+    gate_t, up_t = halves
     home = change_home(layer_in.reshape(rows, width))
-    inner_t = ff_in.T
     early = by_rows(early)
     mix_self = early[0].reshape(parts, own * dh, width)
     query_w = early[1].reshape(width, parts, own * dh)
@@ -812,26 +858,26 @@
         [jnp.full((own, BQ), MASKED, f32), bias, jnp.zeros((own, BQ), f32)], axis=1
     )
 
-    qkv_w, home, inner_t, ext, self_rows, cross_rows, self_limits, cross_limits = lax.optimization_barrier(
-        (qkv_w, home, inner_t, ext, self_rows, cross_rows, self_limits, cross_limits)
+    qkv_w, home, gate_t, ext, self_rows, cross_rows, self_limits, cross_limits = lax.optimization_barrier(
+        (qkv_w, home, gate_t, ext, self_rows, cross_rows, self_limits, cross_limits)
     )
     qkv_w = qkv_w.reshape(width, parts, own * 3 * dh)
 
     stream = home.astype(f32)
     normed_first = norm_apply(stream, gain_first).astype(bf16)
     qkv_tok = jnp.einsum("td,dge->gte", normed_first, qkv_w, preferred_element_type=f32).astype(bf16)
-    qkv_tok, cross_out, cotangent, encoder = lax.optimization_barrier((qkv_tok, cross_out, cotangent, encoder))
-    mix_cross = gather(cross_out).reshape(parts, own * dh, width)
     others = change_home(jnp.concatenate([cotangent.reshape(rows, width), encoder.reshape(-1, width)]))
     grad_low, enc_flat = others[:rows], others[rows:]
     (qkv,) = swap([qkv_tok], 10)
+    qkv, cross_out, grad_low = lax.optimization_barrier((qkv, cross_out, grad_low))
+    if rows == cross_out.shape[0]:
+        mix_cross, grad_group = lax.all_gather(jnp.stack([cross_out, grad_low]), "fsdp", axis=1, tiled=True)
+    else:
+        mix_cross, grad_group = gather(cross_out), gather(grad_low)
+    mix_cross = mix_cross.reshape(parts, own * dh, width)
     qkv = qkv.reshape(length, own * 3 * dh)
     out_self, self_t, self_lse = self_forward(self_limits, self_rows, ext, qkv)
-    out_self, grad_low = lax.optimization_barrier((out_self, grad_low))
-    grad_group = gather(grad_low)
-    by_kernel = (width // fan) % 128 == 0
-    fars = [tuple(far for far in range(fan) if (far + 2) % 3 == i) if by_kernel else () for i in range(3)]
-    self_tok, *halves = swap([out_self.reshape(parts, local, own * dh)], 14, fars[0], inner_t)
+    (self_tok,) = swap([out_self.reshape(parts, local, own * dh)], 11)
     after_self = stream + jnp.einsum("gtc,gcd->td", self_tok, mix_self, preferred_element_type=f32)
     normed_second = norm_apply(after_self, gain_second).astype(bf16)
     query_tok = jnp.einsum("td,dgc->gtc", normed_second, query_w, preferred_element_type=f32).astype(bf16)
@@ -839,14 +885,10 @@
         "td,sdge->sgte", enc_flat, pairs_w.reshape(2, width, parts // 2, -1), preferred_element_type=f32
     )
     pairs_tok = pairs_tok.astype(bf16).reshape(parts, enc_local, -1)
-    query_cross, pairs, *halves = swap([query_tok, pairs_tok], 15, fars[1], inner_t, halves)
+    query_cross, pairs = swap([query_tok, pairs_tok], 12)
     query_cross, pairs = query_cross.reshape(length, own * dh), pairs.reshape(keys, own * 2 * dh)
     out_cross, cross_t, cross_lse = cross_forward(cross_limits, cross_rows, query_cross, pairs)
-    cross_tok, *halves = swap([out_cross.reshape(parts, local, own * dh)], 16, fars[2], inner_t, halves)
-    if not by_kernel:
-        halves = spread(jnp.transpose(inner_t.reshape(2, fan, units, -1), (1, 0, 2, 3)))
-        halves = [jnp.transpose(halves[:, i], (1, 0, 2)).reshape(units, width) for i in range(2)]
-    gate_t, up_t = halves
+    (cross_tok,) = swap([out_cross.reshape(parts, local, own * dh)], 11)
     after_cross = after_self + jnp.einsum("gtc,gcd->td", cross_tok, mix_cross, preferred_element_type=f32)
     normed_third = norm_apply(after_cross, gain_third).astype(bf16)
     normed_group = gather(normed_third)
@@ -869,9 +911,7 @@
     grad_third_in, outer_part, grad_units = lax.optimization_barrier((grad_third_in, outer_part, grad_units))
     if by_kernel:
         grad_units = jnp.stack([g.reshape(parts, units // parts, width) for g in grad_units], axis=1)
-        part_units = lax.psum_scatter(
-            grad_units.reshape(3 * units, width), "seq", scatter_dimension=0, tiled=True
-        )
+        part_units = grad_units.reshape(3 * units, width)
     grad_third_in = grad_third_in.astype(f32)
     grad_from_third, grad_gain_third = norm_back(after_cross, gain_third, grad_third_in)
     grad_middle = grad_low.astype(f32) + grad_from_third

time: 682 us -> 688 us (level)
  waiting for transfers between devices: 79.3 us -> 43.5 us
  Pallas kernels: 373 us -> 401 us
  starting transfers between devices: 21.2 us -> 30.1 us
    pallas_call x2, Pallas kernels: 146 us -> 187 us  [ring_call(): pl.pallas_call(body, name=name, out_shape=[jax.ShapeDtypeStruct(s, d) for...]
    reduce_scatter x3, waiting for transfers between devices: 45.5 us -> 17.5 us  [scatter(): return lax.psum_scatter(grad, 'fsdp', scatter_dimension=0, tiled=True)]
    pallas_call x9, Pallas kernels: 172 us -> 155 us  [swap(): pl.pallas_call(functools.partial(swap_kernel, n, fan, count, fars, not fa...]
    all_gather x4 -> x2, waiting for transfers between devices: 27.7 us -> 18.1 us  [shards(): gather = lambda v: lax.all_gather(v, 'fsdp', axis=0, tiled=True)]
    ppermute x5, starting transfers between devices: 19.3 us -> 28.9 us  [change_home(): return lax.ppermute(value, ('seq', 'fsdp'), pairs)]
    unnamed x155 -> x163, local copies, waits for them, and re-layouts: 39.2 us -> 40.5 us
  transfers between devices with their start and end apart: 14 -> 12, of which waited for: 6 -> 4; matrix products, arithmetic and copies ran while one was open for 19% -> 16% of each run, Pallas kernels for 55% -> 54%
where the time goes in v8:
time: 688 us; the launch traced here: 679 us
  Pallas kernels  401 us (58%)
  matrix products  74.8 us (11%)
  local copies, waits for them, and re-layouts  65.5 us (10%)
  waiting for transfers between devices  43.5 us (6%)
  other arithmetic  35.7 us (5%)
  starting transfers between devices  30.1 us (4%)
  between operations  15.4 us (2%)
  blocking collectives  12.2 us (2%)
    pallas_call x2, Pallas kernels, ring_call(): pl.pallas_call(body, name=name, out_shape=[jax.ShapeDtypeStruct(s, d) for...  187 us
    pallas_call x9, Pallas kernels, swap(): pl.pallas_call(functools.partial(swap_kernel, n, fan, count, fars, not fa...  155 us
    pallas_call x4, Pallas kernels, call(): pl.pallas_call(body, name=name, out_shape=[jax.ShapeDtypeStruct(s, d) for...  59.6 us
    unnamed x163, local copies, waits for them, and re-layouts  40.5 us
    ppermute x5, starting transfers between devices, change_home(): return lax.ppermute(value, ('seq', 'fsdp'), pairs)  28.9 us
    all_gather x2, waiting for transfers between devices, shards(): gather = lambda v: lax.all_gather(v, 'fsdp', axis=0, tiled=True)  18.1 us
    reduce_scatter x3, waiting for transfers between devices, scatter(): return lax.psum_scatter(grad, 'fsdp', scatter_dimension=0, tiled=True)  17.5 us
  transfers between devices with their start and end apart: 12, of which 4 were waited for; matrix products, arithmetic and copies ran while one was open for 16% of the time, Pallas kernels for 54%

profile of v8, /device:TPU:1, one launch (start us, length us, event | category | flops | bytes accessed | tf_op | source)
XLA Modules:
  0.0 678.5 jit_solution(15195643113941248406)
XLA Ops:
  9.6 6.1 all-gather.1
  18.5 4.9 collective-permute-start
  36.1 7.1 %collective-permute-done.1 = s32[8,128]{1,0:T(8,128)S(1)} collective-permute-done((s32[8,128]{1,0:T(8,128)S(1)}, s32[8,128]{1,0:T(8,128)S(1)}, u32[]{:S(2)}, u32[]{:S(2)}) %collective-permute-start.1) | collective-permute-done | bytes 4128 | tf_op jit(solution)/shard_map/ppermute | solution.py:751
  43.8 49.4 %swap.9 = (s32[8,8,128]{2,1,0:T(8,128)}, bf16[704,1024]{1,0:T(8,128)(2,1)}, bf16[704,1024]{1,0:T(8,128)(2,1)}) custom-call(s32[8,8,128]{2,1,0:T(8,128)} %broadcast_in_dim.95.refs_0_, bf16[5632,256]{1,0:T(8,128)(2,1)} %bitcast.253), custom_call_target="tpu_custom_call" | custom-call | bytes 16384 | tf_op jit(solution)/shard_map/swap/pallas_call | solution.py:710
  97.9 5.2 fusion.64
  104.7 5.9 fusion.17.refs_0_
  110.6 20.9 %swap.10 = bf16[8,256,384]{2,1,0:T(8,128)(2,1)} custom-call(bf16[8,256,384]{2,1,0:T(8,128)(2,1)} %fusion.17.refs_0_), custom_call_target="tpu_custom_call" | custom-call | bytes 1572864 | tf_op jit(solution)/shard_map/swap/pallas_call | solution.py:710
  134.6 18.3 %self_forward.1 = (bf16[2048,128]{1,0:T(8,128)(2,1)S(1)}, f32[128,2048]{1,0:T(8,128)S(1)}, f32[2,2048]{1,0:T(2,128)S(1)}) custom-call(s32[2,8]{1,0:T(2,128)S(1)} %pad_add_fusion.1.lim_ref, s32[8,2048]{1,0:T(8,128)S(1)} %broadcast_in_dim.102.rows_ref, f32[2,1536]{1,0:T(2,128)S(1)} %maximum_maximum_fusion.ext_ref, bf16[2048,384]{1,0:T(8,128)(2,1)S(1)} %bitcast.230), custom_call_target="tpu_custom_call" | custom-call | bytes 1650752 | tf_op jit(solution)/shard_map/self_forward/pallas_call | solution.py:257
  154.7 8.9 %swap.11 = bf16[8,256,128]{2,1,0:T(8,128)(2,1)} custom-call(bf16[8,256,128]{2,1,0:T(8,128)(2,1)} %bitcast.240), custom_call_target="tpu_custom_call" | custom-call | bytes 524288 | tf_op jit(solution)/shard_map/swap/pallas_call | solution.py:710
  163.7 4.7 fusion.74
  181.1 12.8 %swap.12 = (bf16[8,256,128]{2,1,0:T(8,128)(2,1)}, bf16[8,64,256]{2,1,0:T(8,128)(2,1)}) custom-call(bf16[8,256,128]{2,1,0:T(8,128)(2,1)} %fusion.23.refs_0_, bf16[8,64,256]{2,1,0:T(8,128)(2,1)} %bitcast.279), custom_call_target="tpu_custom_call" | custom-call | bytes 786432 | tf_op jit(solution)/shard_map/swap/pallas_call | solution.py:710
  196.0 8.6 %cross_forward.1 = (bf16[2048,128]{1,0:T(8,128)(2,1)S(1)}, f32[128,2048]{1,0:T(8,128)S(1)}, f32[2,2048]{1,0:T(2,128)S(1)}) custom-call(s32[2,8]{1,0:T(2,128)S(1)} %pad_add_fusion.2.lim_ref, s32[8,2048]{1,0:T(8,128)S(1)} %add_add_fusion.3.rows_ref, bf16[2048,128]{1,0:T(8,128)(2,1)S(1)} %bitcast.232, bf16[512,256]{1,0:T(8,128)(2,1)S(1)} %bitcast.237), custom_call_target="tpu_custom_call" | custom-call | bytes 852032 | tf_op jit(solution)/shard_map/cross_forward/pallas_call | solution.py:257
  206.3 9.5 %swap.13 = bf16[8,256,128]{2,1,0:T(8,128)(2,1)} custom-call(bf16[8,256,128]{2,1,0:T(8,128)(2,1)} %bitcast.241), custom_call_target="tpu_custom_call" | custom-call | bytes 524288 | tf_op jit(solution)/shard_map/swap/pallas_call | solution.py:710
  222.7 4.9 fusion.15
  227.5 18.1 %all-gather.13.cloned.1.call-done = bf16[1024,1024]{1,0:T(8,128)(2,1)} async-done(((bf16[256,1024]{1,0:T(8,128)(2,1)}), bf16[1024,1024]{1,0:T(8,128)(2,1)}) %all-gather.13.cloned.1.call-update) | async-done | bytes 2097168 | tf_op jit(solution)/shard_map/all_gather | solution.py:802
  249.6 4.7 multiply_convert_fusion
  260.3 4.7 convolution_convert_fusion.5.part_ref
  274.0 17.2 %reduce-scatter.4.cloned.1.call-done = bf16[256,1024]{1,0:T(8,128)(2,1)} async-done(((bf16[1024,1024]{1,0:T(8,128)(2,1)}), bf16[256,1024]{1,0:T(8,128)(2,1)}) %reduce-scatter.4.cloned.1.call-update) | async-done | bytes 524304 | tf_op jit(solution)/shard_map/reduce_scatter | solution.py:773
  296.8 10.1 %swap.14 = bf16[8,256,128]{2,1,0:T(8,128)(2,1)} custom-call(bf16[8,256,128]{2,1,0:T(8,128)(2,1)} %fusion.24.refs_0_), custom_call_target="tpu_custom_call" | custom-call | bytes 524288 | tf_op jit(solution)/shard_map/swap/pallas_call | solution.py:710
  309.2 10.2 %cross_backward.1 = (bf16[2048,128]{1,0:T(8,128)(2,1)S(1)}, bf16[512,256]{1,0:T(8,128)(2,1)S(1)}) custom-call(s32[2,8]{1,0:T(2,128)S(1)} %pad_add_fusion.2.lim_ref, s32[8,2048]{1,0:T(8,128)S(1)} %add_add_fusion.3.rows_ref, bf16[2048,128]{1,0:T(8,128)(2,1)S(1)} %bitcast.233, bf16[512,256]{1,0:T(8,128)(2,1)S(1)} %bitcast.238, bf16[2048,128]{1,0:T(8,128)(2,1)S(1)} %bitcast.234, ...), custom_call_target="tpu_custom_call" | custom-call | bytes 2441280 | tf_op jit(solution)/shard_map/cross_backward/pallas_call | solution.py:257
  320.9 11.9 %swap.15 = (bf16[8,256,128]{2,1,0:T(8,128)(2,1)}, bf16[8,64,256]{2,1,0:T(8,128)(2,1)}) custom-call(bf16[8,256,128]{2,1,0:T(8,128)(2,1)} %bitcast.239, bf16[8,64,256]{2,1,0:T(8,128)(2,1)} %bitcast.242), custom_call_target="tpu_custom_call" | custom-call | bytes 786432 | tf_op jit(solution)/shard_map/swap/pallas_call | solution.py:710
  346.6 6.1 pad_maximum_fusion
  353.6 9.6 %swap.16 = bf16[8,256,128]{2,1,0:T(8,128)(2,1)} custom-call(bf16[8,256,128]{2,1,0:T(8,128)(2,1)} %fusion.25.refs_0_), custom_call_target="tpu_custom_call" | custom-call | bytes 524288 | tf_op jit(solution)/shard_map/swap/pallas_call | solution.py:710
  364.3 22.5 %self_backward.1 = (bf16[2048,384]{1,0:T(8,128)(2,1)S(1)}, f32[2,5,512]{2,1,0:T(8,128)S(1)}) custom-call(s32[2,8]{1,0:T(2,128)S(1)} %pad_add_fusion.1.lim_ref, s32[8,2048]{1,0:T(8,128)S(1)} %broadcast_in_dim.102.rows_ref, f32[2,1536]{1,0:T(2,128)S(1)} %maximum_maximum_fusion.ext_ref, bf16[2048,384]{1,0:T(8,128)(2,1)S(1)} %bitcast.231, ...), custom_call_target="tpu_custom_call" | custom-call | bytes 3240000 | tf_op jit(solution)/shard_map/self_backward/pallas_call | solution.py:257
  388.0 21.4 %swap.17 = bf16[8,256,384]{2,1,0:T(8,128)(2,1)} custom-call(bf16[8,256,384]{2,1,0:T(8,128)(2,1)} %bitcast.236), custom_call_target="tpu_custom_call" | custom-call | bytes 1572864 | tf_op jit(solution)/shard_map/swap/pallas_call | solution.py:710
  411.9 5.7 fusion.33
  417.6 6.2 psum.7
  438.5 4.9 collective-permute-start.3
  443.4 107.5 %units_total.1 = (bf16[5632,256]{1,0:T(8,128)(2,1)}, bf16[704,1024]{1,0:T(8,128)(2,1)S(1)}, f32[256,1024]{1,0:T(8,128)S(1)}) custom-call(bf16[2112,1024]{1,0:T(8,128)(2,1)} %bitcast.252, bf16[1024,1024]{1,0:T(8,128)(2,1)S(1)} %copy-done.5), custom_call_target="tpu_custom_call" | custom-call | bytes 385351680 | tf_op jit(solution)/shard_map/units_total/pallas_call | solution.py:440
  554.3 79.5 %ring_total.1 = (bf16[256,5120]{1,0:T(8,128)(2,1)S(1)}, bf16[256,3072]{1,0:T(8,128)(2,1)S(1)}, bf16[64,128]{1,0:T(8,128)(2,1)S(1)}) custom-call(bf16[256,5120]{1,0:T(8,128)(2,1)} %reduce-scatter.6.cloned.1.call-done.refs_0_, bf16[256,3072]{1,0:T(8,128)(2,1)S(1)} %copy-done.11, bf16[64,128]{1,0:T(8,128)(2,1)S(1)} %pad_bitcast_fusion.refs_2_), custom_call_target="tpu_custom_call" | custom-call | bytes 252641280 | tf_op jit(solution)/shard_map/ring_total/pallas_call | solution.py:440
  636.9 12.7 %collective-permute-start.4 = (bf16[256,1024]{1,0:T(8,128)(2,1)}, bf16[256,1024]{1,0:T(8,128)(2,1)S(1)}, u32[]{:S(2)}, u32[]{:S(2)}) collective-permute-start(bf16[256,1024]{1,0:T(8,128)(2,1)} %add_convert_fusion.1), channel_id=1, source_target_pairs={{0,0},{1,16},{2,2},{3,18},{4,4},{5,20},{6,6},{7,22},{8,8},{9,24},{... | collective-permute-start | bytes 1572872 | tf_op jit(solution)/shard_map/ppermute | solution.py:751
  659.8 6.3 copy.119
  (290 shorter events, 136.6 us)
Async XLA Ops:
  7.2 215.5 %copy-start = (bf16[704,1024]{1,0:T(8,128)(2,1)S(1)}, bf16[704,1024]{1,0:T(8,128)(2,1)}, u32[]{:S(2)}) copy-start(bf16[704,1024]{1,0:T(8,128)(2,1)} %param.32) | copy-start | bytes 4325380
  7.2 8.5 %copy-start.51 = (bf16[256,16,128]{2,1,0:T(8,128)(2,1)S(1)}, bf16[256,16,128]{2,1,0:T(8,128)(2,1)}, u32[]{:S(2)}) copy-start(bf16[256,16,128]{2,1,0:T(8,128)(2,1)} %param.28) | copy-start | bytes 3145732
  7.2 97.3 %all-gather.7.cloned.1.call-start = ((), (), s32[]{:S(2)}) async-start(), calls=%async_computation.3 | async-start | bytes 7864320 | tf_op jit(solution)/shard_map/all_gather | solution.py:802
  7.9 155.7 %all-gather.9.cloned.1.call-start = ((), (), s32[]{:S(2)}) async-start(), calls=%async_computation.4 | async-start | bytes 10485760 | tf_op jit(solution)/shard_map/all_gather | solution.py:814
  18.4 5.0 copy-start.60
  18.4 5.0 copy-start.61
  18.4 6.9 %copy-start.53 = (bf16[1,256,1024]{2,1,0:T(8,128)(2,1)S(1)}, bf16[1,256,1024]{2,1,0:T(8,128)(2,1)}, u32[]{:S(2)}) copy-start(bf16[1,256,1024]{2,1,0:T(8,128)(2,1)} %param.33) | copy-start | bytes 1572868
  18.4 6.9 %copy-start.57 = (bf16[1,64,1024]{2,1,0:T(8,128)(2,1)S(1)}, bf16[1,64,1024]{2,1,0:T(8,128)(2,1)}, u32[]{:S(2)}) copy-start(bf16[1,64,1024]{2,1,0:T(8,128)(2,1)} %param.18) | copy-start | bytes 393220
  18.5 12.4 %copy-start.58 = (s32[2048]{0:T(1024)S(1)}, s32[2048]{0:T(1024)}, u32[]{:S(2)}) copy-start(s32[2048]{0:T(1024)} %param.21) | copy-start | bytes 24580
  18.5 197.3 %all-gather.11.cloned.1.call-start = ((), (), s32[]{:S(2)}) async-start(), calls=%async_computation.5 | async-start | bytes 5242880 | tf_op jit(solution)/shard_map/all_gather | solution.py:874
  18.5 86.0 %collective-permute-start = (bf16[256,1024]{1,0:T(8,128)(2,1)}, bf16[256,1024]{1,0:T(8,128)(2,1)S(1)}, u32[]{:S(2)}, u32[]{:S(2)}) collective-permute-start(bf16[256,1024]{1,0:T(8,128)(2,1)} %bitcast), channel_id=1, source_target_pairs={{0,0},{1,16},{2,2},{3,18},{4,4},{5,20},{6,6},{7,22},{8,8},{9,24},{... | collective-permute-start | bytes 1572872 | tf_op jit(solution)/shard_map/ppermute | solution.py:751
  23.4 19.7 %collective-permute-start.1 = (s32[8,128]{1,0:T(8,128)S(1)}, s32[8,128]{1,0:T(8,128)S(1)}, u32[]{:S(2)}, u32[]{:S(2)}) collective-permute-start(s32[8,128]{1,0:T(8,128)S(1)} %pad_bitcast_fusion.1), channel_id=1, source_target_pairs={{0,0},{1,16},{2,2},{3,18},{4,4},{5,20},{6,6},{7,22},{8,8},{9,24},{... | collective-permute-start | bytes 12296 | tf_op jit(solution)/shard_map/ppermute | solution.py:751
  26.3 77.3 %collective-permute-start.2 = (bf16[320,1024]{1,0:T(8,128)(2,1)}, bf16[320,1024]{1,0:T(8,128)(2,1)S(1)}, u32[]{:S(2)}, u32[]{:S(2)}) collective-permute-start(bf16[320,1024]{1,0:T(8,128)(2,1)} %pad_maximum_fusion.4), channel_id=1, source_target_pairs={{0,0},{1,16},{2,2},{3,18},{4,4},{5,20},{6,6},{7,22},{8,8},{9,24},{... | collective-permute-start | bytes 1966088 | tf_op jit(solution)/shard_map/ppermute | solution.py:751
  103.6 7.0 %copy-start.52 = (bf16[320,1024]{1,0:T(8,128)(2,1)}, bf16[320,1024]{1,0:T(8,128)(2,1)S(1)}, u32[]{:S(2)}) copy-start(bf16[320,1024]{1,0:T(8,128)(2,1)S(1)} %collective-permute-done.2) | copy-start | bytes 1966084
  104.5 6.1 copy-start.36
  134.0 111.6 %all-gather.13.cloned.1.call-start = ((), (), s32[]{:S(2)}) async-start(), calls=%async_computation.6 | async-start | bytes 2621440 | tf_op jit(solution)/shard_map/all_gather | solution.py:802
  222.4 68.8 %reduce-scatter.4.cloned.1.call-start = ((), (), s32[]{:S(2)}) async-start(), calls=%async_computation.7 | async-start | bytes 2621440 | tf_op jit(solution)/shard_map/reduce_scatter | solution.py:773
  260.0 178.4 %reduce-scatter.6.cloned.1.call-start = ((), (), s32[]{:S(2)}) async-start(), calls=%async_computation.8 | async-start | bytes 13107200 | tf_op jit(solution)/shard_map/reduce_scatter | solution.py:773
  271.2 20.0 %copy-start.26 = (f32[256,1024]{1,0:T(8,128)S(1)}, f32[256,1024]{1,0:T(8,128)}, u32[]{:S(2)}) copy-start(f32[256,1024]{1,0:T(8,128)} %copy-done.25) | copy-start | bytes 3145732
  295.2 11.7 %copy-start.7 = (bf16[8,256,128]{2,1,0:T(8,128)(2,1)S(1)}, bf16[8,256,128]{2,1,0:T(8,128)(2,1)}, u32[]{:S(2)}) copy-start(bf16[8,256,128]{2,1,0:T(8,128)(2,1)} %get-tuple-element.81) | copy-start | bytes 1572868
  295.2 11.7 %copy-start.20 = (bf16[8,64,256]{2,1,0:T(8,128)(2,1)S(1)}, bf16[8,64,256]{2,1,0:T(8,128)(2,1)}, u32[]{:S(2)}) copy-start(bf16[8,64,256]{2,1,0:T(8,128)(2,1)} %get-tuple-element.82) | copy-start | bytes 786436
  352.8 10.4 %copy-start.16 = (f32[128,2048]{1,0:T(8,128)S(1)}, f32[128,2048]{1,0:T(8,128)}, u32[]{:S(2)}) copy-start(f32[128,2048]{1,0:T(8,128)} %copy-done.15) | copy-start | bytes 3145732
  352.8 200.1 %reduce-scatter.8.cloned.1.call-start = ((), (), s32[]{:S(2)}) async-start(), calls=%async_computation.9 | async-start | bytes 7864320 | tf_op jit(solution)/shard_map/reduce_scatter | solution.py:773
  423.8 4.9 copy-start.33
  423.8 4.9 copy-start.39
  423.8 4.9 copy-start.44
  438.4 4.9 copy-start.5
  438.5 113.5 %copy-start.27 = (f32[256,1024]{1,0:T(8,128)S(1)}, f32[256,1024]{1,0:T(8,128)}, u32[]{:S(2)}) copy-start(f32[256,1024]{1,0:T(8,128)} %copy-done.25) | copy-start | bytes 3145732
  438.5 196.5 %collective-permute-start.3 = (bf16[320,1024]{1,0:T(8,128)(2,1)}, bf16[320,1024]{1,0:T(8,128)(2,1)S(1)}, u32[]{:S(2)}, u32[]{:S(2)}) collective-permute-start(bf16[320,1024]{1,0:T(8,128)(2,1)} %pad_maximum_fusion.5), channel_id=1, source_target_pairs={{0,0},{1,16},{2,2},{3,18},{4,4},{5,20},{6,6},{7,22},{8,8},{9,24},{... | collective-permute-start | bytes 1966088 | tf_op jit(solution)/shard_map/ppermute | solution.py:751
  634.9 18.5 %copy-start.3 = (bf16[256,5120]{1,0:T(8,128)(2,1)}, bf16[256,5120]{1,0:T(8,128)(2,1)S(1)}, u32[]{:S(2)}) copy-start(bf16[256,5120]{1,0:T(8,128)(2,1)S(1)} %get-tuple-element.119) | copy-start | bytes 7864324
  636.9 33.8 %collective-permute-start.4 = (bf16[256,1024]{1,0:T(8,128)(2,1)}, bf16[256,1024]{1,0:T(8,128)(2,1)S(1)}, u32[]{:S(2)}, u32[]{:S(2)}) collective-permute-start(bf16[256,1024]{1,0:T(8,128)(2,1)} %add_convert_fusion.1), channel_id=1, source_target_pairs={{0,0},{1,16},{2,2},{3,18},{4,4},{5,20},{6,6},{7,22},{8,8},{9,24},{... | collective-permute-start | bytes 1572872 | tf_op jit(solution)/shard_map/ppermute | solution.py:751
  659.8 6.3 copy-start.14
  (53 other events, 109.2 us)
Sparse Core Ops, SparseCore 0:
  9.6 58.4 all-gather.6
  70.2 64.1 all-gather.8
  136.6 34.4 all-gather.10
  222.6 23.0 all-gather.12
  260.1 31.0 reduce-scatter.3
  352.9 85.4 reduce-scatter.5
  441.1 66.6 reduce-scatter.7

commit v9 on v8

--- a/solution.py
+++ b/solution.py
@@ -25,17 +25,10 @@
     return jnp.transpose(value.astype(jnp.float32), (1, 0))
 
 
-def bias_tiles(ext_ref, tile_ref, own, bk):
-    span = BQ + bk
+def bias_tiles(ext_ref, tile_ref, own):
     for h in range(own):
-        for t in range(tile_ref.shape[1]):
-            first = t * bk
-            line = jnp.broadcast_to(ext_ref[h : h + 1, first : first + span], (bk, span))
-            tile_ref[h, t] = pltpu.roll(line, 0, 1, stride=1, stride_axis=0)[:, bk:]
-
-
-def tile_count(bk):
-    return BQ // bk + REACH // bk
+        line = jnp.broadcast_to(ext_ref[h : h + 1, :], tile_ref.shape[1:])
+        tile_ref[h] = pltpu.roll(line, 0, 1, stride=1, stride_axis=0)
 
 
 def unpack(ref, own, width, picks, flips, base):
@@ -70,7 +63,7 @@
     if high is not None:
         keep = keep & (place < high - first_key)
     else:
-        value = value + tile_ref[own_index, t]
+        value = value + tile_ref[own_index, :, blk(t + 1, BQ)]
     return jnp.where(keep, value, MASKED)
 
 
@@ -85,7 +78,7 @@
 
         def k_block(j, carry):
             keys = blk(j, bk)
-            t = i * (BQ // bk) - j + (BQ // bk - 1)
+            t = i - j
             out = []
             for h in range(own):
                 top, total, acc = carry[h]
@@ -118,7 +111,7 @@
 
 
 def self_forward_kernel(own, bk, lim_ref, rows_ref, ext_ref, x_ref, o_ref, ot_ref, lse_ref, q_t, k_rows, v_t, tile_ref):
-    bias_tiles(ext_ref, tile_ref, own, bk)
+    bias_tiles(ext_ref, tile_ref, own)
     unpack(x_ref, own, 192, [(k_rows, 1)], [(q_t, 0), (v_t, 2)], 0)
     forward_body(own, bk, True, lim_ref, rows_ref, q_t, k_rows, v_t, tile_ref, o_ref, ot_ref, lse_ref)
 
@@ -153,7 +146,7 @@
 
         def k_block(j, carry):
             keys = blk(j, bk)
-            t = i * (BQ // bk) - j + (BQ // bk - 1)
+            t = i - j
             out = []
             for h in range(own):
                 query_t, grad_t, delta, lse = per_head[h]
@@ -164,7 +157,7 @@
                 dv[h, keys, :] += dot(p.astype(jnp.bfloat16), do_rows[h, cols, :])
                 dk[h, keys, :] += dot(ds, q_rows[h, cols, :])
                 if causal:
-                    sum_ref[h, t] += ds.astype(jnp.float32)
+                    sum_ref[h, :, blk(t, BQ)] += ds.astype(jnp.float32)
                 out.append(carry[h] + dot(k_t[h, :, keys], ds))
             return tuple(out)
 
@@ -181,30 +174,31 @@
     lax.fori_loop(0, length // BQ, q_block, 0)
 
 
-def diagonal_sums(sum_ref, u_ref, own, bk):
-    flip = (
-        lax.broadcasted_iota(jnp.int32, (bk, bk), 0) + lax.broadcasted_iota(jnp.int32, (bk, bk), 1) == bk - 1
-    ).astype(jnp.float32)
+def diagonal_sums(sum_ref, u_ref, own):
+    flip = lax.broadcasted_iota(jnp.int32, (BQ, BQ), 0) + lax.broadcasted_iota(jnp.int32, (BQ, BQ), 1) == BQ - 1
+    flip = jnp.where(flip, 1.0, 0.0).astype(jnp.bfloat16)
     for h in range(own):
-        for t in range(sum_ref.shape[1]):
-            upside = jnp.dot(flip, sum_ref[h, t], precision=HIGH, preferred_element_type=jnp.float32)
-            wide = jnp.concatenate([upside, jnp.zeros((bk, bk), jnp.float32)], axis=1)
-            aligned = pltpu.roll(wide, 0, 1, stride=1, stride_axis=0)
-            u_ref[h, t : t + 1, :] = jnp.sum(aligned, axis=0, keepdims=True)
+        grid = sum_ref[h]
+        high = grid.astype(jnp.bfloat16)
+        low = (grid - high.astype(jnp.float32)).astype(jnp.bfloat16)
+        upside = dot(flip, high) + dot(flip, low)
+        wide = jnp.concatenate([upside, jnp.zeros((BQ, BQ), jnp.float32)], axis=1)
+        aligned = pltpu.roll(wide, 0, 1, stride=1, stride_axis=0)
+        u_ref[h : h + 1, :] = jnp.sum(aligned, axis=0, keepdims=True)
 
 
 def self_backward_kernel(
     own, bk, lim_ref, rows_ref, ext_ref, x_ref, do_ref, ot_ref, lse_ref, dx_ref, u_ref,
     q_t, q_rows, k_t, k_rows, v_rows, do_t, do_rows, tile_ref, sum_ref, dq_t, dk, dv,
 ):
-    bias_tiles(ext_ref, tile_ref, own, bk)
+    bias_tiles(ext_ref, tile_ref, own)
     unpack(x_ref, own, 192, [(q_rows, 0), (k_rows, 1), (v_rows, 2)], [(q_t, 0), (k_t, 1)], 0)
     unpack(do_ref, own, 64, [(do_rows, 0)], [(do_t, 0)], 0)
     backward_body(
         own, bk, True, lim_ref, rows_ref, do_ref, ot_ref, lse_ref,
         q_t, q_rows, k_t, k_rows, v_rows, do_t, do_rows, tile_ref, sum_ref, dq_t, dk, dv,
     )
-    diagonal_sums(sum_ref, u_ref, own, bk)
+    diagonal_sums(sum_ref, u_ref, own)
 
     def pack(b, _):
         rows = blk(b, 256)
@@ -266,7 +260,7 @@
     )(*operands)
 
 
-def self_forward(limits, rows, ext, x, bk=256):
+def self_forward(limits, rows, ext, x, bk=BQ):
     length, own = x.shape[0], x.shape[1] // 192
     return call(
         functools.partial(self_forward_kernel, own, bk),
@@ -277,13 +271,13 @@
             ((own, 64, length), bf16),
             ((own, length, 64), bf16),
             ((own, 64, length), bf16),
-            ((own, tile_count(bk), bk, BQ), f32),
+            ((own, BQ, REACH + 2 * BQ), f32),
         ],
         length * length * own * 64,
     )
 
 
-def cross_forward(limits, rows, q, kv, bk=256):
+def cross_forward(limits, rows, q, kv, bk=BQ):
     length, own, keys = q.shape[0], q.shape[1] // 64, kv.shape[0]
     return call(
         functools.partial(cross_forward_kernel, own, bk),
@@ -295,13 +289,13 @@
     )
 
 
-def self_backward(limits, rows, ext, x, grad, o_t, lse, bk=256):
+def self_backward(limits, rows, ext, x, grad, o_t, lse, bk=BQ):
     length, own = x.shape[0], x.shape[1] // 192
     return call(
         functools.partial(self_backward_kernel, own, bk),
         "self_backward",
         [limits, rows, ext, x, grad, o_t, lse],
-        [((length, own * 192), bf16), ((own, tile_count(bk), BQ + bk), f32)],
+        [((length, own * 192), bf16), ((own, REACH + 2 * BQ), f32)],
         [
             ((own, 64, length), bf16),
             ((own, length, 64), bf16),
@@ -310,8 +304,8 @@
             ((own, length, 64), bf16),
             ((own, 64, length), bf16),
             ((own, length, 64), bf16),
-            ((own, tile_count(bk), bk, BQ), f32),
-            ((own, tile_count(bk), bk, BQ), f32),
+            ((own, BQ, REACH + 2 * BQ), f32),
+            ((own, BQ, REACH + BQ), f32),
             ((own * 64, length), f32),
             ((own, length, 64), f32),
             ((own, length, 64), f32),
@@ -320,7 +314,7 @@
     )
 
 
-def cross_backward(limits, rows, q, kv, grad, o_t, lse, bk=256):
+def cross_backward(limits, rows, q, kv, grad, o_t, lse, bk=BQ):
     length, own, keys = q.shape[0], q.shape[1] // 64, kv.shape[0]
     return call(
         functools.partial(cross_backward_kernel, own, bk),
@@ -816,13 +810,7 @@
     both_ids = change_home(jnp.pad(both_ids, (0, 1024 - local - enc_local)).reshape(8, 128))
     inner_t = ff_in.T
     by_kernel = (width // fan) % 128 == 0
-    both_ids, *halves = swap(
-        [jnp.broadcast_to(both_ids[None], (parts, 8, 128))], 13, tuple(range(fan)) if by_kernel else (), inner_t
-    )
-    if not by_kernel:
-        halves = spread(jnp.transpose(inner_t.reshape(2, fan, units, -1), (1, 0, 2, 3)))
-        halves = [jnp.transpose(halves[:, i], (1, 0, 2)).reshape(units, width) for i in range(2)]
-    gate_t, up_t = halves
+    (both_ids,) = swap([jnp.broadcast_to(both_ids[None], (parts, 8, 128))], 13)
     home = change_home(layer_in.reshape(rows, width))
     early = by_rows(early)
     mix_self = early[0].reshape(parts, own * dh, width)
@@ -841,7 +829,7 @@
     enc_first = counts_below(enc_ids, ids)
     enc_last = counts_below(enc_ids, ids + 1)
     blocks = length // BQ
-    bk = 256
+    bk = BQ
     self_rows = jnp.broadcast_to(first_seen[None], (8, length))
     cross_rows = jnp.concatenate([enc_first[None], enc_last[None], jnp.zeros((6, length), jnp.int32)])
     self_limits = jnp.stack(
@@ -858,8 +846,8 @@
         [jnp.full((own, BQ), MASKED, f32), bias, jnp.zeros((own, BQ), f32)], axis=1
     )
 
-    qkv_w, home, gate_t, ext, self_rows, cross_rows, self_limits, cross_limits = lax.optimization_barrier(
-        (qkv_w, home, gate_t, ext, self_rows, cross_rows, self_limits, cross_limits)
+    qkv_w, home, inner_t, ext, self_rows, cross_rows, self_limits, cross_limits = lax.optimization_barrier(
+        (qkv_w, home, inner_t, ext, self_rows, cross_rows, self_limits, cross_limits)
     )
     qkv_w = qkv_w.reshape(width, parts, own * 3 * dh)
 
@@ -868,7 +856,8 @@
     qkv_tok = jnp.einsum("td,dge->gte", normed_first, qkv_w, preferred_element_type=f32).astype(bf16)
     others = change_home(jnp.concatenate([cotangent.reshape(rows, width), encoder.reshape(-1, width)]))
     grad_low, enc_flat = others[:rows], others[rows:]
-    (qkv,) = swap([qkv_tok], 10)
+    fars = [tuple(far for far in range(fan) if by_kernel and min(far, 3) in some) for some in ((2,), (0, 1), (3,))]
+    qkv, *halves = swap([qkv_tok], 17, fars[0], inner_t)
     qkv, cross_out, grad_low = lax.optimization_barrier((qkv, cross_out, grad_low))
     if rows == cross_out.shape[0]:
         mix_cross, grad_group = lax.all_gather(jnp.stack([cross_out, grad_low]), "fsdp", axis=1, tiled=True)
@@ -885,10 +874,14 @@
         "td,sdge->sgte", enc_flat, pairs_w.reshape(2, width, parts // 2, -1), preferred_element_type=f32
     )
     pairs_tok = pairs_tok.astype(bf16).reshape(parts, enc_local, -1)
-    query_cross, pairs = swap([query_tok, pairs_tok], 12)
+    query_cross, pairs, *halves = swap([query_tok, pairs_tok], 15, fars[1], inner_t, halves)
     query_cross, pairs = query_cross.reshape(length, own * dh), pairs.reshape(keys, own * 2 * dh)
     out_cross, cross_t, cross_lse = cross_forward(cross_limits, cross_rows, query_cross, pairs)
-    (cross_tok,) = swap([out_cross.reshape(parts, local, own * dh)], 11)
+    cross_tok, *halves = swap([out_cross.reshape(parts, local, own * dh)], 16, fars[2], inner_t, halves)
+    if not by_kernel:
+        halves = spread(jnp.transpose(inner_t.reshape(2, fan, units, -1), (1, 0, 2, 3)))
+        halves = [jnp.transpose(halves[:, i], (1, 0, 2)).reshape(units, width) for i in range(2)]
+    gate_t, up_t = halves
     after_cross = after_self + jnp.einsum("gtc,gcd->td", cross_tok, mix_cross, preferred_element_type=f32)
     normed_third = norm_apply(after_cross, gain_third).astype(bf16)
     normed_group = gather(normed_third)
@@ -952,7 +945,7 @@
     part_mid = scatter(grad_mid)
     (grad_self,) = swap([grad_self_tok], 11)
     grad_self = grad_self.reshape(length, own * dh)
-    grad_qkv, tile_sums = self_backward(self_limits, self_rows, ext, qkv, grad_self, self_t, self_lse)
+    grad_qkv, diagonals = self_backward(self_limits, self_rows, ext, qkv, grad_self, self_t, self_lse)
     (grad_qkv_tok,) = swap([grad_qkv.reshape(parts, local, own * 3 * dh)], 10)
     grad_qkv_tok = flat(grad_qkv_tok)
     grad_qkv_w = jnp.einsum("td,te->de", normed_first, grad_qkv_tok, preferred_element_type=f32)
@@ -961,12 +954,9 @@
     grad_layer_in = (grad_upper + grad_from_first).astype(bf16)
     if not by_kernel:
         part_units = grad_units
-    bucket_line = jnp.concatenate(
-        [jnp.full((BQ,), -1, jnp.int32), near, jnp.full((BQ + bk,), -1, jnp.int32)]
-    )
-    by_tile = jnp.stack([bucket_line[t * bk + 1 : t * bk + 1 + BQ + bk] for t in range(tile_count(bk))])
-    in_bucket = (by_tile[:, :, None] == jnp.arange(buckets, dtype=jnp.int32)).astype(f32)
-    by_bucket = jnp.einsum("twn,gtw->ng", in_bucket, tile_sums, precision=HIGH)
+    bucket_line = jnp.concatenate([jnp.full((BQ - 1,), -1, jnp.int32), near, jnp.full((BQ + 1,), -1, jnp.int32)])
+    in_bucket = (bucket_line[:, None] == jnp.arange(buckets, dtype=jnp.int32)).astype(f32)
+    by_bucket = jnp.einsum("xn,gx->ng", in_bucket, diagonals, precision=HIGH)
     grad_table = lax.dynamic_update_slice_in_dim(jnp.zeros((buckets, heads), f32), by_bucket, first_head, 1)
 
     gains = jnp.concatenate(

time: 688 us -> 670 us (0.974)
  Pallas kernels: 401 us -> 384 us
    pallas_call x9, Pallas kernels: 155 us -> 144 us  [swap(): pl.pallas_call(functools.partial(swap_kernel, n, fan, count, fars, not fa...]
    pallas_call x4, Pallas kernels: 59.6 us -> 51 us  [call(): pl.pallas_call(body, name=name, out_shape=[jax.ShapeDtypeStruct(s, d) for...]
    unnamed x163 -> x159, local copies, waits for them, and re-layouts: 40.5 us -> 39.6 us
  transfers between devices with their start and end apart: 12 -> 12, of which waited for: 4 -> 5; matrix products, arithmetic and copies ran while one was open for 16% -> 16% of each run, Pallas kernels for 54% -> 53%
where the time goes in v9:
time: 670 us; the launch traced here: 663 us
  Pallas kernels  384 us (57%)
  matrix products  75.2 us (11%)
  local copies, waits for them, and re-layouts  64.4 us (10%)
  waiting for transfers between devices  45.8 us (7%)
  other arithmetic  35.7 us (5%)
  starting transfers between devices  29.3 us (4%)
  between operations  15.5 us (2%)
  blocking collectives  12.9 us (2%)
    pallas_call x2, Pallas kernels, ring_call(): pl.pallas_call(body, name=name, out_shape=[jax.ShapeDtypeStruct(s, d) for...  188 us
    pallas_call x9, Pallas kernels, swap(): pl.pallas_call(functools.partial(swap_kernel, n, fan, count, fars, not fa...  144 us
    pallas_call x4, Pallas kernels, call(): pl.pallas_call(body, name=name, out_shape=[jax.ShapeDtypeStruct(s, d) for...  51 us
    unnamed x159, local copies, waits for them, and re-layouts  39.6 us
    ppermute x5, starting transfers between devices, change_home(): return lax.ppermute(value, ('seq', 'fsdp'), pairs)  27.8 us
    reduce_scatter x3, waiting for transfers between devices, scatter(): return lax.psum_scatter(grad, 'fsdp', scatter_dimension=0, tiled=True)  21.7 us
    all_gather x2, waiting for transfers between devices, shards(): gather = lambda v: lax.all_gather(v, 'fsdp', axis=0, tiled=True)  15.1 us
  transfers between devices with their start and end apart: 12, of which 5 were waited for; matrix products, arithmetic and copies ran while one was open for 16% of the time, Pallas kernels for 53%

profile of v9, /device:TPU:1, one launch (start us, length us, event | category | flops | bytes accessed | tf_op | source)
XLA Modules:
  0.0 662.6 jit_solution(6219520916287163398)
XLA Ops:
  9.6 6.1 all-gather.1
  18.5 4.9 collective-permute-start
  36.1 7.1 %collective-permute-done.1 = s32[8,128]{1,0:T(8,128)S(1)} collective-permute-done((s32[8,128]{1,0:T(8,128)S(1)}, s32[8,128]{1,0:T(8,128)S(1)}, u32[]{:S(2)}, u32[]{:S(2)}) %collective-permute-start.1) | collective-permute-done | bytes 4128 | tf_op jit(solution)/shard_map/ppermute | solution.py:745
  43.8 8.0 %swap.9 = s32[8,8,128]{2,1,0:T(8,128)} custom-call(s32[8,8,128]{2,1,0:T(8,128)} %broadcast_in_dim.101.refs_0_), custom_call_target="tpu_custom_call" | custom-call | bytes 16384 | tf_op jit(solution)/shard_map/swap/pallas_call | solution.py:704
  56.5 5.2 fusion.62
  63.3 5.8 fusion.17.refs_0_
  69.2 34.6 %swap.10 = (bf16[8,256,384]{2,1,0:T(8,128)(2,1)}, bf16[704,1024]{1,0:T(8,128)(2,1)}, bf16[704,1024]{1,0:T(8,128)(2,1)}) custom-call(bf16[8,256,384]{2,1,0:T(8,128)(2,1)} %fusion.17.refs_0_, bf16[5632,256]{1,0:T(8,128)(2,1)} %bitcast.235), custom_call_target="tpu_custom_call" | custom-call | bytes 1572864 | tf_op jit(solution)/shard_map/swap/pallas_call | solution.py:704
  106.6 15.4 %self_forward.1 = (bf16[2048,128]{1,0:T(8,128)(2,1)S(1)}, f32[128,2048]{1,0:T(8,128)S(1)}, f32[2,2048]{1,0:T(2,128)S(1)}) custom-call(s32[2,8]{1,0:T(2,128)S(1)} %pad_add_fusion.1.lim_ref, s32[8,2048]{1,0:T(8,128)S(1)} %broadcast_in_dim.106.rows_ref, f32[2,1536]{1,0:T(2,128)S(1)} %maximum_maximum_fusion.ext_ref, bf16[2048,384]{1,0:T(8,128)(2,1)S(1)} %bitcast.222), custom_call_target="tpu_custom_call" | custom-call | bytes 1650752 | tf_op jit(solution)/shard_map/self_forward/pallas_call | solution.py:251
  123.8 10.2 %swap.11 = bf16[8,256,128]{2,1,0:T(8,128)(2,1)} custom-call(bf16[8,256,128]{2,1,0:T(8,128)(2,1)} %bitcast.233), custom_call_target="tpu_custom_call" | custom-call | bytes 524288 | tf_op jit(solution)/shard_map/swap/pallas_call | solution.py:704
  135.2 4.7 fusion.72
  153.2 22.5 %swap.12 = (bf16[8,256,128]{2,1,0:T(8,128)(2,1)}, bf16[8,64,256]{2,1,0:T(8,128)(2,1)}, bf16[704,1024]{1,0:T(8,128)(2,1)}, bf16[704,1024]{1,0:T(8,128)(2,1)}) custom-call(bf16[8,256,128]{2,1,0:T(8,128)(2,1)} %fusion.23.refs_0_, bf16[8,64,256]{2,1,0:T(8,128)(2,1)} %bitcast.273, ...), custom_call_target="tpu_custom_call", output_to_operand_aliasing={{2}: (3, {}), {3}: (4, {})} | custom-call | bytes 786432 | tf_op jit(solution)/shard_map/swap/pallas_call | solution.py:704
  177.7 7.9 %cross_forward.1 = (bf16[2048,128]{1,0:T(8,128)(2,1)S(1)}, f32[128,2048]{1,0:T(8,128)S(1)}, f32[2,2048]{1,0:T(2,128)S(1)}) custom-call(s32[2,8]{1,0:T(2,128)S(1)} %pad_add_fusion.2.lim_ref, s32[8,2048]{1,0:T(8,128)S(1)} %add_add_fusion.3.rows_ref, bf16[2048,128]{1,0:T(8,128)(2,1)S(1)} %bitcast.224, bf16[512,256]{1,0:T(8,128)(2,1)S(1)} %bitcast.229), custom_call_target="tpu_custom_call" | custom-call | bytes 852032 | tf_op jit(solution)/shard_map/cross_forward/pallas_call | solution.py:251
  187.4 16.0 %swap.13 = (bf16[8,256,128]{2,1,0:T(8,128)(2,1)}, bf16[704,1024]{1,0:T(8,128)(2,1)}, bf16[704,1024]{1,0:T(8,128)(2,1)}) custom-call(bf16[8,256,128]{2,1,0:T(8,128)(2,1)} %bitcast.231, bf16[5632,256]{1,0:T(8,128)(2,1)} %bitcast.237, bf16[704,1024]{1,0:T(8,128)(2,1)} %get-tuple-element.91.refs_2_, ...), custom_call_target="tpu_custom_call", output_to_operand_aliasing={{1}: (2, {}), {2}: (3, {})} | custom-call | bytes 524288 | tf_op jit(solution)/shard_map/swap/pallas_call | solution.py:704
  210.4 4.9 fusion.15
  215.3 15.1 %all-gather.13.cloned.1.call-done = bf16[1024,1024]{1,0:T(8,128)(2,1)} async-done(((bf16[256,1024]{1,0:T(8,128)(2,1)}), bf16[1024,1024]{1,0:T(8,128)(2,1)}) %all-gather.13.cloned.1.call-update) | async-done | bytes 2097168 | tf_op jit(solution)/shard_map/all_gather | solution.py:796
  234.4 4.7 multiply_convert_fusion
  244.9 4.7 convolution_convert_fusion.5.part_ref
  258.4 17.0 %reduce-scatter.4.cloned.1.call-done = bf16[256,1024]{1,0:T(8,128)(2,1)} async-done(((bf16[1024,1024]{1,0:T(8,128)(2,1)}), bf16[256,1024]{1,0:T(8,128)(2,1)}) %reduce-scatter.4.cloned.1.call-update) | async-done | bytes 524304 | tf_op jit(solution)/shard_map/reduce_scatter | solution.py:767
  281.1 10.1 %swap.14 = bf16[8,256,128]{2,1,0:T(8,128)(2,1)} custom-call(bf16[8,256,128]{2,1,0:T(8,128)(2,1)} %fusion.24.refs_0_), custom_call_target="tpu_custom_call" | custom-call | bytes 524288 | tf_op jit(solution)/shard_map/swap/pallas_call | solution.py:704
  293.5 9.5 %cross_backward.1 = (bf16[2048,128]{1,0:T(8,128)(2,1)S(1)}, bf16[512,256]{1,0:T(8,128)(2,1)S(1)}) custom-call(s32[2,8]{1,0:T(2,128)S(1)} %pad_add_fusion.2.lim_ref, s32[8,2048]{1,0:T(8,128)S(1)} %add_add_fusion.3.rows_ref, bf16[2048,128]{1,0:T(8,128)(2,1)S(1)} %bitcast.225, bf16[512,256]{1,0:T(8,128)(2,1)S(1)} %bitcast.230, bf16[2048,128]{1,0:T(8,128)(2,1)S(1)} %bitcast.226, ...), custom_call_target="tpu_custom_call" | custom-call | bytes 2441280 | tf_op jit(solution)/shard_map/cross_backward/pallas_call | solution.py:251
  304.5 11.9 %swap.15 = (bf16[8,256,128]{2,1,0:T(8,128)(2,1)}, bf16[8,64,256]{2,1,0:T(8,128)(2,1)}) custom-call(bf16[8,256,128]{2,1,0:T(8,128)(2,1)} %bitcast.232, bf16[8,64,256]{2,1,0:T(8,128)(2,1)} %bitcast.234), custom_call_target="tpu_custom_call" | custom-call | bytes 786432 | tf_op jit(solution)/shard_map/swap/pallas_call | solution.py:704
  330.2 6.1 pad_maximum_fusion
  336.5 9.6 %swap.16 = bf16[8,256,128]{2,1,0:T(8,128)(2,1)} custom-call(bf16[8,256,128]{2,1,0:T(8,128)(2,1)} %fusion.25.refs_0_), custom_call_target="tpu_custom_call" | custom-call | bytes 524288 | tf_op jit(solution)/shard_map/swap/pallas_call | solution.py:704
  347.2 18.2 %self_backward.1 = (bf16[2048,384]{1,0:T(8,128)(2,1)S(1)}, f32[2,1536]{1,0:T(2,128)S(1)}) custom-call(s32[2,8]{1,0:T(2,128)S(1)} %pad_add_fusion.1.lim_ref, s32[8,2048]{1,0:T(8,128)S(1)} %broadcast_in_dim.106.rows_ref, f32[2,1536]{1,0:T(2,128)S(1)} %maximum_maximum_fusion.ext_ref, bf16[2048,384]{1,0:T(8,128)(2,1)S(1)} %bitcast.223, ...), custom_call_target="tpu_custom_call" | custom-call | bytes 3240000 | tf_op jit(solution)/shard_map/self_backward/pallas_call | solution.py:251
  366.6 21.4 %swap.17 = bf16[8,256,384]{2,1,0:T(8,128)(2,1)} custom-call(bf16[8,256,384]{2,1,0:T(8,128)(2,1)} %bitcast.228), custom_call_target="tpu_custom_call" | custom-call | bytes 1572864 | tf_op jit(solution)/shard_map/swap/pallas_call | solution.py:704
  390.5 5.7 fusion.32
  396.2 6.8 %psum.7 = bf16[4,896]{1,0:T(4,128)(2,1)S(1)} all-reduce(bf16[4,896]{1,0:T(4,128)(2,1)S(1)} %pad_maximum_fusion.6), channel_id=1, replica_groups=mesh['seq'=8,'fsdp'=4] {'fsdp'}, use_global_device_ids=true, to_apply=%region_18.19 | all-reduce | flops 3584 | bytes 14336 | tf_op jit(solution)/shard_map/psum | solution.py:966
  422.1 4.9 collective-permute-start.3
  426.9 108.0 %units_total.1 = (bf16[5632,256]{1,0:T(8,128)(2,1)}, bf16[704,1024]{1,0:T(8,128)(2,1)S(1)}, f32[256,1024]{1,0:T(8,128)S(1)}) custom-call(bf16[2112,1024]{1,0:T(8,128)(2,1)} %bitcast.247, bf16[1024,1024]{1,0:T(8,128)(2,1)S(1)} %copy-done.5), custom_call_target="tpu_custom_call" | custom-call | bytes 385351680 | tf_op jit(solution)/shard_map/units_total/pallas_call | solution.py:434
  538.4 80.5 %ring_total.1 = (bf16[256,5120]{1,0:T(8,128)(2,1)S(1)}, bf16[256,3072]{1,0:T(8,128)(2,1)S(1)}, bf16[64,128]{1,0:T(8,128)(2,1)S(1)}) custom-call(bf16[256,5120]{1,0:T(8,128)(2,1)} %reduce-scatter.6.cloned.1.call-done.refs_0_, bf16[256,3072]{1,0:T(8,128)(2,1)S(1)} %copy-done.11, bf16[64,128]{1,0:T(8,128)(2,1)S(1)} %pad_bitcast_fusion.refs_2_), custom_call_target="tpu_custom_call" | custom-call | bytes 252641280 | tf_op jit(solution)/shard_map/ring_total/pallas_call | solution.py:434
  622.0 11.6 %collective-permute-start.4 = (bf16[256,1024]{1,0:T(8,128)(2,1)}, bf16[256,1024]{1,0:T(8,128)(2,1)S(1)}, u32[]{:S(2)}, u32[]{:S(2)}) collective-permute-start(bf16[256,1024]{1,0:T(8,128)(2,1)} %add_convert_fusion.1), channel_id=1, source_target_pairs={{0,0},{1,16},{2,2},{3,18},{4,4},{5,20},{6,6},{7,22},{8,8},{9,24},{... | collective-permute-start | bytes 1572872 | tf_op jit(solution)/shard_map/ppermute | solution.py:745
  643.8 6.3 copy.119
  (284 shorter events, 141.8 us)
Async XLA Ops:
  7.2 203.2 %copy-start = (bf16[704,1024]{1,0:T(8,128)(2,1)S(1)}, bf16[704,1024]{1,0:T(8,128)(2,1)}, u32[]{:S(2)}) copy-start(bf16[704,1024]{1,0:T(8,128)(2,1)} %param.32) | copy-start | bytes 4325380
  7.2 8.5 %copy-start.52 = (bf16[256,16,128]{2,1,0:T(8,128)(2,1)S(1)}, bf16[256,16,128]{2,1,0:T(8,128)(2,1)}, u32[]{:S(2)}) copy-start(bf16[256,16,128]{2,1,0:T(8,128)(2,1)} %param.28) | copy-start | bytes 3145732
  7.2 55.9 %all-gather.7.cloned.1.call-start = ((), (), s32[]{:S(2)}) async-start(), calls=%async_computation.3 | async-start | bytes 7864320 | tf_op jit(solution)/shard_map/all_gather | solution.py:796
  7.9 127.2 %all-gather.9.cloned.1.call-start = ((), (), s32[]{:S(2)}) async-start(), calls=%async_computation.4 | async-start | bytes 10485760 | tf_op jit(solution)/shard_map/all_gather | solution.py:808
  18.4 5.0 copy-start.60
  18.4 5.0 copy-start.61
  18.4 6.9 %copy-start.54 = (bf16[1,256,1024]{2,1,0:T(8,128)(2,1)S(1)}, bf16[1,256,1024]{2,1,0:T(8,128)(2,1)}, u32[]{:S(2)}) copy-start(bf16[1,256,1024]{2,1,0:T(8,128)(2,1)} %param.33) | copy-start | bytes 1572868
  18.4 6.9 %copy-start.58 = (bf16[1,64,1024]{2,1,0:T(8,128)(2,1)S(1)}, bf16[1,64,1024]{2,1,0:T(8,128)(2,1)}, u32[]{:S(2)}) copy-start(bf16[1,64,1024]{2,1,0:T(8,128)(2,1)} %param.18) | copy-start | bytes 393220
  18.4 12.4 %copy-start.59 = (s32[2048]{0:T(1024)S(1)}, s32[2048]{0:T(1024)}, u32[]{:S(2)}) copy-start(s32[2048]{0:T(1024)} %param.21) | copy-start | bytes 24580
  18.5 184.9 %all-gather.11.cloned.1.call-start = ((), (), s32[]{:S(2)}) async-start(), calls=%async_computation.5 | async-start | bytes 5242880 | tf_op jit(solution)/shard_map/all_gather | solution.py:863
  18.5 44.6 %collective-permute-start = (bf16[256,1024]{1,0:T(8,128)(2,1)}, bf16[256,1024]{1,0:T(8,128)(2,1)S(1)}, u32[]{:S(2)}, u32[]{:S(2)}) collective-permute-start(bf16[256,1024]{1,0:T(8,128)(2,1)} %bitcast), channel_id=1, source_target_pairs={{0,0},{1,16},{2,2},{3,18},{4,4},{5,20},{6,6},{7,22},{8,8},{9,24},{... | collective-permute-start | bytes 1572872 | tf_op jit(solution)/shard_map/ppermute | solution.py:745
  23.4 19.7 %collective-permute-start.1 = (s32[8,128]{1,0:T(8,128)S(1)}, s32[8,128]{1,0:T(8,128)S(1)}, u32[]{:S(2)}, u32[]{:S(2)}) collective-permute-start(s32[8,128]{1,0:T(8,128)S(1)} %pad_bitcast_fusion.1), channel_id=1, source_target_pairs={{0,0},{1,16},{2,2},{3,18},{4,4},{5,20},{6,6},{7,22},{8,8},{9,24},{... | collective-permute-start | bytes 12296 | tf_op jit(solution)/shard_map/ppermute | solution.py:745
  26.3 36.0 %collective-permute-start.2 = (bf16[320,1024]{1,0:T(8,128)(2,1)}, bf16[320,1024]{1,0:T(8,128)(2,1)S(1)}, u32[]{:S(2)}, u32[]{:S(2)}) collective-permute-start(bf16[320,1024]{1,0:T(8,128)(2,1)} %pad_maximum_fusion.4), channel_id=1, source_target_pairs={{0,0},{1,16},{2,2},{3,18},{4,4},{5,20},{6,6},{7,22},{8,8},{9,24},{... | collective-permute-start | bytes 1966088 | tf_op jit(solution)/shard_map/ppermute | solution.py:745
  62.2 6.9 %copy-start.53 = (bf16[320,1024]{1,0:T(8,128)(2,1)}, bf16[320,1024]{1,0:T(8,128)(2,1)S(1)}, u32[]{:S(2)}) copy-start(bf16[320,1024]{1,0:T(8,128)(2,1)S(1)} %collective-permute-done.2) | copy-start | bytes 1966084
  63.1 6.0 copy-start.36
  106.2 124.2 %all-gather.13.cloned.1.call-start = ((), (), s32[]{:S(2)}) async-start(), calls=%async_computation.6 | async-start | bytes 2621440 | tf_op jit(solution)/shard_map/all_gather | solution.py:796
  145.9 4.8 slice-start
  210.0 65.4 %reduce-scatter.4.cloned.1.call-start = ((), (), s32[]{:S(2)}) async-start(), calls=%async_computation.7 | async-start | bytes 2621440 | tf_op jit(solution)/shard_map/reduce_scatter | solution.py:767
  244.3 177.8 %reduce-scatter.6.cloned.1.call-start = ((), (), s32[]{:S(2)}) async-start(), calls=%async_computation.8 | async-start | bytes 13107200 | tf_op jit(solution)/shard_map/reduce_scatter | solution.py:767
  255.6 19.8 %copy-start.26 = (f32[256,1024]{1,0:T(8,128)S(1)}, f32[256,1024]{1,0:T(8,128)}, u32[]{:S(2)}) copy-start(f32[256,1024]{1,0:T(8,128)} %copy-done.25) | copy-start | bytes 3145732
  279.5 11.7 %copy-start.7 = (bf16[8,256,128]{2,1,0:T(8,128)(2,1)S(1)}, bf16[8,256,128]{2,1,0:T(8,128)(2,1)}, u32[]{:S(2)}) copy-start(bf16[8,256,128]{2,1,0:T(8,128)(2,1)} %get-tuple-element.88) | copy-start | bytes 1572868
  279.5 11.7 %copy-start.20 = (bf16[8,64,256]{2,1,0:T(8,128)(2,1)S(1)}, bf16[8,64,256]{2,1,0:T(8,128)(2,1)}, u32[]{:S(2)}) copy-start(bf16[8,64,256]{2,1,0:T(8,128)(2,1)} %get-tuple-element.89) | copy-start | bytes 786436
  336.3 9.7 %copy-start.16 = (f32[128,2048]{1,0:T(8,128)S(1)}, f32[128,2048]{1,0:T(8,128)}, u32[]{:S(2)}) copy-start(f32[128,2048]{1,0:T(8,128)} %copy-done.15) | copy-start | bytes 3145732
  336.3 200.6 %reduce-scatter.8.cloned.1.call-start = ((), (), s32[]{:S(2)}) async-start(), calls=%async_computation.9 | async-start | bytes 7864320 | tf_op jit(solution)/shard_map/reduce_scatter | solution.py:767
  403.1 4.9 copy-start.33
  403.1 4.9 copy-start.43
  422.0 4.9 copy-start.5
  422.1 113.9 %copy-start.27 = (f32[256,1024]{1,0:T(8,128)S(1)}, f32[256,1024]{1,0:T(8,128)}, u32[]{:S(2)}) copy-start(f32[256,1024]{1,0:T(8,128)} %copy-done.25) | copy-start | bytes 3145732
  422.1 198.0 %collective-permute-start.3 = (bf16[320,1024]{1,0:T(8,128)(2,1)}, bf16[320,1024]{1,0:T(8,128)(2,1)S(1)}, u32[]{:S(2)}, u32[]{:S(2)}) collective-permute-start(bf16[320,1024]{1,0:T(8,128)(2,1)} %pad_maximum_fusion.5), channel_id=1, source_target_pairs={{0,0},{1,16},{2,2},{3,18},{4,4},{5,20},{6,6},{7,22},{8,8},{9,24},{... | collective-permute-start | bytes 1966088 | tf_op jit(solution)/shard_map/ppermute | solution.py:745
  620.0 17.4 %copy-start.2 = (bf16[256,5120]{1,0:T(8,128)(2,1)}, bf16[256,5120]{1,0:T(8,128)(2,1)S(1)}, u32[]{:S(2)}) copy-start(bf16[256,5120]{1,0:T(8,128)(2,1)S(1)} %get-tuple-element.129) | copy-start | bytes 7864324
  622.0 32.7 %collective-permute-start.4 = (bf16[256,1024]{1,0:T(8,128)(2,1)}, bf16[256,1024]{1,0:T(8,128)(2,1)S(1)}, u32[]{:S(2)}, u32[]{:S(2)}) collective-permute-start(bf16[256,1024]{1,0:T(8,128)(2,1)} %add_convert_fusion.1), channel_id=1, source_target_pairs={{0,0},{1,16},{2,2},{3,18},{4,4},{5,20},{6,6},{7,22},{8,8},{9,24},{... | collective-permute-start | bytes 1572872 | tf_op jit(solution)/shard_map/ppermute | solution.py:745
  643.8 6.3 copy-start.14
  (51 other events, 107.1 us)
Sparse Core Ops, SparseCore 0:
  9.6 49.7 all-gather.6
  61.5 73.6 all-gather.8
  137.3 40.3 all-gather.10
  210.1 20.2 all-gather.12
  244.4 31.0 reduce-scatter.3
  336.4 85.5 reduce-scatter.5
  424.7 65.3 reduce-scatter.7

commit v10 on v9

--- a/solution.py
+++ b/solution.py
@@ -377,10 +377,12 @@
     return ref.at[pl.ds(chunk * whole + piece * rows, rows), :]
 
 
-def ring_kernel(n, splits, *refs):
+def ring_kernel(n, splits, fan, *refs):
     count = len(splits)
-    x_refs, y_refs, slots = refs[:count], refs[count : 2 * count], refs[2 * count : 3 * count]
-    send_sem, recv_sem = refs[3 * count :]
+    more = 1 if fan else 0
+    x_refs, y_refs = refs[:count], refs[count + more : 2 * count + more]
+    slots = refs[2 * (count + more) : 3 * count + 2 * more]
+    send_sem, recv_sem = refs[3 * count + 2 * more :]
     place, right, left = ring_greet(n, [])
     streams = [(k, piece, piece % 2) for k in range(count) for piece in range(abs(splits[k]))]
 
@@ -403,9 +405,25 @@
         )
         copies[number, step].start()
 
+    def turn_block(number):
+        inner_ref, turned_ref = refs[count], refs[2 * count + 1]
+        rows = inner_ref.shape[0] // (2 * fan * n)
+        half, first = number // (fan // 2), number % (fan // 2) * 2
+        tall = jnp.concatenate(
+            [
+                inner_ref[pl.ds(((chunk * fan + group) * 2 + half) * rows, rows), :].astype(jnp.float32)
+                for group in (first, first + 1)
+                for chunk in range(n)
+            ]
+        )
+        wide = 2 * n * rows
+        turned_ref[:, number * wide : (number + 1) * wide] = jnp.transpose(tall, (1, 0))
+
     for number, (k, piece, down) in enumerate(streams):
         start(number, 0, window(x_refs[k], k, piece, place), window(slots[k], k, piece, 0), down)
     for step in range(n - 1):
+        if step < fan:
+            turn_block(step)
         for number, (k, piece, down) in enumerate(streams):
             copies[number, step].wait_recv()
             chunk = chunk_at(down, step)
@@ -445,14 +463,15 @@
     )(*arrays)
 
 
-def ring_total(arrays, splits, ident):
-    n = lax.axis_size("seq")
+def ring_total(arrays, splits, ident, inner=None):
+    n, fan = lax.axis_size("seq"), lax.axis_size("fsdp")
     streams = sum(abs(s) for s in splits)
+    more = [] if inner is None else [inner]
     return ring_call(
-        functools.partial(ring_kernel, n, splits),
+        functools.partial(ring_kernel, n, splits, 0 if inner is None else fan),
         "ring_total",
-        arrays,
-        [(v.shape, jnp.bfloat16) for v in arrays],
+        arrays + more,
+        [(v.shape, jnp.bfloat16) for v in arrays] + [(v.shape[::-1], jnp.float32) for v in more],
         [pltpu.VMEM((v.shape[0] // n * (n - 1), v.shape[1]), jnp.bfloat16) for v in arrays]
         + [pltpu.SemaphoreType.DMA((streams, 2 * n - 2))] * 2,
         ident,
@@ -460,7 +479,7 @@
 
 
 def units_kernel(
-    n, fan, x_ref, part_ref, inner_ref, outer_ref, sum_ref, slots, acc, landed,
+    n, fan, x_ref, part_ref, few_ref, inner_ref, outer_ref, sum_ref, few_sum_ref, slots, acc, landed, few_landed,
     down_send, down_recv, swap_send, swap_recv, own_sem, send_sem, recv_sem, part_send, part_recv,
 ):
     s, me = lax.axis_index("seq"), lax.axis_index("fsdp")
@@ -468,20 +487,21 @@
     cols = width // fan
     block = 2 * fan * rows
     place, right, left = ring_greet(n, [(me + far) % fan for far in range(1, fan)])
-    tokens = sum_ref.shape[0]
     parts = []
     for far in range(1, fan):
         target = (me + far) % fan
-        one = pltpu.make_async_remote_copy(
-            src_ref=part_ref.at[pl.ds(target * tokens, tokens), :],
-            dst_ref=landed.at[far],
-            send_sem=part_send.at[far],
-            recv_sem=part_recv.at[far],
-            device_id={"fsdp": target},
-            device_id_type=MESH,
-        )
-        one.start()
-        parts.append(one)
+        for which, (src, into) in enumerate(((part_ref, landed), (few_ref, few_landed))):
+            rest = src.shape[0] // fan
+            one = pltpu.make_async_remote_copy(
+                src_ref=src.at[pl.ds(target * rest, rest), :],
+                dst_ref=into.at[far],
+                send_sem=part_send.at[which, far],
+                recv_sem=part_recv.at[which, far],
+                device_id={"fsdp": target},
+                device_id_type=MESH,
+            )
+            one.start()
+            parts.append(one)
 
     sums = {}
 
@@ -556,29 +576,39 @@
         )
         copies[k, piece, step].start()
 
+    def forward(k, step):
+        for piece in range(2):
+            copies[k, piece, step].wait_recv()
+            if step < n - 2:
+                start(k, piece, step + 1)
+
     mine.wait()
     start(0, 0, 0)
     start(0, 1, 0)
+    lead = (n - 1) // 2
+    for step in range(lead):
+        forward(0, step)
     for one in moves:
         one.wait()
     start(1, 0, 0)
     start(1, 1, 0)
     for step in range(n - 1):
-        for k in range(2):
-            for piece in range(2):
-                copies[k, piece, step].wait_recv()
-                if step < n - 2:
-                    start(k, piece, step + 1)
-    total = part_ref[pl.ds(pl.multiple_of(me * tokens, tokens), tokens), :].astype(jnp.float32)
-    for far in range(1, fan):
-        parts[far - 1].wait()
-        total = total + landed[far].astype(jnp.float32)
-    sum_ref[...] = total
+        forward(1, step)
+        if lead + step < n - 1:
+            forward(0, lead + step)
+    for one in parts:
+        one.wait()
+    for src, into, out in ((part_ref, landed, sum_ref), (few_ref, few_landed, few_sum_ref)):
+        rest = src.shape[0] // fan
+        total = src[pl.ds(pl.multiple_of(me * rest, rest), rest), :].astype(jnp.float32)
+        for far in range(1, fan):
+            total = total + into[far].astype(jnp.float32)
+        out[...] = total
     for one in [*copies.values(), *sums.values()]:
         one.wait_send()
 
 
-def units_total(grads, part, ident):
+def units_total(grads, part, few, ident):
     n, fan = lax.axis_size("seq"), lax.axis_size("fsdp")
     rows, width = grads.shape[0] // (3 * n), grads.shape[1]
     tokens = part.shape[0] // fan
@@ -586,19 +616,21 @@
     return ring_call(
         functools.partial(units_kernel, n, fan),
         "units_total",
-        [grads, part],
+        [grads, part, few],
         [
             ((n * 2 * fan * rows, width // fan), jnp.bfloat16),
             ((n * rows, width), jnp.bfloat16),
             ((tokens, part.shape[1]), jnp.float32),
+            ((few.shape[0] // fan, few.shape[1]), jnp.float32),
         ],
         [
             pltpu.VMEM(((n - 1) * 3 * rows, width), jnp.bfloat16),
             pltpu.VMEM((3 * rows, width), jnp.bfloat16),
             pltpu.VMEM((fan, tokens, part.shape[1]), jnp.bfloat16),
+            pltpu.VMEM((fan, few.shape[0] // fan, few.shape[1]), jnp.bfloat16),
         ]
         + [sems(fan, n - 1), sems(fan, n - 1), sems(fan, 2), sems(fan, 2), sems(3)]
-        + [sems(4, n - 1), sems(4, n - 1), sems(fan), sems(fan)],
+        + [sems(4, n - 1), sems(4, n - 1), sems(2, fan), sems(2, fan)],
         ident,
     )
 
@@ -767,18 +799,6 @@
     return lax.psum_scatter(grad, "fsdp", scatter_dimension=0, tiled=True)
 
 
-def over_seq(arrays, splits, ident):
-    n = lax.axis_size("seq")
-    if all(
-        v.shape[0] % (8 * n) == 0
-        and ring_cut(v.shape, s, n)[0] % 8 == 0
-        and v.shape[1] % (128 * max(s, 1)) == 0
-        for v, s in zip(arrays, splits)
-    ):
-        return ring_total(arrays, splits, ident)
-    return [lax.psum(v, "seq") for v in arrays]
-
-
 def shards(
     layer_in, encoder, decoder_ids, encoder_ids, rel_buckets,
     norm_self, self_qkv, self_out, rel_table, norm_cross, cross_q, cross_kv, cross_out, norm_ff, ff_in, ff_out,
@@ -809,7 +829,7 @@
     both_ids = jnp.concatenate([decoder_ids.reshape(-1), encoder_ids.reshape(-1)])
     both_ids = change_home(jnp.pad(both_ids, (0, 1024 - local - enc_local)).reshape(8, 128))
     inner_t = ff_in.T
-    by_kernel = (width // fan) % 128 == 0
+    by_kernel = (width // fan) % 128 == 0 and fan % 2 == 0 and (ff_in.shape[0] // parts) % 8 == 0
     (both_ids,) = swap([jnp.broadcast_to(both_ids[None], (parts, 8, 128))], 13)
     home = change_home(layer_in.reshape(rows, width))
     early = by_rows(early)
@@ -963,10 +983,8 @@
         [g.reshape(-1, part) for g in (grad_gain_first, grad_gain_second, grad_gain_third)], axis=1
     )
     tables = jnp.transpose(grad_table.reshape(buckets, -1, table_own), (1, 0, 2)).reshape(-1, buckets * table_own)
-    small_grads = lax.psum(jnp.concatenate([gains, tables], axis=1).astype(bf16), "fsdp")
-    small_grads = lax.dynamic_index_in_dim(small_grads, lax.axis_index("fsdp"), 0, False)
-    small_size = small_grads.shape[0]
-    small_grads = jnp.pad(small_grads, (0, parts * 1024 - small_size)).reshape(parts * 8, 128)
+    small_grads = jnp.concatenate([gains, tables], axis=1).astype(bf16)
+    small_size = small_grads.shape[1]
     going_home = jnp.concatenate([grad_layer_in, grad_encoder.astype(bf16)])
     going_home, small_grads, grad_qkv_w, part_units, part_mid = lax.optimization_barrier(
         (going_home, small_grads, grad_qkv_w.astype(bf16), part_units, part_mid)
@@ -974,12 +992,19 @@
     part_last = scatter(grad_qkv_w)
     going_home = change_home(going_home)
     if by_kernel:
-        total_inner, total_outer, outer_sum = units_total(part_units, outer_part, 0)
+        few = jnp.pad(small_grads[:, None], ((0, 0), (0, 7), (0, 1024 - small_size))).reshape(fan * 8, 1024)
+        total_inner, total_outer, outer_sum, few = units_total(part_units, outer_part, few, 0)
+        few = jnp.pad(few[0].astype(bf16).reshape(8, 128), ((0, parts * 8 - 8), (0, 0)))
+        total_mid, total_qkv, small_total, total_inner = ring_total(
+            [part_mid, part_last, few], (2, 2, 1), 1, total_inner
+        )
     else:
-        grad_units = [lax.psum(g, "seq") for g in grad_units]
+        grad_units = [lax.psum(g, "seq") for g in part_units]
         total_inner = spread(jnp.transpose(jnp.stack(grad_units[:2]).reshape(2, units, fan, -1), (2, 0, 1, 3)))
+        total_inner = jnp.transpose(total_inner, (3, 1, 0, 2)).reshape(-1, 2 * fan * units).astype(f32)
         total_outer, outer_sum = grad_units[2], scatter(outer_part).astype(f32)
-    total_mid, total_qkv, small_total = over_seq([part_mid, part_last, small_grads], (2, 2, 1), 1)
+        few = lax.dynamic_index_in_dim(lax.psum(small_grads, "fsdp"), lax.axis_index("fsdp"), 0, False)
+        total_mid, total_qkv, small_total = (lax.psum(v, "seq") for v in (part_mid, part_last, few))
     layer_out = (after_cross + outer_sum).astype(bf16)
     layer_out, total_inner, total_outer, total_mid, total_qkv, going_home = lax.optimization_barrier(
         (layer_out, total_inner, total_outer, total_mid, total_qkv, going_home)
@@ -987,11 +1012,6 @@
     layer_out = change_home(layer_out).reshape(seqs, local, width)
     grad_layer_in = going_home[:rows].astype(f32).reshape(seqs, local, width)
     grad_encoder = going_home[rows:].astype(f32).reshape(seqs, enc_local, width)
-    if by_kernel:
-        total_inner = jnp.transpose(total_inner.reshape(parts, fan, 2, units // parts, -1), (4, 2, 1, 0, 3))
-    else:
-        total_inner = jnp.transpose(total_inner, (3, 1, 0, 2))
-    total_inner = total_inner.reshape(-1, 2 * fan * units).astype(f32)
     total_outer, total_mid, total_qkv = (v.astype(f32) for v in (total_outer, total_mid, total_qkv))
     total_query, total_mix_cross = total_mid[:, :width], total_mid[:, 3 * width : 4 * width]
     total_pairs = total_mid[:, width : 3 * width].reshape(-1, heads, 2 * dh)

time: 670 us -> 674 us (level)
  waiting for transfers between devices: 45.8 us -> 57.5 us
  Pallas kernels: 384 us -> 392 us
  local copies, waits for them, and re-layouts: 64.4 us -> 56.9 us
  blocking collectives: 12.9 us -> 6.06 us
    reduce_scatter x3, waiting for transfers between devices: 21.7 us -> 29.1 us  [scatter(): return lax.psum_scatter(grad, 'fsdp', scatter_dimension=0, tiled=True)]
    psum x1 -> x0, blocking collectives: 6.81 us -> none  [shards(): lax.psum(jnp.concatenate([gains, tables], axis=1).astype(bf16), 'fsdp')]
    unnamed x159 -> x156, local copies, waits for them, and re-layouts: 39.6 us -> 35.2 us
  transfers between devices with their start and end apart: 12 -> 12, of which waited for: 5 -> 5; matrix products, arithmetic and copies ran while one was open for 16% -> 14% of each run, Pallas kernels for 53% -> 54%
where the time goes in v10:
time: 674 us; the launch traced here: 670 us
  Pallas kernels  392 us (58%)
  matrix products  74 us (11%)
  waiting for transfers between devices  57.5 us (9%)
  local copies, waits for them, and re-layouts  56.9 us (8%)
  other arithmetic  35.6 us (5%)
  starting transfers between devices  32.4 us (5%)
  between operations  15.5 us (2%)
    pallas_call x2, Pallas kernels, ring_call(): pl.pallas_call(body, name=name, out_shape=[jax.ShapeDtypeStruct(s, d) for...  193 us
    pallas_call x9, Pallas kernels, swap(): pl.pallas_call(functools.partial(swap_kernel, n, fan, count, fars, not fa...  142 us
    pallas_call x4, Pallas kernels, call(): pl.pallas_call(body, name=name, out_shape=[jax.ShapeDtypeStruct(s, d) for...  57.4 us
    unnamed x156, local copies, waits for them, and re-layouts  35.2 us
    ppermute x5, starting transfers between devices, change_home(): return lax.ppermute(value, ('seq', 'fsdp'), pairs)  31 us
    reduce_scatter x3, waiting for transfers between devices, scatter(): return lax.psum_scatter(grad, 'fsdp', scatter_dimension=0, tiled=True)  29.1 us
    all_gather x2, waiting for transfers between devices, shards(): gather = lambda v: lax.all_gather(v, 'fsdp', axis=0, tiled=True)  18.5 us
  transfers between devices with their start and end apart: 12, of which 5 were waited for; matrix products, arithmetic and copies ran while one was open for 14% of the time, Pallas kernels for 54%

profile of v10, /device:TPU:1, one launch (start us, length us, event | category | flops | bytes accessed | tf_op | source)
XLA Modules:
  0.0 670.4 jit_solution(13744515415756657584)
XLA Ops:
  9.6 6.1 all-gather.1
  18.5 4.9 collective-permute-start
  36.1 7.1 %collective-permute-done.1 = s32[8,128]{1,0:T(8,128)S(1)} collective-permute-done((s32[8,128]{1,0:T(8,128)S(1)}, s32[8,128]{1,0:T(8,128)S(1)}, u32[]{:S(2)}, u32[]{:S(2)}) %collective-permute-start.1) | collective-permute-done | bytes 4128 | tf_op jit(solution)/shard_map/ppermute | solution.py:777
  43.8 8.0 %swap.9 = s32[8,8,128]{2,1,0:T(8,128)} custom-call(s32[8,8,128]{2,1,0:T(8,128)} %broadcast_in_dim.104.refs_0_), custom_call_target="tpu_custom_call" | custom-call | bytes 16384 | tf_op jit(solution)/shard_map/swap/pallas_call | solution.py:736
  56.5 5.2 fusion.62
  63.3 5.8 fusion.17.refs_0_
  69.2 34.7 %swap.10 = (bf16[8,256,384]{2,1,0:T(8,128)(2,1)}, bf16[704,1024]{1,0:T(8,128)(2,1)}, bf16[704,1024]{1,0:T(8,128)(2,1)}) custom-call(bf16[8,256,384]{2,1,0:T(8,128)(2,1)} %fusion.17.refs_0_, bf16[5632,256]{1,0:T(8,128)(2,1)} %bitcast.232), custom_call_target="tpu_custom_call" | custom-call | bytes 1572864 | tf_op jit(solution)/shard_map/swap/pallas_call | solution.py:736
  106.7 17.4 %self_forward.1 = (bf16[2048,128]{1,0:T(8,128)(2,1)S(1)}, f32[128,2048]{1,0:T(8,128)S(1)}, f32[2,2048]{1,0:T(2,128)S(1)}) custom-call(s32[2,8]{1,0:T(2,128)S(1)} %pad_add_fusion.1.lim_ref, s32[8,2048]{1,0:T(8,128)S(1)} %broadcast_in_dim.109.rows_ref, f32[2,1536]{1,0:T(2,128)S(1)} %maximum_maximum_fusion.ext_ref, bf16[2048,384]{1,0:T(8,128)(2,1)S(1)} %bitcast.219), custom_call_target="tpu_custom_call" | custom-call | bytes 1650752 | tf_op jit(solution)/shard_map/self_forward/pallas_call | solution.py:251
  125.8 10.1 %swap.11 = bf16[8,256,128]{2,1,0:T(8,128)(2,1)} custom-call(bf16[8,256,128]{2,1,0:T(8,128)(2,1)} %bitcast.230), custom_call_target="tpu_custom_call" | custom-call | bytes 524288 | tf_op jit(solution)/shard_map/swap/pallas_call | solution.py:736
  136.0 4.7 fusion.75
  154.1 21.6 %swap.12 = (bf16[8,256,128]{2,1,0:T(8,128)(2,1)}, bf16[8,64,256]{2,1,0:T(8,128)(2,1)}, bf16[704,1024]{1,0:T(8,128)(2,1)}, bf16[704,1024]{1,0:T(8,128)(2,1)}) custom-call(bf16[8,256,128]{2,1,0:T(8,128)(2,1)} %fusion.23.refs_0_, bf16[8,64,256]{2,1,0:T(8,128)(2,1)} %bitcast.270, ...), custom_call_target="tpu_custom_call", output_to_operand_aliasing={{2}: (3, {}), {3}: (4, {})} | custom-call | bytes 786432 | tf_op jit(solution)/shard_map/swap/pallas_call | solution.py:736
  177.8 9.2 %cross_forward.1 = (bf16[2048,128]{1,0:T(8,128)(2,1)S(1)}, f32[128,2048]{1,0:T(8,128)S(1)}, f32[2,2048]{1,0:T(2,128)S(1)}) custom-call(s32[2,8]{1,0:T(2,128)S(1)} %pad_add_fusion.2.lim_ref, s32[8,2048]{1,0:T(8,128)S(1)} %add_add_fusion.3.rows_ref, bf16[2048,128]{1,0:T(8,128)(2,1)S(1)} %bitcast.221, bf16[512,256]{1,0:T(8,128)(2,1)S(1)} %bitcast.226), custom_call_target="tpu_custom_call" | custom-call | bytes 852032 | tf_op jit(solution)/shard_map/cross_forward/pallas_call | solution.py:251
  188.8 14.6 %swap.13 = (bf16[8,256,128]{2,1,0:T(8,128)(2,1)}, bf16[704,1024]{1,0:T(8,128)(2,1)}, bf16[704,1024]{1,0:T(8,128)(2,1)}) custom-call(bf16[8,256,128]{2,1,0:T(8,128)(2,1)} %bitcast.228, bf16[5632,256]{1,0:T(8,128)(2,1)} %bitcast.234, bf16[704,1024]{1,0:T(8,128)(2,1)} %get-tuple-element.93.refs_2_, ...), custom_call_target="tpu_custom_call", output_to_operand_aliasing={{1}: (2, {}), {2}: (3, {})} | custom-call | bytes 524288 | tf_op jit(solution)/shard_map/swap/pallas_call | solution.py:736
  210.4 4.9 fusion.15
  215.3 18.5 %all-gather.13.cloned.1.call-done = bf16[1024,1024]{1,0:T(8,128)(2,1)} async-done(((bf16[256,1024]{1,0:T(8,128)(2,1)}), bf16[1024,1024]{1,0:T(8,128)(2,1)}) %all-gather.13.cloned.1.call-update) | async-done | bytes 2097168 | tf_op jit(solution)/shard_map/all_gather | solution.py:816
  237.7 4.7 multiply_convert_fusion
  248.3 4.7 convolution_convert_fusion.5.part_ref
  261.8 17.0 %reduce-scatter.4.cloned.1.call-done = bf16[256,1024]{1,0:T(8,128)(2,1)} async-done(((bf16[1024,1024]{1,0:T(8,128)(2,1)}), bf16[256,1024]{1,0:T(8,128)(2,1)}) %reduce-scatter.4.cloned.1.call-update) | async-done | bytes 524304 | tf_op jit(solution)/shard_map/reduce_scatter | solution.py:799
  284.4 10.1 %swap.14 = bf16[8,256,128]{2,1,0:T(8,128)(2,1)} custom-call(bf16[8,256,128]{2,1,0:T(8,128)(2,1)} %fusion.24.refs_0_), custom_call_target="tpu_custom_call" | custom-call | bytes 524288 | tf_op jit(solution)/shard_map/swap/pallas_call | solution.py:736
  296.8 10.7 %cross_backward.1 = (bf16[2048,128]{1,0:T(8,128)(2,1)S(1)}, bf16[512,256]{1,0:T(8,128)(2,1)S(1)}) custom-call(s32[2,8]{1,0:T(2,128)S(1)} %pad_add_fusion.2.lim_ref, s32[8,2048]{1,0:T(8,128)S(1)} %add_add_fusion.3.rows_ref, bf16[2048,128]{1,0:T(8,128)(2,1)S(1)} %bitcast.222, bf16[512,256]{1,0:T(8,128)(2,1)S(1)} %bitcast.227, bf16[2048,128]{1,0:T(8,128)(2,1)S(1)} %bitcast.223, ...), custom_call_target="tpu_custom_call" | custom-call | bytes 2441280 | tf_op jit(solution)/shard_map/cross_backward/pallas_call | solution.py:251
  309.1 11.9 %swap.15 = (bf16[8,256,128]{2,1,0:T(8,128)(2,1)}, bf16[8,64,256]{2,1,0:T(8,128)(2,1)}) custom-call(bf16[8,256,128]{2,1,0:T(8,128)(2,1)} %bitcast.229, bf16[8,64,256]{2,1,0:T(8,128)(2,1)} %bitcast.231), custom_call_target="tpu_custom_call" | custom-call | bytes 786432 | tf_op jit(solution)/shard_map/swap/pallas_call | solution.py:736
  334.7 6.1 pad_maximum_fusion
  341.0 9.6 %swap.16 = bf16[8,256,128]{2,1,0:T(8,128)(2,1)} custom-call(bf16[8,256,128]{2,1,0:T(8,128)(2,1)} %fusion.25.refs_0_), custom_call_target="tpu_custom_call" | custom-call | bytes 524288 | tf_op jit(solution)/shard_map/swap/pallas_call | solution.py:736
  351.8 20.1 %self_backward.1 = (bf16[2048,384]{1,0:T(8,128)(2,1)S(1)}, f32[2,1536]{1,0:T(2,128)S(1)}) custom-call(s32[2,8]{1,0:T(2,128)S(1)} %pad_add_fusion.1.lim_ref, s32[8,2048]{1,0:T(8,128)S(1)} %broadcast_in_dim.109.rows_ref, f32[2,1536]{1,0:T(2,128)S(1)} %maximum_maximum_fusion.ext_ref, bf16[2048,384]{1,0:T(8,128)(2,1)S(1)} %bitcast.220, ...), custom_call_target="tpu_custom_call" | custom-call | bytes 3240000 | tf_op jit(solution)/shard_map/self_backward/pallas_call | solution.py:251
  373.1 21.3 %swap.17 = bf16[8,256,384]{2,1,0:T(8,128)(2,1)} custom-call(bf16[8,256,384]{2,1,0:T(8,128)(2,1)} %bitcast.225), custom_call_target="tpu_custom_call" | custom-call | bytes 1572864 | tf_op jit(solution)/shard_map/swap/pallas_call | solution.py:736
  397.0 4.8 fusion.32
  411.5 4.6 convolution_convert_fusion
  416.1 12.1 %reduce-scatter.6.cloned.1.call-done.refs_0_ = bf16[256,5120]{1,0:T(8,128)(2,1)} async-done(((bf16[1024,5120]{1,0:T(8,128)(2,1)}), bf16[256,5120]{1,0:T(8,128)(2,1)}) %reduce-scatter.6.cloned.1.call-update) | async-done | bytes 2621456 | tf_op jit(solution)/shard_map/reduce_scatter | solution.py:799
  428.2 4.7 collective-permute-start.3
  433.0 110.5 %units_total.1 = (bf16[5632,256]{1,0:T(8,128)(2,1)}, bf16[704,1024]{1,0:T(8,128)(2,1)S(1)}, f32[256,1024]{1,0:T(8,128)S(1)}, f32[8,1024]{1,0:T(8,128)S(1)}) custom-call(bf16[2112,1024]{1,0:T(8,128)(2,1)} %bitcast.243, bf16[1024,1024]{1,0:T(8,128)(2,1)S(1)} %copy-done.3, bf16[32,1024]{1,0:T(8,128)(2,1)S(1)} %pad_bitcast_fusion.few_ref), custom_call_target="tpu_custom_call" | custom-call | bytes 389283840 | tf_op jit(solution)/shard_map/units_total/pallas_call | solution.py:452
  547.0 82.4 %ring_total.1 = (bf16[256,5120]{1,0:T(8,128)(2,1)S(1)}, bf16[256,3072]{1,0:T(8,128)(2,1)S(1)}, bf16[64,128]{1,0:T(8,128)(2,1)S(1)}, f32[256,5632]{1,0:T(8,128)}) custom-call(bf16[256,5120]{1,0:T(8,128)(2,1)} %reduce-scatter.6.cloned.1.call-done.refs_0_, bf16[256,3072]{1,0:T(8,128)(2,1)S(1)} %copy-done.8, bf16[64,128]{1,0:T(8,128)(2,1)S(1)} %pad.14.refs_2_, ...), custom_call_target="tpu_custom_call" | custom-call | bytes 425656320 | tf_op jit(solution)/shard_map/ring_total/pallas_call | solution.py:452
  632.4 14.9 %collective-permute-start.4 = (bf16[256,1024]{1,0:T(8,128)(2,1)}, bf16[256,1024]{1,0:T(8,128)(2,1)S(1)}, u32[]{:S(2)}, u32[]{:S(2)}) collective-permute-start(bf16[256,1024]{1,0:T(8,128)(2,1)} %add_convert_fusion.1), channel_id=1, source_target_pairs={{0,0},{1,16},{2,2},{3,18},{4,4},{5,20},{6,6},{7,22},{8,8},{9,24},{... | collective-permute-start | bytes 1572872 | tf_op jit(solution)/shard_map/ppermute | solution.py:777
  (281 shorter events, 131.8 us)
Async XLA Ops:
  7.2 203.2 %copy-start = (bf16[704,1024]{1,0:T(8,128)(2,1)S(1)}, bf16[704,1024]{1,0:T(8,128)(2,1)}, u32[]{:S(2)}) copy-start(bf16[704,1024]{1,0:T(8,128)(2,1)} %param.32) | copy-start | bytes 4325380
  7.2 8.5 %copy-start.48 = (bf16[256,16,128]{2,1,0:T(8,128)(2,1)S(1)}, bf16[256,16,128]{2,1,0:T(8,128)(2,1)}, u32[]{:S(2)}) copy-start(bf16[256,16,128]{2,1,0:T(8,128)(2,1)} %param.28) | copy-start | bytes 3145732
  7.2 55.9 %all-gather.7.cloned.1.call-start = ((), (), s32[]{:S(2)}) async-start(), calls=%async_computation.3 | async-start | bytes 7864320 | tf_op jit(solution)/shard_map/all_gather | solution.py:816
  7.9 128.1 %all-gather.9.cloned.1.call-start = ((), (), s32[]{:S(2)}) async-start(), calls=%async_computation.4 | async-start | bytes 10485760 | tf_op jit(solution)/shard_map/all_gather | solution.py:828
  18.4 5.0 copy-start.56
  18.4 5.0 copy-start.57
  18.4 6.9 %copy-start.50 = (bf16[1,256,1024]{2,1,0:T(8,128)(2,1)S(1)}, bf16[1,256,1024]{2,1,0:T(8,128)(2,1)}, u32[]{:S(2)}) copy-start(bf16[1,256,1024]{2,1,0:T(8,128)(2,1)} %param.33) | copy-start | bytes 1572868
  18.4 6.9 %copy-start.54 = (bf16[1,64,1024]{2,1,0:T(8,128)(2,1)S(1)}, bf16[1,64,1024]{2,1,0:T(8,128)(2,1)}, u32[]{:S(2)}) copy-start(bf16[1,64,1024]{2,1,0:T(8,128)(2,1)} %param.18) | copy-start | bytes 393220
  18.4 12.4 %copy-start.55 = (s32[2048]{0:T(1024)S(1)}, s32[2048]{0:T(1024)}, u32[]{:S(2)}) copy-start(s32[2048]{0:T(1024)} %param.21) | copy-start | bytes 24580
  18.5 184.9 %all-gather.11.cloned.1.call-start = ((), (), s32[]{:S(2)}) async-start(), calls=%async_computation.5 | async-start | bytes 5242880 | tf_op jit(solution)/shard_map/all_gather | solution.py:883
  18.5 44.6 %collective-permute-start = (bf16[256,1024]{1,0:T(8,128)(2,1)}, bf16[256,1024]{1,0:T(8,128)(2,1)S(1)}, u32[]{:S(2)}, u32[]{:S(2)}) collective-permute-start(bf16[256,1024]{1,0:T(8,128)(2,1)} %bitcast), channel_id=1, source_target_pairs={{0,0},{1,16},{2,2},{3,18},{4,4},{5,20},{6,6},{7,22},{8,8},{9,24},{... | collective-permute-start | bytes 1572872 | tf_op jit(solution)/shard_map/ppermute | solution.py:777
  23.4 19.7 %collective-permute-start.1 = (s32[8,128]{1,0:T(8,128)S(1)}, s32[8,128]{1,0:T(8,128)S(1)}, u32[]{:S(2)}, u32[]{:S(2)}) collective-permute-start(s32[8,128]{1,0:T(8,128)S(1)} %pad_bitcast_fusion.1), channel_id=1, source_target_pairs={{0,0},{1,16},{2,2},{3,18},{4,4},{5,20},{6,6},{7,22},{8,8},{9,24},{... | collective-permute-start | bytes 12296 | tf_op jit(solution)/shard_map/ppermute | solution.py:777
  26.3 36.0 %collective-permute-start.2 = (bf16[320,1024]{1,0:T(8,128)(2,1)}, bf16[320,1024]{1,0:T(8,128)(2,1)S(1)}, u32[]{:S(2)}, u32[]{:S(2)}) collective-permute-start(bf16[320,1024]{1,0:T(8,128)(2,1)} %pad_maximum_fusion.4), channel_id=1, source_target_pairs={{0,0},{1,16},{2,2},{3,18},{4,4},{5,20},{6,6},{7,22},{8,8},{9,24},{... | collective-permute-start | bytes 1966088 | tf_op jit(solution)/shard_map/ppermute | solution.py:777
  62.2 6.9 %copy-start.49 = (bf16[320,1024]{1,0:T(8,128)(2,1)}, bf16[320,1024]{1,0:T(8,128)(2,1)S(1)}, u32[]{:S(2)}) copy-start(bf16[320,1024]{1,0:T(8,128)(2,1)S(1)} %collective-permute-done.2) | copy-start | bytes 1966084
  63.1 6.0 copy-start.34
  106.3 127.5 %all-gather.13.cloned.1.call-start = ((), (), s32[]{:S(2)}) async-start(), calls=%async_computation.6 | async-start | bytes 2621440 | tf_op jit(solution)/shard_map/all_gather | solution.py:816
  210.0 68.8 %reduce-scatter.4.cloned.1.call-start = ((), (), s32[]{:S(2)}) async-start(), calls=%async_computation.7 | async-start | bytes 2621440 | tf_op jit(solution)/shard_map/reduce_scatter | solution.py:799
  237.7 4.7 copy-start.37
  247.6 180.5 %reduce-scatter.6.cloned.1.call-start = ((), (), s32[]{:S(2)}) async-start(), calls=%async_computation.8 | async-start | bytes 13107200 | tf_op jit(solution)/shard_map/reduce_scatter | solution.py:799
  248.3 4.7 copy-start.59
  259.0 19.8 %copy-start.24 = (f32[256,1024]{1,0:T(8,128)S(1)}, f32[256,1024]{1,0:T(8,128)}, u32[]{:S(2)}) copy-start(f32[256,1024]{1,0:T(8,128)} %copy-done.23) | copy-start | bytes 3145732
  282.8 11.7 %copy-start.5 = (bf16[8,256,128]{2,1,0:T(8,128)(2,1)S(1)}, bf16[8,256,128]{2,1,0:T(8,128)(2,1)}, u32[]{:S(2)}) copy-start(bf16[8,256,128]{2,1,0:T(8,128)(2,1)} %get-tuple-element.90) | copy-start | bytes 1572868
  282.8 11.7 %copy-start.18 = (bf16[8,64,256]{2,1,0:T(8,128)(2,1)S(1)}, bf16[8,64,256]{2,1,0:T(8,128)(2,1)}, u32[]{:S(2)}) copy-start(bf16[8,64,256]{2,1,0:T(8,128)(2,1)} %get-tuple-element.91) | copy-start | bytes 786436
  340.9 9.8 %copy-start.14 = (f32[128,2048]{1,0:T(8,128)S(1)}, f32[128,2048]{1,0:T(8,128)}, u32[]{:S(2)}) copy-start(f32[128,2048]{1,0:T(8,128)} %copy-done.13) | copy-start | bytes 3145732
  340.9 204.7 %reduce-scatter.8.cloned.1.call-start = ((), (), s32[]{:S(2)}) async-start(), calls=%async_computation.9 | async-start | bytes 7864320 | tf_op jit(solution)/shard_map/reduce_scatter | solution.py:799
  401.9 4.8 copy-start.31
  428.2 4.8 copy-start.3
  428.2 202.3 %collective-permute-start.3 = (bf16[320,1024]{1,0:T(8,128)(2,1)}, bf16[320,1024]{1,0:T(8,128)(2,1)S(1)}, u32[]{:S(2)}, u32[]{:S(2)}) collective-permute-start(bf16[320,1024]{1,0:T(8,128)(2,1)} %pad_maximum_fusion.5), channel_id=1, source_target_pairs={{0,0},{1,16},{2,2},{3,18},{4,4},{5,20},{6,6},{7,22},{8,8},{9,24},{... | collective-permute-start | bytes 1966088 | tf_op jit(solution)/shard_map/ppermute | solution.py:777
  433.0 111.6 %copy-start.25 = (f32[256,1024]{1,0:T(8,128)S(1)}, f32[256,1024]{1,0:T(8,128)}, u32[]{:S(2)}) copy-start(f32[256,1024]{1,0:T(8,128)} %copy-done.23) | copy-start | bytes 3145732
  632.4 27.6 %collective-permute-start.4 = (bf16[256,1024]{1,0:T(8,128)(2,1)}, bf16[256,1024]{1,0:T(8,128)(2,1)S(1)}, u32[]{:S(2)}, u32[]{:S(2)}) collective-permute-start(bf16[256,1024]{1,0:T(8,128)(2,1)} %add_convert_fusion.1), channel_id=1, source_target_pairs={{0,0},{1,16},{2,2},{3,18},{4,4},{5,20},{6,6},{7,22},{8,8},{9,24},{... | collective-permute-start | bytes 1572872 | tf_op jit(solution)/shard_map/ppermute | solution.py:777
  651.9 8.9 %slice-start.1 = ((s8[5767168]{0:T(1024)(128)(4,1)}), s8[4194304]{0:T(1024)(128)(4,1)S(1)}, s32[]{:S(2)}) async-start(s8[5767168]{0:T(1024)(128)(4,1)} %bitcast.248), calls=%async_computation.11 | async-start | bytes 8388608
  653.6 7.2 %slice-start.2 = ((s8[5767168]{0:T(1024)(128)(4,1)}), s8[1572864]{0:T(1024)(128)(4,1)S(1)}, s32[]{:S(2)}) async-start(s8[5767168]{0:T(1024)(128)(4,1)} %bitcast.248), calls=%async_computation.12 | async-start | bytes 3145728
  (49 other events, 99.9 us)
Sparse Core Ops, SparseCore 0:
  9.6 49.7 all-gather.6
  61.5 73.6 all-gather.8
  137.3 40.0 all-gather.10
  210.2 23.5 all-gather.12
  247.7 31.0 reduce-scatter.3
  341.0 87.1 reduce-scatter.5
  430.9 66.8 reduce-scatter.7

commit v11 on v10

--- a/solution.py
+++ b/solution.py
@@ -930,6 +930,7 @@
     grad_middle = grad_low.astype(f32) + grad_from_third
     middle_low = grad_middle.astype(bf16)
     grad_mix_cross = jnp.einsum("gtc,td->gcd", cross_tok, middle_low, preferred_element_type=f32)
+    part_cross = scatter(grad_mix_cross.reshape(width, width).astype(bf16))
     grad_cross_tok = jnp.einsum("td,gcd->gtc", middle_low, mix_cross, preferred_element_type=f32).astype(bf16)
     (grad_cross,) = swap([grad_cross_tok], 11)
     grad_cross = grad_cross.reshape(length, own * dh)
@@ -956,7 +957,6 @@
         [
             grad_query_w.astype(bf16),
             grad_pairs_w.astype(bf16),
-            grad_mix_cross.reshape(width, width).astype(bf16),
             grad_mix_self.reshape(width, width).astype(bf16),
         ],
         axis=1,
@@ -986,17 +986,16 @@
     small_grads = jnp.concatenate([gains, tables], axis=1).astype(bf16)
     small_size = small_grads.shape[1]
     going_home = jnp.concatenate([grad_layer_in, grad_encoder.astype(bf16)])
-    going_home, small_grads, grad_qkv_w, part_units, part_mid = lax.optimization_barrier(
-        (going_home, small_grads, grad_qkv_w.astype(bf16), part_units, part_mid)
+    going_home, small_grads, grad_qkv_w, part_units, part_cross, part_mid = lax.optimization_barrier(
+        (change_home(going_home), small_grads, grad_qkv_w.astype(bf16), part_units, part_cross, part_mid)
     )
     part_last = scatter(grad_qkv_w)
-    going_home = change_home(going_home)
     if by_kernel:
         few = jnp.pad(small_grads[:, None], ((0, 0), (0, 7), (0, 1024 - small_size))).reshape(fan * 8, 1024)
         total_inner, total_outer, outer_sum, few = units_total(part_units, outer_part, few, 0)
         few = jnp.pad(few[0].astype(bf16).reshape(8, 128), ((0, parts * 8 - 8), (0, 0)))
-        total_mid, total_qkv, small_total, total_inner = ring_total(
-            [part_mid, part_last, few], (2, 2, 1), 1, total_inner
+        total_cross, total_mid, total_qkv, small_total, total_inner = ring_total(
+            [part_cross, part_mid, part_last, few], (2, 2, 2, 1), 1, total_inner
         )
     else:
         grad_units = [lax.psum(g, "seq") for g in part_units]
@@ -1004,18 +1003,20 @@
         total_inner = jnp.transpose(total_inner, (3, 1, 0, 2)).reshape(-1, 2 * fan * units).astype(f32)
         total_outer, outer_sum = grad_units[2], scatter(outer_part).astype(f32)
         few = lax.dynamic_index_in_dim(lax.psum(small_grads, "fsdp"), lax.axis_index("fsdp"), 0, False)
-        total_mid, total_qkv, small_total = (lax.psum(v, "seq") for v in (part_mid, part_last, few))
+        total_cross, total_mid, total_qkv, small_total = (
+            lax.psum(v, "seq") for v in (part_cross, part_mid, part_last, few)
+        )
     layer_out = (after_cross + outer_sum).astype(bf16)
-    layer_out, total_inner, total_outer, total_mid, total_qkv, going_home = lax.optimization_barrier(
-        (layer_out, total_inner, total_outer, total_mid, total_qkv, going_home)
+    layer_out, total_inner, total_outer, total_cross, total_mid, total_qkv, going_home = lax.optimization_barrier(
+        (layer_out, total_inner, total_outer, total_cross, total_mid, total_qkv, going_home)
     )
     layer_out = change_home(layer_out).reshape(seqs, local, width)
     grad_layer_in = going_home[:rows].astype(f32).reshape(seqs, local, width)
     grad_encoder = going_home[rows:].astype(f32).reshape(seqs, enc_local, width)
     total_outer, total_mid, total_qkv = (v.astype(f32) for v in (total_outer, total_mid, total_qkv))
-    total_query, total_mix_cross = total_mid[:, :width], total_mid[:, 3 * width : 4 * width]
+    total_query, total_mix_cross = total_mid[:, :width], total_cross.astype(f32)
     total_pairs = total_mid[:, width : 3 * width].reshape(-1, heads, 2 * dh)
-    total_mix_self, total_qkv = total_mid[:, 4 * width :], total_qkv.reshape(-1, heads, 3 * dh)
+    total_mix_self, total_qkv = total_mid[:, 3 * width :], total_qkv.reshape(-1, heads, 3 * dh)
     mine = small_total.reshape(-1)[:small_size].astype(f32)
     total_gain_first, total_gain_second, total_gain_third = (mine[i * part : (i + 1) * part] for i in range(3))
     total_table = mine[3 * part :].reshape(buckets, table_own)

time: 674 us -> 664 us (0.985)
  Pallas kernels: 392 us -> 376 us
    reduce_scatter x3 -> x4, waiting for transfers between devices: 29.1 us -> 17.8 us  [scatter(): return lax.psum_scatter(grad, 'fsdp', scatter_dimension=0, tiled=True)]
    pallas_call x2, Pallas kernels: 193 us -> 182 us  [ring_call(): pl.pallas_call(body, name=name, out_shape=[jax.ShapeDtypeStruct(s, d) for...]
    ppermute x5, waiting for transfers between devices: 9.14 us -> 16.8 us  [change_home(): return lax.ppermute(value, ('seq', 'fsdp'), pairs)]
    unnamed x156 -> x168, local copies, waits for them, and re-layouts: 35.2 us -> 38.5 us
  transfers between devices with their start and end apart: 12 -> 13, of which waited for: 5 -> 7; matrix products, arithmetic and copies ran while one was open for 14% -> 16% of each run, Pallas kernels for 54% -> 44%
where the time goes in v11:
time: 664 us; the launch traced here: 660 us
  Pallas kernels  376 us (57%)
  matrix products  72.8 us (11%)
  waiting for transfers between devices  61.9 us (9%)
  local copies, waits for them, and re-layouts  60.8 us (9%)
  other arithmetic  35.5 us (5%)
  starting transfers between devices  31.9 us (5%)
  between operations  15.8 us (2%)
    pallas_call x2, Pallas kernels, ring_call(): pl.pallas_call(body, name=name, out_shape=[jax.ShapeDtypeStruct(s, d) for...  182 us
    pallas_call x9, Pallas kernels, swap(): pl.pallas_call(functools.partial(swap_kernel, n, fan, count, fars, not fa...  136 us
    pallas_call x4, Pallas kernels, call(): pl.pallas_call(body, name=name, out_shape=[jax.ShapeDtypeStruct(s, d) for...  57.1 us
    unnamed x168, local copies, waits for them, and re-layouts  38.5 us
    ppermute x5, starting transfers between devices, change_home(): return lax.ppermute(value, ('seq', 'fsdp'), pairs)  30.1 us
    all_gather x2, waiting for transfers between devices, shards(): gather = lambda v: lax.all_gather(v, 'fsdp', axis=0, tiled=True)  23.2 us
    reduce_scatter x4, waiting for transfers between devices, scatter(): return lax.psum_scatter(grad, 'fsdp', scatter_dimension=0, tiled=True)  17.8 us
    ppermute x5, waiting for transfers between devices, change_home(): return lax.ppermute(value, ('seq', 'fsdp'), pairs)  16.8 us
  transfers between devices with their start and end apart: 13, of which 7 were waited for; matrix products, arithmetic and copies ran while one was open for 16% of the time, Pallas kernels for 44%

profile of v11, /device:TPU:1, one launch (start us, length us, event | category | flops | bytes accessed | tf_op | source)
XLA Modules:
  0.0 660.3 jit_solution(7341150505022615337)
XLA Ops:
  9.8 6.1 all-gather.1
  18.3 4.7 collective-permute-start.1
  36.3 4.9 swap.9
  45.9 5.2 fusion.62
  59.6 5.8 fusion.17.refs_0_
  65.4 30.5 %swap.10 = (bf16[8,256,384]{2,1,0:T(8,128)(2,1)}, bf16[704,1024]{1,0:T(8,128)(2,1)}, bf16[704,1024]{1,0:T(8,128)(2,1)}) custom-call(bf16[8,256,384]{2,1,0:T(8,128)(2,1)} %fusion.17.refs_0_, bf16[5632,256]{1,0:T(8,128)(2,1)} %bitcast.232), custom_call_target="tpu_custom_call" | custom-call | bytes 1572864 | tf_op jit(solution)/shard_map/swap/pallas_call | solution.py:736
  98.8 18.1 %self_forward.1 = (bf16[2048,128]{1,0:T(8,128)(2,1)S(1)}, f32[128,2048]{1,0:T(8,128)S(1)}, f32[2,2048]{1,0:T(2,128)S(1)}) custom-call(s32[2,8]{1,0:T(2,128)S(1)} %pad_add_fusion.1.lim_ref, s32[8,2048]{1,0:T(8,128)S(1)} %broadcast_in_dim.109.rows_ref, f32[2,1536]{1,0:T(2,128)S(1)} %maximum_maximum_fusion.ext_ref, bf16[2048,384]{1,0:T(8,128)(2,1)S(1)} %bitcast.219), custom_call_target="tpu_custom_call" | custom-call | bytes 1650752 | tf_op jit(solution)/shard_map/self_forward/pallas_call | solution.py:251
  118.6 9.8 %swap.11 = bf16[8,256,128]{2,1,0:T(8,128)(2,1)} custom-call(bf16[8,256,128]{2,1,0:T(8,128)(2,1)} %bitcast.230), custom_call_target="tpu_custom_call" | custom-call | bytes 524288 | tf_op jit(solution)/shard_map/swap/pallas_call | solution.py:736
  131.7 4.7 fusion.75
  148.3 23.5 %swap.12 = (bf16[8,256,128]{2,1,0:T(8,128)(2,1)}, bf16[8,64,256]{2,1,0:T(8,128)(2,1)}, bf16[704,1024]{1,0:T(8,128)(2,1)}, bf16[704,1024]{1,0:T(8,128)(2,1)}) custom-call(bf16[8,256,128]{2,1,0:T(8,128)(2,1)} %fusion.23.refs_0_, bf16[8,64,256]{2,1,0:T(8,128)(2,1)} %bitcast.268, ...), custom_call_target="tpu_custom_call", output_to_operand_aliasing={{2}: (3, {}), {3}: (4, {})} | custom-call | bytes 786432 | tf_op jit(solution)/shard_map/swap/pallas_call | solution.py:736
  173.8 8.6 %cross_forward.1 = (bf16[2048,128]{1,0:T(8,128)(2,1)S(1)}, f32[128,2048]{1,0:T(8,128)S(1)}, f32[2,2048]{1,0:T(2,128)S(1)}) custom-call(s32[2,8]{1,0:T(2,128)S(1)} %pad_add_fusion.2.lim_ref, s32[8,2048]{1,0:T(8,128)S(1)} %add_add_fusion.3.rows_ref, bf16[2048,128]{1,0:T(8,128)(2,1)S(1)} %bitcast.221, bf16[512,256]{1,0:T(8,128)(2,1)S(1)} %bitcast.226), custom_call_target="tpu_custom_call" | custom-call | bytes 852032 | tf_op jit(solution)/shard_map/cross_forward/pallas_call | solution.py:251
  184.2 14.6 %swap.13 = (bf16[8,256,128]{2,1,0:T(8,128)(2,1)}, bf16[704,1024]{1,0:T(8,128)(2,1)}, bf16[704,1024]{1,0:T(8,128)(2,1)}) custom-call(bf16[8,256,128]{2,1,0:T(8,128)(2,1)} %bitcast.228, bf16[5632,256]{1,0:T(8,128)(2,1)} %bitcast.234, bf16[704,1024]{1,0:T(8,128)(2,1)} %get-tuple-element.96.refs_2_, ...), custom_call_target="tpu_custom_call", output_to_operand_aliasing={{1}: (2, {}), {2}: (3, {})} | custom-call | bytes 524288 | tf_op jit(solution)/shard_map/swap/pallas_call | solution.py:736
  204.6 4.9 fusion.15
  209.5 18.9 %all-gather.13.cloned.1.call-done = bf16[1024,1024]{1,0:T(8,128)(2,1)} async-done(((bf16[256,1024]{1,0:T(8,128)(2,1)}), bf16[1024,1024]{1,0:T(8,128)(2,1)}) %all-gather.13.cloned.1.call-update) | async-done | bytes 2097168 | tf_op jit(solution)/shard_map/all_gather | solution.py:816
  232.4 4.7 multiply_convert_fusion
  242.5 4.7 convolution_convert_fusion.5.part_ref
  255.7 17.8 %reduce-scatter.5.cloned.1.call-done = bf16[256,1024]{1,0:T(8,128)(2,1)} async-done(((bf16[1024,1024]{1,0:T(8,128)(2,1)}), bf16[256,1024]{1,0:T(8,128)(2,1)}) %reduce-scatter.5.cloned.1.call-update) | async-done | bytes 524304 | tf_op jit(solution)/shard_map/reduce_scatter | solution.py:799
  283.2 10.2 %swap.14 = bf16[8,256,128]{2,1,0:T(8,128)(2,1)} custom-call(bf16[8,256,128]{2,1,0:T(8,128)(2,1)} %fusion.24.refs_0_), custom_call_target="tpu_custom_call" | custom-call | bytes 524288 | tf_op jit(solution)/shard_map/swap/pallas_call | solution.py:736
  295.6 9.9 %cross_backward.1 = (bf16[2048,128]{1,0:T(8,128)(2,1)S(1)}, bf16[512,256]{1,0:T(8,128)(2,1)S(1)}) custom-call(s32[2,8]{1,0:T(2,128)S(1)} %pad_add_fusion.2.lim_ref, s32[8,2048]{1,0:T(8,128)S(1)} %add_add_fusion.3.rows_ref, bf16[2048,128]{1,0:T(8,128)(2,1)S(1)} %bitcast.222, bf16[512,256]{1,0:T(8,128)(2,1)S(1)} %bitcast.227, bf16[2048,128]{1,0:T(8,128)(2,1)S(1)} %bitcast.223, ...), custom_call_target="tpu_custom_call" | custom-call | bytes 2441280 | tf_op jit(solution)/shard_map/cross_backward/pallas_call | solution.py:251
  307.1 11.9 %swap.15 = (bf16[8,256,128]{2,1,0:T(8,128)(2,1)}, bf16[8,64,256]{2,1,0:T(8,128)(2,1)}) custom-call(bf16[8,256,128]{2,1,0:T(8,128)(2,1)} %bitcast.229, bf16[8,64,256]{2,1,0:T(8,128)(2,1)} %bitcast.231), custom_call_target="tpu_custom_call" | custom-call | bytes 786432 | tf_op jit(solution)/shard_map/swap/pallas_call | solution.py:736
  336.7 9.6 %swap.16 = bf16[8,256,128]{2,1,0:T(8,128)(2,1)} custom-call(bf16[8,256,128]{2,1,0:T(8,128)(2,1)} %fusion.25.refs_0_), custom_call_target="tpu_custom_call" | custom-call | bytes 524288 | tf_op jit(solution)/shard_map/swap/pallas_call | solution.py:736
  347.5 20.5 %self_backward.1 = (bf16[2048,384]{1,0:T(8,128)(2,1)S(1)}, f32[2,1536]{1,0:T(2,128)S(1)}) custom-call(s32[2,8]{1,0:T(2,128)S(1)} %pad_add_fusion.1.lim_ref, s32[8,2048]{1,0:T(8,128)S(1)} %broadcast_in_dim.109.rows_ref, f32[2,1536]{1,0:T(2,128)S(1)} %maximum_maximum_fusion.ext_ref, bf16[2048,384]{1,0:T(8,128)(2,1)S(1)} %bitcast.220, ...), custom_call_target="tpu_custom_call" | custom-call | bytes 3240000 | tf_op jit(solution)/shard_map/self_backward/pallas_call | solution.py:251
  369.1 21.2 %swap.17 = bf16[8,256,384]{2,1,0:T(8,128)(2,1)} custom-call(bf16[8,256,384]{2,1,0:T(8,128)(2,1)} %bitcast.225), custom_call_target="tpu_custom_call" | custom-call | bytes 1572864 | tf_op jit(solution)/shard_map/swap/pallas_call | solution.py:736
  392.9 5.8 fusion.32
  404.9 7.7 %collective-permute-start.3 = (bf16[320,1024]{1,0:T(8,128)(2,1)}, bf16[320,1024]{1,0:T(8,128)(2,1)S(1)}, u32[]{:S(2)}, u32[]{:S(2)}) collective-permute-start(bf16[320,1024]{1,0:T(8,128)(2,1)} %pad_maximum_fusion.5), channel_id=1, source_target_pairs={{0,0},{1,16},{2,2},{3,18},{4,4},{5,20},{6,6},{7,22},{8,8},{9,24},{... | collective-permute-start | bytes 1966088 | tf_op jit(solution)/shard_map/ppermute | solution.py:777
  415.0 4.7 convolution_convert_fusion
  419.7 8.2 %collective-permute-done.3 = bf16[320,1024]{1,0:T(8,128)(2,1)S(1)} collective-permute-done((bf16[320,1024]{1,0:T(8,128)(2,1)}, bf16[320,1024]{1,0:T(8,128)(2,1)S(1)}, u32[]{:S(2)}, u32[]{:S(2)}) %collective-permute-start.3) | collective-permute-done | bytes 655392 | tf_op jit(solution)/shard_map/ppermute | solution.py:777
  429.7 98.2 %units_total.1 = (bf16[5632,256]{1,0:T(8,128)(2,1)}, bf16[704,1024]{1,0:T(8,128)(2,1)S(1)}, f32[256,1024]{1,0:T(8,128)S(1)}, f32[8,1024]{1,0:T(8,128)S(1)}) custom-call(bf16[2112,1024]{1,0:T(8,128)(2,1)} %bitcast.243, bf16[1024,1024]{1,0:T(8,128)(2,1)S(1)} %copy-done.3, bf16[32,1024]{1,0:T(8,128)(2,1)S(1)} %pad_bitcast_fusion.few_ref), custom_call_target="tpu_custom_call" | custom-call | bytes 389283840 | tf_op jit(solution)/shard_map/units_total/pallas_call | solution.py:452
  530.4 84.0 %ring_total.1 = (bf16[256,1024]{1,0:T(8,128)(2,1)S(1)}, bf16[256,4096]{1,0:T(8,128)(2,1)}, bf16[256,3072]{1,0:T(8,128)(2,1)S(1)}, bf16[64,128]{1,0:T(8,128)(2,1)S(1)}, f32[256,5632]{1,0:T(8,128)}) custom-call(bf16[256,1024]{1,0:T(8,128)(2,1)S(1)} %copy-done.16, bf16[256,4096]{1,0:T(8,128)(2,1)} %reduce-scatter.9.cloned.1.call-done.refs_1_, ...), custom_call_target="tpu_custom_call" | custom-call | bytes 425656320 | tf_op jit(solution)/shard_map/ring_total/pallas_call | solution.py:452
  622.6 11.2 %collective-permute-start.4 = (bf16[256,1024]{1,0:T(8,128)(2,1)}, bf16[256,1024]{1,0:T(8,128)(2,1)S(1)}, u32[]{:S(2)}, u32[]{:S(2)}) collective-permute-start(bf16[256,1024]{1,0:T(8,128)(2,1)} %add_convert_fusion.1), channel_id=1, source_target_pairs={{0,0},{1,16},{2,2},{3,18},{4,4},{5,20},{6,6},{7,22},{8,8},{9,24},{... | collective-permute-start | bytes 1572872 | tf_op jit(solution)/shard_map/ppermute | solution.py:777
  640.5 6.0 collective-permute-done.4
  647.3 5.7 copy.139
  (296 shorter events, 142.3 us)
Async XLA Ops:
  7.2 197.4 %copy-start = (bf16[704,1024]{1,0:T(8,128)(2,1)S(1)}, bf16[704,1024]{1,0:T(8,128)(2,1)}, u32[]{:S(2)}) copy-start(bf16[704,1024]{1,0:T(8,128)(2,1)} %param.32) | copy-start | bytes 4325380
  7.2 52.1 %all-gather.7.cloned.1.call-start = ((), (), s32[]{:S(2)}) async-start(), calls=%async_computation.4 | async-start | bytes 7864320 | tf_op jit(solution)/shard_map/all_gather | solution.py:816
  8.0 123.7 %all-gather.9.cloned.1.call-start = ((), (), s32[]{:S(2)}) async-start(), calls=%async_computation.5 | async-start | bytes 10485760 | tf_op jit(solution)/shard_map/all_gather | solution.py:828
  8.8 7.1 %copy-start.58 = (bf16[256,1024]{1,0:T(8,128)(2,1)S(1)}, bf16[256,1024]{1,0:T(8,128)(2,1)}, u32[]{:S(2)}) copy-start(bf16[256,1024]{1,0:T(8,128)(2,1)} %param.27) | copy-start | bytes 1572868
  17.6 7.4 %copy-start.57 = (bf16[1,256,1024]{2,1,0:T(8,128)(2,1)S(1)}, bf16[1,256,1024]{2,1,0:T(8,128)(2,1)}, u32[]{:S(2)}) copy-start(bf16[1,256,1024]{2,1,0:T(8,128)(2,1)} %param.33) | copy-start | bytes 1572868
  17.6 7.4 %copy-start.60 = (bf16[1,64,1024]{2,1,0:T(8,128)(2,1)S(1)}, bf16[1,64,1024]{2,1,0:T(8,128)(2,1)}, u32[]{:S(2)}) copy-start(bf16[1,64,1024]{2,1,0:T(8,128)(2,1)} %param.18) | copy-start | bytes 393220
  17.6 13.1 %copy-start.61 = (s32[2048]{0:T(1024)S(1)}, s32[2048]{0:T(1024)}, u32[]{:S(2)}) copy-start(s32[2048]{0:T(1024)} %param.21) | copy-start | bytes 24580
  17.6 181.2 %all-gather.11.cloned.1.call-start = ((), (), s32[]{:S(2)}) async-start(), calls=%async_computation.6 | async-start | bytes 5242880 | tf_op jit(solution)/shard_map/all_gather | solution.py:883
  18.3 17.4 %collective-permute-start.1 = (s32[8,128]{1,0:T(8,128)S(1)}, s32[8,128]{1,0:T(8,128)S(1)}, u32[]{:S(2)}, u32[]{:S(2)}) collective-permute-start(s32[8,128]{1,0:T(8,128)S(1)} %pad_bitcast_fusion.1), channel_id=1, source_target_pairs={{0,0},{1,16},{2,2},{3,18},{4,4},{5,20},{6,6},{7,22},{8,8},{9,24},{... | collective-permute-start | bytes 12296 | tf_op jit(solution)/shard_map/ppermute | solution.py:777
  23.0 32.2 %collective-permute-start = (bf16[256,1024]{1,0:T(8,128)(2,1)}, bf16[256,1024]{1,0:T(8,128)(2,1)S(1)}, u32[]{:S(2)}, u32[]{:S(2)}) collective-permute-start(bf16[256,1024]{1,0:T(8,128)(2,1)} %bitcast.300), channel_id=1, source_target_pairs={{0,0},{1,16},{2,2},{3,18},{4,4},{5,20},{6,6},{7,22},{8,8},{9,24},{... | collective-permute-start | bytes 1572872 | tf_op jit(solution)/shard_map/ppermute | solution.py:777
  25.8 28.4 %collective-permute-start.2 = (bf16[320,1024]{1,0:T(8,128)(2,1)}, bf16[320,1024]{1,0:T(8,128)(2,1)S(1)}, u32[]{:S(2)}, u32[]{:S(2)}) collective-permute-start(bf16[320,1024]{1,0:T(8,128)(2,1)} %pad_maximum_fusion.4), channel_id=1, source_target_pairs={{0,0},{1,16},{2,2},{3,18},{4,4},{5,20},{6,6},{7,22},{8,8},{9,24},{... | collective-permute-start | bytes 1966088 | tf_op jit(solution)/shard_map/ppermute | solution.py:777
  54.3 11.1 %copy-start.56 = (bf16[320,1024]{1,0:T(8,128)(2,1)}, bf16[320,1024]{1,0:T(8,128)(2,1)S(1)}, u32[]{:S(2)}) copy-start(bf16[320,1024]{1,0:T(8,128)(2,1)S(1)} %collective-permute-done.2) | copy-start | bytes 1966084
  55.2 10.3 %copy-start.36 = (bf16[256,1024]{1,0:T(8,128)(2,1)}, bf16[256,1024]{1,0:T(8,128)(2,1)S(1)}, u32[]{:S(2)}) copy-start(bf16[256,1024]{1,0:T(8,128)(2,1)S(1)} %collective-permute-done) | copy-start | bytes 1572868
  98.4 130.0 %all-gather.13.cloned.1.call-start = ((), (), s32[]{:S(2)}) async-start(), calls=%async_computation.7 | async-start | bytes 2621440 | tf_op jit(solution)/shard_map/all_gather | solution.py:816
  204.0 69.5 %reduce-scatter.5.cloned.1.call-start = ((), (), s32[]{:S(2)}) async-start(), calls=%async_computation.8 | async-start | bytes 2621440 | tf_op jit(solution)/shard_map/reduce_scatter | solution.py:799
  242.3 185.6 %reduce-scatter.7.cloned.1.call-start = ((), (), s32[]{:S(2)}) async-start(), calls=%async_computation.9 | async-start | bytes 2621440 | tf_op jit(solution)/shard_map/reduce_scatter | solution.py:799
  252.8 20.7 %copy-start.24 = (f32[256,1024]{1,0:T(8,128)S(1)}, f32[256,1024]{1,0:T(8,128)}, u32[]{:S(2)}) copy-start(f32[256,1024]{1,0:T(8,128)} %copy-done.23) | copy-start | bytes 3145732
  279.5 13.8 %copy-start.5 = (bf16[8,256,128]{2,1,0:T(8,128)(2,1)S(1)}, bf16[8,256,128]{2,1,0:T(8,128)(2,1)}, u32[]{:S(2)}) copy-start(bf16[8,256,128]{2,1,0:T(8,128)(2,1)} %get-tuple-element.93) | copy-start | bytes 1572868
  279.5 13.8 %copy-start.15 = (bf16[8,64,256]{2,1,0:T(8,128)(2,1)S(1)}, bf16[8,64,256]{2,1,0:T(8,128)(2,1)}, u32[]{:S(2)}) copy-start(bf16[8,64,256]{2,1,0:T(8,128)(2,1)} %get-tuple-element.94) | copy-start | bytes 786436
  279.5 148.3 %reduce-scatter.9.cloned.1.call-start = ((), (), s32[]{:S(2)}) async-start(), calls=%async_computation.10 | async-start | bytes 10485760 | tf_op jit(solution)/shard_map/reduce_scatter | solution.py:799
  307.1 14.9 %copy-start.31 = (f32[256,1024]{1,0:T(8,128)S(1)}, f32[256,1024]{1,0:T(8,128)}, u32[]{:S(2)}) copy-start(f32[256,1024]{1,0:T(8,128)} %copy-done.29) | copy-start | bytes 3145732
  336.2 10.0 %copy-start.11 = (f32[128,2048]{1,0:T(8,128)S(1)}, f32[128,2048]{1,0:T(8,128)}, u32[]{:S(2)}) copy-start(f32[128,2048]{1,0:T(8,128)} %copy-done.10) | copy-start | bytes 3145732
  336.3 192.6 %reduce-scatter.11.cloned.1.call-start = ((), (), s32[]{:S(2)}) async-start(), calls=%async_computation.11 | async-start | bytes 7864320 | tf_op jit(solution)/shard_map/reduce_scatter | solution.py:799
  403.7 9.0 %copy-start.49 = (bf16[704,1024]{1,0:T(8,128)(2,1)S(1)}, bf16[704,1024]{1,0:T(8,128)(2,1)}, u32[]{:S(2)}) copy-start(bf16[704,1024]{1,0:T(8,128)(2,1)} %fusion.16) | copy-start | bytes 4325380
  403.7 9.0 %copy-start.50 = (bf16[704,1024]{1,0:T(8,128)(2,1)S(1)}, bf16[704,1024]{1,0:T(8,128)(2,1)}, u32[]{:S(2)}) copy-start(bf16[704,1024]{1,0:T(8,128)(2,1)} %convolution_convert_fusion.7) | copy-start | bytes 4325380
  403.7 9.0 %copy-start.51 = (bf16[704,1024]{1,0:T(8,128)(2,1)S(1)}, bf16[704,1024]{1,0:T(8,128)(2,1)}, u32[]{:S(2)}) copy-start(bf16[704,1024]{1,0:T(8,128)(2,1)} %convolution_convert_fusion.8) | copy-start | bytes 4325380
  404.9 22.9 %collective-permute-start.3 = (bf16[320,1024]{1,0:T(8,128)(2,1)}, bf16[320,1024]{1,0:T(8,128)(2,1)S(1)}, u32[]{:S(2)}, u32[]{:S(2)}) collective-permute-start(bf16[320,1024]{1,0:T(8,128)(2,1)} %pad_maximum_fusion.5), channel_id=1, source_target_pairs={{0,0},{1,16},{2,2},{3,18},{4,4},{5,20},{6,6},{7,22},{8,8},{9,24},{... | collective-permute-start | bytes 1966088 | tf_op jit(solution)/shard_map/ppermute | solution.py:777
  429.7 98.2 %copy-start.25 = (f32[256,1024]{1,0:T(8,128)S(1)}, f32[256,1024]{1,0:T(8,128)}, u32[]{:S(2)}) copy-start(f32[256,1024]{1,0:T(8,128)} %copy-done.23) | copy-start | bytes 3145732
  620.7 13.1 %copy-start.55 = (bf16[320,1024]{1,0:T(8,128)(2,1)S(1)}, bf16[320,1024]{1,0:T(8,128)(2,1)}, u32[]{:S(2)}) copy-start(bf16[320,1024]{1,0:T(8,128)(2,1)} %copy-done.54) | copy-start | bytes 1966084
  620.7 14.2 %copy-start.18 = (bf16[256,1024]{1,0:T(8,128)(2,1)S(1)}, bf16[256,1024]{1,0:T(8,128)(2,1)}, u32[]{:S(2)}) copy-start(bf16[256,1024]{1,0:T(8,128)(2,1)} %copy-done.17) | copy-start | bytes 1572868
  622.6 16.3 %copy-start.39 = (bf16[256,4096]{1,0:T(8,128)(2,1)S(1)}, bf16[256,4096]{1,0:T(8,128)(2,1)}, u32[]{:S(2)}) copy-start(bf16[256,4096]{1,0:T(8,128)(2,1)} %get-tuple-element.138) | copy-start | bytes 6291460
  622.6 23.9 %collective-permute-start.4 = (bf16[256,1024]{1,0:T(8,128)(2,1)}, bf16[256,1024]{1,0:T(8,128)(2,1)S(1)}, u32[]{:S(2)}, u32[]{:S(2)}) collective-permute-start(bf16[256,1024]{1,0:T(8,128)(2,1)} %add_convert_fusion.1), channel_id=1, source_target_pairs={{0,0},{1,16},{2,2},{3,18},{4,4},{5,20},{6,6},{7,22},{8,8},{9,24},{... | collective-permute-start | bytes 1572872 | tf_op jit(solution)/shard_map/ppermute | solution.py:777
  (56 other events, 127.2 us)
Sparse Core Ops, SparseCore 0:
  9.6 49.7 all-gather.6
  61.5 70.1 all-gather.8
  133.9 40.8 all-gather.10
  204.1 24.2 all-gather.12
  242.4 31.0 reduce-scatter.4
  279.6 31.4 reduce-scatter.6
  336.4 74.2 reduce-scatter.8
  428.0 69.0 reduce-scatter.10

commit v12 on v11

--- a/solution.py
+++ b/solution.py
@@ -335,6 +335,97 @@
         ],
         length * keys * own * 320,
     )
+
+
+def rows_of(blocks_ref):
+    return jnp.concatenate([blocks_ref[g] for g in range(blocks_ref.shape[0])], axis=1)
+
+
+def against(a, b):
+    return lax.dot_general(a, b, (((1,), (1,)), ((), ())), preferred_element_type=jnp.float32)
+
+
+def into_kernel(tok_ref, home_ref, gain_ref, enc_ref, w_ref, after_ref, norm_ref, query_ref, pairs_ref):
+    which = pl.program_id(0)
+
+    @pl.when(which == 0)
+    def _():
+        value = home_ref[...].astype(jnp.float32) + dot(rows_of(tok_ref), w_ref[0])
+        after_ref[...] = value
+        scale = lax.rsqrt(jnp.mean(value * value, axis=1, keepdims=True) + EPS)
+        norm_ref[...] = (value * scale * gain_ref[...]).astype(jnp.bfloat16)
+
+    @pl.when(which == 1)
+    def _():
+        query = dot(norm_ref[...], w_ref[0]).astype(jnp.bfloat16)
+        cols = query_ref.shape[2]
+        for g in range(query_ref.shape[0]):
+            query_ref[g] = query[:, g * cols : (g + 1) * cols]
+
+    for half in range(2):
+
+        @pl.when(which == 2 + half)
+        def _():
+            pairs = dot(enc_ref[...], w_ref[0]).astype(jnp.bfloat16)
+            groups, cols = pairs_ref.shape[0] // 2, pairs_ref.shape[2]
+            for g in range(groups):
+                pairs_ref[half * groups + g] = pairs[:, g * cols : (g + 1) * cols]
+
+
+def outof_kernel(
+    dq_ref, dkv_ref, after_ref, gain_ref, middle_ref, w_ref,
+    upper_ref, low_ref, out_ref, gain_grad_ref, enc_grad_ref, dq_flat_ref, dkv_flat_ref, enc_sum,
+):
+    which = pl.program_id(0)
+
+    @pl.when(which == 0)
+    def _():
+        grad_query = rows_of(dq_ref)
+        dq_flat_ref[...] = grad_query
+        dkv_flat_ref[...] = rows_of(dkv_ref)
+        grad = against(grad_query, w_ref[0])
+        value = after_ref[...]
+        unit = value * lax.rsqrt(jnp.mean(value * value, axis=1, keepdims=True) + EPS)
+        gain_grad_ref[...] = jnp.sum(grad * unit, axis=0, keepdims=True)
+        scale = lax.rsqrt(jnp.mean(value * value, axis=1, keepdims=True) + EPS)
+        grad = grad * gain_ref[...]
+        inner = jnp.mean(grad * unit, axis=1, keepdims=True)
+        upper = middle_ref[...] + scale * (grad - unit * inner)
+        upper_ref[...] = upper
+        low_ref[...] = upper.astype(jnp.bfloat16)
+
+    @pl.when(which == 1)
+    def _():
+        grad = against(low_ref[...], w_ref[0]).astype(jnp.bfloat16)
+        cols = out_ref.shape[2]
+        for g in range(out_ref.shape[0]):
+            out_ref[g] = grad[:, g * cols : (g + 1) * cols]
+
+    width = w_ref.shape[1]
+
+    @pl.when(which == 2)
+    def _():
+        enc_sum[...] = against(dkv_flat_ref[:, :width], w_ref[0])
+
+    @pl.when(which == 3)
+    def _():
+        enc_grad_ref[...] = (enc_sum[...] + against(dkv_flat_ref[:, width:], w_ref[0])).astype(jnp.bfloat16)
+
+
+def over_weights(body, name, arrays, weights, order, outs, scratch=()):
+    count, rows, cols = weights.shape
+    whole = lambda shape: pl.BlockSpec(shape, lambda i: (0,) * len(shape))
+    return pl.pallas_call(
+        body,
+        name=name,
+        grid=(count,),
+        out_shape=[jax.ShapeDtypeStruct(s, d) for s, d in outs],
+        in_specs=[whole(v.shape) for v in arrays] + [pl.BlockSpec((1, rows, cols), lambda i: (order(i), 0, 0))],
+        out_specs=[whole(s) for s, _ in outs],
+        scratch_shapes=[pltpu.VMEM(s, d) for s, d in scratch],
+        compiler_params=pltpu.CompilerParams(vmem_limit_bytes=40 << 20, dimension_semantics=("arbitrary",)),
+        cost_estimate=pl.CostEstimate(flops=0, bytes_accessed=weights.size * 2, transcendentals=0),
+    )(*arrays, weights)
 
 
 MESH = pl.DeviceIdType.MESH
@@ -487,22 +578,6 @@
     cols = width // fan
     block = 2 * fan * rows
     place, right, left = ring_greet(n, [(me + far) % fan for far in range(1, fan)])
-    parts = []
-    for far in range(1, fan):
-        target = (me + far) % fan
-        for which, (src, into) in enumerate(((part_ref, landed), (few_ref, few_landed))):
-            rest = src.shape[0] // fan
-            one = pltpu.make_async_remote_copy(
-                src_ref=src.at[pl.ds(target * rest, rest), :],
-                dst_ref=into.at[far],
-                send_sem=part_send.at[which, far],
-                recv_sem=part_recv.at[which, far],
-                device_id={"fsdp": target},
-                device_id_type=MESH,
-            )
-            one.start()
-            parts.append(one)
-
     sums = {}
 
     def piece_of(ref, at, piece):
@@ -590,6 +665,21 @@
         forward(0, step)
     for one in moves:
         one.wait()
+    parts = []
+    for far in range(1, fan):
+        target = (me + far) % fan
+        for which, (src, into) in enumerate(((part_ref, landed), (few_ref, few_landed))):
+            rest = src.shape[0] // fan
+            one = pltpu.make_async_remote_copy(
+                src_ref=src.at[pl.ds(target * rest, rest), :],
+                dst_ref=into.at[far],
+                send_sem=part_send.at[which, far],
+                recv_sem=part_recv.at[which, far],
+                device_id={"fsdp": target},
+                device_id_type=MESH,
+            )
+            one.start()
+            parts.append(one)
     start(1, 0, 0)
     start(1, 1, 0)
     for step in range(n - 1):
@@ -833,10 +923,6 @@
     (both_ids,) = swap([jnp.broadcast_to(both_ids[None], (parts, 8, 128))], 13)
     home = change_home(layer_in.reshape(rows, width))
     early = by_rows(early)
-    mix_self = early[0].reshape(parts, own * dh, width)
-    query_w = early[1].reshape(width, parts, own * dh)
-    pairs_w = early[2:]
-
     gain_first, gain_second, gain_third = (
         small[:, i * part : (i + 1) * part].reshape(width).astype(f32) for i in range(3)
     )
@@ -887,13 +973,19 @@
     qkv = qkv.reshape(length, own * 3 * dh)
     out_self, self_t, self_lse = self_forward(self_limits, self_rows, ext, qkv)
     (self_tok,) = swap([out_self.reshape(parts, local, own * dh)], 11)
-    after_self = stream + jnp.einsum("gtc,gcd->td", self_tok, mix_self, preferred_element_type=f32)
-    normed_second = norm_apply(after_self, gain_second).astype(bf16)
-    query_tok = jnp.einsum("td,dgc->gtc", normed_second, query_w, preferred_element_type=f32).astype(bf16)
-    pairs_tok = jnp.einsum(
-        "td,sdge->sgte", enc_flat, pairs_w.reshape(2, width, parts // 2, -1), preferred_element_type=f32
-    )
-    pairs_tok = pairs_tok.astype(bf16).reshape(parts, enc_local, -1)
+    after_self, normed_second, query_tok, pairs_tok = over_weights(
+        into_kernel,
+        "self_out_to_cross",
+        [self_tok, home, gain_second.reshape(1, width), enc_flat],
+        early,
+        lambda i: i,
+        [
+            ((rows, width), f32),
+            ((rows, width), bf16),
+            ((parts, rows, own * dh), bf16),
+            ((parts, enc_local, own * 2 * dh), bf16),
+        ],
+    )
     query_cross, pairs, *halves = swap([query_tok, pairs_tok], 15, fars[1], inner_t, halves)
     query_cross, pairs = query_cross.reshape(length, own * dh), pairs.reshape(keys, own * 2 * dh)
     out_cross, cross_t, cross_lse = cross_forward(cross_limits, cross_rows, query_cross, pairs)
@@ -940,19 +1032,28 @@
     grad_query_tok, grad_pairs_tok = swap(
         [grad_query.reshape(parts, local, own * dh), grad_pairs.reshape(parts, enc_local, own * 2 * dh)], 12
     )
-    grad_query_tok, grad_pairs_tok = flat(grad_query_tok), flat(grad_pairs_tok)
+    (
+        grad_upper, upper_low, grad_self_tok, grad_gain_second, grad_encoder, grad_query_tok, grad_pairs_tok
+    ) = over_weights(
+        outof_kernel,
+        "cross_to_self_out",
+        [grad_query_tok, grad_pairs_tok, after_self, gain_second.reshape(1, width), grad_middle],
+        early,
+        lambda i: jnp.where(i < 2, 1 - i, i),
+        [
+            ((rows, width), f32),
+            ((rows, width), bf16),
+            ((parts, rows, own * dh), bf16),
+            ((1, width), f32),
+            ((enc_local, width), bf16),
+            ((rows, width), bf16),
+            ((enc_local, 2 * width), bf16),
+        ],
+        [((enc_local, width), f32)],
+    )
     grad_query_w = jnp.einsum("td,te->de", normed_second, grad_query_tok, preferred_element_type=f32)
-    grad_second_in = jnp.einsum("te,de->td", grad_query_tok, query_w.reshape(width, -1), preferred_element_type=f32)
     grad_pairs_w = jnp.einsum("td,te->de", enc_flat, grad_pairs_tok, preferred_element_type=f32)
-    grad_encoder = sum(
-        jnp.einsum("te,de->td", grad_pairs_tok[:, i * width : (i + 1) * width], pairs_w[i], preferred_element_type=f32)
-        for i in range(2)
-    )
-    grad_from_second, grad_gain_second = norm_back(after_self, gain_second, grad_second_in)
-    grad_upper = grad_middle + grad_from_second
-    upper_low = grad_upper.astype(bf16)
     grad_mix_self = jnp.einsum("gtc,td->gcd", self_tok, upper_low, preferred_element_type=f32)
-    grad_self_tok = jnp.einsum("td,gcd->gtc", upper_low, mix_self, preferred_element_type=f32).astype(bf16)
     grad_mid = jnp.concatenate(
         [
             grad_query_w.astype(bf16),

time: 664 us -> 666 us (level); the launches traced: 660 us -> 655 us
  matrix products: 72.8 us -> 58.3 us
  Pallas kernels: 376 us -> 386 us
  local copies, waits for them, and re-layouts: 60.8 us -> 69 us
  waiting for transfers between devices: 61.9 us -> 54.2 us
    unnamed x168 -> x228, local copies, waits for them, and re-layouts: 38.5 us -> 56.2 us
    dot_general x7 -> x0, matrix products: 14 us -> none  [the longest x2 4.88 us: shards(): jnp.einsum('te,de->td', grad_pairs_tok[:, i * width:(i + 1) * width], pai...]
  transfers between devices with their start and end apart: 13 -> 13, of which waited for: 7 -> 6; matrix products, arithmetic and copies ran while one was open for 16% -> 13% of each run, Pallas kernels for 44% -> 46%
where the time goes in v12:
time: 666 us; the launch traced here: 655 us
  Pallas kernels  386 us (58%)
  local copies, waits for them, and re-layouts  69 us (10%)
  matrix products  58.3 us (9%)
  waiting for transfers between devices  54.2 us (8%)
  other arithmetic  37.9 us (6%)
  starting transfers between devices  27.4 us (4%)
  between operations  16 us (2%)
    pallas_call x2, Pallas kernels, ring_call(): pl.pallas_call(body, name=name, out_shape=[jax.ShapeDtypeStruct(s, d) for...  181 us
    pallas_call x9, Pallas kernels, swap(): pl.pallas_call(functools.partial(swap_kernel, n, fan, count, fars, not fa...  141 us
    pallas_call x4, Pallas kernels, call(): pl.pallas_call(body, name=name, out_shape=[jax.ShapeDtypeStruct(s, d) for...  57.1 us
    unnamed x228, local copies, waits for them, and re-layouts  56.2 us
    ppermute x5, starting transfers between devices, change_home(): return lax.ppermute(value, ('seq', 'fsdp'), pairs)  25.9 us
    all_gather x2, waiting for transfers between devices, shards(): gather = lambda v: lax.all_gather(v, 'fsdp', axis=0, tiled=True)  18 us
    reduce_scatter x4, waiting for transfers between devices, scatter(): return lax.psum_scatter(grad, 'fsdp', scatter_dimension=0, tiled=True)  17.8 us
    ppermute x5, waiting for transfers between devices, change_home(): return lax.ppermute(value, ('seq', 'fsdp'), pairs)  17.5 us
  transfers between devices with their start and end apart: 13, of which 6 were waited for; matrix products, arithmetic and copies ran while one was open for 13% of the time, Pallas kernels for 46%

profile of v12, /device:TPU:1, one launch (start us, length us, event | category | flops | bytes accessed | tf_op | source)
XLA Modules:
  0.0 654.6 jit_solution(13802329186445827430)
XLA Ops:
  9.8 6.1 all-gather.1
  18.3 4.7 collective-permute-start.1
  25.0 4.5 collective-permute-start.2
  31.2 4.5 copy.79
  36.3 4.9 swap.9
  45.9 5.2 fusion.38
  60.2 5.8 fusion.10.refs_0_
  66.1 31.4 %swap.10 = (bf16[8,256,384]{2,1,0:T(8,128)(2,1)}, bf16[704,1024]{1,0:T(8,128)(2,1)}, bf16[704,1024]{1,0:T(8,128)(2,1)}) custom-call(bf16[8,256,384]{2,1,0:T(8,128)(2,1)} %fusion.10.refs_0_, bf16[5632,256]{1,0:T(8,128)(2,1)} %bitcast.182), custom_call_target="tpu_custom_call" | custom-call | bytes 1572864 | tf_op jit(solution)/shard_map/swap/pallas_call | solution.py:826
  105.0 17.4 %self_forward.1 = (bf16[2048,128]{1,0:T(8,128)(2,1)S(1)}, f32[128,2048]{1,0:T(8,128)S(1)}, f32[2,2048]{1,0:T(2,128)S(1)}) custom-call(s32[2,8]{1,0:T(2,128)S(1)} %copy-done.50, s32[8,2048]{1,0:T(8,128)S(1)} %copy-done.25, f32[2,1536]{1,0:T(2,128)S(1)} %maximum_maximum_fusion.ext_ref, bf16[2048,384]{1,0:T(8,128)(2,1)S(1)} %bitcast.167), custom_call_target="tpu_custom_call" | custom-call | bytes 1650752 | tf_op jit(solution)/shard_map/self_forward/pallas_call | solution.py:251
  124.7 10.0 %swap.11.tok_ref = bf16[8,256,128]{2,1,0:T(8,128)(2,1)} custom-call(bf16[8,256,128]{2,1,0:T(8,128)(2,1)} %bitcast.178), custom_call_target="tpu_custom_call" | custom-call | bytes 524288 | tf_op jit(solution)/shard_map/swap/pallas_call | solution.py:826
  146.0 26.6 %swap.12 = (bf16[8,256,128]{2,1,0:T(8,128)(2,1)}, bf16[8,64,256]{2,1,0:T(8,128)(2,1)}, bf16[704,1024]{1,0:T(8,128)(2,1)}, bf16[704,1024]{1,0:T(8,128)(2,1)}) custom-call(bf16[8,256,128]{2,1,0:T(8,128)(2,1)} %copy-done.34, bf16[8,64,256]{2,1,0:T(8,128)(2,1)} %copy-done.42, bf16[5632,256]{1,0:T(8,128)(2,1)} %bitcast.183, ...), custom_call_target="tpu_custom_call", output_to_operand_aliasing={{2}: (3, {}), {3}: (4, {})} | custom-call | bytes 786432 | tf_op jit(solution)/shard_map/swap/pallas_call | solution.py:826
  176.2 9.2 %cross_forward.1 = (bf16[2048,128]{1,0:T(8,128)(2,1)S(1)}, f32[128,2048]{1,0:T(8,128)S(1)}, f32[2,2048]{1,0:T(2,128)S(1)}) custom-call(s32[2,8]{1,0:T(2,128)S(1)} %copy-done.48, s32[8,2048]{1,0:T(8,128)S(1)} %copy-done.27, bf16[2048,128]{1,0:T(8,128)(2,1)S(1)} %bitcast.169, bf16[512,256]{1,0:T(8,128)(2,1)S(1)} %bitcast.174), custom_call_target="tpu_custom_call" | custom-call | bytes 852032 | tf_op jit(solution)/shard_map/cross_forward/pallas_call | solution.py:251
  187.8 15.3 %swap.13 = (bf16[8,256,128]{2,1,0:T(8,128)(2,1)}, bf16[704,1024]{1,0:T(8,128)(2,1)}, bf16[704,1024]{1,0:T(8,128)(2,1)}) custom-call(bf16[8,256,128]{2,1,0:T(8,128)(2,1)} %bitcast.176, bf16[5632,256]{1,0:T(8,128)(2,1)} %bitcast.184, bf16[704,1024]{1,0:T(8,128)(2,1)} %get-tuple-element.110.refs_2_, ...), custom_call_target="tpu_custom_call", output_to_operand_aliasing={{1}: (2, {}), {2}: (3, {})} | custom-call | bytes 524288 | tf_op jit(solution)/shard_map/swap/pallas_call | solution.py:826
  209.0 4.9 fusion.8
  213.8 13.8 %all-gather.13.cloned.1.call-done = bf16[1024,1024]{1,0:T(8,128)(2,1)} async-done(((bf16[256,1024]{1,0:T(8,128)(2,1)}), bf16[1024,1024]{1,0:T(8,128)(2,1)}) %all-gather.13.cloned.1.call-update) | async-done | bytes 2097168 | tf_op jit(solution)/shard_map/all_gather | solution.py:906
  231.6 4.7 multiply_convert_fusion
  241.7 4.7 convolution_convert_fusion.5.part_ref
  254.8 17.8 %reduce-scatter.5.cloned.1.call-done = bf16[256,1024]{1,0:T(8,128)(2,1)} async-done(((bf16[1024,1024]{1,0:T(8,128)(2,1)}), bf16[256,1024]{1,0:T(8,128)(2,1)}) %reduce-scatter.5.cloned.1.call-update) | async-done | bytes 524304 | tf_op jit(solution)/shard_map/reduce_scatter | solution.py:889
  281.8 10.1 %swap.14 = bf16[8,256,128]{2,1,0:T(8,128)(2,1)} custom-call(bf16[8,256,128]{2,1,0:T(8,128)(2,1)} %fusion.16.refs_0_), custom_call_target="tpu_custom_call" | custom-call | bytes 524288 | tf_op jit(solution)/shard_map/swap/pallas_call | solution.py:826
  295.4 10.6 %cross_backward.1 = (bf16[2048,128]{1,0:T(8,128)(2,1)S(1)}, bf16[512,256]{1,0:T(8,128)(2,1)S(1)}) custom-call(s32[2,8]{1,0:T(2,128)S(1)} %copy-done.49, s32[8,2048]{1,0:T(8,128)S(1)} %copy-done.28, bf16[2048,128]{1,0:T(8,128)(2,1)S(1)} %bitcast.170, bf16[512,256]{1,0:T(8,128)(2,1)S(1)} %bitcast.175, bf16[2048,128]{1,0:T(8,128)(2,1)S(1)} %bitcast.171, ...), custom_call_target="tpu_custom_call" | custom-call | bytes 2441280 | tf_op jit(solution)/shard_map/cross_backward/pallas_call | solution.py:251
  307.4 11.9 %swap.15 = (bf16[8,256,128]{2,1,0:T(8,128)(2,1)}, bf16[8,64,256]{2,1,0:T(8,128)(2,1)}) custom-call(bf16[8,256,128]{2,1,0:T(8,128)(2,1)} %bitcast.177, bf16[8,64,256]{2,1,0:T(8,128)(2,1)} %bitcast.179), custom_call_target="tpu_custom_call" | custom-call | bytes 786432 | tf_op jit(solution)/shard_map/swap/pallas_call | solution.py:826
  338.4 9.6 %swap.16 = bf16[8,256,128]{2,1,0:T(8,128)(2,1)} custom-call(bf16[8,256,128]{2,1,0:T(8,128)(2,1)} %copy-done.37), custom_call_target="tpu_custom_call" | custom-call | bytes 524288 | tf_op jit(solution)/shard_map/swap/pallas_call | solution.py:826
  349.1 19.9 %self_backward.1 = (bf16[2048,384]{1,0:T(8,128)(2,1)S(1)}, f32[2,1536]{1,0:T(2,128)S(1)}) custom-call(s32[2,8]{1,0:T(2,128)S(1)} %copy-done.51, s32[8,2048]{1,0:T(8,128)S(1)} %copy-done.26, f32[2,1536]{1,0:T(2,128)S(1)} %maximum_maximum_fusion.ext_ref, bf16[2048,384]{1,0:T(8,128)(2,1)S(1)} %bitcast.168, bf16[2048,128]{1,0:T(8,128)(2,1)S(1)} %bitcast.172, ...), custom_call_target="tpu_custom_call" | custom-call | bytes 3240000 | tf_op jit(solution)/shard_map/self_backward/pallas_call | solution.py:251
  370.2 21.4 %swap.17 = bf16[8,256,384]{2,1,0:T(8,128)(2,1)} custom-call(bf16[8,256,384]{2,1,0:T(8,128)(2,1)} %bitcast.173), custom_call_target="tpu_custom_call" | custom-call | bytes 1572864 | tf_op jit(solution)/shard_map/swap/pallas_call | solution.py:826
  394.2 5.8 fusion.18
  406.4 4.7 convolution_convert_fusion
  411.0 10.6 %collective-permute-done.3 = bf16[320,1024]{1,0:T(8,128)(2,1)S(1)} collective-permute-done((bf16[320,1024]{1,0:T(8,128)(2,1)S(1)}, bf16[320,1024]{1,0:T(8,128)(2,1)S(1)}, u32[]{:S(2)}, u32[]{:S(2)}) %collective-permute-start.3) | collective-permute-done | bytes 655392 | tf_op jit(solution)/shard_map/ppermute | solution.py:867
  423.5 97.6 %units_total.1 = (bf16[5632,256]{1,0:T(8,128)(2,1)}, bf16[704,1024]{1,0:T(8,128)(2,1)S(1)}, f32[256,1024]{1,0:T(8,128)S(1)}, f32[8,1024]{1,0:T(8,128)S(1)}) custom-call(bf16[2112,1024]{1,0:T(8,128)(2,1)} %bitcast.191, bf16[1024,1024]{1,0:T(8,128)(2,1)S(1)} %copy-done.10, bf16[32,1024]{1,0:T(8,128)(2,1)S(1)} %pad_bitcast_fusion.few_ref), custom_call_target="tpu_custom_call" | custom-call | bytes 389283840 | tf_op jit(solution)/shard_map/units_total/pallas_call | solution.py:543
  523.5 83.8 %ring_total.1 = (bf16[256,1024]{1,0:T(8,128)(2,1)S(1)}, bf16[256,4096]{1,0:T(8,128)(2,1)}, bf16[256,3072]{1,0:T(8,128)(2,1)S(1)}, bf16[64,128]{1,0:T(8,128)(2,1)S(1)}, f32[256,5632]{1,0:T(8,128)}) custom-call(bf16[256,1024]{1,0:T(8,128)(2,1)S(1)} %copy-done.30, bf16[256,4096]{1,0:T(8,128)(2,1)} %reduce-scatter.9.cloned.1.call-done.refs_1_, ...), custom_call_target="tpu_custom_call" | custom-call | bytes 425656320 | tf_op jit(solution)/shard_map/ring_total/pallas_call | solution.py:543
  615.6 12.5 %collective-permute-start.4 = (bf16[256,1024]{1,0:T(8,128)(2,1)}, bf16[256,1024]{1,0:T(8,128)(2,1)S(1)}, u32[]{:S(2)}, u32[]{:S(2)}) collective-permute-start(bf16[256,1024]{1,0:T(8,128)(2,1)} %add_convert_fusion.1), channel_id=1, source_target_pairs={{0,0},{1,16},{2,2},{3,18},{4,4},{5,20},{6,6},{7,22},{8,8},{9,24},{... | collective-permute-start | bytes 1572872 | tf_op jit(solution)/shard_map/ppermute | solution.py:867
  634.8 6.0 collective-permute-done.4
  641.6 5.7 copy.127
  (344 shorter events, 136.9 us)
Async XLA Ops:
  7.2 201.8 %copy-start = (bf16[704,1024]{1,0:T(8,128)(2,1)S(1)}, bf16[704,1024]{1,0:T(8,128)(2,1)}, u32[]{:S(2)}) copy-start(bf16[704,1024]{1,0:T(8,128)(2,1)} %param.32) | copy-start | bytes 4325380
  7.2 52.1 %all-gather.7.cloned.1.call-start = ((), (), s32[]{:S(2)}) async-start(), calls=%async_computation.4 | async-start | bytes 7864320 | tf_op jit(solution)/shard_map/all_gather | solution.py:906
  8.0 126.8 %all-gather.9.cloned.1.call-start = ((), (), s32[]{:S(2)}) async-start(), calls=%async_computation.5 | async-start | bytes 10485760 | tf_op jit(solution)/shard_map/all_gather | solution.py:918
  17.6 12.3 %copy-start.91 = (s32[2048]{0:T(1024)S(1)}, s32[2048]{0:T(1024)}, u32[]{:S(2)}) copy-start(s32[2048]{0:T(1024)} %param.21) | copy-start | bytes 24580
  17.6 185.5 %all-gather.11.cloned.1.call-start = ((), (), s32[]{:S(2)}) async-start(), calls=%async_computation.6 | async-start | bytes 5242880 | tf_op jit(solution)/shard_map/all_gather | solution.py:969
  18.3 17.4 %collective-permute-start.1 = (s32[8,128]{1,0:T(8,128)S(1)}, s32[8,128]{1,0:T(8,128)S(1)}, u32[]{:S(2)}, u32[]{:S(2)}) collective-permute-start(s32[8,128]{1,0:T(8,128)S(1)} %pad_bitcast_fusion.1), channel_id=1, source_target_pairs={{0,0},{1,16},{2,2},{3,18},{4,4},{5,20},{6,6},{7,22},{8,8},{9,24},{... | collective-permute-start | bytes 12296 | tf_op jit(solution)/shard_map/ppermute | solution.py:867
  23.0 32.2 %collective-permute-start = (bf16[256,1024]{1,0:T(8,128)(2,1)}, bf16[256,1024]{1,0:T(8,128)(2,1)S(1)}, u32[]{:S(2)}, u32[]{:S(2)}) collective-permute-start(bf16[256,1024]{1,0:T(8,128)(2,1)} %bitcast), channel_id=1, source_target_pairs={{0,0},{1,16},{2,2},{3,18},{4,4},{5,20},{6,6},{7,22},{8,8},{9,24},{... | collective-permute-start | bytes 1572872 | tf_op jit(solution)/shard_map/ppermute | solution.py:867
  25.0 29.3 %collective-permute-start.2 = (bf16[320,1024]{1,0:T(8,128)(2,1)S(1)}, bf16[320,1024]{1,0:T(8,128)(2,1)S(1)}, u32[]{:S(2)}, u32[]{:S(2)}) collective-permute-start(bf16[320,1024]{1,0:T(8,128)(2,1)S(1)} %pad_maximum_fusion.4), channel_id=1, source_target_pairs={{0,0},{1,16},{2,2},{3,18},{4,4},{5,20},{6,6},{7,22},{8,8},{9,24},{... | collective-permute-start | bytes 1966088 | tf_op jit(solution)/shard_map/ppermute | solution.py:867
  35.7 30.4 %copy-start.75 = (f32[1,2,4,128]{3,1,2,0:T(2,128)}, f32[1,2,4,128]{3,1,2,0:T(2,128)S(1)}, u32[]{:S(2)}) copy-start(f32[1,2,4,128]{3,1,2,0:T(2,128)S(1)} %copy.109) | copy-start | bytes 12292
  54.3 11.8 %copy-start.69 = (bf16[320,1024]{1,0:T(8,128)(2,1)}, bf16[320,1024]{1,0:T(8,128)(2,1)S(1)}, u32[]{:S(2)}) copy-start(bf16[320,1024]{1,0:T(8,128)(2,1)S(1)} %collective-permute-done.2) | copy-start | bytes 1966084
  99.9 127.8 %all-gather.13.cloned.1.call-start = ((), (), s32[]{:S(2)}) async-start(), calls=%async_computation.7 | async-start | bytes 2621440 | tf_op jit(solution)/shard_map/all_gather | solution.py:906
  208.4 64.2 %reduce-scatter.5.cloned.1.call-start = ((), (), s32[]{:S(2)}) async-start(), calls=%async_computation.8 | async-start | bytes 2621440 | tf_op jit(solution)/shard_map/reduce_scatter | solution.py:889
  241.5 180.2 %reduce-scatter.7.cloned.1.call-start = ((), (), s32[]{:S(2)}) async-start(), calls=%async_computation.9 | async-start | bytes 2621440 | tf_op jit(solution)/shard_map/reduce_scatter | solution.py:889
  252.0 20.7 %copy-start.55 = (f32[256,1024]{1,0:T(8,128)S(1)}, f32[256,1024]{1,0:T(8,128)}, u32[]{:S(2)}) copy-start(f32[256,1024]{1,0:T(8,128)} %copy-done.54) | copy-start | bytes 3145732
  252.0 20.7 %copy-start.79 = (f32[1,2,4,128]{3,1,2,0:T(2,128)S(1)}, f32[1,2,4,128]{3,1,2,0:T(2,128)}, u32[]{:S(2)}) copy-start(f32[1,2,4,128]{3,1,2,0:T(2,128)} %copy.111) | copy-start | bytes 12292
  252.0 20.7 %copy-start.85 = (f32[256]{0:T(256)S(1)}, f32[256]{0:T(256)}, u32[]{:S(2)}) copy-start(f32[256]{0:T(256)} %copy-done.84) | copy-start | bytes 3076
  252.0 22.7 %copy-start.89 = (f32[256]{0:T(256)S(1)}, f32[256]{0:T(256)}, u32[]{:S(2)}) copy-start(f32[256]{0:T(256)} %copy-done.88) | copy-start | bytes 3076
  278.4 13.6 %copy-start.24 = (bf16[8,64,256]{2,1,0:T(8,128)(2,1)S(1)}, bf16[8,64,256]{2,1,0:T(8,128)(2,1)}, u32[]{:S(2)}) copy-start(bf16[8,64,256]{2,1,0:T(8,128)(2,1)} %get-tuple-element.108) | copy-start | bytes 786436
  278.4 13.6 %copy-start.28 = (s32[8,2048]{1,0:T(8,128)S(1)}, s32[8,2048]{1,0:T(8,128)}, u32[]{:S(2)}) copy-start(s32[8,2048]{1,0:T(8,128)} %add_add_fusion.2.rows_ref) | copy-start | bytes 196612
  278.4 13.6 %copy-start.47 = (f32[2,2048]{1,0:T(2,128)S(1)}, f32[2,2048]{1,0:T(2,128)}, u32[]{:S(2)}) copy-start(f32[2,2048]{1,0:T(2,128)} %copy-done.46) | copy-start | bytes 49156
  278.4 13.6 %copy-start.49 = (s32[2,8]{1,0:T(2,128)S(1)}, s32[2,8]{1,0:T(2,128)}, u32[]{:S(2)}) copy-start(s32[2,8]{1,0:T(2,128)} %pad_add_fusion.2.lim_ref) | copy-start | bytes 196
  278.4 143.2 %reduce-scatter.9.cloned.1.call-start = ((), (), s32[]{:S(2)}) async-start(), calls=%async_computation.10 | async-start | bytes 10485760 | tf_op jit(solution)/shard_map/reduce_scatter | solution.py:889
  337.6 10.3 %copy-start.26 = (s32[8,2048]{1,0:T(8,128)S(1)}, s32[8,2048]{1,0:T(8,128)}, u32[]{:S(2)}) copy-start(s32[8,2048]{1,0:T(8,128)} %broadcast_in_dim.102.rows_ref) | copy-start | bytes 196612
  337.6 10.3 %copy-start.45 = (f32[2,2048]{1,0:T(2,128)S(1)}, f32[2,2048]{1,0:T(2,128)}, u32[]{:S(2)}) copy-start(f32[2,2048]{1,0:T(2,128)} %copy-done.44) | copy-start | bytes 49156
  337.6 10.4 %copy-start.51 = (s32[2,8]{1,0:T(2,128)S(1)}, s32[2,8]{1,0:T(2,128)}, u32[]{:S(2)}) copy-start(s32[2,8]{1,0:T(2,128)} %pad_add_fusion.1.lim_ref) | copy-start | bytes 196
  337.7 184.4 %reduce-scatter.11.cloned.1.call-start = ((), (), s32[]{:S(2)}) async-start(), calls=%async_computation.11 | async-start | bytes 7864320 | tf_op jit(solution)/shard_map/reduce_scatter | solution.py:889
  401.8 19.8 %collective-permute-start.3 = (bf16[320,1024]{1,0:T(8,128)(2,1)S(1)}, bf16[320,1024]{1,0:T(8,128)(2,1)S(1)}, u32[]{:S(2)}, u32[]{:S(2)}) collective-permute-start(bf16[320,1024]{1,0:T(8,128)(2,1)S(1)} %pad_maximum_fusion.5), channel_id=1, source_target_pairs={{0,0},{1,16},{2,2},{3,18},{4,4},{5,20},{6,6},{7,22},{8,8},{9,24},{... | collective-permute-start | bytes 1966088 | tf_op jit(solution)/shard_map/ppermute | solution.py:867
  423.5 97.7 %copy-start.57 = (f32[256,1024]{1,0:T(8,128)S(1)}, f32[256,1024]{1,0:T(8,128)}, u32[]{:S(2)}) copy-start(f32[256,1024]{1,0:T(8,128)} %copy-done.54) | copy-start | bytes 3145732
  613.6 14.5 %copy-start.71 = (bf16[320,1024]{1,0:T(8,128)(2,1)S(1)}, bf16[320,1024]{1,0:T(8,128)(2,1)}, u32[]{:S(2)}) copy-start(bf16[320,1024]{1,0:T(8,128)(2,1)} %copy-done.70) | copy-start | bytes 1966084
  613.7 15.6 %copy-start.32 = (bf16[256,1024]{1,0:T(8,128)(2,1)S(1)}, bf16[256,1024]{1,0:T(8,128)(2,1)}, u32[]{:S(2)}) copy-start(bf16[256,1024]{1,0:T(8,128)(2,1)} %copy-done.31) | copy-start | bytes 1572868
  615.6 17.7 %copy-start.59 = (bf16[256,4096]{1,0:T(8,128)(2,1)S(1)}, bf16[256,4096]{1,0:T(8,128)(2,1)}, u32[]{:S(2)}) copy-start(bf16[256,4096]{1,0:T(8,128)(2,1)} %get-tuple-element.160) | copy-start | bytes 6291460
  615.6 25.2 %collective-permute-start.4 = (bf16[256,1024]{1,0:T(8,128)(2,1)}, bf16[256,1024]{1,0:T(8,128)(2,1)S(1)}, u32[]{:S(2)}, u32[]{:S(2)}) collective-permute-start(bf16[256,1024]{1,0:T(8,128)(2,1)} %add_convert_fusion.1), channel_id=1, source_target_pairs={{0,0},{1,16},{2,2},{3,18},{4,4},{5,20},{6,6},{7,22},{8,8},{9,24},{... | collective-permute-start | bytes 1572872 | tf_op jit(solution)/shard_map/ppermute | solution.py:867
  (85 other events, 214.9 us)
Sparse Core Ops, SparseCore 0:
  9.6 49.7 all-gather.6
  61.5 70.9 all-gather.8
  134.6 40.4 all-gather.10
  208.6 19.0 all-gather.12
  241.6 31.0 reduce-scatter.4
  278.5 31.3 reduce-scatter.6
  337.8 71.6 reduce-scatter.8
  421.8 61.2 reduce-scatter.10

commit v13 on v12

--- a/solution.py
+++ b/solution.py
@@ -836,6 +836,88 @@
     )(*operands)
 
 
+def entry_kernel(n, w_ref, few_ref, out_ref, few_out_ref, side_sem, ring_send, ring_recv, pass_send, pass_recv, own_sem, few_sem):
+    s, me = lax.axis_index("seq"), lax.axis_index("fsdp")
+    core, y = me % 2, me // 2
+    partner, across = 2 * y + 1 - core, 2 * (1 - y) + core
+    far = 2 * (1 - y) + 1 - core
+    rows, cols = w_ref.shape
+    chunk_rows = rows // n
+    half_rows = chunk_rows // 2
+    place, right, left = ring_greet(n, [partner, across, far])
+
+    def columns(of):
+        return pl.ds(pl.multiple_of(of * cols, 128), cols)
+
+    def copy(src, dst, send, recv, device):
+        one = pltpu.make_async_remote_copy(
+            src_ref=src, dst_ref=dst, send_sem=send, recv_sem=recv, device_id=device, device_id_type=MESH
+        )
+        one.start()
+        return one
+
+    def window(chunk, half):
+        return out_ref.at[pl.ds(chunk * chunk_rows + half * half_rows, half_rows), columns(across)]
+
+    mine = pl.ds(s * chunk_rows, chunk_rows)
+    first = copy(
+        w_ref.at[mine, :], out_ref.at[mine, columns(me)], side_sem.at[0], side_sem.at[1], {"fsdp": across}
+    )
+    others = []
+    for i, to in enumerate((partner, across, far)):
+        others.append(copy(few_ref, few_out_ref.at[me], few_sem.at[0, i], few_sem.at[1, i], {"fsdp": to}))
+    others.append(copy(w_ref, out_ref.at[:, columns(me)], side_sem.at[2], side_sem.at[3], {"fsdp": partner}))
+    own = [
+        pltpu.make_async_copy(w_ref, out_ref.at[:, columns(me)], own_sem.at[0]),
+        pltpu.make_async_copy(few_ref, few_out_ref.at[me], own_sem.at[1]),
+    ]
+    for one in own:
+        one.start()
+
+    travel = {}
+
+    def send(half, step):
+        chunk = ring_index((place + step) % n if half else (place + n - step) % n, n)
+        view = window(chunk, half)
+        if step < n - 1:
+            to = left if half else right
+            travel[half, step] = copy(view, view, ring_send.at[half, step], ring_recv.at[half, step], {"seq": to})
+        others.append(copy(view, view, pass_send.at[half, step], pass_recv.at[half, step], {"fsdp": partner}))
+
+    first.wait()
+    for half in range(2):
+        send(half, 0)
+    for step in range(n - 1):
+        for half in range(2):
+            travel[half, step].wait_recv()
+            send(half, step + 1)
+    for one in travel.values():
+        one.wait_send()
+    for one in others + own:
+        one.wait()
+
+
+def entry(w, few, ident):
+    n, fan = lax.axis_size("seq"), lax.axis_size("fsdp")
+    rows, cols = w.shape
+    sems = lambda *shape: pltpu.SemaphoreType.DMA(shape)
+    return pl.pallas_call(
+        functools.partial(entry_kernel, n),
+        name="entry",
+        out_shape=[
+            jax.ShapeDtypeStruct((rows, cols * fan), w.dtype),
+            jax.ShapeDtypeStruct((fan,) + few.shape, few.dtype),
+        ],
+        in_specs=[pl.BlockSpec(memory_space=pltpu.VMEM)] * 2,
+        out_specs=[pl.BlockSpec(memory_space=pl.ANY)] * 2,
+        scratch_shapes=[sems(4), sems(2, n - 1), sems(2, n - 1), sems(2, n), sems(2, n), sems(2), sems(2, 3)],
+        compiler_params=pltpu.CompilerParams(
+            collective_id=ident, has_side_effects=True, vmem_limit_bytes=24 << 20
+        ),
+        cost_estimate=pl.CostEstimate(flops=0, bytes_accessed=w.size * 2, transcendentals=0),
+    )(w, few)
+
+
 def norm_apply(value, gain):
     return value * lax.rsqrt(jnp.mean(value * value, axis=-1, keepdims=True) + EPS) * gain
 
@@ -910,19 +992,24 @@
     part = norm_self.shape[0]
     pair, half, rank = team(parts)
 
-    qkv_w = gather(self_qkv)
+    by_kernel = fan == 4 and (width // fan) % 128 == 0 and (ff_in.shape[0] // parts) % 8 == 0
     small = jnp.concatenate([norm_self, norm_cross, norm_ff, rel_table.reshape(-1)])
-    small = lax.all_gather(small, "fsdp", axis=0, tiled=False)
     early = by_rows(jnp.stack([self_out, cross_q, *jnp.split(cross_kv.reshape(-1, 2 * width), 2, axis=1)]))
     small, early = lax.optimization_barrier((small, early))
-    early = lax.all_gather(early, "fsdp", axis=1, tiled=True)
+    qkv_t = jnp.transpose(self_qkv, (1, 2, 0)).reshape(heads * 3 * dh, -1)
+    if by_kernel:
+        few = jnp.pad(small, (0, 1024 - small.shape[0])).reshape(8, 128)
+        qkv_t, few = entry(qkv_t, few, 18)
+        small = few.reshape(fan, 1024)[:, : small.shape[0]]
+    else:
+        qkv_t = lax.all_gather(qkv_t, "fsdp", axis=1, tiled=True)
+        small = lax.all_gather(small, "fsdp", axis=0, tiled=False)
+    early = by_rows(lax.all_gather(early, "fsdp", axis=1, tiled=True))
     both_ids = jnp.concatenate([decoder_ids.reshape(-1), encoder_ids.reshape(-1)])
     both_ids = change_home(jnp.pad(both_ids, (0, 1024 - local - enc_local)).reshape(8, 128))
     inner_t = ff_in.T
-    by_kernel = (width // fan) % 128 == 0 and fan % 2 == 0 and (ff_in.shape[0] // parts) % 8 == 0
     (both_ids,) = swap([jnp.broadcast_to(both_ids[None], (parts, 8, 128))], 13)
     home = change_home(layer_in.reshape(rows, width))
-    early = by_rows(early)
     gain_first, gain_second, gain_third = (
         small[:, i * part : (i + 1) * part].reshape(width).astype(f32) for i in range(3)
     )
@@ -952,24 +1039,24 @@
         [jnp.full((own, BQ), MASKED, f32), bias, jnp.zeros((own, BQ), f32)], axis=1
     )
 
-    qkv_w, home, inner_t, ext, self_rows, cross_rows, self_limits, cross_limits = lax.optimization_barrier(
-        (qkv_w, home, inner_t, ext, self_rows, cross_rows, self_limits, cross_limits)
-    )
-    qkv_w = qkv_w.reshape(width, parts, own * 3 * dh)
+    qkv_t, home, inner_t, ext, self_rows, cross_rows, self_limits, cross_limits = lax.optimization_barrier(
+        (qkv_t, home, inner_t, ext, self_rows, cross_rows, self_limits, cross_limits)
+    )
 
     stream = home.astype(f32)
     normed_first = norm_apply(stream, gain_first).astype(bf16)
-    qkv_tok = jnp.einsum("td,dge->gte", normed_first, qkv_w, preferred_element_type=f32).astype(bf16)
+    qkv_tok = jnp.einsum(
+        "td,ged->gte", normed_first, qkv_t.reshape(parts, own * 3 * dh, width), preferred_element_type=f32
+    ).astype(bf16)
     others = change_home(jnp.concatenate([cotangent.reshape(rows, width), encoder.reshape(-1, width)]))
     grad_low, enc_flat = others[:rows], others[rows:]
     fars = [tuple(far for far in range(fan) if by_kernel and min(far, 3) in some) for some in ((2,), (0, 1), (3,))]
     qkv, *halves = swap([qkv_tok], 17, fars[0], inner_t)
     qkv, cross_out, grad_low = lax.optimization_barrier((qkv, cross_out, grad_low))
     if rows == cross_out.shape[0]:
-        mix_cross, grad_group = lax.all_gather(jnp.stack([cross_out, grad_low]), "fsdp", axis=1, tiled=True)
+        apart = lax.all_gather(jnp.stack([cross_out, grad_low]), "fsdp", axis=1, tiled=True)
     else:
-        mix_cross, grad_group = gather(cross_out), gather(grad_low)
-    mix_cross = mix_cross.reshape(parts, own * dh, width)
+        apart = (gather(cross_out), gather(grad_low))
     qkv = qkv.reshape(length, own * 3 * dh)
     out_self, self_t, self_lse = self_forward(self_limits, self_rows, ext, qkv)
     (self_tok,) = swap([out_self.reshape(parts, local, own * dh)], 11)
@@ -994,6 +1081,9 @@
         halves = spread(jnp.transpose(inner_t.reshape(2, fan, units, -1), (1, 0, 2, 3)))
         halves = [jnp.transpose(halves[:, i], (1, 0, 2)).reshape(units, width) for i in range(2)]
     gate_t, up_t = halves
+    cross_tok, apart = lax.optimization_barrier((cross_tok, apart))
+    mix_cross, grad_group = apart
+    mix_cross = mix_cross.reshape(parts, own * dh, width)
     after_cross = after_self + jnp.einsum("gtc,gcd->td", cross_tok, mix_cross, preferred_element_type=f32)
     normed_third = norm_apply(after_cross, gain_third).astype(bf16)
     normed_group = gather(normed_third)
@@ -1070,7 +1160,7 @@
     (grad_qkv_tok,) = swap([grad_qkv.reshape(parts, local, own * 3 * dh)], 10)
     grad_qkv_tok = flat(grad_qkv_tok)
     grad_qkv_w = jnp.einsum("td,te->de", normed_first, grad_qkv_tok, preferred_element_type=f32)
-    grad_first_in = jnp.einsum("te,de->td", grad_qkv_tok, qkv_w.reshape(width, -1), preferred_element_type=f32)
+    grad_first_in = jnp.dot(grad_qkv_tok, qkv_t, preferred_element_type=f32)
     grad_from_first, grad_gain_first = norm_back(stream, gain_first, grad_first_in)
     grad_layer_in = (grad_upper + grad_from_first).astype(bf16)
     if not by_kernel:

time: 666 us -> 681 us (1.023)
  Pallas kernels: 386 us -> 415 us
    pallas_call x0 -> x1, Pallas kernels: none -> 51.4 us  [entry(): pl.pallas_call(functools.partial(entry_kernel, n), name='entry', out_shap...]
    pallas_call x9, Pallas kernels: 141 us -> 116 us  [swap(): pl.pallas_call(functools.partial(swap_kernel, n, fan, count, fars, not fa...]
    all_gather x2 -> x1, waiting for transfers between devices: 18 us -> 15.1 us  [shards(): gather = lambda v: lax.all_gather(v, 'fsdp', axis=0, tiled=True)]
    unnamed x228 -> x227, local copies, waits for them, and re-layouts: 56.2 us -> 55.9 us
  transfers between devices with their start and end apart: 13 -> 12, of which waited for: 6 -> 4; matrix products, arithmetic and copies ran while one was open for 13% -> 12% of each run, Pallas kernels for 46% -> 49%
where the time goes in v13:
time: 681 us; the launch traced here: 670 us
  Pallas kernels  415 us (61%)
  local copies, waits for them, and re-layouts  68.5 us (10%)
  matrix products  58.1 us (9%)
  waiting for transfers between devices  49.6 us (7%)
  other arithmetic  33.8 us (5%)
  starting transfers between devices  28.7 us (4%)
  between operations  16.1 us (2%)
    pallas_call x2, Pallas kernels, ring_call(): pl.pallas_call(body, name=name, out_shape=[jax.ShapeDtypeStruct(s, d) for...  181 us
    pallas_call x9, Pallas kernels, swap(): pl.pallas_call(functools.partial(swap_kernel, n, fan, count, fars, not fa...  116 us
    pallas_call x4, Pallas kernels, call(): pl.pallas_call(body, name=name, out_shape=[jax.ShapeDtypeStruct(s, d) for...  60.9 us
    unnamed x227, local copies, waits for them, and re-layouts  55.9 us
    pallas_call x1, Pallas kernels, entry(): pl.pallas_call(functools.partial(entry_kernel, n), name='entry', out_shap...  51.4 us
    ppermute x5, starting transfers between devices, change_home(): return lax.ppermute(value, ('seq', 'fsdp'), pairs)  27.3 us
    reduce_scatter x4, waiting for transfers between devices, scatter(): return lax.psum_scatter(grad, 'fsdp', scatter_dimension=0, tiled=True)  17.8 us
    ppermute x5, waiting for transfers between devices, change_home(): return lax.ppermute(value, ('seq', 'fsdp'), pairs)  16.5 us
  transfers between devices with their start and end apart: 12, of which 4 were waited for; matrix products, arithmetic and copies ran while one was open for 12% of the time, Pallas kernels for 49%

profile of v13, /device:TPU:1, one launch (start us, length us, event | category | flops | bytes accessed | tf_op | source)
XLA Modules:
  0.0 669.7 jit_solution(2231703691283243034)
XLA Ops:
  11.7 5.6 collective-permute-start.1
  19.4 4.5 collective-permute-start.2
  25.6 51.4 %entry.1 = (bf16[3072,1024]{1,0:T(8,128)(2,1)S(1)}, bf16[4,8,128]{2,1,0:T(8,128)(2,1)S(1)}) custom-call(bf16[3072,256]{1,0:T(8,128)(2,1)S(1)} %bitcast.180, bf16[8,128]{1,0:T(8,128)(2,1)S(1)} %pad_bitcast_fusion.2.few_ref), custom_call_target="tpu_custom_call" | custom-call | bytes 1572864 | tf_op jit(solution)/shard_map/entry/pallas_call | solution.py:904
  80.4 4.5 copy.48
  85.6 6.1 swap.9
  96.3 5.2 fusion.44
  102.3 5.8 fusion.16.refs_0_
  108.1 21.1 %swap.10 = (bf16[8,256,384]{2,1,0:T(8,128)(2,1)}, bf16[704,1024]{1,0:T(8,128)(2,1)}, bf16[704,1024]{1,0:T(8,128)(2,1)}) custom-call(bf16[8,256,384]{2,1,0:T(8,128)(2,1)} %fusion.16.refs_0_, bf16[5632,256]{1,0:T(8,128)(2,1)} %bitcast.191), custom_call_target="tpu_custom_call" | custom-call | bytes 1572864 | tf_op jit(solution)/shard_map/swap/pallas_call | solution.py:826
  134.7 17.4 %self_forward.1 = (bf16[2048,128]{1,0:T(8,128)(2,1)S(1)}, f32[128,2048]{1,0:T(8,128)S(1)}, f32[2,2048]{1,0:T(2,128)S(1)}) custom-call(s32[2,8]{1,0:T(2,128)S(1)} %pad_add_fusion.1.lim_ref, s32[8,2048]{1,0:T(8,128)S(1)} %broadcast_in_dim.102.rows_ref, f32[2,1536]{1,0:T(2,128)S(1)} %maximum_maximum_fusion.ext_ref, bf16[2048,384]{1,0:T(8,128)(2,1)S(1)} %bitcast.174), custom_call_target="tpu_custom_call" | custom-call | bytes 1650752 | tf_op jit(solution)/shard_map/self_forward/pallas_call | solution.py:251
  154.5 8.6 %swap.11.tok_ref = bf16[8,256,128]{2,1,0:T(8,128)(2,1)} custom-call(bf16[8,256,128]{2,1,0:T(8,128)(2,1)} %bitcast.186), custom_call_target="tpu_custom_call" | custom-call | bytes 524288 | tf_op jit(solution)/shard_map/swap/pallas_call | solution.py:826
  173.5 14.5 %swap.12 = (bf16[8,256,128]{2,1,0:T(8,128)(2,1)}, bf16[8,64,256]{2,1,0:T(8,128)(2,1)}, bf16[704,1024]{1,0:T(8,128)(2,1)}, bf16[704,1024]{1,0:T(8,128)(2,1)}) custom-call(bf16[8,256,128]{2,1,0:T(8,128)(2,1)} %copy-done.37, bf16[8,64,256]{2,1,0:T(8,128)(2,1)} %copy-done.45, bf16[5632,256]{1,0:T(8,128)(2,1)} %bitcast.192, ...), custom_call_target="tpu_custom_call", output_to_operand_aliasing={{2}: (3, {}), {3}: (4, {})} | custom-call | bytes 786432 | tf_op jit(solution)/shard_map/swap/pallas_call | solution.py:826
  190.0 11.2 %cross_forward.1 = (bf16[2048,128]{1,0:T(8,128)(2,1)S(1)}, f32[128,2048]{1,0:T(8,128)S(1)}, f32[2,2048]{1,0:T(2,128)S(1)}) custom-call(s32[2,8]{1,0:T(2,128)S(1)} %pad_add_fusion.2.lim_ref, s32[8,2048]{1,0:T(8,128)S(1)} %add_add_fusion.2.rows_ref, bf16[2048,128]{1,0:T(8,128)(2,1)S(1)} %bitcast.176, bf16[512,256]{1,0:T(8,128)(2,1)S(1)} %bitcast.182), custom_call_target="tpu_custom_call" | custom-call | bytes 852032 | tf_op jit(solution)/shard_map/cross_forward/pallas_call | solution.py:251
  203.6 12.5 %swap.13 = (bf16[8,256,128]{2,1,0:T(8,128)(2,1)}, bf16[704,1024]{1,0:T(8,128)(2,1)}, bf16[704,1024]{1,0:T(8,128)(2,1)}) custom-call(bf16[8,256,128]{2,1,0:T(8,128)(2,1)} %bitcast.184, bf16[5632,256]{1,0:T(8,128)(2,1)} %bitcast.193, bf16[704,1024]{1,0:T(8,128)(2,1)} %get-tuple-element.116.refs_2_, ...), custom_call_target="tpu_custom_call", output_to_operand_aliasing={{1}: (2, {}), {2}: (3, {})} | custom-call | bytes 524288 | tf_op jit(solution)/shard_map/swap/pallas_call | solution.py:826
  221.8 4.9 fusion.9
  226.7 15.1 %all-gather.8.cloned.1.call-done = bf16[1024,1024]{1,0:T(8,128)(2,1)} async-done(((bf16[256,1024]{1,0:T(8,128)(2,1)}), bf16[1024,1024]{1,0:T(8,128)(2,1)}) %all-gather.8.cloned.1.call-update) | async-done | bytes 2097168 | tf_op jit(solution)/shard_map/all_gather | solution.py:988
  245.7 4.7 multiply_convert_fusion
  255.9 4.7 convolution_convert_fusion.5.part_ref
  269.0 17.8 %reduce-scatter.5.cloned.1.call-done = bf16[256,1024]{1,0:T(8,128)(2,1)} async-done(((bf16[1024,1024]{1,0:T(8,128)(2,1)}), bf16[256,1024]{1,0:T(8,128)(2,1)}) %reduce-scatter.5.cloned.1.call-update) | async-done | bytes 524304 | tf_op jit(solution)/shard_map/reduce_scatter | solution.py:971
  295.9 10.1 %swap.14 = bf16[8,256,128]{2,1,0:T(8,128)(2,1)} custom-call(bf16[8,256,128]{2,1,0:T(8,128)(2,1)} %fusion.22.refs_0_), custom_call_target="tpu_custom_call" | custom-call | bytes 524288 | tf_op jit(solution)/shard_map/swap/pallas_call | solution.py:826
  307.2 12.4 %cross_backward.1 = (bf16[2048,128]{1,0:T(8,128)(2,1)S(1)}, bf16[512,256]{1,0:T(8,128)(2,1)S(1)}) custom-call(s32[2,8]{1,0:T(2,128)S(1)} %copy-done.52, s32[8,2048]{1,0:T(8,128)S(1)} %copy-done.32, bf16[2048,128]{1,0:T(8,128)(2,1)S(1)} %bitcast.177, bf16[512,256]{1,0:T(8,128)(2,1)S(1)} %bitcast.183, bf16[2048,128]{1,0:T(8,128)(2,1)S(1)} %bitcast.178, ...), custom_call_target="tpu_custom_call" | custom-call | bytes 2441280 | tf_op jit(solution)/shard_map/cross_backward/pallas_call | solution.py:251
  321.1 11.9 %swap.15 = (bf16[8,256,128]{2,1,0:T(8,128)(2,1)}, bf16[8,64,256]{2,1,0:T(8,128)(2,1)}) custom-call(bf16[8,256,128]{2,1,0:T(8,128)(2,1)} %bitcast.185, bf16[8,64,256]{2,1,0:T(8,128)(2,1)} %bitcast.187), custom_call_target="tpu_custom_call" | custom-call | bytes 786432 | tf_op jit(solution)/shard_map/swap/pallas_call | solution.py:826
  352.0 9.6 %swap.16 = bf16[8,256,128]{2,1,0:T(8,128)(2,1)} custom-call(bf16[8,256,128]{2,1,0:T(8,128)(2,1)} %copy-done.40), custom_call_target="tpu_custom_call" | custom-call | bytes 524288 | tf_op jit(solution)/shard_map/swap/pallas_call | solution.py:826
  364.4 19.9 %self_backward.1 = (bf16[2048,384]{1,0:T(8,128)(2,1)S(1)}, f32[2,1536]{1,0:T(2,128)S(1)}) custom-call(s32[2,8]{1,0:T(2,128)S(1)} %copy-done.54, s32[8,2048]{1,0:T(8,128)S(1)} %copy-done.30, f32[2,1536]{1,0:T(2,128)S(1)} %maximum_maximum_fusion.ext_ref, bf16[2048,384]{1,0:T(8,128)(2,1)S(1)} %bitcast.175, bf16[2048,128]{1,0:T(8,128)(2,1)S(1)} %bitcast.179, ...), custom_call_target="tpu_custom_call" | custom-call | bytes 3240000 | tf_op jit(solution)/shard_map/self_backward/pallas_call | solution.py:251
  385.5 21.4 %swap.17 = bf16[8,256,384]{2,1,0:T(8,128)(2,1)} custom-call(bf16[8,256,384]{2,1,0:T(8,128)(2,1)} %bitcast.181), custom_call_target="tpu_custom_call" | custom-call | bytes 1572864 | tf_op jit(solution)/shard_map/swap/pallas_call | solution.py:826
  410.3 5.4 fusion.24
  421.0 4.7 convolution_convert_fusion
  425.7 10.6 %collective-permute-done.3 = bf16[320,1024]{1,0:T(8,128)(2,1)S(1)} collective-permute-done((bf16[320,1024]{1,0:T(8,128)(2,1)S(1)}, bf16[320,1024]{1,0:T(8,128)(2,1)S(1)}, u32[]{:S(2)}, u32[]{:S(2)}) %collective-permute-start.3) | collective-permute-done | bytes 655392 | tf_op jit(solution)/shard_map/ppermute | solution.py:949
  438.6 97.3 %units_total.1 = (bf16[5632,256]{1,0:T(8,128)(2,1)}, bf16[704,1024]{1,0:T(8,128)(2,1)S(1)}, f32[256,1024]{1,0:T(8,128)S(1)}, f32[8,1024]{1,0:T(8,128)S(1)}) custom-call(bf16[2112,1024]{1,0:T(8,128)(2,1)} %bitcast.198, bf16[1024,1024]{1,0:T(8,128)(2,1)S(1)} %copy-done.11, bf16[32,1024]{1,0:T(8,128)(2,1)S(1)} %pad_bitcast_fusion.few_ref), custom_call_target="tpu_custom_call" | custom-call | bytes 389283840 | tf_op jit(solution)/shard_map/units_total/pallas_call | solution.py:543
  538.8 83.5 %ring_total.1 = (bf16[256,1024]{1,0:T(8,128)(2,1)S(1)}, bf16[256,4096]{1,0:T(8,128)(2,1)}, bf16[256,3072]{1,0:T(8,128)(2,1)S(1)}, bf16[64,128]{1,0:T(8,128)(2,1)S(1)}, f32[256,5632]{1,0:T(8,128)}) custom-call(bf16[256,1024]{1,0:T(8,128)(2,1)S(1)} %copy-done.33, bf16[256,4096]{1,0:T(8,128)(2,1)} %reduce-scatter.9.cloned.1.call-done.refs_1_, ...), custom_call_target="tpu_custom_call" | custom-call | bytes 425656320 | tf_op jit(solution)/shard_map/ring_total/pallas_call | solution.py:543
  630.5 12.7 %collective-permute-start.4 = (bf16[256,1024]{1,0:T(8,128)(2,1)}, bf16[256,1024]{1,0:T(8,128)(2,1)S(1)}, u32[]{:S(2)}, u32[]{:S(2)}) collective-permute-start(bf16[256,1024]{1,0:T(8,128)(2,1)} %add_convert_fusion.1), channel_id=1, source_target_pairs={{0,0},{1,16},{2,2},{3,18},{4,4},{5,20},{6,6},{7,22},{8,8},{9,24},{... | collective-permute-start | bytes 1572872 | tf_op jit(solution)/shard_map/ppermute | solution.py:949
  649.9 6.0 collective-permute-done.4
  656.7 5.7 copy.95
  (341 shorter events, 126.9 us)
Async XLA Ops:
  7.2 214.6 %copy-start = (bf16[704,1024]{1,0:T(8,128)(2,1)S(1)}, bf16[704,1024]{1,0:T(8,128)(2,1)}, u32[]{:S(2)}) copy-start(bf16[704,1024]{1,0:T(8,128)(2,1)} %param.32) | copy-start | bytes 4325380
  7.2 156.9 %all-gather.4.cloned.1.call-start = ((), (), s32[]{:S(2)}) async-start(), calls=%async_computation.4 | async-start | bytes 10485760 | tf_op jit(solution)/shard_map/all_gather | solution.py:1007
  11.6 68.2 %copy-start.91 = (s32[2048]{0:T(1024)S(1)}, s32[2048]{0:T(1024)}, u32[]{:S(2)}) copy-start(s32[2048]{0:T(1024)} %param.21) | copy-start | bytes 24580
  11.7 204.5 %all-gather.6.cloned.1.call-start = ((), (), s32[]{:S(2)}) async-start(), calls=%async_computation.5 | async-start | bytes 5242880 | tf_op jit(solution)/shard_map/all_gather | solution.py:1057
  11.7 73.2 %collective-permute-start.1 = (s32[8,128]{1,0:T(8,128)S(1)}, s32[8,128]{1,0:T(8,128)S(1)}, u32[]{:S(2)}, u32[]{:S(2)}) collective-permute-start(s32[8,128]{1,0:T(8,128)S(1)} %pad_bitcast_fusion.1), channel_id=1, source_target_pairs={{0,0},{1,16},{2,2},{3,18},{4,4},{5,20},{6,6},{7,22},{8,8},{9,24},{... | collective-permute-start | bytes 12296 | tf_op jit(solution)/shard_map/ppermute | solution.py:949
  17.4 84.7 %collective-permute-start = (bf16[256,1024]{1,0:T(8,128)(2,1)}, bf16[256,1024]{1,0:T(8,128)(2,1)S(1)}, u32[]{:S(2)}, u32[]{:S(2)}) collective-permute-start(bf16[256,1024]{1,0:T(8,128)(2,1)} %bitcast.7), channel_id=1, source_target_pairs={{0,0},{1,16},{2,2},{3,18},{4,4},{5,20},{6,6},{7,22},{8,8},{9,24},{... | collective-permute-start | bytes 1572872 | tf_op jit(solution)/shard_map/ppermute | solution.py:949
  19.4 109.9 %collective-permute-start.2 = (bf16[320,1024]{1,0:T(8,128)(2,1)S(1)}, bf16[320,1024]{1,0:T(8,128)(2,1)}, u32[]{:S(2)}, u32[]{:S(2)}) collective-permute-start(bf16[320,1024]{1,0:T(8,128)(2,1)S(1)} %pad_maximum_fusion.4), channel_id=1, source_target_pairs={{0,0},{1,16},{2,2},{3,18},{4,4},{5,20},{6,6},{7,22},{8,8},{9,24},{... | collective-permute-start | bytes 1966088 | tf_op jit(solution)/shard_map/ppermute | solution.py:949
  84.9 23.2 %copy-start.76 = (f32[1,2,4,128]{3,1,2,0:T(2,128)}, f32[1,2,4,128]{3,1,2,0:T(2,128)S(1)}, u32[]{:S(2)}) copy-start(f32[1,2,4,128]{3,1,2,0:T(2,128)S(1)} %copy.77) | copy-start | bytes 12292
  101.9 31.4 %copy-start.53 = (s32[2,8]{1,0:T(2,128)}, s32[2,8]{1,0:T(2,128)S(1)}, u32[]{:S(2)}) copy-start(s32[2,8]{1,0:T(2,128)S(1)} %pad_add_fusion.1.lim_ref) | copy-start | bytes 196
  101.9 86.1 %copy-start.51 = (s32[2,8]{1,0:T(2,128)}, s32[2,8]{1,0:T(2,128)S(1)}, u32[]{:S(2)}) copy-start(s32[2,8]{1,0:T(2,128)S(1)} %pad_add_fusion.2.lim_ref) | copy-start | bytes 196
  102.0 86.0 %copy-start.31 = (s32[8,2048]{1,0:T(8,128)}, s32[8,2048]{1,0:T(8,128)S(1)}, u32[]{:S(2)}) copy-start(s32[8,2048]{1,0:T(8,128)S(1)} %add_add_fusion.2.rows_ref) | copy-start | bytes 196612
  102.1 31.3 %copy-start.29 = (s32[8,2048]{1,0:T(8,128)}, s32[8,2048]{1,0:T(8,128)S(1)}, u32[]{:S(2)}) copy-start(s32[8,2048]{1,0:T(8,128)S(1)} %broadcast_in_dim.102.rows_ref) | copy-start | bytes 196612
  130.3 21.8 %copy-start.63 = (bf16[256,1024]{1,0:T(8,128)(2,1)}, bf16[256,1024]{1,0:T(8,128)(2,1)S(1)}, u32[]{:S(2)}) copy-start(bf16[256,1024]{1,0:T(8,128)(2,1)S(1)} %slice.126) | copy-start | bytes 1572868
  132.7 109.1 %all-gather.8.cloned.1.call-start = ((), (), s32[]{:S(2)}) async-start(), calls=%async_computation.6 | async-start | bytes 2621440 | tf_op jit(solution)/shard_map/all_gather | solution.py:988
  173.5 44.5 %copy-start.9 = (f32[256,1024]{1,0:T(8,128)}, f32[256,1024]{1,0:T(8,128)S(1)}, u32[]{:S(2)}) copy-start(f32[256,1024]{1,0:T(8,128)S(1)} %get-tuple-element.106.after_ref) | copy-start | bytes 3145732
  219.9 66.9 %copy-start.85 = (f32[256]{0:T(256)}, f32[256]{0:T(256)S(1)}, u32[]{:S(2)}) copy-start(f32[256]{0:T(256)S(1)} %fusion.49) | copy-start | bytes 3076
  221.3 65.5 %reduce-scatter.5.cloned.1.call-start = ((), (), s32[]{:S(2)}) async-start(), calls=%async_computation.7 | async-start | bytes 2621440 | tf_op jit(solution)/shard_map/reduce_scatter | solution.py:971
  255.6 180.6 %reduce-scatter.7.cloned.1.call-start = ((), (), s32[]{:S(2)}) async-start(), calls=%async_computation.8 | async-start | bytes 2621440 | tf_op jit(solution)/shard_map/reduce_scatter | solution.py:971
  266.2 20.6 %copy-start.56 = (f32[256,1024]{1,0:T(8,128)S(1)}, f32[256,1024]{1,0:T(8,128)}, u32[]{:S(2)}) copy-start(f32[256,1024]{1,0:T(8,128)} %copy-done.55) | copy-start | bytes 3145732
  266.2 20.7 %copy-start.80 = (f32[1,2,4,128]{3,1,2,0:T(2,128)S(1)}, f32[1,2,4,128]{3,1,2,0:T(2,128)}, u32[]{:S(2)}) copy-start(f32[1,2,4,128]{3,1,2,0:T(2,128)} %copy.79) | copy-start | bytes 12292
  266.2 22.7 %copy-start.89 = (f32[256]{0:T(256)S(1)}, f32[256]{0:T(256)}, u32[]{:S(2)}) copy-start(f32[256]{0:T(256)} %copy-done.88) | copy-start | bytes 3076
  266.2 22.7 %copy-start.64 = (bf16[256,1024]{1,0:T(8,128)(2,1)S(1)}, bf16[256,1024]{1,0:T(8,128)(2,1)}, u32[]{:S(2)}) copy-start(bf16[256,1024]{1,0:T(8,128)(2,1)} %copy-done.63) | copy-start | bytes 1572868
  292.3 13.8 %copy-start.13 = (bf16[8,256,128]{2,1,0:T(8,128)(2,1)S(1)}, bf16[8,256,128]{2,1,0:T(8,128)(2,1)}, u32[]{:S(2)}) copy-start(bf16[8,256,128]{2,1,0:T(8,128)(2,1)} %get-tuple-element.113) | copy-start | bytes 1572868
  292.3 13.8 %copy-start.24 = (f32[128,2048]{1,0:T(8,128)S(1)}, f32[128,2048]{1,0:T(8,128)}, u32[]{:S(2)}) copy-start(f32[128,2048]{1,0:T(8,128)} %copy-done.23) | copy-start | bytes 3145732
  292.4 143.8 %reduce-scatter.9.cloned.1.call-start = ((), (), s32[]{:S(2)}) async-start(), calls=%async_computation.9 | async-start | bytes 10485760 | tf_op jit(solution)/shard_map/reduce_scatter | solution.py:971
  351.3 185.6 %reduce-scatter.11.cloned.1.call-start = ((), (), s32[]{:S(2)}) async-start(), calls=%async_computation.10 | async-start | bytes 7864320 | tf_op jit(solution)/shard_map/reduce_scatter | solution.py:971
  416.1 20.1 %collective-permute-start.3 = (bf16[320,1024]{1,0:T(8,128)(2,1)S(1)}, bf16[320,1024]{1,0:T(8,128)(2,1)S(1)}, u32[]{:S(2)}, u32[]{:S(2)}) collective-permute-start(bf16[320,1024]{1,0:T(8,128)(2,1)S(1)} %pad_maximum_fusion.5), channel_id=1, source_target_pairs={{0,0},{1,16},{2,2},{3,18},{4,4},{5,20},{6,6},{7,22},{8,8},{9,24},{... | collective-permute-start | bytes 1966088 | tf_op jit(solution)/shard_map/ppermute | solution.py:949
  438.6 97.3 %copy-start.57 = (f32[256,1024]{1,0:T(8,128)S(1)}, f32[256,1024]{1,0:T(8,128)}, u32[]{:S(2)}) copy-start(f32[256,1024]{1,0:T(8,128)} %copy-done.55) | copy-start | bytes 3145732
  628.5 14.7 %copy-start.72 = (bf16[320,1024]{1,0:T(8,128)(2,1)S(1)}, bf16[320,1024]{1,0:T(8,128)(2,1)}, u32[]{:S(2)}) copy-start(bf16[320,1024]{1,0:T(8,128)(2,1)} %copy-done.71) | copy-start | bytes 1966084
  628.5 15.8 %copy-start.35 = (bf16[256,1024]{1,0:T(8,128)(2,1)S(1)}, bf16[256,1024]{1,0:T(8,128)(2,1)}, u32[]{:S(2)}) copy-start(bf16[256,1024]{1,0:T(8,128)(2,1)} %copy-done.34) | copy-start | bytes 1572868
  630.5 17.9 %copy-start.60 = (bf16[256,4096]{1,0:T(8,128)(2,1)S(1)}, bf16[256,4096]{1,0:T(8,128)(2,1)}, u32[]{:S(2)}) copy-start(bf16[256,4096]{1,0:T(8,128)(2,1)} %get-tuple-element.168) | copy-start | bytes 6291460
  630.5 25.4 %collective-permute-start.4 = (bf16[256,1024]{1,0:T(8,128)(2,1)}, bf16[256,1024]{1,0:T(8,128)(2,1)S(1)}, u32[]{:S(2)}, u32[]{:S(2)}) collective-permute-start(bf16[256,1024]{1,0:T(8,128)(2,1)} %add_convert_fusion.1), channel_id=1, source_target_pairs={{0,0},{1,16},{2,2},{3,18},{4,4},{5,20},{6,6},{7,22},{8,8},{9,24},{... | collective-permute-start | bytes 1572872 | tf_op jit(solution)/shard_map/ppermute | solution.py:949
  (84 other events, 280.3 us)
Sparse Core Ops, SparseCore 0:
  11.8 65.0 all-gather.3
  132.8 34.6 all-gather.5
  221.4 20.3 all-gather.7
  255.7 31.0 reduce-scatter.4
  292.4 31.4 reduce-scatter.6
  351.4 69.8 reduce-scatter.8
  437.2 59.1 reduce-scatter.10

commit v14 on v12

--- a/solution.py
+++ b/solution.py
@@ -508,7 +508,7 @@
             ]
         )
         wide = 2 * n * rows
-        turned_ref[:, number * wide : (number + 1) * wide] = jnp.transpose(tall, (1, 0))
+        turned_ref[:, number * wide : (number + 1) * wide] = jnp.transpose(tall, (1, 0)).astype(jnp.bfloat16)
 
     for number, (k, piece, down) in enumerate(streams):
         start(number, 0, window(x_refs[k], k, piece, place), window(slots[k], k, piece, 0), down)
@@ -562,7 +562,7 @@
         functools.partial(ring_kernel, n, splits, 0 if inner is None else fan),
         "ring_total",
         arrays + more,
-        [(v.shape, jnp.bfloat16) for v in arrays] + [(v.shape[::-1], jnp.float32) for v in more],
+        [(v.shape, jnp.bfloat16) for v in arrays] + [(v.shape[::-1], jnp.bfloat16) for v in more],
         [pltpu.VMEM((v.shape[0] // n * (n - 1), v.shape[1]), jnp.bfloat16) for v in arrays]
         + [pltpu.SemaphoreType.DMA((streams, 2 * n - 2))] * 2,
         ident,
@@ -1013,10 +1013,10 @@
         jnp.einsum("tf,td->fd", g, y, preferred_element_type=f32).astype(bf16)
         for g, y in ((grad_gate, normed_group), (grad_up, normed_group), (hidden, grad_group))
     ]
-    grad_third_in, outer_part, grad_units = lax.optimization_barrier((grad_third_in, outer_part, grad_units))
     if by_kernel:
         grad_units = jnp.stack([g.reshape(parts, units // parts, width) for g in grad_units], axis=1)
-        part_units = grad_units.reshape(3 * units, width)
+        grad_units = grad_units.reshape(3 * units, width)
+    grad_third_in, outer_part, part_units = lax.optimization_barrier((grad_third_in, outer_part, grad_units))
     grad_third_in = grad_third_in.astype(f32)
     grad_from_third, grad_gain_third = norm_back(after_cross, gain_third, grad_third_in)
     grad_middle = grad_low.astype(f32) + grad_from_third
@@ -1070,11 +1070,10 @@
     (grad_qkv_tok,) = swap([grad_qkv.reshape(parts, local, own * 3 * dh)], 10)
     grad_qkv_tok = flat(grad_qkv_tok)
     grad_qkv_w = jnp.einsum("td,te->de", normed_first, grad_qkv_tok, preferred_element_type=f32)
+    grad_qkv_w, grad_qkv_tok = lax.optimization_barrier((grad_qkv_w.astype(bf16), grad_qkv_tok))
     grad_first_in = jnp.einsum("te,de->td", grad_qkv_tok, qkv_w.reshape(width, -1), preferred_element_type=f32)
     grad_from_first, grad_gain_first = norm_back(stream, gain_first, grad_first_in)
     grad_layer_in = (grad_upper + grad_from_first).astype(bf16)
-    if not by_kernel:
-        part_units = grad_units
     bucket_line = jnp.concatenate([jnp.full((BQ - 1,), -1, jnp.int32), near, jnp.full((BQ + 1,), -1, jnp.int32)])
     in_bucket = (bucket_line[:, None] == jnp.arange(buckets, dtype=jnp.int32)).astype(f32)
     by_bucket = jnp.einsum("xn,gx->ng", in_bucket, diagonals, precision=HIGH)
@@ -1087,10 +1086,10 @@
     small_grads = jnp.concatenate([gains, tables], axis=1).astype(bf16)
     small_size = small_grads.shape[1]
     going_home = jnp.concatenate([grad_layer_in, grad_encoder.astype(bf16)])
-    going_home, small_grads, grad_qkv_w, part_units, part_cross, part_mid = lax.optimization_barrier(
-        (change_home(going_home), small_grads, grad_qkv_w.astype(bf16), part_units, part_cross, part_mid)
-    )
     part_last = scatter(grad_qkv_w)
+    going_home, small_grads, part_units, part_cross, part_mid = lax.optimization_barrier(
+        (change_home(going_home), small_grads, part_units, part_cross, part_mid)
+    )
     if by_kernel:
         few = jnp.pad(small_grads[:, None], ((0, 0), (0, 7), (0, 1024 - small_size))).reshape(fan * 8, 1024)
         total_inner, total_outer, outer_sum, few = units_total(part_units, outer_part, few, 0)
@@ -1114,7 +1113,9 @@
     layer_out = change_home(layer_out).reshape(seqs, local, width)
     grad_layer_in = going_home[:rows].astype(f32).reshape(seqs, local, width)
     grad_encoder = going_home[rows:].astype(f32).reshape(seqs, enc_local, width)
-    total_outer, total_mid, total_qkv = (v.astype(f32) for v in (total_outer, total_mid, total_qkv))
+    total_inner, total_outer, total_mid, total_qkv = (
+        v.astype(f32) for v in (total_inner, total_outer, total_mid, total_qkv)
+    )
     total_query, total_mix_cross = total_mid[:, :width], total_cross.astype(f32)
     total_pairs = total_mid[:, width : 3 * width].reshape(-1, heads, 2 * dh)
     total_mix_self, total_qkv = total_mid[:, 3 * width :], total_qkv.reshape(-1, heads, 3 * dh)

time: 666 us -> 671 us (level)
    unnamed x228 -> x219, local copies, waits for them, and re-layouts: 56.2 us -> 56.6 us
  transfers between devices with their start and end apart: 13 -> 13, of which waited for: 6 -> 6; matrix products, arithmetic and copies ran while one was open for 13% -> 12% of each run, Pallas kernels for 46% -> 46%
where the time goes in v14:
time: 671 us; the launch traced here: 661 us
  Pallas kernels  382 us (57%)
  local copies, waits for them, and re-layouts  69.4 us (10%)
  waiting for transfers between devices  59.5 us (9%)
  matrix products  54.7 us (8%)
  other arithmetic  39.2 us (6%)
  starting transfers between devices  33.4 us (5%)
  between operations  16 us (2%)
    pallas_call x2, Pallas kernels, ring_call(): pl.pallas_call(body, name=name, out_shape=[jax.ShapeDtypeStruct(s, d) for...  180 us
    pallas_call x9, Pallas kernels, swap(): pl.pallas_call(functools.partial(swap_kernel, n, fan, count, fars, not fa...  143 us
    unnamed x219, local copies, waits for them, and re-layouts  56.6 us
    pallas_call x4, Pallas kernels, call(): pl.pallas_call(body, name=name, out_shape=[jax.ShapeDtypeStruct(s, d) for...  53.2 us
    ppermute x5, starting transfers between devices, change_home(): return lax.ppermute(value, ('seq', 'fsdp'), pairs)  31.9 us
    all_gather x2, waiting for transfers between devices, shards(): gather = lambda v: lax.all_gather(v, 'fsdp', axis=0, tiled=True)  21.1 us
    ppermute x5, waiting for transfers between devices, change_home(): return lax.ppermute(value, ('seq', 'fsdp'), pairs)  21 us
    reduce_scatter x4, waiting for transfers between devices, scatter(): return lax.psum_scatter(grad, 'fsdp', scatter_dimension=0, tiled=True)  16.6 us
  transfers between devices with their start and end apart: 13, of which 6 were waited for; matrix products, arithmetic and copies ran while one was open for 12% of the time, Pallas kernels for 46%

profile of v14, /device:TPU:1, one launch (start us, length us, event | category | flops | bytes accessed | tf_op | source)
XLA Modules:
  0.0 660.7 jit_solution(492348337258617844)
XLA Ops:
  9.8 6.1 all-gather.1
  18.3 4.7 collective-permute-start.1
  25.0 4.5 collective-permute-start.2
  31.2 4.5 copy.79
  36.3 4.9 swap.9
  45.9 5.2 fusion.38
  55.2 4.2 all-gather.7.cloned.1.call-done
  60.2 5.8 fusion.10.refs_0_
  66.1 31.4 %swap.10 = (bf16[8,256,384]{2,1,0:T(8,128)(2,1)}, bf16[704,1024]{1,0:T(8,128)(2,1)}, bf16[704,1024]{1,0:T(8,128)(2,1)}) custom-call(bf16[8,256,384]{2,1,0:T(8,128)(2,1)} %fusion.10.refs_0_, bf16[5632,256]{1,0:T(8,128)(2,1)} %bitcast.182), custom_call_target="tpu_custom_call" | custom-call | bytes 1572864 | tf_op jit(solution)/shard_map/swap/pallas_call | solution.py:826
  105.0 15.4 %self_forward.1 = (bf16[2048,128]{1,0:T(8,128)(2,1)S(1)}, f32[128,2048]{1,0:T(8,128)S(1)}, f32[2,2048]{1,0:T(2,128)S(1)}) custom-call(s32[2,8]{1,0:T(2,128)S(1)} %copy-done.52, s32[8,2048]{1,0:T(8,128)S(1)} %copy-done.27, f32[2,1536]{1,0:T(2,128)S(1)} %maximum_maximum_fusion.ext_ref, bf16[2048,384]{1,0:T(8,128)(2,1)S(1)} %bitcast.167), custom_call_target="tpu_custom_call" | custom-call | bytes 1650752 | tf_op jit(solution)/shard_map/self_forward/pallas_call | solution.py:251
  122.7 10.0 %swap.11.tok_ref = bf16[8,256,128]{2,1,0:T(8,128)(2,1)} custom-call(bf16[8,256,128]{2,1,0:T(8,128)(2,1)} %bitcast.178), custom_call_target="tpu_custom_call" | custom-call | bytes 524288 | tf_op jit(solution)/shard_map/swap/pallas_call | solution.py:826
  144.0 28.6 %swap.12 = (bf16[8,256,128]{2,1,0:T(8,128)(2,1)}, bf16[8,64,256]{2,1,0:T(8,128)(2,1)}, bf16[704,1024]{1,0:T(8,128)(2,1)}, bf16[704,1024]{1,0:T(8,128)(2,1)}) custom-call(bf16[8,256,128]{2,1,0:T(8,128)(2,1)} %copy-done.36, bf16[8,64,256]{2,1,0:T(8,128)(2,1)} %copy-done.44, bf16[5632,256]{1,0:T(8,128)(2,1)} %bitcast.183, ...), custom_call_target="tpu_custom_call", output_to_operand_aliasing={{2}: (3, {}), {3}: (4, {})} | custom-call | bytes 786432 | tf_op jit(solution)/shard_map/swap/pallas_call | solution.py:826
  176.2 9.2 %cross_forward.1 = (bf16[2048,128]{1,0:T(8,128)(2,1)S(1)}, f32[128,2048]{1,0:T(8,128)S(1)}, f32[2,2048]{1,0:T(2,128)S(1)}) custom-call(s32[2,8]{1,0:T(2,128)S(1)} %copy-done.50, s32[8,2048]{1,0:T(8,128)S(1)} %copy-done.29, bf16[2048,128]{1,0:T(8,128)(2,1)S(1)} %bitcast.169, bf16[512,256]{1,0:T(8,128)(2,1)S(1)} %bitcast.174), custom_call_target="tpu_custom_call" | custom-call | bytes 852032 | tf_op jit(solution)/shard_map/cross_forward/pallas_call | solution.py:251
  187.8 15.3 %swap.13 = (bf16[8,256,128]{2,1,0:T(8,128)(2,1)}, bf16[704,1024]{1,0:T(8,128)(2,1)}, bf16[704,1024]{1,0:T(8,128)(2,1)}) custom-call(bf16[8,256,128]{2,1,0:T(8,128)(2,1)} %bitcast.176, bf16[5632,256]{1,0:T(8,128)(2,1)} %bitcast.184, bf16[704,1024]{1,0:T(8,128)(2,1)} %get-tuple-element.109.refs_2_, ...), custom_call_target="tpu_custom_call", output_to_operand_aliasing={{1}: (2, {}), {2}: (3, {})} | custom-call | bytes 524288 | tf_op jit(solution)/shard_map/swap/pallas_call | solution.py:826
  208.8 4.9 fusion.8
  213.7 16.9 %all-gather.13.cloned.1.call-done = bf16[1024,1024]{1,0:T(8,128)(2,1)} async-done(((bf16[256,1024]{1,0:T(8,128)(2,1)}), bf16[1024,1024]{1,0:T(8,128)(2,1)}) %all-gather.13.cloned.1.call-update) | async-done | bytes 2097168 | tf_op jit(solution)/shard_map/all_gather | solution.py:906
  234.6 4.7 multiply_convert_fusion
  259.1 16.5 %reduce-scatter.5.cloned.1.call-done = bf16[256,1024]{1,0:T(8,128)(2,1)} async-done(((bf16[1024,1024]{1,0:T(8,128)(2,1)}), bf16[256,1024]{1,0:T(8,128)(2,1)}) %reduce-scatter.5.cloned.1.call-update) | async-done | bytes 524304 | tf_op jit(solution)/shard_map/reduce_scatter | solution.py:889
  285.8 10.1 %swap.14 = bf16[8,256,128]{2,1,0:T(8,128)(2,1)} custom-call(bf16[8,256,128]{2,1,0:T(8,128)(2,1)} %fusion.16.refs_0_), custom_call_target="tpu_custom_call" | custom-call | bytes 524288 | tf_op jit(solution)/shard_map/swap/pallas_call | solution.py:826
  299.3 10.6 %cross_backward.1 = (bf16[2048,128]{1,0:T(8,128)(2,1)S(1)}, bf16[512,256]{1,0:T(8,128)(2,1)S(1)}) custom-call(s32[2,8]{1,0:T(2,128)S(1)} %copy-done.51, s32[8,2048]{1,0:T(8,128)S(1)} %copy-done.30, bf16[2048,128]{1,0:T(8,128)(2,1)S(1)} %bitcast.170, bf16[512,256]{1,0:T(8,128)(2,1)S(1)} %bitcast.175, bf16[2048,128]{1,0:T(8,128)(2,1)S(1)} %bitcast.171, ...), custom_call_target="tpu_custom_call" | custom-call | bytes 2441280 | tf_op jit(solution)/shard_map/cross_backward/pallas_call | solution.py:251
  311.3 11.9 %swap.15 = (bf16[8,256,128]{2,1,0:T(8,128)(2,1)}, bf16[8,64,256]{2,1,0:T(8,128)(2,1)}) custom-call(bf16[8,256,128]{2,1,0:T(8,128)(2,1)} %bitcast.177, bf16[8,64,256]{2,1,0:T(8,128)(2,1)} %bitcast.179), custom_call_target="tpu_custom_call" | custom-call | bytes 786432 | tf_op jit(solution)/shard_map/swap/pallas_call | solution.py:826
  341.9 9.6 %swap.16 = bf16[8,256,128]{2,1,0:T(8,128)(2,1)} custom-call(bf16[8,256,128]{2,1,0:T(8,128)(2,1)} %copy-done.39), custom_call_target="tpu_custom_call" | custom-call | bytes 524288 | tf_op jit(solution)/shard_map/swap/pallas_call | solution.py:826
  352.9 18.0 %self_backward.1 = (bf16[2048,384]{1,0:T(8,128)(2,1)S(1)}, f32[2,1536]{1,0:T(2,128)S(1)}) custom-call(s32[2,8]{1,0:T(2,128)S(1)} %copy-done.53, s32[8,2048]{1,0:T(8,128)S(1)} %copy-done.28, f32[2,1536]{1,0:T(2,128)S(1)} %maximum_maximum_fusion.ext_ref, bf16[2048,384]{1,0:T(8,128)(2,1)S(1)} %bitcast.168, bf16[2048,128]{1,0:T(8,128)(2,1)S(1)} %bitcast.172, ...), custom_call_target="tpu_custom_call" | custom-call | bytes 3240000 | tf_op jit(solution)/shard_map/self_backward/pallas_call | solution.py:251
  372.0 21.4 %swap.17 = bf16[8,256,384]{2,1,0:T(8,128)(2,1)} custom-call(bf16[8,256,384]{2,1,0:T(8,128)(2,1)} %bitcast.173), custom_call_target="tpu_custom_call" | custom-call | bytes 1572864 | tf_op jit(solution)/shard_map/swap/pallas_call | solution.py:826
  395.2 4.7 convolution_convert_fusion
  399.9 4.9 fusion.18
  405.3 6.9 %collective-permute-start.3 = (bf16[320,1024]{1,0:T(8,128)(2,1)S(1)}, bf16[320,1024]{1,0:T(8,128)(2,1)S(1)}, u32[]{:S(2)}, u32[]{:S(2)}) collective-permute-start(bf16[320,1024]{1,0:T(8,128)(2,1)S(1)} %pad_maximum_fusion.5), channel_id=1, source_target_pairs={{0,0},{1,16},{2,2},{3,18},{4,4},{5,20},{6,6},{7,22},{8,8},{9,24},{... | collective-permute-start | bytes 1966088 | tf_op jit(solution)/shard_map/ppermute | solution.py:867
  413.2 14.1 %collective-permute-done.3 = bf16[320,1024]{1,0:T(8,128)(2,1)S(1)} collective-permute-done((bf16[320,1024]{1,0:T(8,128)(2,1)S(1)}, bf16[320,1024]{1,0:T(8,128)(2,1)S(1)}, u32[]{:S(2)}, u32[]{:S(2)}) %collective-permute-start.3) | collective-permute-done | bytes 655392 | tf_op jit(solution)/shard_map/ppermute | solution.py:867
  430.1 98.5 %units_total.1 = (bf16[5632,256]{1,0:T(8,128)(2,1)}, bf16[704,1024]{1,0:T(8,128)(2,1)S(1)}, f32[256,1024]{1,0:T(8,128)S(1)}, f32[8,1024]{1,0:T(8,128)S(1)}) custom-call(bf16[2112,1024]{1,0:T(8,128)(2,1)} %bitcast.191, bf16[1024,1024]{1,0:T(8,128)(2,1)S(1)} %copy-done.10, bf16[32,1024]{1,0:T(8,128)(2,1)S(1)} %pad_bitcast_fusion.few_ref), custom_call_target="tpu_custom_call" | custom-call | bytes 389283840 | tf_op jit(solution)/shard_map/units_total/pallas_call | solution.py:543
  531.0 81.4 %ring_total.1 = (bf16[256,1024]{1,0:T(8,128)(2,1)S(1)}, bf16[256,4096]{1,0:T(8,128)(2,1)}, bf16[256,3072]{1,0:T(8,128)(2,1)S(1)}, bf16[64,128]{1,0:T(8,128)(2,1)S(1)}, bf16[256,5632]{1,0:T(8,128)(2,1)}) custom-call(bf16[256,1024]{1,0:T(8,128)(2,1)S(1)} %copy-done.32, bf16[256,4096]{1,0:T(8,128)(2,1)} %reduce-scatter.9.cloned.1.call-done.refs_1_, ...), custom_call_target="tpu_custom_call" | custom-call | bytes 425656320 | tf_op jit(solution)/shard_map/ring_total/pallas_call | solution.py:543
  625.0 13.8 %collective-permute-start.4 = (bf16[256,1024]{1,0:T(8,128)(2,1)}, bf16[256,1024]{1,0:T(8,128)(2,1)}, u32[]{:S(2)}, u32[]{:S(2)}) collective-permute-start(bf16[256,1024]{1,0:T(8,128)(2,1)} %add_convert_fusion.1), channel_id=1, source_target_pairs={{0,0},{1,16},{2,2},{3,18},{4,4},{5,20},{6,6},{7,22},{8,8},{9,24},{... | collective-permute-start | bytes 1572872 | tf_op jit(solution)/shard_map/ppermute | solution.py:867
  645.6 6.0 collective-permute-done.4
  (336 shorter events, 139.9 us)
Async XLA Ops:
  7.2 201.7 %copy-start = (bf16[704,1024]{1,0:T(8,128)(2,1)S(1)}, bf16[704,1024]{1,0:T(8,128)(2,1)}, u32[]{:S(2)}) copy-start(bf16[704,1024]{1,0:T(8,128)(2,1)} %param.32) | copy-start | bytes 4325380
  7.2 52.1 %all-gather.7.cloned.1.call-start = ((), (), s32[]{:S(2)}) async-start(), calls=%async_computation.4 | async-start | bytes 7864320 | tf_op jit(solution)/shard_map/all_gather | solution.py:906
  8.0 124.8 %all-gather.9.cloned.1.call-start = ((), (), s32[]{:S(2)}) async-start(), calls=%async_computation.5 | async-start | bytes 10485760 | tf_op jit(solution)/shard_map/all_gather | solution.py:918
  17.6 12.3 %copy-start.88 = (s32[2048]{0:T(1024)S(1)}, s32[2048]{0:T(1024)}, u32[]{:S(2)}) copy-start(s32[2048]{0:T(1024)} %param.21) | copy-start | bytes 24580
  17.6 185.5 %all-gather.11.cloned.1.call-start = ((), (), s32[]{:S(2)}) async-start(), calls=%async_computation.6 | async-start | bytes 5242880 | tf_op jit(solution)/shard_map/all_gather | solution.py:969
  18.3 17.4 %collective-permute-start.1 = (s32[8,128]{1,0:T(8,128)S(1)}, s32[8,128]{1,0:T(8,128)S(1)}, u32[]{:S(2)}, u32[]{:S(2)}) collective-permute-start(s32[8,128]{1,0:T(8,128)S(1)} %pad_bitcast_fusion.1), channel_id=1, source_target_pairs={{0,0},{1,16},{2,2},{3,18},{4,4},{5,20},{6,6},{7,22},{8,8},{9,24},{... | collective-permute-start | bytes 12296 | tf_op jit(solution)/shard_map/ppermute | solution.py:867
  23.0 32.2 %collective-permute-start = (bf16[256,1024]{1,0:T(8,128)(2,1)}, bf16[256,1024]{1,0:T(8,128)(2,1)S(1)}, u32[]{:S(2)}, u32[]{:S(2)}) collective-permute-start(bf16[256,1024]{1,0:T(8,128)(2,1)} %bitcast), channel_id=1, source_target_pairs={{0,0},{1,16},{2,2},{3,18},{4,4},{5,20},{6,6},{7,22},{8,8},{9,24},{... | collective-permute-start | bytes 1572872 | tf_op jit(solution)/shard_map/ppermute | solution.py:867
  25.0 29.3 %collective-permute-start.2 = (bf16[320,1024]{1,0:T(8,128)(2,1)S(1)}, bf16[320,1024]{1,0:T(8,128)(2,1)S(1)}, u32[]{:S(2)}, u32[]{:S(2)}) collective-permute-start(bf16[320,1024]{1,0:T(8,128)(2,1)S(1)} %pad_maximum_fusion.4), channel_id=1, source_target_pairs={{0,0},{1,16},{2,2},{3,18},{4,4},{5,20},{6,6},{7,22},{8,8},{9,24},{... | collective-permute-start | bytes 1966088 | tf_op jit(solution)/shard_map/ppermute | solution.py:867
  35.7 30.4 %copy-start.75 = (f32[1,2,4,128]{3,1,2,0:T(2,128)}, f32[1,2,4,128]{3,1,2,0:T(2,128)S(1)}, u32[]{:S(2)}) copy-start(f32[1,2,4,128]{3,1,2,0:T(2,128)S(1)} %copy.109) | copy-start | bytes 12292
  54.3 11.8 %copy-start.69 = (bf16[320,1024]{1,0:T(8,128)(2,1)}, bf16[320,1024]{1,0:T(8,128)(2,1)S(1)}, u32[]{:S(2)}) copy-start(bf16[320,1024]{1,0:T(8,128)(2,1)S(1)} %collective-permute-done.2) | copy-start | bytes 1966084
  99.9 130.8 %all-gather.13.cloned.1.call-start = ((), (), s32[]{:S(2)}) async-start(), calls=%async_computation.7 | async-start | bytes 2621440 | tf_op jit(solution)/shard_map/all_gather | solution.py:906
  208.5 67.2 %reduce-scatter.5.cloned.1.call-start = ((), (), s32[]{:S(2)}) async-start(), calls=%async_computation.8 | async-start | bytes 2621440 | tf_op jit(solution)/shard_map/reduce_scatter | solution.py:889
  244.5 182.8 %reduce-scatter.7.cloned.1.call-start = ((), (), s32[]{:S(2)}) async-start(), calls=%async_computation.9 | async-start | bytes 2621440 | tf_op jit(solution)/shard_map/reduce_scatter | solution.py:889
  282.4 13.6 %copy-start.26 = (bf16[8,64,256]{2,1,0:T(8,128)(2,1)S(1)}, bf16[8,64,256]{2,1,0:T(8,128)(2,1)}, u32[]{:S(2)}) copy-start(bf16[8,64,256]{2,1,0:T(8,128)(2,1)} %get-tuple-element.107) | copy-start | bytes 786436
  282.4 13.6 %copy-start.30 = (s32[8,2048]{1,0:T(8,128)S(1)}, s32[8,2048]{1,0:T(8,128)}, u32[]{:S(2)}) copy-start(s32[8,2048]{1,0:T(8,128)} %add_add_fusion.2.rows_ref) | copy-start | bytes 196612
  282.4 13.6 %copy-start.49 = (f32[2,2048]{1,0:T(2,128)S(1)}, f32[2,2048]{1,0:T(2,128)}, u32[]{:S(2)}) copy-start(f32[2,2048]{1,0:T(2,128)} %copy-done.48) | copy-start | bytes 49156
  282.4 13.6 %copy-start.51 = (s32[2,8]{1,0:T(2,128)S(1)}, s32[2,8]{1,0:T(2,128)}, u32[]{:S(2)}) copy-start(s32[2,8]{1,0:T(2,128)} %pad_add_fusion.2.lim_ref) | copy-start | bytes 196
  282.4 144.8 %reduce-scatter.9.cloned.1.call-start = ((), (), s32[]{:S(2)}) async-start(), calls=%async_computation.10 | async-start | bytes 10485760 | tf_op jit(solution)/shard_map/reduce_scatter | solution.py:889
  341.6 9.9 %copy-start.18 = (f32[128,2048]{1,0:T(8,128)S(1)}, f32[128,2048]{1,0:T(8,128)}, u32[]{:S(2)}) copy-start(f32[128,2048]{1,0:T(8,128)} %copy-done.17) | copy-start | bytes 3145732
  341.6 10.0 %copy-start.28 = (s32[8,2048]{1,0:T(8,128)S(1)}, s32[8,2048]{1,0:T(8,128)}, u32[]{:S(2)}) copy-start(s32[8,2048]{1,0:T(8,128)} %broadcast_in_dim.102.rows_ref) | copy-start | bytes 196612
  341.6 10.0 %copy-start.47 = (f32[2,2048]{1,0:T(2,128)S(1)}, f32[2,2048]{1,0:T(2,128)}, u32[]{:S(2)}) copy-start(f32[2,2048]{1,0:T(2,128)} %copy-done.46) | copy-start | bytes 49156
  341.6 10.0 %copy-start.53 = (s32[2,8]{1,0:T(2,128)S(1)}, s32[2,8]{1,0:T(2,128)}, u32[]{:S(2)}) copy-start(s32[2,8]{1,0:T(2,128)} %pad_add_fusion.1.lim_ref) | copy-start | bytes 196
  341.7 187.9 %reduce-scatter.11.cloned.1.call-start = ((), (), s32[]{:S(2)}) async-start(), calls=%async_computation.11 | async-start | bytes 7864320 | tf_op jit(solution)/shard_map/reduce_scatter | solution.py:889
  405.3 21.9 %collective-permute-start.3 = (bf16[320,1024]{1,0:T(8,128)(2,1)S(1)}, bf16[320,1024]{1,0:T(8,128)(2,1)S(1)}, u32[]{:S(2)}, u32[]{:S(2)}) collective-permute-start(bf16[320,1024]{1,0:T(8,128)(2,1)S(1)} %pad_maximum_fusion.5), channel_id=1, source_target_pairs={{0,0},{1,16},{2,2},{3,18},{4,4},{5,20},{6,6},{7,22},{8,8},{9,24},{... | collective-permute-start | bytes 1966088 | tf_op jit(solution)/shard_map/ppermute | solution.py:867
  430.1 99.5 %copy-start.32 = (bf16[256,1024]{1,0:T(8,128)(2,1)S(1)}, bf16[256,1024]{1,0:T(8,128)(2,1)}, u32[]{:S(2)}) copy-start(bf16[256,1024]{1,0:T(8,128)(2,1)} %reduce-scatter.7.cloned.1.call-done.refs_0_) | copy-start | bytes 1572868
  531.0 81.5 %copy-start.24 = (f32[256,1024]{1,0:T(8,128)S(1)}, f32[256,1024]{1,0:T(8,128)}, u32[]{:S(2)}) copy-start(f32[256,1024]{1,0:T(8,128)} %copy-done.23) | copy-start | bytes 3145732
  531.0 81.5 %copy-start.58 = (f32[256,1024]{1,0:T(8,128)S(1)}, f32[256,1024]{1,0:T(8,128)}, u32[]{:S(2)}) copy-start(f32[256,1024]{1,0:T(8,128)} %copy-done.56) | copy-start | bytes 3145732
  623.0 15.8 %copy-start.71 = (bf16[320,1024]{1,0:T(8,128)(2,1)S(1)}, bf16[320,1024]{1,0:T(8,128)(2,1)}, u32[]{:S(2)}) copy-start(bf16[320,1024]{1,0:T(8,128)(2,1)} %copy-done.70) | copy-start | bytes 1966084
  623.0 16.9 %copy-start.34 = (bf16[256,1024]{1,0:T(8,128)(2,1)S(1)}, bf16[256,1024]{1,0:T(8,128)(2,1)}, u32[]{:S(2)}) copy-start(bf16[256,1024]{1,0:T(8,128)(2,1)} %copy-done.33) | copy-start | bytes 1572868
  625.0 19.1 %copy-start.61 = (bf16[256,4096]{1,0:T(8,128)(2,1)S(1)}, bf16[256,4096]{1,0:T(8,128)(2,1)}, u32[]{:S(2)}) copy-start(bf16[256,4096]{1,0:T(8,128)(2,1)} %get-tuple-element.158) | copy-start | bytes 6291460
  625.0 26.6 %collective-permute-start.4 = (bf16[256,1024]{1,0:T(8,128)(2,1)}, bf16[256,1024]{1,0:T(8,128)(2,1)}, u32[]{:S(2)}, u32[]{:S(2)}) collective-permute-start(bf16[256,1024]{1,0:T(8,128)(2,1)} %add_convert_fusion.1), channel_id=1, source_target_pairs={{0,0},{1,16},{2,2},{3,18},{4,4},{5,20},{6,6},{7,22},{8,8},{9,24},{... | collective-permute-start | bytes 1572872 | tf_op jit(solution)/shard_map/ppermute | solution.py:867
  642.3 11.1 %copy-start.1 = (bf16[704,1024]{1,0:T(8,128)(2,1)S(1)}, bf16[704,1024]{1,0:T(8,128)(2,1)}, u32[]{:S(2)}) copy-start(bf16[704,1024]{1,0:T(8,128)(2,1)} %param.32) | copy-start | bytes 4325380
  (81 other events, 197.5 us)
Sparse Core Ops, SparseCore 0:
  9.6 49.7 all-gather.6
  61.5 70.9 all-gather.8
  134.6 40.4 all-gather.10
  208.6 21.9 all-gather.12
  244.6 31.0 reduce-scatter.4
  282.5 31.3 reduce-scatter.6
  341.8 73.5 reduce-scatter.8
  418.1 58.3 reduce-scatter.10

commit v15 on v14

--- a/solution.py
+++ b/solution.py
@@ -962,7 +962,7 @@
     qkv_tok = jnp.einsum("td,dge->gte", normed_first, qkv_w, preferred_element_type=f32).astype(bf16)
     others = change_home(jnp.concatenate([cotangent.reshape(rows, width), encoder.reshape(-1, width)]))
     grad_low, enc_flat = others[:rows], others[rows:]
-    fars = [tuple(far for far in range(fan) if by_kernel and min(far, 3) in some) for some in ((2,), (0, 1), (3,))]
+    fars = [tuple(far for far in range(fan) if by_kernel and (far == 2) == first) for first in (True, False)]
     qkv, *halves = swap([qkv_tok], 17, fars[0], inner_t)
     qkv, cross_out, grad_low = lax.optimization_barrier((qkv, cross_out, grad_low))
     if rows == cross_out.shape[0]:
@@ -986,10 +986,10 @@
             ((parts, enc_local, own * 2 * dh), bf16),
         ],
     )
-    query_cross, pairs, *halves = swap([query_tok, pairs_tok], 15, fars[1], inner_t, halves)
+    query_cross, pairs = swap([query_tok, pairs_tok], 12)
     query_cross, pairs = query_cross.reshape(length, own * dh), pairs.reshape(keys, own * 2 * dh)
     out_cross, cross_t, cross_lse = cross_forward(cross_limits, cross_rows, query_cross, pairs)
-    cross_tok, *halves = swap([out_cross.reshape(parts, local, own * dh)], 16, fars[2], inner_t, halves)
+    cross_tok, *halves = swap([out_cross.reshape(parts, local, own * dh)], 16, fars[1], inner_t, halves)
     if not by_kernel:
         halves = spread(jnp.transpose(inner_t.reshape(2, fan, units, -1), (1, 0, 2, 3)))
         halves = [jnp.transpose(halves[:, i], (1, 0, 2)).reshape(units, width) for i in range(2)]

time: 671 us -> 664 us (0.990)
    pallas_call x9, Pallas kernels: 143 us -> 134 us  [swap(): pl.pallas_call(functools.partial(swap_kernel, n, fan, count, fars, not fa...]
    unnamed x219 -> x213, local copies, waits for them, and re-layouts: 56.6 us -> 54 us
  transfers between devices with their start and end apart: 13 -> 13, of which waited for: 6 -> 6; matrix products, arithmetic and copies ran while one was open for 12% -> 13% of each run, Pallas kernels for 46% -> 45%
where the time goes in v15:
time: 664 us; the launch traced here: 657 us
  Pallas kernels  376 us (57%)
  local copies, waits for them, and re-layouts  66.7 us (10%)
  waiting for transfers between devices  60.6 us (9%)
  matrix products  55.6 us (8%)
  other arithmetic  41.9 us (6%)
  starting transfers between devices  33.2 us (5%)
  between operations  16 us (2%)
    pallas_call x2, Pallas kernels, ring_call(): pl.pallas_call(body, name=name, out_shape=[jax.ShapeDtypeStruct(s, d) for...  179 us
    pallas_call x9, Pallas kernels, swap(): pl.pallas_call(functools.partial(swap_kernel, n, fan, count, fars, not fa...  134 us
    pallas_call x4, Pallas kernels, call(): pl.pallas_call(body, name=name, out_shape=[jax.ShapeDtypeStruct(s, d) for...  57.1 us
    unnamed x213, local copies, waits for them, and re-layouts  54 us
    ppermute x5, starting transfers between devices, change_home(): return lax.ppermute(value, ('seq', 'fsdp'), pairs)  31.6 us
    all_gather x2, waiting for transfers between devices, shards(): gather = lambda v: lax.all_gather(v, 'fsdp', axis=0, tiled=True)  22 us
    ppermute x5, waiting for transfers between devices, change_home(): return lax.ppermute(value, ('seq', 'fsdp'), pairs)  21.2 us
    reduce_scatter x4, waiting for transfers between devices, scatter(): return lax.psum_scatter(grad, 'fsdp', scatter_dimension=0, tiled=True)  16.6 us
  transfers between devices with their start and end apart: 13, of which 6 were waited for; matrix products, arithmetic and copies ran while one was open for 13% of the time, Pallas kernels for 45%

profile of v15, /device:TPU:1, one launch (start us, length us, event | category | flops | bytes accessed | tf_op | source)
XLA Modules:
  0.0 656.6 jit_solution(17596706503760049684)
XLA Ops:
  9.8 6.1 all-gather.1
  18.3 4.7 collective-permute-start.1
  25.0 4.5 collective-permute-start.2
  30.9 4.5 copy.77
  36.1 4.9 swap.9
  45.7 5.2 fusion.38
  55.2 4.2 all-gather.7.cloned.1.call-done
  60.2 5.8 fusion.10.refs_0_
  66.1 31.4 %swap.10 = (bf16[8,256,384]{2,1,0:T(8,128)(2,1)}, bf16[704,1024]{1,0:T(8,128)(2,1)}, bf16[704,1024]{1,0:T(8,128)(2,1)}) custom-call(bf16[8,256,384]{2,1,0:T(8,128)(2,1)} %fusion.10.refs_0_, bf16[5632,256]{1,0:T(8,128)(2,1)} %bitcast.182), custom_call_target="tpu_custom_call" | custom-call | bytes 1572864 | tf_op jit(solution)/shard_map/swap/pallas_call | solution.py:826
  105.0 18.1 %self_forward.1 = (bf16[2048,128]{1,0:T(8,128)(2,1)S(1)}, f32[128,2048]{1,0:T(8,128)S(1)}, f32[2,2048]{1,0:T(2,128)S(1)}) custom-call(s32[2,8]{1,0:T(2,128)S(1)} %copy-done.52, s32[8,2048]{1,0:T(8,128)S(1)} %copy-done.27, f32[2,1536]{1,0:T(2,128)S(1)} %maximum_maximum_fusion.ext_ref, bf16[2048,384]{1,0:T(8,128)(2,1)S(1)} %bitcast.167), custom_call_target="tpu_custom_call" | custom-call | bytes 1650752 | tf_op jit(solution)/shard_map/self_forward/pallas_call | solution.py:251
  125.4 10.0 %swap.11.tok_ref = bf16[8,256,128]{2,1,0:T(8,128)(2,1)} custom-call(bf16[8,256,128]{2,1,0:T(8,128)(2,1)} %bitcast.178), custom_call_target="tpu_custom_call" | custom-call | bytes 524288 | tf_op jit(solution)/shard_map/swap/pallas_call | solution.py:826
  146.7 13.5 %swap.12 = (bf16[8,256,128]{2,1,0:T(8,128)(2,1)}, bf16[8,64,256]{2,1,0:T(8,128)(2,1)}) custom-call(bf16[8,256,128]{2,1,0:T(8,128)(2,1)} %copy-done.38, bf16[8,64,256]{2,1,0:T(8,128)(2,1)} %copy-done.45), custom_call_target="tpu_custom_call" | custom-call | bytes 786432 | tf_op jit(solution)/shard_map/swap/pallas_call | solution.py:826
  163.8 8.6 %cross_forward.1 = (bf16[2048,128]{1,0:T(8,128)(2,1)S(1)}, f32[128,2048]{1,0:T(8,128)S(1)}, f32[2,2048]{1,0:T(2,128)S(1)}) custom-call(s32[2,8]{1,0:T(2,128)S(1)} %copy-done.50, s32[8,2048]{1,0:T(8,128)S(1)} %copy-done.29, bf16[2048,128]{1,0:T(8,128)(2,1)S(1)} %bitcast.169, bf16[512,256]{1,0:T(8,128)(2,1)S(1)} %bitcast.174), custom_call_target="tpu_custom_call" | custom-call | bytes 852032 | tf_op jit(solution)/shard_map/cross_forward/pallas_call | solution.py:251
  174.8 21.2 %swap.13 = (bf16[8,256,128]{2,1,0:T(8,128)(2,1)}, bf16[704,1024]{1,0:T(8,128)(2,1)}, bf16[704,1024]{1,0:T(8,128)(2,1)}) custom-call(bf16[8,256,128]{2,1,0:T(8,128)(2,1)} %bitcast.176, bf16[5632,256]{1,0:T(8,128)(2,1)} %bitcast.183, bf16[704,1024]{1,0:T(8,128)(2,1)} %get-tuple-element.105.refs_2_, ...), custom_call_target="tpu_custom_call", output_to_operand_aliasing={{1}: (2, {}), {2}: (3, {})} | custom-call | bytes 524288 | tf_op jit(solution)/shard_map/swap/pallas_call | solution.py:826
  203.3 4.9 fusion.8
  208.2 17.9 %all-gather.13.cloned.1.call-done = bf16[1024,1024]{1,0:T(8,128)(2,1)} async-done(((bf16[256,1024]{1,0:T(8,128)(2,1)}), bf16[1024,1024]{1,0:T(8,128)(2,1)}) %all-gather.13.cloned.1.call-update) | async-done | bytes 2097168 | tf_op jit(solution)/shard_map/all_gather | solution.py:906
  230.0 4.7 multiply_convert_fusion
  254.5 16.5 %reduce-scatter.5.cloned.1.call-done = bf16[256,1024]{1,0:T(8,128)(2,1)} async-done(((bf16[1024,1024]{1,0:T(8,128)(2,1)}), bf16[256,1024]{1,0:T(8,128)(2,1)}) %reduce-scatter.5.cloned.1.call-update) | async-done | bytes 524304 | tf_op jit(solution)/shard_map/reduce_scatter | solution.py:889
  281.3 10.1 %swap.14 = bf16[8,256,128]{2,1,0:T(8,128)(2,1)} custom-call(bf16[8,256,128]{2,1,0:T(8,128)(2,1)} %fusion.16.refs_0_), custom_call_target="tpu_custom_call" | custom-call | bytes 524288 | tf_op jit(solution)/shard_map/swap/pallas_call | solution.py:826
  294.8 9.9 %cross_backward.1 = (bf16[2048,128]{1,0:T(8,128)(2,1)S(1)}, bf16[512,256]{1,0:T(8,128)(2,1)S(1)}) custom-call(s32[2,8]{1,0:T(2,128)S(1)} %copy-done.51, s32[8,2048]{1,0:T(8,128)S(1)} %copy-done.30, bf16[2048,128]{1,0:T(8,128)(2,1)S(1)} %bitcast.170, bf16[512,256]{1,0:T(8,128)(2,1)S(1)} %bitcast.175, bf16[2048,128]{1,0:T(8,128)(2,1)S(1)} %bitcast.171, ...), custom_call_target="tpu_custom_call" | custom-call | bytes 2441280 | tf_op jit(solution)/shard_map/cross_backward/pallas_call | solution.py:251
  306.3 11.9 %swap.15 = (bf16[8,256,128]{2,1,0:T(8,128)(2,1)}, bf16[8,64,256]{2,1,0:T(8,128)(2,1)}) custom-call(bf16[8,256,128]{2,1,0:T(8,128)(2,1)} %bitcast.177, bf16[8,64,256]{2,1,0:T(8,128)(2,1)} %bitcast.179), custom_call_target="tpu_custom_call" | custom-call | bytes 786432 | tf_op jit(solution)/shard_map/swap/pallas_call | solution.py:826
  336.8 9.6 %swap.16 = bf16[8,256,128]{2,1,0:T(8,128)(2,1)} custom-call(bf16[8,256,128]{2,1,0:T(8,128)(2,1)} %copy-done.39), custom_call_target="tpu_custom_call" | custom-call | bytes 524288 | tf_op jit(solution)/shard_map/swap/pallas_call | solution.py:826
  347.6 20.5 %self_backward.1 = (bf16[2048,384]{1,0:T(8,128)(2,1)S(1)}, f32[2,1536]{1,0:T(2,128)S(1)}) custom-call(s32[2,8]{1,0:T(2,128)S(1)} %copy-done.53, s32[8,2048]{1,0:T(8,128)S(1)} %copy-done.28, f32[2,1536]{1,0:T(2,128)S(1)} %maximum_maximum_fusion.ext_ref, bf16[2048,384]{1,0:T(8,128)(2,1)S(1)} %bitcast.168, bf16[2048,128]{1,0:T(8,128)(2,1)S(1)} %bitcast.172, ...), custom_call_target="tpu_custom_call" | custom-call | bytes 3240000 | tf_op jit(solution)/shard_map/self_backward/pallas_call | solution.py:251
  369.3 21.4 %swap.17 = bf16[8,256,384]{2,1,0:T(8,128)(2,1)} custom-call(bf16[8,256,384]{2,1,0:T(8,128)(2,1)} %bitcast.173), custom_call_target="tpu_custom_call" | custom-call | bytes 1572864 | tf_op jit(solution)/shard_map/swap/pallas_call | solution.py:826
  392.5 4.6 convolution_convert_fusion
  397.2 4.9 fusion.18
  402.6 7.5 %collective-permute-start.3 = (bf16[320,1024]{1,0:T(8,128)(2,1)S(1)}, bf16[320,1024]{1,0:T(8,128)(2,1)S(1)}, u32[]{:S(2)}, u32[]{:S(2)}) collective-permute-start(bf16[320,1024]{1,0:T(8,128)(2,1)S(1)} %pad_maximum_fusion.5), channel_id=1, source_target_pairs={{0,0},{1,16},{2,2},{3,18},{4,4},{5,20},{6,6},{7,22},{8,8},{9,24},{... | collective-permute-start | bytes 1966088 | tf_op jit(solution)/shard_map/ppermute | solution.py:867
  411.1 14.1 %collective-permute-done.3 = bf16[320,1024]{1,0:T(8,128)(2,1)S(1)} collective-permute-done((bf16[320,1024]{1,0:T(8,128)(2,1)S(1)}, bf16[320,1024]{1,0:T(8,128)(2,1)S(1)}, u32[]{:S(2)}, u32[]{:S(2)}) %collective-permute-start.3) | collective-permute-done | bytes 655392 | tf_op jit(solution)/shard_map/ppermute | solution.py:867
  427.1 96.9 %units_total.1 = (bf16[5632,256]{1,0:T(8,128)(2,1)}, bf16[704,1024]{1,0:T(8,128)(2,1)S(1)}, f32[256,1024]{1,0:T(8,128)S(1)}, f32[8,1024]{1,0:T(8,128)S(1)}) custom-call(bf16[2112,1024]{1,0:T(8,128)(2,1)} %bitcast.190, bf16[1024,1024]{1,0:T(8,128)(2,1)S(1)} %copy-done.10, bf16[32,1024]{1,0:T(8,128)(2,1)S(1)} %pad_bitcast_fusion.few_ref), custom_call_target="tpu_custom_call" | custom-call | bytes 389283840 | tf_op jit(solution)/shard_map/units_total/pallas_call | solution.py:543
  526.5 82.3 %ring_total.1 = (bf16[256,1024]{1,0:T(8,128)(2,1)S(1)}, bf16[256,4096]{1,0:T(8,128)(2,1)}, bf16[256,3072]{1,0:T(8,128)(2,1)S(1)}, bf16[64,128]{1,0:T(8,128)(2,1)S(1)}, bf16[256,5632]{1,0:T(8,128)(2,1)}) custom-call(bf16[256,1024]{1,0:T(8,128)(2,1)S(1)} %copy-done.32, bf16[256,4096]{1,0:T(8,128)(2,1)} %reduce-scatter.9.cloned.1.call-done.refs_1_, ...), custom_call_target="tpu_custom_call" | custom-call | bytes 425656320 | tf_op jit(solution)/shard_map/ring_total/pallas_call | solution.py:543
  621.7 13.0 %collective-permute-start.4 = (bf16[256,1024]{1,0:T(8,128)(2,1)}, bf16[256,1024]{1,0:T(8,128)(2,1)}, u32[]{:S(2)}, u32[]{:S(2)}) collective-permute-start(bf16[256,1024]{1,0:T(8,128)(2,1)} %add_convert_fusion.1), channel_id=1, source_target_pairs={{0,0},{1,16},{2,2},{3,18},{4,4},{5,20},{6,6},{7,22},{8,8},{9,24},{... | collective-permute-start | bytes 1572872 | tf_op jit(solution)/shard_map/ppermute | solution.py:867
  641.5 6.0 collective-permute-done.4
  (330 shorter events, 141.1 us)
Async XLA Ops:
  7.2 196.1 %copy-start = (bf16[704,1024]{1,0:T(8,128)(2,1)S(1)}, bf16[704,1024]{1,0:T(8,128)(2,1)}, u32[]{:S(2)}) copy-start(bf16[704,1024]{1,0:T(8,128)(2,1)} %param.32) | copy-start | bytes 4325380
  7.2 52.1 %all-gather.7.cloned.1.call-start = ((), (), s32[]{:S(2)}) async-start(), calls=%async_computation.4 | async-start | bytes 7864320 | tf_op jit(solution)/shard_map/all_gather | solution.py:906
  8.0 127.5 %all-gather.9.cloned.1.call-start = ((), (), s32[]{:S(2)}) async-start(), calls=%async_computation.5 | async-start | bytes 10485760 | tf_op jit(solution)/shard_map/all_gather | solution.py:918
  17.6 12.3 %copy-start.85 = (s32[2048]{0:T(1024)S(1)}, s32[2048]{0:T(1024)}, u32[]{:S(2)}) copy-start(s32[2048]{0:T(1024)} %param.21) | copy-start | bytes 24580
  17.6 178.3 %all-gather.11.cloned.1.call-start = ((), (), s32[]{:S(2)}) async-start(), calls=%async_computation.6 | async-start | bytes 5242880 | tf_op jit(solution)/shard_map/all_gather | solution.py:969
  18.3 17.2 %collective-permute-start.1 = (s32[8,128]{1,0:T(8,128)S(1)}, s32[8,128]{1,0:T(8,128)S(1)}, u32[]{:S(2)}, u32[]{:S(2)}) collective-permute-start(s32[8,128]{1,0:T(8,128)S(1)} %pad_bitcast_fusion.1), channel_id=1, source_target_pairs={{0,0},{1,16},{2,2},{3,18},{4,4},{5,20},{6,6},{7,22},{8,8},{9,24},{... | collective-permute-start | bytes 12296 | tf_op jit(solution)/shard_map/ppermute | solution.py:867
  23.0 32.2 %collective-permute-start = (bf16[256,1024]{1,0:T(8,128)(2,1)}, bf16[256,1024]{1,0:T(8,128)(2,1)S(1)}, u32[]{:S(2)}, u32[]{:S(2)}) collective-permute-start(bf16[256,1024]{1,0:T(8,128)(2,1)} %bitcast), channel_id=1, source_target_pairs={{0,0},{1,16},{2,2},{3,18},{4,4},{5,20},{6,6},{7,22},{8,8},{9,24},{... | collective-permute-start | bytes 1572872 | tf_op jit(solution)/shard_map/ppermute | solution.py:867
  25.0 29.3 %collective-permute-start.2 = (bf16[320,1024]{1,0:T(8,128)(2,1)S(1)}, bf16[320,1024]{1,0:T(8,128)(2,1)S(1)}, u32[]{:S(2)}, u32[]{:S(2)}) collective-permute-start(bf16[320,1024]{1,0:T(8,128)(2,1)S(1)} %pad_maximum_fusion.4), channel_id=1, source_target_pairs={{0,0},{1,16},{2,2},{3,18},{4,4},{5,20},{6,6},{7,22},{8,8},{9,24},{... | collective-permute-start | bytes 1966088 | tf_op jit(solution)/shard_map/ppermute | solution.py:867
  35.5 30.6 %copy-start.72 = (f32[1,2,4,128]{3,1,2,0:T(2,128)}, f32[1,2,4,128]{3,1,2,0:T(2,128)S(1)}, u32[]{:S(2)}) copy-start(f32[1,2,4,128]{3,1,2,0:T(2,128)S(1)} %copy.107) | copy-start | bytes 12292
  54.3 11.8 %copy-start.66 = (bf16[320,1024]{1,0:T(8,128)(2,1)}, bf16[320,1024]{1,0:T(8,128)(2,1)S(1)}, u32[]{:S(2)}) copy-start(bf16[320,1024]{1,0:T(8,128)(2,1)S(1)} %collective-permute-done.2) | copy-start | bytes 1966084
  99.9 126.2 %all-gather.13.cloned.1.call-start = ((), (), s32[]{:S(2)}) async-start(), calls=%async_computation.7 | async-start | bytes 2621440 | tf_op jit(solution)/shard_map/all_gather | solution.py:906
  202.9 68.1 %reduce-scatter.5.cloned.1.call-start = ((), (), s32[]{:S(2)}) async-start(), calls=%async_computation.8 | async-start | bytes 2621440 | tf_op jit(solution)/shard_map/reduce_scatter | solution.py:889
  239.8 185.3 %reduce-scatter.7.cloned.1.call-start = ((), (), s32[]{:S(2)}) async-start(), calls=%async_computation.9 | async-start | bytes 2621440 | tf_op jit(solution)/shard_map/reduce_scatter | solution.py:889
  277.9 13.6 %copy-start.26 = (bf16[8,64,256]{2,1,0:T(8,128)(2,1)S(1)}, bf16[8,64,256]{2,1,0:T(8,128)(2,1)}, u32[]{:S(2)}) copy-start(bf16[8,64,256]{2,1,0:T(8,128)(2,1)} %get-tuple-element.103) | copy-start | bytes 786436
  277.9 13.6 %copy-start.30 = (s32[8,2048]{1,0:T(8,128)S(1)}, s32[8,2048]{1,0:T(8,128)}, u32[]{:S(2)}) copy-start(s32[8,2048]{1,0:T(8,128)} %add_add_fusion.2.rows_ref) | copy-start | bytes 196612
  278.0 13.6 %copy-start.49 = (f32[2,2048]{1,0:T(2,128)S(1)}, f32[2,2048]{1,0:T(2,128)}, u32[]{:S(2)}) copy-start(f32[2,2048]{1,0:T(2,128)} %copy-done.48) | copy-start | bytes 49156
  278.0 13.6 %copy-start.51 = (s32[2,8]{1,0:T(2,128)S(1)}, s32[2,8]{1,0:T(2,128)}, u32[]{:S(2)}) copy-start(s32[2,8]{1,0:T(2,128)} %pad_add_fusion.2.lim_ref) | copy-start | bytes 196
  278.0 147.2 %reduce-scatter.9.cloned.1.call-start = ((), (), s32[]{:S(2)}) async-start(), calls=%async_computation.10 | async-start | bytes 10485760 | tf_op jit(solution)/shard_map/reduce_scatter | solution.py:889
  336.5 9.9 %copy-start.18 = (f32[128,2048]{1,0:T(8,128)S(1)}, f32[128,2048]{1,0:T(8,128)}, u32[]{:S(2)}) copy-start(f32[128,2048]{1,0:T(8,128)} %copy-done.17) | copy-start | bytes 3145732
  336.5 9.9 %copy-start.28 = (s32[8,2048]{1,0:T(8,128)S(1)}, s32[8,2048]{1,0:T(8,128)}, u32[]{:S(2)}) copy-start(s32[8,2048]{1,0:T(8,128)} %broadcast_in_dim.102.rows_ref) | copy-start | bytes 196612
  336.5 9.9 %copy-start.47 = (f32[2,2048]{1,0:T(2,128)S(1)}, f32[2,2048]{1,0:T(2,128)}, u32[]{:S(2)}) copy-start(f32[2,2048]{1,0:T(2,128)} %copy-done.46) | copy-start | bytes 49156
  336.5 10.0 %copy-start.53 = (s32[2,8]{1,0:T(2,128)S(1)}, s32[2,8]{1,0:T(2,128)}, u32[]{:S(2)}) copy-start(s32[2,8]{1,0:T(2,128)} %pad_add_fusion.1.lim_ref) | copy-start | bytes 196
  336.5 188.5 %reduce-scatter.11.cloned.1.call-start = ((), (), s32[]{:S(2)}) async-start(), calls=%async_computation.11 | async-start | bytes 7864320 | tf_op jit(solution)/shard_map/reduce_scatter | solution.py:889
  402.6 22.5 %collective-permute-start.3 = (bf16[320,1024]{1,0:T(8,128)(2,1)S(1)}, bf16[320,1024]{1,0:T(8,128)(2,1)S(1)}, u32[]{:S(2)}, u32[]{:S(2)}) collective-permute-start(bf16[320,1024]{1,0:T(8,128)(2,1)S(1)} %pad_maximum_fusion.5), channel_id=1, source_target_pairs={{0,0},{1,16},{2,2},{3,18},{4,4},{5,20},{6,6},{7,22},{8,8},{9,24},{... | collective-permute-start | bytes 1966088 | tf_op jit(solution)/shard_map/ppermute | solution.py:867
  425.1 98.9 %copy-start.67 = (bf16[320,1024]{1,0:T(8,128)(2,1)}, bf16[320,1024]{1,0:T(8,128)(2,1)S(1)}, u32[]{:S(2)}) copy-start(bf16[320,1024]{1,0:T(8,128)(2,1)S(1)} %collective-permute-done.3) | copy-start | bytes 1966084
  427.1 97.9 %copy-start.32 = (bf16[256,1024]{1,0:T(8,128)(2,1)S(1)}, bf16[256,1024]{1,0:T(8,128)(2,1)}, u32[]{:S(2)}) copy-start(bf16[256,1024]{1,0:T(8,128)(2,1)} %reduce-scatter.7.cloned.1.call-done.refs_0_) | copy-start | bytes 1572868
  526.5 82.4 %copy-start.24 = (f32[256,1024]{1,0:T(8,128)S(1)}, f32[256,1024]{1,0:T(8,128)}, u32[]{:S(2)}) copy-start(f32[256,1024]{1,0:T(8,128)} %copy-done.23) | copy-start | bytes 3145732
  619.8 14.9 %copy-start.68 = (bf16[320,1024]{1,0:T(8,128)(2,1)S(1)}, bf16[320,1024]{1,0:T(8,128)(2,1)}, u32[]{:S(2)}) copy-start(bf16[320,1024]{1,0:T(8,128)(2,1)} %copy-done.67) | copy-start | bytes 1966084
  619.8 16.0 %copy-start.34 = (bf16[256,1024]{1,0:T(8,128)(2,1)S(1)}, bf16[256,1024]{1,0:T(8,128)(2,1)}, u32[]{:S(2)}) copy-start(bf16[256,1024]{1,0:T(8,128)(2,1)} %copy-done.33) | copy-start | bytes 1572868
  621.7 18.2 %copy-start.58 = (bf16[256,4096]{1,0:T(8,128)(2,1)S(1)}, bf16[256,4096]{1,0:T(8,128)(2,1)}, u32[]{:S(2)}) copy-start(bf16[256,4096]{1,0:T(8,128)(2,1)} %get-tuple-element.154) | copy-start | bytes 6291460
  621.7 25.7 %collective-permute-start.4 = (bf16[256,1024]{1,0:T(8,128)(2,1)}, bf16[256,1024]{1,0:T(8,128)(2,1)}, u32[]{:S(2)}, u32[]{:S(2)}) collective-permute-start(bf16[256,1024]{1,0:T(8,128)(2,1)} %add_convert_fusion.1), channel_id=1, source_target_pairs={{0,0},{1,16},{2,2},{3,18},{4,4},{5,20},{6,6},{7,22},{8,8},{9,24},{... | collective-permute-start | bytes 1572872 | tf_op jit(solution)/shard_map/ppermute | solution.py:867
  638.2 11.1 %copy-start.1 = (bf16[704,1024]{1,0:T(8,128)(2,1)S(1)}, bf16[704,1024]{1,0:T(8,128)(2,1)}, u32[]{:S(2)}) copy-start(bf16[704,1024]{1,0:T(8,128)(2,1)} %param.32) | copy-start | bytes 4325380
  (78 other events, 201.2 us)
Sparse Core Ops, SparseCore 0:
  9.6 49.7 all-gather.6
  61.5 70.8 all-gather.8
  134.6 33.6 all-gather.10
  203.1 22.8 all-gather.12
  240.0 31.0 reduce-scatter.4
  278.1 31.3 reduce-scatter.6
  336.6 74.1 reduce-scatter.8
  413.5 58.3 reduce-scatter.10

commit v16 on v15

--- a/solution.py
+++ b/solution.py
@@ -423,7 +423,7 @@
         in_specs=[whole(v.shape) for v in arrays] + [pl.BlockSpec((1, rows, cols), lambda i: (order(i), 0, 0))],
         out_specs=[whole(s) for s, _ in outs],
         scratch_shapes=[pltpu.VMEM(s, d) for s, d in scratch],
-        compiler_params=pltpu.CompilerParams(vmem_limit_bytes=40 << 20, dimension_semantics=("arbitrary",)),
+        compiler_params=pltpu.CompilerParams(vmem_limit_bytes=62 << 20, dimension_semantics=("arbitrary",)),
         cost_estimate=pl.CostEstimate(flops=0, bytes_accessed=weights.size * 2, transcendentals=0),
     )(*arrays, weights)
 
@@ -475,7 +475,9 @@
     slots = refs[2 * (count + more) : 3 * count + 2 * more]
     send_sem, recv_sem = refs[3 * count + 2 * more :]
     place, right, left = ring_greet(n, [])
-    streams = [(k, piece, piece % 2) for k in range(count) for piece in range(abs(splits[k]))]
+    streams = [
+        (k, piece, (piece if abs(splits[k]) > 1 else k) % 2) for k in range(count) for piece in range(abs(splits[k]))
+    ]
 
     def window(ref, k, piece, chunk):
         return ring_window(ref, x_refs[k].shape, splits[k], n, piece, chunk)
@@ -1054,14 +1056,8 @@
     grad_query_w = jnp.einsum("td,te->de", normed_second, grad_query_tok, preferred_element_type=f32)
     grad_pairs_w = jnp.einsum("td,te->de", enc_flat, grad_pairs_tok, preferred_element_type=f32)
     grad_mix_self = jnp.einsum("gtc,td->gcd", self_tok, upper_low, preferred_element_type=f32)
-    grad_mid = jnp.concatenate(
-        [
-            grad_query_w.astype(bf16),
-            grad_pairs_w.astype(bf16),
-            grad_mix_self.reshape(width, width).astype(bf16),
-        ],
-        axis=1,
-    )
+    grad_mid = jnp.concatenate([grad_query_w.astype(bf16), grad_pairs_w.astype(bf16)], axis=1)
+    part_self = scatter(grad_mix_self.reshape(width, width).astype(bf16))
     grad_self_tok, grad_mid = lax.optimization_barrier((grad_self_tok, grad_mid))
     part_mid = scatter(grad_mid)
     (grad_self,) = swap([grad_self_tok], 11)
@@ -1094,8 +1090,8 @@
         few = jnp.pad(small_grads[:, None], ((0, 0), (0, 7), (0, 1024 - small_size))).reshape(fan * 8, 1024)
         total_inner, total_outer, outer_sum, few = units_total(part_units, outer_part, few, 0)
         few = jnp.pad(few[0].astype(bf16).reshape(8, 128), ((0, parts * 8 - 8), (0, 0)))
-        total_cross, total_mid, total_qkv, small_total, total_inner = ring_total(
-            [part_cross, part_mid, part_last, few], (2, 2, 2, 1), 1, total_inner
+        total_cross, total_self, total_mid, total_qkv, small_total, total_inner = ring_total(
+            [part_cross, part_self, part_mid, part_last, few], (1, 1, 2, 2, 1), 1, total_inner
         )
     else:
         grad_units = [lax.psum(g, "seq") for g in part_units]
@@ -1103,12 +1099,14 @@
         total_inner = jnp.transpose(total_inner, (3, 1, 0, 2)).reshape(-1, 2 * fan * units).astype(f32)
         total_outer, outer_sum = grad_units[2], scatter(outer_part).astype(f32)
         few = lax.dynamic_index_in_dim(lax.psum(small_grads, "fsdp"), lax.axis_index("fsdp"), 0, False)
-        total_cross, total_mid, total_qkv, small_total = (
-            lax.psum(v, "seq") for v in (part_cross, part_mid, part_last, few)
+        total_cross, total_self, total_mid, total_qkv, small_total = (
+            lax.psum(v, "seq") for v in (part_cross, part_self, part_mid, part_last, few)
         )
     layer_out = (after_cross + outer_sum).astype(bf16)
-    layer_out, total_inner, total_outer, total_cross, total_mid, total_qkv, going_home = lax.optimization_barrier(
-        (layer_out, total_inner, total_outer, total_cross, total_mid, total_qkv, going_home)
+    layer_out, total_inner, total_outer, total_cross, total_self, total_mid, total_qkv, going_home = (
+        lax.optimization_barrier(
+            (layer_out, total_inner, total_outer, total_cross, total_self, total_mid, total_qkv, going_home)
+        )
     )
     layer_out = change_home(layer_out).reshape(seqs, local, width)
     grad_layer_in = going_home[:rows].astype(f32).reshape(seqs, local, width)
@@ -1117,8 +1115,8 @@
         v.astype(f32) for v in (total_inner, total_outer, total_mid, total_qkv)
     )
     total_query, total_mix_cross = total_mid[:, :width], total_cross.astype(f32)
-    total_pairs = total_mid[:, width : 3 * width].reshape(-1, heads, 2 * dh)
-    total_mix_self, total_qkv = total_mid[:, 3 * width :], total_qkv.reshape(-1, heads, 3 * dh)
+    total_pairs = total_mid[:, width:].reshape(-1, heads, 2 * dh)
+    total_mix_self, total_qkv = total_self.astype(f32), total_qkv.reshape(-1, heads, 3 * dh)
     mine = small_total.reshape(-1)[:small_size].astype(f32)
     total_gain_first, total_gain_second, total_gain_third = (mine[i * part : (i + 1) * part] for i in range(3))
     total_table = mine[3 * part :].reshape(buckets, table_own)

time: 664 us -> 641 us (0.965)
  the two profiles are of different devices: /device:TPU:1 before, /device:TPU:0 now
where the time goes in v16:
time: 641 us; the launch traced here: 630 us
  Pallas kernels  416 us (65%)
  matrix products  57.2 us (9%)
  local copies, waits for them, and re-layouts  44.2 us (7%)
  waiting for transfers between devices  42.2 us (7%)
  other arithmetic  35.6 us (6%)
  between operations  15.2 us (2%)
  starting transfers between devices  13 us (2%)
    pallas_call x2, Pallas kernels, ring_call(): pl.pallas_call(body, name=name, out_shape=[jax.ShapeDtypeStruct(s, d) for...  208 us
    pallas_call x9, Pallas kernels, swap(): pl.pallas_call(functools.partial(swap_kernel, n, fan, count, fars, not fa...  141 us
    pallas_call x4, Pallas kernels, call(): pl.pallas_call(body, name=name, out_shape=[jax.ShapeDtypeStruct(s, d) for...  50.6 us
    unnamed x151, local copies, waits for them, and re-layouts  32.3 us
    all_gather x2, waiting for transfers between devices, shards(): gather = lambda v: lax.all_gather(v, 'fsdp', axis=0, tiled=True)  21.8 us
    reduce_scatter x5, waiting for transfers between devices, scatter(): return lax.psum_scatter(grad, 'fsdp', scatter_dimension=0, tiled=True)  17 us
    pallas_call x2, Pallas kernels, over_weights(): pl.pallas_call(body, name=name, grid=(count,), out_shape=[jax.ShapeDtypeS...  15.6 us
  transfers between devices with their start and end apart: 14, of which 4 were waited for; matrix products, arithmetic and copies ran while one was open for 15% of the time, Pallas kernels for 53%

profile of v16, /device:TPU:0, one launch (start us, length us, event | category | flops | bytes accessed | tf_op | source)
XLA Modules:
  0.0 629.7 jit_solution(17437359889127958462)
XLA Ops:
  9.9 6.2 all-gather.1
  24.3 4.6 copy.77
  29.5 12.4 %swap.9 = s32[8,8,128]{2,1,0:T(8,128)} custom-call(s32[8,8,128]{2,1,0:T(8,128)} %broadcast_in_dim.97.refs_0_), custom_call_target="tpu_custom_call" | custom-call | bytes 16384 | tf_op jit(solution)/shard_map/swap/pallas_call | solution.py:828
  46.6 5.2 fusion.38
  53.4 6.2 all-gather.7.cloned.1.call-done
  59.8 5.8 fusion.10.refs_0_
  65.6 32.3 %swap.10 = (bf16[8,256,384]{2,1,0:T(8,128)(2,1)}, bf16[704,1024]{1,0:T(8,128)(2,1)}, bf16[704,1024]{1,0:T(8,128)(2,1)}) custom-call(bf16[8,256,384]{2,1,0:T(8,128)(2,1)} %fusion.10.refs_0_, bf16[5632,256]{1,0:T(8,128)(2,1)} %bitcast.180), custom_call_target="tpu_custom_call" | custom-call | bytes 1572864 | tf_op jit(solution)/shard_map/swap/pallas_call | solution.py:828
  103.8 14.7 %self_forward.1 = (bf16[2048,128]{1,0:T(8,128)(2,1)S(1)}, f32[128,2048]{1,0:T(8,128)S(1)}, f32[2,2048]{1,0:T(2,128)S(1)}) custom-call(s32[2,8]{1,0:T(2,128)S(1)} %pad_add_fusion.1.lim_ref, s32[8,2048]{1,0:T(8,128)S(1)} %broadcast_in_dim.102.rows_ref, f32[2,1536]{1,0:T(2,128)S(1)} %maximum_maximum_fusion.ext_ref, bf16[2048,384]{1,0:T(8,128)(2,1)S(1)} %bitcast.167), custom_call_target="tpu_custom_call" | custom-call | bytes 1650752 | tf_op jit(solution)/shard_map/self_forward/pallas_call | solution.py:251
  120.3 9.1 %swap.11.tok_ref = bf16[8,256,128]{2,1,0:T(8,128)(2,1)} custom-call(bf16[8,256,128]{2,1,0:T(8,128)(2,1)} %bitcast.178), custom_call_target="tpu_custom_call" | custom-call | bytes 524288 | tf_op jit(solution)/shard_map/swap/pallas_call | solution.py:828
  131.9 7.1 %self_out_to_cross.1 = (f32[256,1024]{1,0:T(8,128)}, bf16[256,1024]{1,0:T(8,128)(2,1)}, bf16[8,256,128]{2,1,0:T(8,128)(2,1)}, bf16[8,64,256]{2,1,0:T(8,128)(2,1)}) custom-call(bf16[8,256,128]{2,1,0:T(8,128)(2,1)} %swap.11.tok_ref, bf16[256,1024]{1,0:T(8,128)(2,1)} %copy-done.30, f32[1,1024]{1,0:T(1,128)} %bitcast.216, bf16[64,1024]{1,0:T(8,128)(2,1)} %slice.116.enc_ref, ...), custom_call_target="tpu_custom_call" | custom-call | bytes 8388608 | tf_op jit(solution)/shard_map/self_out_to_cross/pallas_call | solution.py:418
  139.0 12.6 %swap.12 = (bf16[8,256,128]{2,1,0:T(8,128)(2,1)}, bf16[8,64,256]{2,1,0:T(8,128)(2,1)}) custom-call(bf16[8,256,128]{2,1,0:T(8,128)(2,1)} %get-tuple-element.102.refs_0_, bf16[8,64,256]{2,1,0:T(8,128)(2,1)} %get-tuple-element.103.refs_1_), custom_call_target="tpu_custom_call" | custom-call | bytes 786432 | tf_op jit(solution)/shard_map/swap/pallas_call | solution.py:828
  153.7 8.6 %cross_forward.1 = (bf16[2048,128]{1,0:T(8,128)(2,1)S(1)}, f32[128,2048]{1,0:T(8,128)S(1)}, f32[2,2048]{1,0:T(2,128)S(1)}) custom-call(s32[2,8]{1,0:T(2,128)S(1)} %pad_add_fusion.2.lim_ref, s32[8,2048]{1,0:T(8,128)S(1)} %add_add_fusion.2.rows_ref, bf16[2048,128]{1,0:T(8,128)(2,1)S(1)} %bitcast.169, bf16[512,256]{1,0:T(8,128)(2,1)S(1)} %bitcast.174), custom_call_target="tpu_custom_call" | custom-call | bytes 852032 | tf_op jit(solution)/shard_map/cross_forward/pallas_call | solution.py:251
  164.0 21.5 %swap.13 = (bf16[8,256,128]{2,1,0:T(8,128)(2,1)}, bf16[704,1024]{1,0:T(8,128)(2,1)}, bf16[704,1024]{1,0:T(8,128)(2,1)}) custom-call(bf16[8,256,128]{2,1,0:T(8,128)(2,1)} %bitcast.176, bf16[5632,256]{1,0:T(8,128)(2,1)} %bitcast.181, bf16[704,1024]{1,0:T(8,128)(2,1)} %get-tuple-element.107.refs_2_, ...), custom_call_target="tpu_custom_call", output_to_operand_aliasing={{1}: (2, {}), {2}: (3, {})} | custom-call | bytes 524288 | tf_op jit(solution)/shard_map/swap/pallas_call | solution.py:828
  191.1 4.9 fusion.8
  196.0 15.7 %all-gather.13.cloned.1.call-done = bf16[1024,1024]{1,0:T(8,128)(2,1)} async-done(((bf16[256,1024]{1,0:T(8,128)(2,1)}), bf16[1024,1024]{1,0:T(8,128)(2,1)}) %all-gather.13.cloned.1.call-update) | async-done | bytes 2097168 | tf_op jit(solution)/shard_map/all_gather | solution.py:908
  211.7 3.8 fusion.50
  215.6 4.7 multiply_convert_fusion
  222.2 3.3 add_convert_fusion
  226.1 3.8 convolution_convert_fusion.8
  240.1 17.0 %reduce-scatter.6.cloned.1.call-done = bf16[256,1024]{1,0:T(8,128)(2,1)} async-done(((bf16[1024,1024]{1,0:T(8,128)(2,1)}), bf16[256,1024]{1,0:T(8,128)(2,1)}) %reduce-scatter.6.cloned.1.call-update) | async-done | bytes 524304 | tf_op jit(solution)/shard_map/reduce_scatter | solution.py:891
  265.7 10.0 %swap.14 = bf16[8,256,128]{2,1,0:T(8,128)(2,1)} custom-call(bf16[8,256,128]{2,1,0:T(8,128)(2,1)} %fusion.16.refs_0_), custom_call_target="tpu_custom_call" | custom-call | bytes 524288 | tf_op jit(solution)/shard_map/swap/pallas_call | solution.py:828
  276.8 9.9 %cross_backward.1 = (bf16[2048,128]{1,0:T(8,128)(2,1)S(1)}, bf16[512,256]{1,0:T(8,128)(2,1)S(1)}) custom-call(s32[2,8]{1,0:T(2,128)S(1)} %pad_add_fusion.2.lim_ref, s32[8,2048]{1,0:T(8,128)S(1)} %add_add_fusion.2.rows_ref, bf16[2048,128]{1,0:T(8,128)(2,1)S(1)} %bitcast.170, bf16[512,256]{1,0:T(8,128)(2,1)S(1)} %bitcast.175, bf16[2048,128]{1,0:T(8,128)(2,1)S(1)} %bitcast.171, ...), custom_call_target="tpu_custom_call" | custom-call | bytes 2441280 | tf_op jit(solution)/shard_map/cross_backward/pallas_call | solution.py:251
  288.2 12.6 %swap.15 = (bf16[8,256,128]{2,1,0:T(8,128)(2,1)}, bf16[8,64,256]{2,1,0:T(8,128)(2,1)}) custom-call(bf16[8,256,128]{2,1,0:T(8,128)(2,1)} %bitcast.177, bf16[8,64,256]{2,1,0:T(8,128)(2,1)} %bitcast.179), custom_call_target="tpu_custom_call" | custom-call | bytes 786432 | tf_op jit(solution)/shard_map/swap/pallas_call | solution.py:828
  300.9 8.5 %cross_to_self_out.1 = (f32[256,1024]{1,0:T(8,128)}, bf16[256,1024]{1,0:T(8,128)(2,1)}, bf16[8,256,128]{2,1,0:T(8,128)(2,1)}, f32[1,1024]{1,0:T(1,128)}, bf16[64...) custom-call(bf16[8,256,128]{2,1,0:T(8,128)(2,1)} %get-tuple-element.119.dq_ref, ...), custom_call_target="tpu_custom_call" | custom-call | bytes 8388608 | tf_op jit(solution)/shard_map/cross_to_self_out/pallas_call | solution.py:418
  320.2 9.6 %swap.16 = bf16[8,256,128]{2,1,0:T(8,128)(2,1)} custom-call(bf16[8,256,128]{2,1,0:T(8,128)(2,1)} %get-tuple-element.126.refs_0_), custom_call_target="tpu_custom_call" | custom-call | bytes 524288 | tf_op jit(solution)/shard_map/swap/pallas_call | solution.py:828
  330.9 17.4 %self_backward.1 = (bf16[2048,384]{1,0:T(8,128)(2,1)S(1)}, f32[2,1536]{1,0:T(2,128)S(1)}) custom-call(s32[2,8]{1,0:T(2,128)S(1)} %pad_add_fusion.1.lim_ref, s32[8,2048]{1,0:T(8,128)S(1)} %broadcast_in_dim.102.rows_ref, f32[2,1536]{1,0:T(2,128)S(1)} %maximum_maximum_fusion.ext_ref, bf16[2048,384]{1,0:T(8,128)(2,1)S(1)} %bitcast.168, ...), custom_call_target="tpu_custom_call" | custom-call | bytes 3240000 | tf_op jit(solution)/shard_map/self_backward/pallas_call | solution.py:251
  349.4 21.2 %swap.17 = bf16[8,256,384]{2,1,0:T(8,128)(2,1)} custom-call(bf16[8,256,384]{2,1,0:T(8,128)(2,1)} %bitcast.173), custom_call_target="tpu_custom_call" | custom-call | bytes 1572864 | tf_op jit(solution)/shard_map/swap/pallas_call | solution.py:828
  372.4 4.6 convolution_convert_fusion
  377.1 4.9 fusion.18
  387.7 123.7 %units_total.1 = (bf16[5632,256]{1,0:T(8,128)(2,1)}, bf16[704,1024]{1,0:T(8,128)(2,1)S(1)}, f32[256,1024]{1,0:T(8,128)S(1)}, f32[8,1024]{1,0:T(8,128)S(1)}) custom-call(bf16[2112,1024]{1,0:T(8,128)(2,1)} %bitcast.188, bf16[1024,1024]{1,0:T(8,128)(2,1)S(1)} %copy-done.4, bf16[32,1024]{1,0:T(8,128)(2,1)S(1)} %pad_bitcast_fusion.few_ref), custom_call_target="tpu_custom_call" | custom-call | bytes 389283840 | tf_op jit(solution)/shard_map/units_total/pallas_call | solution.py:545
  513.5 84.8 %ring_total.1 = (bf16[256,1024]{1,0:T(8,128)(2,1)S(1)}, bf16[256,1024]{1,0:T(8,128)(2,1)S(1)}, bf16[256,3072]{1,0:T(8,128)(2,1)S(1)}, bf16[256,3072]{1,0:T(8,128...) custom-call(bf16[256,1024]{1,0:T(8,128)(2,1)S(1)} %copy-done.16, bf16[256,1024]{1,0:T(8,128)(2,1)S(1)} %copy-done.17, ...), custom_call_target="tpu_custom_call" | custom-call | bytes 425656320 | tf_op jit(solution)/shard_map/ring_total/pallas_call | solution.py:545
  599.4 5.4 collective-permute-start.4
  (272 shorter events, 102.4 us)
Async XLA Ops:
  7.2 184.0 %copy-start = (bf16[704,1024]{1,0:T(8,128)(2,1)S(1)}, bf16[704,1024]{1,0:T(8,128)(2,1)}, u32[]{:S(2)}) copy-start(bf16[704,1024]{1,0:T(8,128)(2,1)} %param.32) | copy-start | bytes 4325380
  7.2 52.3 %all-gather.7.cloned.1.call-start = ((), (), s32[]{:S(2)}) async-start(), calls=%async_computation.5 | async-start | bytes 7864320 | tf_op jit(solution)/shard_map/all_gather | solution.py:908
  8.0 123.9 %all-gather.9.cloned.1.call-start = ((), (), s32[]{:S(2)}) async-start(), calls=%async_computation.6 | async-start | bytes 10485760 | tf_op jit(solution)/shard_map/all_gather | solution.py:920
  8.0 8.1 %copy-start.47 = (bf16[256,1024]{1,0:T(8,128)(2,1)S(1)}, bf16[256,1024]{1,0:T(8,128)(2,1)}, u32[]{:S(2)}) copy-start(bf16[256,1024]{1,0:T(8,128)(2,1)} %param.27) | copy-start | bytes 1572868
  18.8 5.0 copy-start.52
  18.8 166.7 %all-gather.11.cloned.1.call-start = ((), (), s32[]{:S(2)}) async-start(), calls=%async_computation.7 | async-start | bytes 5242880 | tf_op jit(solution)/shard_map/all_gather | solution.py:971
  19.5 9.3 %collective-permute-start.1 = (s32[8,128]{1,0:T(8,128)S(1)}, s32[8,128]{1,0:T(8,128)S(1)}, u32[]{:S(2)}, u32[]{:S(2)}) collective-permute-start(s32[8,128]{1,0:T(8,128)S(1)} %pad_bitcast_fusion.1), channel_id=1, source_target_pairs={{0,0},{1,16},{2,2},{3,18},{4,4},{5,20},{6,6},{7,22},{8,8},{9,24},{... | collective-permute-start | bytes 12296 | tf_op jit(solution)/shard_map/ppermute | solution.py:869
  20.2 33.2 %collective-permute-start = (bf16[256,1024]{1,0:T(8,128)(2,1)}, bf16[256,1024]{1,0:T(8,128)(2,1)S(1)}, u32[]{:S(2)}, u32[]{:S(2)}) collective-permute-start(bf16[256,1024]{1,0:T(8,128)(2,1)} %bitcast), channel_id=1, source_target_pairs={{0,0},{1,16},{2,2},{3,18},{4,4},{5,20},{6,6},{7,22},{8,8},{9,24},{... | collective-permute-start | bytes 1572872 | tf_op jit(solution)/shard_map/ppermute | solution.py:869
  22.1 30.2 %collective-permute-start.2 = (bf16[320,1024]{1,0:T(8,128)(2,1)S(1)}, bf16[320,1024]{1,0:T(8,128)(2,1)}, u32[]{:S(2)}, u32[]{:S(2)}) collective-permute-start(bf16[320,1024]{1,0:T(8,128)(2,1)S(1)} %pad_maximum_fusion.4), channel_id=1, source_target_pairs={{0,0},{1,16},{2,2},{3,18},{4,4},{5,20},{6,6},{7,22},{8,8},{9,24},{... | collective-permute-start | bytes 1966088 | tf_op jit(solution)/shard_map/ppermute | solution.py:869
  53.4 44.6 %copy-start.33 = (bf16[256,1024]{1,0:T(8,128)(2,1)}, bf16[256,1024]{1,0:T(8,128)(2,1)S(1)}, u32[]{:S(2)}) copy-start(bf16[256,1024]{1,0:T(8,128)(2,1)S(1)} %slice.115) | copy-start | bytes 1572868
  53.4 12.2 %copy-start.30 = (bf16[256,1024]{1,0:T(8,128)(2,1)}, bf16[256,1024]{1,0:T(8,128)(2,1)S(1)}, u32[]{:S(2)}) copy-start(bf16[256,1024]{1,0:T(8,128)(2,1)S(1)} %collective-permute-done.home_ref) | copy-start | bytes 1572868
  100.1 111.5 %all-gather.13.cloned.1.call-start = ((), (), s32[]{:S(2)}) async-start(), calls=%async_computation.8 | async-start | bytes 2621440 | tf_op jit(solution)/shard_map/all_gather | solution.py:908
  189.6 68.9 %copy-start.26 = (f32[256,1024]{1,0:T(8,128)}, f32[256,1024]{1,0:T(8,128)S(1)}, u32[]{:S(2)}) copy-start(f32[256,1024]{1,0:T(8,128)S(1)} %get-tuple-element.256) | copy-start | bytes 3145732
  190.8 66.3 %reduce-scatter.6.cloned.1.call-start = ((), (), s32[]{:S(2)}) async-start(), calls=%async_computation.9 | async-start | bytes 2621440 | tf_op jit(solution)/shard_map/reduce_scatter | solution.py:891
  215.6 4.7 copy-start.38
  225.5 161.3 %reduce-scatter.8.cloned.1.call-start = ((), (), s32[]{:S(2)}) async-start(), calls=%async_computation.10 | async-start | bytes 2621440 | tf_op jit(solution)/shard_map/reduce_scatter | solution.py:891
  262.2 13.5 %copy-start.6 = (bf16[8,256,128]{2,1,0:T(8,128)(2,1)S(1)}, bf16[8,256,128]{2,1,0:T(8,128)(2,1)}, u32[]{:S(2)}) copy-start(bf16[8,256,128]{2,1,0:T(8,128)(2,1)} %get-tuple-element.104) | copy-start | bytes 1572868
  262.2 13.5 %copy-start.13 = (f32[128,2048]{1,0:T(8,128)S(1)}, f32[128,2048]{1,0:T(8,128)}, u32[]{:S(2)}) copy-start(f32[128,2048]{1,0:T(8,128)} %copy-done.12) | copy-start | bytes 3145732
  262.2 13.5 %copy-start.15 = (bf16[8,64,256]{2,1,0:T(8,128)(2,1)S(1)}, bf16[8,64,256]{2,1,0:T(8,128)(2,1)}, u32[]{:S(2)}) copy-start(bf16[8,64,256]{2,1,0:T(8,128)(2,1)} %get-tuple-element.105) | copy-start | bytes 786436
  262.2 124.7 %reduce-scatter.10.cloned.1.call-start = ((), (), s32[]{:S(2)}) async-start(), calls=%async_computation.11 | async-start | bytes 7864320 | tf_op jit(solution)/shard_map/reduce_scatter | solution.py:891
  300.9 8.5 %copy-start.45 = (bf16[256,1024]{1,0:T(8,128)(2,1)S(1)}, bf16[256,1024]{1,0:T(8,128)(2,1)}, u32[]{:S(2)}) copy-start(bf16[256,1024]{1,0:T(8,128)(2,1)} %get-tuple-element.123) | copy-start | bytes 1572868
  316.7 195.7 %reduce-scatter.12.cloned.1.call-start = ((), (), s32[]{:S(2)}) async-start(), calls=%async_computation.12 | async-start | bytes 2621440 | tf_op jit(solution)/shard_map/reduce_scatter | solution.py:891
  319.9 9.9 %copy-start.3 = (bf16[8,256,384]{2,1,0:T(8,128)(2,1)S(1)}, bf16[8,256,384]{2,1,0:T(8,128)(2,1)}, u32[]{:S(2)}) copy-start(bf16[8,256,384]{2,1,0:T(8,128)(2,1)} %get-tuple-element.96) | copy-start | bytes 4718596
  319.9 9.9 %copy-start.11 = (f32[128,2048]{1,0:T(8,128)S(1)}, f32[128,2048]{1,0:T(8,128)}, u32[]{:S(2)}) copy-start(f32[128,2048]{1,0:T(8,128)} %copy-done.10) | copy-start | bytes 3145732
  320.0 192.4 %reduce-scatter.14.cloned.1.call-start = ((), (), s32[]{:S(2)}) async-start(), calls=%async_computation.13 | async-start | bytes 7864320 | tf_op jit(solution)/shard_map/reduce_scatter | solution.py:891
  377.1 4.9 copy-start.41
  382.0 4.7 copy-start.51
  382.0 5.6 copy-start.4
  383.8 3.0 collective-permute-start.3
  387.7 123.8 %copy-start.27 = (f32[256,1024]{1,0:T(8,128)S(1)}, f32[256,1024]{1,0:T(8,128)}, u32[]{:S(2)}) copy-start(f32[256,1024]{1,0:T(8,128)} %copy-done.26) | copy-start | bytes 3145732
  599.4 21.6 %collective-permute-start.4 = (bf16[256,1024]{1,0:T(8,128)(2,1)}, bf16[256,1024]{1,0:T(8,128)(2,1)}, u32[]{:S(2)}, u32[]{:S(2)}) collective-permute-start(bf16[256,1024]{1,0:T(8,128)(2,1)} %add_convert_fusion.1), channel_id=1, source_target_pairs={{0,0},{1,16},{2,2},{3,18},{4,4},{5,20},{6,6},{7,22},{8,8},{9,24},{... | collective-permute-start | bytes 1572872 | tf_op jit(solution)/shard_map/ppermute | solution.py:869
  616.3 6.6 %copy-start.1 = (bf16[704,1024]{1,0:T(8,128)(2,1)S(1)}, bf16[704,1024]{1,0:T(8,128)(2,1)}, u32[]{:S(2)}) copy-start(bf16[704,1024]{1,0:T(8,128)(2,1)} %param.32) | copy-start | bytes 4325380
  (48 other events, 93.5 us)
Sparse Core Ops, SparseCore 0:
  9.6 49.9 all-gather.6
  61.7 70.1 all-gather.8
  134.1 33.5 all-gather.10
  190.9 20.6 all-gather.12
  225.6 31.4 reduce-scatter.5
  262.3 31.4 reduce-scatter.7
  316.8 57.7 reduce-scatter.9
  377.9 31.4 reduce-scatter.11
  411.9 66.2 reduce-scatter.13

commit v17 on v15

--- a/solution.py
+++ b/solution.py
@@ -423,7 +423,7 @@
         in_specs=[whole(v.shape) for v in arrays] + [pl.BlockSpec((1, rows, cols), lambda i: (order(i), 0, 0))],
         out_specs=[whole(s) for s, _ in outs],
         scratch_shapes=[pltpu.VMEM(s, d) for s, d in scratch],
-        compiler_params=pltpu.CompilerParams(vmem_limit_bytes=40 << 20, dimension_semantics=("arbitrary",)),
+        compiler_params=pltpu.CompilerParams(vmem_limit_bytes=62 << 20, dimension_semantics=("arbitrary",)),
         cost_estimate=pl.CostEstimate(flops=0, bytes_accessed=weights.size * 2, transcendentals=0),
     )(*arrays, weights)
 
@@ -475,7 +475,9 @@
     slots = refs[2 * (count + more) : 3 * count + 2 * more]
     send_sem, recv_sem = refs[3 * count + 2 * more :]
     place, right, left = ring_greet(n, [])
-    streams = [(k, piece, piece % 2) for k in range(count) for piece in range(abs(splits[k]))]
+    streams = [
+        (k, piece, (piece if abs(splits[k]) > 1 else k) % 2) for k in range(count) for piece in range(abs(splits[k]))
+    ]
 
     def window(ref, k, piece, chunk):
         return ring_window(ref, x_refs[k].shape, splits[k], n, piece, chunk)

time: 664 us -> 646 us (0.973)
  local copies, waits for them, and re-layouts: 66.7 us -> 46.5 us
  Pallas kernels: 376 us -> 389 us
  starting transfers between devices: 33.2 us -> 25.9 us
  other arithmetic: 41.9 us -> 35.2 us
    unnamed x213 -> x151, local copies, waits for them, and re-layouts: 54 us -> 32.9 us
    pallas_call x2, Pallas kernels: 6.04 us -> 15.6 us  [over_weights(): pl.pallas_call(body, name=name, grid=(count,), out_shape=[jax.ShapeDtypeS...]
    ppermute x5, starting transfers between devices: 31.6 us -> 24.4 us  [change_home(): return lax.ppermute(value, ('seq', 'fsdp'), pairs)]
  transfers between devices with their start and end apart: 13 -> 13, of which waited for: 6 -> 7; matrix products, arithmetic and copies ran while one was open for 13% -> 13% of each run, Pallas kernels for 45% -> 48%
where the time goes in v17:
time: 646 us; the launch traced here: 636 us
  Pallas kernels  389 us (60%)
  waiting for transfers between devices  61.6 us (10%)
  matrix products  55.9 us (9%)
  local copies, waits for them, and re-layouts  46.5 us (7%)
  other arithmetic  35.2 us (5%)
  starting transfers between devices  25.9 us (4%)
  between operations  15.6 us (2%)
    pallas_call x2, Pallas kernels, ring_call(): pl.pallas_call(body, name=name, out_shape=[jax.ShapeDtypeStruct(s, d) for...  183 us
    pallas_call x9, Pallas kernels, swap(): pl.pallas_call(functools.partial(swap_kernel, n, fan, count, fars, not fa...  131 us
    pallas_call x4, Pallas kernels, call(): pl.pallas_call(body, name=name, out_shape=[jax.ShapeDtypeStruct(s, d) for...  59.7 us
    unnamed x151, local copies, waits for them, and re-layouts  32.9 us
    ppermute x5, waiting for transfers between devices, change_home(): return lax.ppermute(value, ('seq', 'fsdp'), pairs)  26 us
    ppermute x5, starting transfers between devices, change_home(): return lax.ppermute(value, ('seq', 'fsdp'), pairs)  24.4 us
    all_gather x2, waiting for transfers between devices, shards(): gather = lambda v: lax.all_gather(v, 'fsdp', axis=0, tiled=True)  18 us
    reduce_scatter x4, waiting for transfers between devices, scatter(): return lax.psum_scatter(grad, 'fsdp', scatter_dimension=0, tiled=True)  16.6 us
  transfers between devices with their start and end apart: 13, of which 7 were waited for; matrix products, arithmetic and copies ran while one was open for 13% of the time, Pallas kernels for 48%

profile of v17, /device:TPU:1, one launch (start us, length us, event | category | flops | bytes accessed | tf_op | source)
XLA Modules:
  0.0 636.1 jit_solution(7612410571626934555)
XLA Ops:
  9.9 6.1 all-gather.1
  19.4 4.7 collective-permute-start.1
  26.1 4.5 collective-permute-start.2
  31.4 4.5 copy.77
  36.6 4.9 swap.9
  46.2 5.2 fusion.38
  59.6 5.8 fusion.10.refs_0_
  65.4 30.6 %swap.10 = (bf16[8,256,384]{2,1,0:T(8,128)(2,1)}, bf16[704,1024]{1,0:T(8,128)(2,1)}, bf16[704,1024]{1,0:T(8,128)(2,1)}) custom-call(bf16[8,256,384]{2,1,0:T(8,128)(2,1)} %fusion.10.refs_0_, bf16[5632,256]{1,0:T(8,128)(2,1)} %bitcast.180), custom_call_target="tpu_custom_call" | custom-call | bytes 1572864 | tf_op jit(solution)/shard_map/swap/pallas_call | solution.py:828
  101.8 18.1 %self_forward.1 = (bf16[2048,128]{1,0:T(8,128)(2,1)S(1)}, f32[128,2048]{1,0:T(8,128)S(1)}, f32[2,2048]{1,0:T(2,128)S(1)}) custom-call(s32[2,8]{1,0:T(2,128)S(1)} %pad_add_fusion.1.lim_ref, s32[8,2048]{1,0:T(8,128)S(1)} %broadcast_in_dim.102.rows_ref, f32[2,1536]{1,0:T(2,128)S(1)} %maximum_maximum_fusion.ext_ref, bf16[2048,384]{1,0:T(8,128)(2,1)S(1)} %bitcast.167), custom_call_target="tpu_custom_call" | custom-call | bytes 1650752 | tf_op jit(solution)/shard_map/self_forward/pallas_call | solution.py:251
  121.6 9.8 %swap.11.tok_ref = bf16[8,256,128]{2,1,0:T(8,128)(2,1)} custom-call(bf16[8,256,128]{2,1,0:T(8,128)(2,1)} %bitcast.178), custom_call_target="tpu_custom_call" | custom-call | bytes 524288 | tf_op jit(solution)/shard_map/swap/pallas_call | solution.py:828
  131.7 7.1 %self_out_to_cross.1 = (f32[256,1024]{1,0:T(8,128)}, bf16[256,1024]{1,0:T(8,128)(2,1)}, bf16[8,256,128]{2,1,0:T(8,128)(2,1)}, bf16[8,64,256]{2,1,0:T(8,128)(2,1)}) custom-call(bf16[8,256,128]{2,1,0:T(8,128)(2,1)} %swap.11.tok_ref, bf16[256,1024]{1,0:T(8,128)(2,1)} %copy-done.28, f32[1,1024]{1,0:T(1,128)} %bitcast.217, bf16[64,1024]{1,0:T(8,128)(2,1)} %slice.120.enc_ref, ...), custom_call_target="tpu_custom_call" | custom-call | bytes 8388608 | tf_op jit(solution)/shard_map/self_out_to_cross/pallas_call | solution.py:418
  138.8 13.6 %swap.12 = (bf16[8,256,128]{2,1,0:T(8,128)(2,1)}, bf16[8,64,256]{2,1,0:T(8,128)(2,1)}) custom-call(bf16[8,256,128]{2,1,0:T(8,128)(2,1)} %get-tuple-element.100.refs_0_, bf16[8,64,256]{2,1,0:T(8,128)(2,1)} %get-tuple-element.101.refs_1_), custom_call_target="tpu_custom_call" | custom-call | bytes 786432 | tf_op jit(solution)/shard_map/swap/pallas_call | solution.py:828
  154.4 9.9 %cross_forward.1 = (bf16[2048,128]{1,0:T(8,128)(2,1)S(1)}, f32[128,2048]{1,0:T(8,128)S(1)}, f32[2,2048]{1,0:T(2,128)S(1)}) custom-call(s32[2,8]{1,0:T(2,128)S(1)} %pad_add_fusion.2.lim_ref, s32[8,2048]{1,0:T(8,128)S(1)} %add_add_fusion.2.rows_ref, bf16[2048,128]{1,0:T(8,128)(2,1)S(1)} %bitcast.169, bf16[512,256]{1,0:T(8,128)(2,1)S(1)} %bitcast.174), custom_call_target="tpu_custom_call" | custom-call | bytes 852032 | tf_op jit(solution)/shard_map/cross_forward/pallas_call | solution.py:251
  166.1 19.4 %swap.13 = (bf16[8,256,128]{2,1,0:T(8,128)(2,1)}, bf16[704,1024]{1,0:T(8,128)(2,1)}, bf16[704,1024]{1,0:T(8,128)(2,1)}) custom-call(bf16[8,256,128]{2,1,0:T(8,128)(2,1)} %bitcast.176, bf16[5632,256]{1,0:T(8,128)(2,1)} %bitcast.181, bf16[704,1024]{1,0:T(8,128)(2,1)} %get-tuple-element.105.refs_2_, ...), custom_call_target="tpu_custom_call", output_to_operand_aliasing={{1}: (2, {}), {2}: (3, {})} | custom-call | bytes 524288 | tf_op jit(solution)/shard_map/swap/pallas_call | solution.py:828
  191.1 4.9 fusion.8
  195.9 15.2 %all-gather.13.cloned.1.call-done = bf16[1024,1024]{1,0:T(8,128)(2,1)} async-done(((bf16[256,1024]{1,0:T(8,128)(2,1)}), bf16[1024,1024]{1,0:T(8,128)(2,1)}) %all-gather.13.cloned.1.call-update) | async-done | bytes 2097168 | tf_op jit(solution)/shard_map/all_gather | solution.py:908
  215.1 4.7 multiply_convert_fusion
  239.6 16.5 %reduce-scatter.5.cloned.1.call-done = bf16[256,1024]{1,0:T(8,128)(2,1)} async-done(((bf16[1024,1024]{1,0:T(8,128)(2,1)}), bf16[256,1024]{1,0:T(8,128)(2,1)}) %reduce-scatter.5.cloned.1.call-update) | async-done | bytes 524304 | tf_op jit(solution)/shard_map/reduce_scatter | solution.py:891
  264.8 10.1 %swap.14 = bf16[8,256,128]{2,1,0:T(8,128)(2,1)} custom-call(bf16[8,256,128]{2,1,0:T(8,128)(2,1)} %fusion.16.refs_0_), custom_call_target="tpu_custom_call" | custom-call | bytes 524288 | tf_op jit(solution)/shard_map/swap/pallas_call | solution.py:828
  276.0 11.2 %cross_backward.1 = (bf16[2048,128]{1,0:T(8,128)(2,1)S(1)}, bf16[512,256]{1,0:T(8,128)(2,1)S(1)}) custom-call(s32[2,8]{1,0:T(2,128)S(1)} %pad_add_fusion.2.lim_ref, s32[8,2048]{1,0:T(8,128)S(1)} %add_add_fusion.2.rows_ref, bf16[2048,128]{1,0:T(8,128)(2,1)S(1)} %bitcast.170, bf16[512,256]{1,0:T(8,128)(2,1)S(1)} %bitcast.175, bf16[2048,128]{1,0:T(8,128)(2,1)S(1)} %bitcast.171, ...), custom_call_target="tpu_custom_call" | custom-call | bytes 2441280 | tf_op jit(solution)/shard_map/cross_backward/pallas_call | solution.py:251
  288.7 11.9 %swap.15 = (bf16[8,256,128]{2,1,0:T(8,128)(2,1)}, bf16[8,64,256]{2,1,0:T(8,128)(2,1)}) custom-call(bf16[8,256,128]{2,1,0:T(8,128)(2,1)} %bitcast.177, bf16[8,64,256]{2,1,0:T(8,128)(2,1)} %bitcast.179), custom_call_target="tpu_custom_call" | custom-call | bytes 786432 | tf_op jit(solution)/shard_map/swap/pallas_call | solution.py:828
  300.6 8.5 %cross_to_self_out.1 = (f32[256,1024]{1,0:T(8,128)}, bf16[256,1024]{1,0:T(8,128)(2,1)}, bf16[8,256,128]{2,1,0:T(8,128)(2,1)}, f32[1,1024]{1,0:T(1,128)}, bf16[64...) custom-call(bf16[8,256,128]{2,1,0:T(8,128)(2,1)} %get-tuple-element.117.dq_ref, ...), custom_call_target="tpu_custom_call" | custom-call | bytes 8388608 | tf_op jit(solution)/shard_map/cross_to_self_out/pallas_call | solution.py:418
  318.2 9.6 %swap.16 = bf16[8,256,128]{2,1,0:T(8,128)(2,1)} custom-call(bf16[8,256,128]{2,1,0:T(8,128)(2,1)} %get-tuple-element.125.refs_0_), custom_call_target="tpu_custom_call" | custom-call | bytes 524288 | tf_op jit(solution)/shard_map/swap/pallas_call | solution.py:828
  329.1 20.5 %self_backward.1 = (bf16[2048,384]{1,0:T(8,128)(2,1)S(1)}, f32[2,1536]{1,0:T(2,128)S(1)}) custom-call(s32[2,8]{1,0:T(2,128)S(1)} %pad_add_fusion.1.lim_ref, s32[8,2048]{1,0:T(8,128)S(1)} %broadcast_in_dim.102.rows_ref, f32[2,1536]{1,0:T(2,128)S(1)} %maximum_maximum_fusion.ext_ref, bf16[2048,384]{1,0:T(8,128)(2,1)S(1)} %bitcast.168, ...), custom_call_target="tpu_custom_call" | custom-call | bytes 3240000 | tf_op jit(solution)/shard_map/self_backward/pallas_call | solution.py:251
  350.8 21.2 %swap.17 = bf16[8,256,384]{2,1,0:T(8,128)(2,1)} custom-call(bf16[8,256,384]{2,1,0:T(8,128)(2,1)} %bitcast.173), custom_call_target="tpu_custom_call" | custom-call | bytes 1572864 | tf_op jit(solution)/shard_map/swap/pallas_call | solution.py:828
  373.7 4.6 convolution_convert_fusion
  378.4 4.9 fusion.18
  388.2 16.9 %collective-permute-done.3 = bf16[320,1024]{1,0:T(8,128)(2,1)S(1)} collective-permute-done((bf16[320,1024]{1,0:T(8,128)(2,1)}, bf16[320,1024]{1,0:T(8,128)(2,1)S(1)}, u32[]{:S(2)}, u32[]{:S(2)}) %collective-permute-start.3) | collective-permute-done | bytes 655392 | tf_op jit(solution)/shard_map/ppermute | solution.py:869
  406.0 99.4 %units_total.1 = (bf16[5632,256]{1,0:T(8,128)(2,1)}, bf16[704,1024]{1,0:T(8,128)(2,1)S(1)}, f32[256,1024]{1,0:T(8,128)S(1)}, f32[8,1024]{1,0:T(8,128)S(1)}) custom-call(bf16[2112,1024]{1,0:T(8,128)(2,1)} %bitcast.188, bf16[1024,1024]{1,0:T(8,128)(2,1)S(1)} %copy-done.4, bf16[32,1024]{1,0:T(8,128)(2,1)S(1)} %pad_bitcast_fusion.few_ref), custom_call_target="tpu_custom_call" | custom-call | bytes 389283840 | tf_op jit(solution)/shard_map/units_total/pallas_call | solution.py:545
  508.9 83.5 %ring_total.1 = (bf16[256,1024]{1,0:T(8,128)(2,1)S(1)}, bf16[256,4096]{1,0:T(8,128)(2,1)}, bf16[256,3072]{1,0:T(8,128)(2,1)S(1)}, bf16[64,128]{1,0:T(8,128)(2,1)S(1)}, bf16[256,5632]{1,0:T(8,128)(2,1)}) custom-call(bf16[256,1024]{1,0:T(8,128)(2,1)S(1)} %copy-done.19, bf16[256,4096]{1,0:T(8,128)(2,1)} %reduce-scatter.9.cloned.1.call-done.refs_1_, ...), custom_call_target="tpu_custom_call" | custom-call | bytes 425656320 | tf_op jit(solution)/shard_map/ring_total/pallas_call | solution.py:545
  604.7 11.0 %collective-permute-start.4 = (bf16[256,1024]{1,0:T(8,128)(2,1)S(1)}, bf16[256,1024]{1,0:T(8,128)(2,1)S(1)}, u32[]{:S(2)}, u32[]{:S(2)}) collective-permute-start(bf16[256,1024]{1,0:T(8,128)(2,1)S(1)} %copy-done.43), channel_id=1, source_target_pairs={{0,0},{1,16},{2,2},{3,18},{4,4},{5,20},{6,6},{7,22},{8,8},{9,24},{... | collective-permute-start | bytes 1572872 | tf_op jit(solution)/shard_map/ppermute | solution.py:869
  622.7 5.5 collective-permute-done.4
  (268 shorter events, 116.0 us)
Async XLA Ops:
  7.2 183.9 %copy-start = (bf16[704,1024]{1,0:T(8,128)(2,1)S(1)}, bf16[704,1024]{1,0:T(8,128)(2,1)}, u32[]{:S(2)}) copy-start(bf16[704,1024]{1,0:T(8,128)(2,1)} %param.32) | copy-start | bytes 4325380
  7.2 52.1 %all-gather.7.cloned.1.call-start = ((), (), s32[]{:S(2)}) async-start(), calls=%async_computation.4 | async-start | bytes 7864320 | tf_op jit(solution)/shard_map/all_gather | solution.py:908
  8.0 123.7 %all-gather.9.cloned.1.call-start = ((), (), s32[]{:S(2)}) async-start(), calls=%async_computation.5 | async-start | bytes 10485760 | tf_op jit(solution)/shard_map/all_gather | solution.py:920
  8.0 8.0 %copy-start.47 = (bf16[256,1024]{1,0:T(8,128)(2,1)S(1)}, bf16[256,1024]{1,0:T(8,128)(2,1)}, u32[]{:S(2)}) copy-start(bf16[256,1024]{1,0:T(8,128)(2,1)} %param.27) | copy-start | bytes 1572868
  18.7 7.4 %copy-start.44 = (bf16[1,256,1024]{2,1,0:T(8,128)(2,1)S(1)}, bf16[1,256,1024]{2,1,0:T(8,128)(2,1)}, u32[]{:S(2)}) copy-start(bf16[1,256,1024]{2,1,0:T(8,128)(2,1)} %param.33) | copy-start | bytes 1572868
  18.7 7.4 %copy-start.49 = (bf16[1,64,1024]{2,1,0:T(8,128)(2,1)S(1)}, bf16[1,64,1024]{2,1,0:T(8,128)(2,1)}, u32[]{:S(2)}) copy-start(bf16[1,64,1024]{2,1,0:T(8,128)(2,1)} %param.18) | copy-start | bytes 393220
  18.7 12.3 %copy-start.52 = (s32[2048]{0:T(1024)S(1)}, s32[2048]{0:T(1024)}, u32[]{:S(2)}) copy-start(s32[2048]{0:T(1024)} %param.21) | copy-start | bytes 24580
  18.7 166.8 %all-gather.11.cloned.1.call-start = ((), (), s32[]{:S(2)}) async-start(), calls=%async_computation.6 | async-start | bytes 5242880 | tf_op jit(solution)/shard_map/all_gather | solution.py:971
  19.4 16.6 %collective-permute-start.1 = (s32[8,128]{1,0:T(8,128)S(1)}, s32[8,128]{1,0:T(8,128)S(1)}, u32[]{:S(2)}, u32[]{:S(2)}) collective-permute-start(s32[8,128]{1,0:T(8,128)S(1)} %pad_bitcast_fusion.1), channel_id=1, source_target_pairs={{0,0},{1,16},{2,2},{3,18},{4,4},{5,20},{6,6},{7,22},{8,8},{9,24},{... | collective-permute-start | bytes 12296 | tf_op jit(solution)/shard_map/ppermute | solution.py:869
  24.1 32.5 %collective-permute-start = (bf16[256,1024]{1,0:T(8,128)(2,1)}, bf16[256,1024]{1,0:T(8,128)(2,1)S(1)}, u32[]{:S(2)}, u32[]{:S(2)}) collective-permute-start(bf16[256,1024]{1,0:T(8,128)(2,1)} %bitcast), channel_id=1, source_target_pairs={{0,0},{1,16},{2,2},{3,18},{4,4},{5,20},{6,6},{7,22},{8,8},{9,24},{... | collective-permute-start | bytes 1572872 | tf_op jit(solution)/shard_map/ppermute | solution.py:869
  26.1 29.4 %collective-permute-start.2 = (bf16[320,1024]{1,0:T(8,128)(2,1)S(1)}, bf16[320,1024]{1,0:T(8,128)(2,1)}, u32[]{:S(2)}, u32[]{:S(2)}) collective-permute-start(bf16[320,1024]{1,0:T(8,128)(2,1)S(1)} %pad_maximum_fusion.4), channel_id=1, source_target_pairs={{0,0},{1,16},{2,2},{3,18},{4,4},{5,20},{6,6},{7,22},{8,8},{9,24},{... | collective-permute-start | bytes 1966088 | tf_op jit(solution)/shard_map/ppermute | solution.py:869
  56.5 39.5 %copy-start.32 = (bf16[256,1024]{1,0:T(8,128)(2,1)}, bf16[256,1024]{1,0:T(8,128)(2,1)S(1)}, u32[]{:S(2)}) copy-start(bf16[256,1024]{1,0:T(8,128)(2,1)S(1)} %slice.119) | copy-start | bytes 1572868
  56.6 8.9 %copy-start.28 = (bf16[256,1024]{1,0:T(8,128)(2,1)}, bf16[256,1024]{1,0:T(8,128)(2,1)S(1)}, u32[]{:S(2)}) copy-start(bf16[256,1024]{1,0:T(8,128)(2,1)S(1)} %collective-permute-done.home_ref) | copy-start | bytes 1572868
  98.2 112.9 %all-gather.13.cloned.1.call-start = ((), (), s32[]{:S(2)}) async-start(), calls=%async_computation.7 | async-start | bytes 2621440 | tf_op jit(solution)/shard_map/all_gather | solution.py:908
  189.6 68.0 %copy-start.24 = (f32[256,1024]{1,0:T(8,128)}, f32[256,1024]{1,0:T(8,128)S(1)}, u32[]{:S(2)}) copy-start(f32[256,1024]{1,0:T(8,128)S(1)} %get-tuple-element.254) | copy-start | bytes 3145732
  190.7 65.4 %reduce-scatter.5.cloned.1.call-start = ((), (), s32[]{:S(2)}) async-start(), calls=%async_computation.8 | async-start | bytes 2621440 | tf_op jit(solution)/shard_map/reduce_scatter | solution.py:891
  224.9 180.2 %reduce-scatter.7.cloned.1.call-start = ((), (), s32[]{:S(2)}) async-start(), calls=%async_computation.9 | async-start | bytes 2621440 | tf_op jit(solution)/shard_map/reduce_scatter | solution.py:891
  261.2 13.7 %copy-start.6 = (bf16[8,256,128]{2,1,0:T(8,128)(2,1)S(1)}, bf16[8,256,128]{2,1,0:T(8,128)(2,1)}, u32[]{:S(2)}) copy-start(bf16[8,256,128]{2,1,0:T(8,128)(2,1)} %get-tuple-element.102) | copy-start | bytes 1572868
  261.2 13.7 %copy-start.14 = (f32[128,2048]{1,0:T(8,128)S(1)}, f32[128,2048]{1,0:T(8,128)}, u32[]{:S(2)}) copy-start(f32[128,2048]{1,0:T(8,128)} %copy-done.13) | copy-start | bytes 3145732
  261.2 13.7 %copy-start.18 = (bf16[8,64,256]{2,1,0:T(8,128)(2,1)S(1)}, bf16[8,64,256]{2,1,0:T(8,128)(2,1)}, u32[]{:S(2)}) copy-start(bf16[8,64,256]{2,1,0:T(8,128)(2,1)} %get-tuple-element.103) | copy-start | bytes 786436
  261.3 143.8 %reduce-scatter.9.cloned.1.call-start = ((), (), s32[]{:S(2)}) async-start(), calls=%async_computation.10 | async-start | bytes 10485760 | tf_op jit(solution)/shard_map/reduce_scatter | solution.py:891
  300.6 8.5 %copy-start.31 = (bf16[8,256,128]{2,1,0:T(8,128)(2,1)S(1)}, bf16[8,256,128]{2,1,0:T(8,128)(2,1)}, u32[]{:S(2)}) copy-start(bf16[8,256,128]{2,1,0:T(8,128)(2,1)} %swap.11.tok_ref) | copy-start | bytes 1572868
  317.9 9.9 %copy-start.3 = (bf16[8,256,384]{2,1,0:T(8,128)(2,1)S(1)}, bf16[8,256,384]{2,1,0:T(8,128)(2,1)}, u32[]{:S(2)}) copy-start(bf16[8,256,384]{2,1,0:T(8,128)(2,1)} %get-tuple-element.94) | copy-start | bytes 4718596
  317.9 9.9 %copy-start.12 = (f32[128,2048]{1,0:T(8,128)S(1)}, f32[128,2048]{1,0:T(8,128)}, u32[]{:S(2)}) copy-start(f32[128,2048]{1,0:T(8,128)} %copy-done.11) | copy-start | bytes 3145732
  317.9 188.5 %reduce-scatter.11.cloned.1.call-start = ((), (), s32[]{:S(2)}) async-start(), calls=%async_computation.11 | async-start | bytes 7864320 | tf_op jit(solution)/shard_map/reduce_scatter | solution.py:891
  383.3 22.6 %copy-start.4 = (bf16[1024,1024]{1,0:T(8,128)(2,1)S(1)}, bf16[1024,1024]{1,0:T(8,128)(2,1)}, u32[]{:S(2)}) copy-start(bf16[1024,1024]{1,0:T(8,128)(2,1)} %convolution_convert_fusion.5.part_ref) | copy-start | bytes 6291460
  385.1 20.0 %collective-permute-start.3 = (bf16[320,1024]{1,0:T(8,128)(2,1)}, bf16[320,1024]{1,0:T(8,128)(2,1)S(1)}, u32[]{:S(2)}, u32[]{:S(2)}) collective-permute-start(bf16[320,1024]{1,0:T(8,128)(2,1)} %pad_maximum_fusion.5), channel_id=1, source_target_pairs={{0,0},{1,16},{2,2},{3,18},{4,4},{5,20},{6,6},{7,22},{8,8},{9,24},{... | collective-permute-start | bytes 1966088 | tf_op jit(solution)/shard_map/ppermute | solution.py:869
  508.9 83.6 %copy-start.16 = (f32[256,1024]{1,0:T(8,128)S(1)}, f32[256,1024]{1,0:T(8,128)}, u32[]{:S(2)}) copy-start(f32[256,1024]{1,0:T(8,128)} %copy-done.15) | copy-start | bytes 3145732
  508.9 83.6 %copy-start.25 = (f32[256,1024]{1,0:T(8,128)S(1)}, f32[256,1024]{1,0:T(8,128)}, u32[]{:S(2)}) copy-start(f32[256,1024]{1,0:T(8,128)} %copy-done.24) | copy-start | bytes 3145732
  602.7 13.0 %copy-start.42 = (bf16[320,1024]{1,0:T(8,128)(2,1)S(1)}, bf16[320,1024]{1,0:T(8,128)(2,1)}, u32[]{:S(2)}) copy-start(bf16[320,1024]{1,0:T(8,128)(2,1)} %copy-done.41) | copy-start | bytes 1966084
  604.7 23.5 %collective-permute-start.4 = (bf16[256,1024]{1,0:T(8,128)(2,1)S(1)}, bf16[256,1024]{1,0:T(8,128)(2,1)S(1)}, u32[]{:S(2)}, u32[]{:S(2)}) collective-permute-start(bf16[256,1024]{1,0:T(8,128)(2,1)S(1)} %copy-done.43), channel_id=1, source_target_pairs={{0,0},{1,16},{2,2},{3,18},{4,4},{5,20},{6,6},{7,22},{8,8},{9,24},{... | collective-permute-start | bytes 1572872 | tf_op jit(solution)/shard_map/ppermute | solution.py:869
  619.2 9.7 %copy-start.1 = (bf16[704,1024]{1,0:T(8,128)(2,1)S(1)}, bf16[704,1024]{1,0:T(8,128)(2,1)}, u32[]{:S(2)}) copy-start(bf16[704,1024]{1,0:T(8,128)(2,1)} %param.32) | copy-start | bytes 4325380
  (47 other events, 97.7 us)
Sparse Core Ops, SparseCore 0:
  9.6 49.7 all-gather.6
  61.5 70.1 all-gather.8
  133.9 33.6 all-gather.10
  190.9 20.2 all-gather.12
  225.1 31.0 reduce-scatter.4
  261.3 31.4 reduce-scatter.6
  318.1 70.4 reduce-scatter.8
  391.2 58.3 reduce-scatter.10

commit v18 on v16

--- a/solution.py
+++ b/solution.py
@@ -255,7 +255,7 @@
         in_specs=[SMEM] + [VMEM] * (len(operands) - 1),
         out_specs=[VMEM] * len(outs),
         scratch_shapes=[pltpu.VMEM(s, d) for s, d in scratch],
-        compiler_params=pltpu.CompilerParams(vmem_limit_bytes=40 << 20),
+        compiler_params=pltpu.CompilerParams(vmem_limit_bytes=62 << 20),
         cost_estimate=pl.CostEstimate(flops=0, bytes_accessed=size, transcendentals=0),
     )(*operands)
 

time: 641 us -> 640 us (level)
  the two profiles are of different devices: /device:TPU:0 before, /device:TPU:1 now
where the time goes in v18:
time: 640 us; the launch traced here: 630 us
  Pallas kernels  399 us (62%)
  waiting for transfers between devices  59.2 us (9%)
  matrix products  55.4 us (9%)
  other arithmetic  38 us (6%)
  local copies, waits for them, and re-layouts  30.7 us (5%)
  starting transfers between devices  26.5 us (4%)
  between operations  15.2 us (2%)
    pallas_call x2, Pallas kernels, ring_call(): pl.pallas_call(body, name=name, out_shape=[jax.ShapeDtypeStruct(s, d) for...  183 us
    pallas_call x9, Pallas kernels, swap(): pl.pallas_call(functools.partial(swap_kernel, n, fan, count, fars, not fa...  135 us
    pallas_call x4, Pallas kernels, call(): pl.pallas_call(body, name=name, out_shape=[jax.ShapeDtypeStruct(s, d) for...  65.4 us
    ppermute x5, starting transfers between devices, change_home(): return lax.ppermute(value, ('seq', 'fsdp'), pairs)  25 us
    all_gather x2, waiting for transfers between devices, shards(): gather = lambda v: lax.all_gather(v, 'fsdp', axis=0, tiled=True)  22.7 us
    unnamed x129, local copies, waits for them, and re-layouts  20.1 us
    ppermute x5, waiting for transfers between devices, change_home(): return lax.ppermute(value, ('seq', 'fsdp'), pairs)  17.5 us
    reduce_scatter x5, waiting for transfers between devices, scatter(): return lax.psum_scatter(grad, 'fsdp', scatter_dimension=0, tiled=True)  16.5 us
  transfers between devices with their start and end apart: 14, of which 6 were waited for; matrix products, arithmetic and copies ran while one was open for 14% of the time, Pallas kernels for 50%

profile of v18, /device:TPU:1, one launch (start us, length us, event | category | flops | bytes accessed | tf_op | source)
XLA Modules:
  0.0 630.0 jit_solution(9927157513533142636)
XLA Ops:
  9.8 6.1 all-gather.1
  18.3 4.7 collective-permute-start.1
  25.0 4.5 collective-permute-start.2
  31.5 4.5 copy.77
  36.7 4.9 swap.9
  46.3 5.2 fusion.38
  54.3 5.0 all-gather.7.cloned.1.call-done
  60.2 5.8 fusion.10.refs_0_
  66.0 31.3 %swap.10 = (bf16[8,256,384]{2,1,0:T(8,128)(2,1)}, bf16[704,1024]{1,0:T(8,128)(2,1)}, bf16[704,1024]{1,0:T(8,128)(2,1)}) custom-call(bf16[8,256,384]{2,1,0:T(8,128)(2,1)} %fusion.10.refs_0_, bf16[5632,256]{1,0:T(8,128)(2,1)} %bitcast.167), custom_call_target="tpu_custom_call" | custom-call | bytes 1572864 | tf_op jit(solution)/shard_map/swap/pallas_call | solution.py:828
  100.8 20.1 %self_forward.1 = (bf16[2048,128]{1,0:T(8,128)(2,1)}, f32[128,2048]{1,0:T(8,128)}, f32[2,2048]{1,0:T(2,128)}) custom-call(s32[2,8]{1,0:T(2,128)} %pad_add_fusion.1.lim_ref, s32[8,2048]{1,0:T(8,128)} %broadcast_in_dim.102.rows_ref, f32[2,1536]{1,0:T(2,128)} %maximum_maximum_fusion.ext_ref, bf16[2048,384]{1,0:T(8,128)(2,1)} %bitcast.178), custom_call_target="tpu_custom_call" | custom-call | bytes 1650752 | tf_op jit(solution)/shard_map/self_forward/pallas_call | solution.py:251
  120.8 9.9 %swap.11.tok_ref = bf16[8,256,128]{2,1,0:T(8,128)(2,1)} custom-call(bf16[8,256,128]{2,1,0:T(8,128)(2,1)} %bitcast.199), custom_call_target="tpu_custom_call" | custom-call | bytes 524288 | tf_op jit(solution)/shard_map/swap/pallas_call | solution.py:828
  132.3 7.1 %self_out_to_cross.1 = (f32[256,1024]{1,0:T(8,128)}, bf16[256,1024]{1,0:T(8,128)(2,1)}, bf16[8,256,128]{2,1,0:T(8,128)(2,1)}, bf16[8,64,256]{2,1,0:T(8,128)(2,1)}) custom-call(bf16[8,256,128]{2,1,0:T(8,128)(2,1)} %swap.11.tok_ref, bf16[256,1024]{1,0:T(8,128)(2,1)} %copy-done.14, f32[1,1024]{1,0:T(1,128)} %bitcast.216, bf16[64,1024]{1,0:T(8,128)(2,1)} %slice.116.enc_ref, ...), custom_call_target="tpu_custom_call" | custom-call | bytes 8388608 | tf_op jit(solution)/shard_map/self_out_to_cross/pallas_call | solution.py:418
  139.5 11.7 %swap.12 = (bf16[8,256,128]{2,1,0:T(8,128)(2,1)}, bf16[8,64,256]{2,1,0:T(8,128)(2,1)}) custom-call(bf16[8,256,128]{2,1,0:T(8,128)(2,1)} %get-tuple-element.102.refs_0_, bf16[8,64,256]{2,1,0:T(8,128)(2,1)} %get-tuple-element.103.refs_1_), custom_call_target="tpu_custom_call" | custom-call | bytes 786432 | tf_op jit(solution)/shard_map/swap/pallas_call | solution.py:828
  151.1 10.2 %cross_forward.1 = (bf16[2048,128]{1,0:T(8,128)(2,1)}, f32[128,2048]{1,0:T(8,128)}, f32[2,2048]{1,0:T(2,128)}) custom-call(s32[2,8]{1,0:T(2,128)} %pad_add_fusion.2.lim_ref, s32[8,2048]{1,0:T(8,128)} %add_add_fusion.2.rows_ref, bf16[2048,128]{1,0:T(8,128)(2,1)} %bitcast.185, bf16[512,256]{1,0:T(8,128)(2,1)} %bitcast.194), custom_call_target="tpu_custom_call" | custom-call | bytes 852032 | tf_op jit(solution)/shard_map/cross_forward/pallas_call | solution.py:251
  161.4 24.4 %swap.13 = (bf16[8,256,128]{2,1,0:T(8,128)(2,1)}, bf16[704,1024]{1,0:T(8,128)(2,1)}, bf16[704,1024]{1,0:T(8,128)(2,1)}) custom-call(bf16[8,256,128]{2,1,0:T(8,128)(2,1)} %bitcast.196, bf16[5632,256]{1,0:T(8,128)(2,1)} %bitcast.168, bf16[704,1024]{1,0:T(8,128)(2,1)} %get-tuple-element.107.refs_2_, ...), custom_call_target="tpu_custom_call", output_to_operand_aliasing={{1}: (2, {}), {2}: (3, {})} | custom-call | bytes 524288 | tf_op jit(solution)/shard_map/swap/pallas_call | solution.py:828
  190.5 4.9 fusion.8
  195.3 17.7 %all-gather.13.cloned.1.call-done = bf16[1024,1024]{1,0:T(8,128)(2,1)} async-done(((bf16[256,1024]{1,0:T(8,128)(2,1)}), bf16[1024,1024]{1,0:T(8,128)(2,1)}) %all-gather.13.cloned.1.call-update) | async-done | bytes 2097168 | tf_op jit(solution)/shard_map/all_gather | solution.py:908
  217.0 4.7 multiply_convert_fusion
  241.5 16.5 %reduce-scatter.6.cloned.1.call-done = bf16[256,1024]{1,0:T(8,128)(2,1)} async-done(((bf16[1024,1024]{1,0:T(8,128)(2,1)}), bf16[256,1024]{1,0:T(8,128)(2,1)}) %reduce-scatter.6.cloned.1.call-update) | async-done | bytes 524304 | tf_op jit(solution)/shard_map/reduce_scatter | solution.py:891
  265.0 10.2 %swap.14 = bf16[8,256,128]{2,1,0:T(8,128)(2,1)} custom-call(bf16[8,256,128]{2,1,0:T(8,128)(2,1)} %fusion.16.refs_0_), custom_call_target="tpu_custom_call" | custom-call | bytes 524288 | tf_op jit(solution)/shard_map/swap/pallas_call | solution.py:828
  275.1 11.8 %cross_backward.1 = (bf16[2048,128]{1,0:T(8,128)(2,1)}, bf16[512,256]{1,0:T(8,128)(2,1)}) custom-call(s32[2,8]{1,0:T(2,128)} %pad_add_fusion.2.lim_ref, s32[8,2048]{1,0:T(8,128)} %add_add_fusion.2.rows_ref, bf16[2048,128]{1,0:T(8,128)(2,1)} %bitcast.186, bf16[512,256]{1,0:T(8,128)(2,1)} %bitcast.195, bf16[2048,128]{1,0:T(8,128)(2,1)} %bitcast.187, ...), custom_call_target="tpu_custom_call" | custom-call | bytes 2441280 | tf_op jit(solution)/shard_map/cross_backward/pallas_call | solution.py:251
  287.0 11.9 %swap.15 = (bf16[8,256,128]{2,1,0:T(8,128)(2,1)}, bf16[8,64,256]{2,1,0:T(8,128)(2,1)}) custom-call(bf16[8,256,128]{2,1,0:T(8,128)(2,1)} %bitcast.197, bf16[8,64,256]{2,1,0:T(8,128)(2,1)} %bitcast.203), custom_call_target="tpu_custom_call" | custom-call | bytes 786432 | tf_op jit(solution)/shard_map/swap/pallas_call | solution.py:828
  298.9 8.5 %cross_to_self_out.1 = (f32[256,1024]{1,0:T(8,128)}, bf16[256,1024]{1,0:T(8,128)(2,1)}, bf16[8,256,128]{2,1,0:T(8,128)(2,1)}, f32[1,1024]{1,0:T(1,128)}, bf16[64...) custom-call(bf16[8,256,128]{2,1,0:T(8,128)(2,1)} %get-tuple-element.119.dq_ref, ...), custom_call_target="tpu_custom_call" | custom-call | bytes 8388608 | tf_op jit(solution)/shard_map/cross_to_self_out/pallas_call | solution.py:418
  318.3 9.6 %swap.16 = bf16[8,256,128]{2,1,0:T(8,128)(2,1)} custom-call(bf16[8,256,128]{2,1,0:T(8,128)(2,1)} %get-tuple-element.126.refs_0_), custom_call_target="tpu_custom_call" | custom-call | bytes 524288 | tf_op jit(solution)/shard_map/swap/pallas_call | solution.py:828
  327.9 23.3 %self_backward.1 = (bf16[2048,384]{1,0:T(8,128)(2,1)}, f32[2,1536]{1,0:T(2,128)}) custom-call(s32[2,8]{1,0:T(2,128)} %pad_add_fusion.1.lim_ref, s32[8,2048]{1,0:T(8,128)} %broadcast_in_dim.102.rows_ref, f32[2,1536]{1,0:T(2,128)} %maximum_maximum_fusion.ext_ref, bf16[2048,384]{1,0:T(8,128)(2,1)} %bitcast.179, bf16[2048,128]{1,0:T(8,128)(2,1)} %bitcast.188, ...), custom_call_target="tpu_custom_call" | custom-call | bytes 3240000 | tf_op jit(solution)/shard_map/self_backward/pallas_call | solution.py:251
  351.2 21.4 %swap.17 = bf16[8,256,384]{2,1,0:T(8,128)(2,1)} custom-call(bf16[8,256,384]{2,1,0:T(8,128)(2,1)} %bitcast.189), custom_call_target="tpu_custom_call" | custom-call | bytes 1572864 | tf_op jit(solution)/shard_map/swap/pallas_call | solution.py:828
  374.3 4.6 convolution_convert_fusion
  379.0 4.9 fusion.18
  388.8 16.9 %collective-permute-done.3 = bf16[320,1024]{1,0:T(8,128)(2,1)S(1)} collective-permute-done((bf16[320,1024]{1,0:T(8,128)(2,1)}, bf16[320,1024]{1,0:T(8,128)(2,1)S(1)}, u32[]{:S(2)}, u32[]{:S(2)}) %collective-permute-start.3) | collective-permute-done | bytes 655392 | tf_op jit(solution)/shard_map/ppermute | solution.py:869
  406.7 99.6 %units_total.1 = (bf16[5632,256]{1,0:T(8,128)(2,1)}, bf16[704,1024]{1,0:T(8,128)(2,1)S(1)}, f32[256,1024]{1,0:T(8,128)S(1)}, f32[8,1024]{1,0:T(8,128)S(1)}) custom-call(bf16[2112,1024]{1,0:T(8,128)(2,1)} %bitcast.175, bf16[1024,1024]{1,0:T(8,128)(2,1)S(1)} %copy-done.2, bf16[32,1024]{1,0:T(8,128)(2,1)S(1)} %pad_bitcast_fusion.few_ref), custom_call_target="tpu_custom_call" | custom-call | bytes 389283840 | tf_op jit(solution)/shard_map/units_total/pallas_call | solution.py:545
  508.3 83.1 %ring_total.1 = (bf16[256,1024]{1,0:T(8,128)(2,1)S(1)}, bf16[256,1024]{1,0:T(8,128)(2,1)S(1)}, bf16[256,3072]{1,0:T(8,128)(2,1)S(1)}, bf16[256,3072]{1,0:T(8,128...) custom-call(bf16[256,1024]{1,0:T(8,128)(2,1)S(1)} %copy-done.3, bf16[256,1024]{1,0:T(8,128)(2,1)S(1)} %copy-done.4, ...), custom_call_target="tpu_custom_call" | custom-call | bytes 425656320 | tf_op jit(solution)/shard_map/ring_total/pallas_call | solution.py:545
  593.5 11.6 %collective-permute-start.4 = (bf16[256,1024]{1,0:T(8,128)(2,1)S(1)}, bf16[256,1024]{1,0:T(8,128)(2,1)}, u32[]{:S(2)}, u32[]{:S(2)}) collective-permute-start(bf16[256,1024]{1,0:T(8,128)(2,1)S(1)} %copy-done.29), channel_id=1, source_target_pairs={{0,0},{1,16},{2,2},{3,18},{4,4},{5,20},{6,6},{7,22},{8,8},{9,24},{... | collective-permute-start | bytes 1572872 | tf_op jit(solution)/shard_map/ppermute | solution.py:869
  (250 shorter events, 98.2 us)
Async XLA Ops:
  7.2 183.3 %copy-start = (bf16[704,1024]{1,0:T(8,128)(2,1)S(1)}, bf16[704,1024]{1,0:T(8,128)(2,1)}, u32[]{:S(2)}) copy-start(bf16[704,1024]{1,0:T(8,128)(2,1)} %param.32) | copy-start | bytes 4325380
  7.2 52.1 %all-gather.7.cloned.1.call-start = ((), (), s32[]{:S(2)}) async-start(), calls=%async_computation.5 | async-start | bytes 7864320 | tf_op jit(solution)/shard_map/all_gather | solution.py:908
  8.0 124.4 %all-gather.9.cloned.1.call-start = ((), (), s32[]{:S(2)}) async-start(), calls=%async_computation.6 | async-start | bytes 10485760 | tf_op jit(solution)/shard_map/all_gather | solution.py:920
  8.8 7.1 %copy-start.33 = (bf16[256,1024]{1,0:T(8,128)(2,1)S(1)}, bf16[256,1024]{1,0:T(8,128)(2,1)}, u32[]{:S(2)}) copy-start(bf16[256,1024]{1,0:T(8,128)(2,1)} %param.27) | copy-start | bytes 1572868
  8.8 7.1 %copy-start.34 = (bf16[256,1024]{1,0:T(8,128)(2,1)S(1)}, bf16[256,1024]{1,0:T(8,128)(2,1)}, u32[]{:S(2)}) copy-start(bf16[256,1024]{1,0:T(8,128)(2,1)} %param.24) | copy-start | bytes 1572868
  17.6 7.4 %copy-start.30 = (bf16[1,256,1024]{2,1,0:T(8,128)(2,1)S(1)}, bf16[1,256,1024]{2,1,0:T(8,128)(2,1)}, u32[]{:S(2)}) copy-start(bf16[1,256,1024]{2,1,0:T(8,128)(2,1)} %param.33) | copy-start | bytes 1572868
  17.6 7.4 %copy-start.36 = (bf16[1,64,1024]{2,1,0:T(8,128)(2,1)S(1)}, bf16[1,64,1024]{2,1,0:T(8,128)(2,1)}, u32[]{:S(2)}) copy-start(bf16[1,64,1024]{2,1,0:T(8,128)(2,1)} %param.18) | copy-start | bytes 393220
  17.6 12.3 %copy-start.42 = (s32[2048]{0:T(1024)S(1)}, s32[2048]{0:T(1024)}, u32[]{:S(2)}) copy-start(s32[2048]{0:T(1024)} %param.21) | copy-start | bytes 24580
  17.6 168.2 %all-gather.11.cloned.1.call-start = ((), (), s32[]{:S(2)}) async-start(), calls=%async_computation.7 | async-start | bytes 5242880 | tf_op jit(solution)/shard_map/all_gather | solution.py:971
  18.3 17.8 %collective-permute-start.1 = (s32[8,128]{1,0:T(8,128)S(1)}, s32[8,128]{1,0:T(8,128)S(1)}, u32[]{:S(2)}, u32[]{:S(2)}) collective-permute-start(s32[8,128]{1,0:T(8,128)S(1)} %pad_bitcast_fusion.1), channel_id=1, source_target_pairs={{0,0},{1,16},{2,2},{3,18},{4,4},{5,20},{6,6},{7,22},{8,8},{9,24},{... | collective-permute-start | bytes 12296 | tf_op jit(solution)/shard_map/ppermute | solution.py:869
  23.0 31.3 %collective-permute-start = (bf16[256,1024]{1,0:T(8,128)(2,1)}, bf16[256,1024]{1,0:T(8,128)(2,1)S(1)}, u32[]{:S(2)}, u32[]{:S(2)}) collective-permute-start(bf16[256,1024]{1,0:T(8,128)(2,1)} %bitcast), channel_id=1, source_target_pairs={{0,0},{1,16},{2,2},{3,18},{4,4},{5,20},{6,6},{7,22},{8,8},{9,24},{... | collective-permute-start | bytes 1572872 | tf_op jit(solution)/shard_map/ppermute | solution.py:869
  25.0 29.3 %collective-permute-start.2 = (bf16[320,1024]{1,0:T(8,128)(2,1)S(1)}, bf16[320,1024]{1,0:T(8,128)(2,1)S(1)}, u32[]{:S(2)}, u32[]{:S(2)}) collective-permute-start(bf16[320,1024]{1,0:T(8,128)(2,1)S(1)} %pad_maximum_fusion.4), channel_id=1, source_target_pairs={{0,0},{1,16},{2,2},{3,18},{4,4},{5,20},{6,6},{7,22},{8,8},{9,24},{... | collective-permute-start | bytes 1966088 | tf_op jit(solution)/shard_map/ppermute | solution.py:869
  54.3 45.8 %copy-start.26 = (bf16[320,1024]{1,0:T(8,128)(2,1)}, bf16[320,1024]{1,0:T(8,128)(2,1)S(1)}, u32[]{:S(2)}) copy-start(bf16[320,1024]{1,0:T(8,128)(2,1)S(1)} %collective-permute-done.2) | copy-start | bytes 1966084
  54.3 11.7 %copy-start.14 = (bf16[256,1024]{1,0:T(8,128)(2,1)}, bf16[256,1024]{1,0:T(8,128)(2,1)S(1)}, u32[]{:S(2)}) copy-start(bf16[256,1024]{1,0:T(8,128)(2,1)S(1)} %collective-permute-done.home_ref) | copy-start | bytes 1572868
  60.2 5.9 copy-start.39
  99.4 113.6 %all-gather.13.cloned.1.call-start = ((), (), s32[]{:S(2)}) async-start(), calls=%async_computation.8 | async-start | bytes 2621440 | tf_op jit(solution)/shard_map/all_gather | solution.py:908
  189.0 70.5 %copy-start.9 = (f32[256,1024]{1,0:T(8,128)}, f32[256,1024]{1,0:T(8,128)S(1)}, u32[]{:S(2)}) copy-start(f32[256,1024]{1,0:T(8,128)S(1)} %get-tuple-element.256) | copy-start | bytes 3145732
  190.1 67.9 %reduce-scatter.6.cloned.1.call-start = ((), (), s32[]{:S(2)}) async-start(), calls=%async_computation.9 | async-start | bytes 2621440 | tf_op jit(solution)/shard_map/reduce_scatter | solution.py:891
  217.0 4.7 copy-start.21
  226.9 178.9 %reduce-scatter.8.cloned.1.call-start = ((), (), s32[]{:S(2)}) async-start(), calls=%async_computation.10 | async-start | bytes 2621440 | tf_op jit(solution)/shard_map/reduce_scatter | solution.py:891
  263.0 142.7 %reduce-scatter.10.cloned.1.call-start = ((), (), s32[]{:S(2)}) async-start(), calls=%async_computation.11 | async-start | bytes 7864320 | tf_op jit(solution)/shard_map/reduce_scatter | solution.py:891
  298.9 8.5 %copy-start.31 = (bf16[256,1024]{1,0:T(8,128)(2,1)S(1)}, bf16[256,1024]{1,0:T(8,128)(2,1)}, u32[]{:S(2)}) copy-start(bf16[256,1024]{1,0:T(8,128)(2,1)} %get-tuple-element.123) | copy-start | bytes 1572868
  314.8 192.4 %reduce-scatter.12.cloned.1.call-start = ((), (), s32[]{:S(2)}) async-start(), calls=%async_computation.12 | async-start | bytes 2621440 | tf_op jit(solution)/shard_map/reduce_scatter | solution.py:891
  318.0 189.2 %reduce-scatter.14.cloned.1.call-start = ((), (), s32[]{:S(2)}) async-start(), calls=%async_computation.13 | async-start | bytes 7864320 | tf_op jit(solution)/shard_map/reduce_scatter | solution.py:891
  379.0 4.9 copy-start.40
  379.0 4.9 copy-start.25
  383.9 4.8 copy-start.41
  384.0 22.7 %copy-start.2 = (bf16[1024,1024]{1,0:T(8,128)(2,1)S(1)}, bf16[1024,1024]{1,0:T(8,128)(2,1)}, u32[]{:S(2)}) copy-start(bf16[1024,1024]{1,0:T(8,128)(2,1)} %convolution_convert_fusion.5.part_ref) | copy-start | bytes 6291460
  385.7 20.0 %collective-permute-start.3 = (bf16[320,1024]{1,0:T(8,128)(2,1)}, bf16[320,1024]{1,0:T(8,128)(2,1)S(1)}, u32[]{:S(2)}, u32[]{:S(2)}) collective-permute-start(bf16[320,1024]{1,0:T(8,128)(2,1)} %pad_maximum_fusion.5), channel_id=1, source_target_pairs={{0,0},{1,16},{2,2},{3,18},{4,4},{5,20},{6,6},{7,22},{8,8},{9,24},{... | collective-permute-start | bytes 1966088 | tf_op jit(solution)/shard_map/ppermute | solution.py:869
  406.6 99.6 %copy-start.10 = (f32[256,1024]{1,0:T(8,128)S(1)}, f32[256,1024]{1,0:T(8,128)}, u32[]{:S(2)}) copy-start(f32[256,1024]{1,0:T(8,128)} %copy-done.9) | copy-start | bytes 3145732
  593.5 27.9 %collective-permute-start.4 = (bf16[256,1024]{1,0:T(8,128)(2,1)S(1)}, bf16[256,1024]{1,0:T(8,128)(2,1)}, u32[]{:S(2)}, u32[]{:S(2)}) collective-permute-start(bf16[256,1024]{1,0:T(8,128)(2,1)S(1)} %copy-done.29), channel_id=1, source_target_pairs={{0,0},{1,16},{2,2},{3,18},{4,4},{5,20},{6,6},{7,22},{8,8},{9,24},{... | collective-permute-start | bytes 1572872 | tf_op jit(solution)/shard_map/ppermute | solution.py:869
  616.6 6.6 %copy-start.1 = (bf16[704,1024]{1,0:T(8,128)(2,1)S(1)}, bf16[704,1024]{1,0:T(8,128)(2,1)}, u32[]{:S(2)}) copy-start(bf16[704,1024]{1,0:T(8,128)(2,1)} %param.32) | copy-start | bytes 4325380
  (37 other events, 77.0 us)
Sparse Core Ops, SparseCore 0:
  9.6 49.7 all-gather.6
  61.5 70.7 all-gather.8
  134.5 37.7 all-gather.10
  190.2 22.7 all-gather.12
  227.0 31.0 reduce-scatter.5
  263.1 31.3 reduce-scatter.7
  314.9 58.9 reduce-scatter.9
  377.1 31.4 reduce-scatter.11
  411.1 64.1 reduce-scatter.13

commit v19 on v18

--- a/solution.py
+++ b/solution.py
@@ -550,7 +550,7 @@
         out_specs=[pl.BlockSpec(memory_space=pltpu.VMEM)] * len(outs),
         scratch_shapes=scratch,
         compiler_params=pltpu.CompilerParams(
-            collective_id=ident, has_side_effects=True, vmem_limit_bytes=48 << 20
+            collective_id=ident, has_side_effects=True, vmem_limit_bytes=62 << 20
         ),
         cost_estimate=pl.CostEstimate(flops=0, bytes_accessed=60 * size, transcendentals=0),
     )(*arrays)

time: 640 us -> 647 us (1.011)
    unnamed x129 -> x123, local copies, waits for them, and re-layouts: 20.1 us -> 17.5 us
  transfers between devices with their start and end apart: 14 -> 14, of which waited for: 6 -> 6; matrix products, arithmetic and copies ran while one was open for 14% -> 15% of each run, Pallas kernels for 50% -> 50%
where the time goes in v19:
time: 647 us; the launch traced here: 639 us
  Pallas kernels  401 us (62%)
  waiting for transfers between devices  60.1 us (9%)
  matrix products  55.4 us (9%)
  other arithmetic  40.3 us (6%)
  starting transfers between devices  31 us (5%)
  local copies, waits for them, and re-layouts  30.1 us (5%)
  between operations  15.3 us (2%)
    pallas_call x2, Pallas kernels, ring_call(): pl.pallas_call(body, name=name, out_shape=[jax.ShapeDtypeStruct(s, d) for...  184 us
    pallas_call x9, Pallas kernels, swap(): pl.pallas_call(functools.partial(swap_kernel, n, fan, count, fars, not fa...  135 us
    pallas_call x4, Pallas kernels, call(): pl.pallas_call(body, name=name, out_shape=[jax.ShapeDtypeStruct(s, d) for...  65.5 us
    ppermute x5, starting transfers between devices, change_home(): return lax.ppermute(value, ('seq', 'fsdp'), pairs)  29.4 us
    all_gather x2, waiting for transfers between devices, shards(): gather = lambda v: lax.all_gather(v, 'fsdp', axis=0, tiled=True)  26.4 us
    unnamed x123, local copies, waits for them, and re-layouts  17.5 us
    reduce_scatter x5, waiting for transfers between devices, scatter(): return lax.psum_scatter(grad, 'fsdp', scatter_dimension=0, tiled=True)  16.6 us
    pallas_call x2, Pallas kernels, over_weights(): pl.pallas_call(body, name=name, grid=(count,), out_shape=[jax.ShapeDtypeS...  15.6 us
  transfers between devices with their start and end apart: 14, of which 6 were waited for; matrix products, arithmetic and copies ran while one was open for 15% of the time, Pallas kernels for 50%

profile of v19, /device:TPU:1, one launch (start us, length us, event | category | flops | bytes accessed | tf_op | source)
XLA Modules:
  0.0 639.0 jit_solution(4453431378388513953)
XLA Ops:
  9.8 6.1 all-gather.1
  18.3 4.7 collective-permute-start.1
  25.0 4.5 collective-permute-start.2
  36.7 4.9 swap.9
  46.3 5.2 fusion.38
  54.3 5.0 all-gather.7.cloned.1.call-done
  60.2 5.8 fusion.10.refs_0_
  66.0 31.2 %swap.10 = (bf16[8,256,384]{2,1,0:T(8,128)(2,1)}, bf16[704,1024]{1,0:T(8,128)(2,1)}, bf16[704,1024]{1,0:T(8,128)(2,1)}) custom-call(bf16[8,256,384]{2,1,0:T(8,128)(2,1)} %fusion.10.refs_0_, bf16[5632,256]{1,0:T(8,128)(2,1)} %bitcast.167), custom_call_target="tpu_custom_call" | custom-call | bytes 1572864 | tf_op jit(solution)/shard_map/swap/pallas_call | solution.py:828
  100.8 20.1 %self_forward.1 = (bf16[2048,128]{1,0:T(8,128)(2,1)}, f32[128,2048]{1,0:T(8,128)}, f32[2,2048]{1,0:T(2,128)}) custom-call(s32[2,8]{1,0:T(2,128)} %pad_add_fusion.1.lim_ref, s32[8,2048]{1,0:T(8,128)} %broadcast_in_dim.102.rows_ref, f32[2,1536]{1,0:T(2,128)} %maximum_maximum_fusion.ext_ref, bf16[2048,384]{1,0:T(8,128)(2,1)} %bitcast.178), custom_call_target="tpu_custom_call" | custom-call | bytes 1650752 | tf_op jit(solution)/shard_map/self_forward/pallas_call | solution.py:251
  120.8 9.9 %swap.11.tok_ref = bf16[8,256,128]{2,1,0:T(8,128)(2,1)} custom-call(bf16[8,256,128]{2,1,0:T(8,128)(2,1)} %bitcast.199), custom_call_target="tpu_custom_call" | custom-call | bytes 524288 | tf_op jit(solution)/shard_map/swap/pallas_call | solution.py:828
  132.3 7.1 %self_out_to_cross.1 = (f32[256,1024]{1,0:T(8,128)}, bf16[256,1024]{1,0:T(8,128)(2,1)}, bf16[8,256,128]{2,1,0:T(8,128)(2,1)}, bf16[8,64,256]{2,1,0:T(8,128)(2,1)}) custom-call(bf16[8,256,128]{2,1,0:T(8,128)(2,1)} %swap.11.tok_ref, bf16[256,1024]{1,0:T(8,128)(2,1)} %copy-done.7, f32[1,1024]{1,0:T(1,128)} %bitcast.216, bf16[64,1024]{1,0:T(8,128)(2,1)} %slice.116.enc_ref, ...), custom_call_target="tpu_custom_call" | custom-call | bytes 8388608 | tf_op jit(solution)/shard_map/self_out_to_cross/pallas_call | solution.py:418
  139.4 11.6 %swap.12 = (bf16[8,256,128]{2,1,0:T(8,128)(2,1)}, bf16[8,64,256]{2,1,0:T(8,128)(2,1)}) custom-call(bf16[8,256,128]{2,1,0:T(8,128)(2,1)} %get-tuple-element.102.refs_0_, bf16[8,64,256]{2,1,0:T(8,128)(2,1)} %get-tuple-element.103.refs_1_), custom_call_target="tpu_custom_call" | custom-call | bytes 786432 | tf_op jit(solution)/shard_map/swap/pallas_call | solution.py:828
  151.1 10.2 %cross_forward.1 = (bf16[2048,128]{1,0:T(8,128)(2,1)}, f32[128,2048]{1,0:T(8,128)}, f32[2,2048]{1,0:T(2,128)}) custom-call(s32[2,8]{1,0:T(2,128)} %pad_add_fusion.2.lim_ref, s32[8,2048]{1,0:T(8,128)} %add_add_fusion.2.rows_ref, bf16[2048,128]{1,0:T(8,128)(2,1)} %bitcast.185, bf16[512,256]{1,0:T(8,128)(2,1)} %bitcast.194), custom_call_target="tpu_custom_call" | custom-call | bytes 852032 | tf_op jit(solution)/shard_map/cross_forward/pallas_call | solution.py:251
  161.3 24.5 %swap.13 = (bf16[8,256,128]{2,1,0:T(8,128)(2,1)}, bf16[704,1024]{1,0:T(8,128)(2,1)}, bf16[704,1024]{1,0:T(8,128)(2,1)}) custom-call(bf16[8,256,128]{2,1,0:T(8,128)(2,1)} %bitcast.196, bf16[5632,256]{1,0:T(8,128)(2,1)} %bitcast.168, bf16[704,1024]{1,0:T(8,128)(2,1)} %get-tuple-element.107.refs_2_, ...), custom_call_target="tpu_custom_call", output_to_operand_aliasing={{1}: (2, {}), {2}: (3, {})} | custom-call | bytes 524288 | tf_op jit(solution)/shard_map/swap/pallas_call | solution.py:828
  190.5 4.9 fusion.8
  195.4 21.3 %all-gather.13.cloned.1.call-done = bf16[1024,1024]{1,0:T(8,128)(2,1)} async-done(((bf16[256,1024]{1,0:T(8,128)(2,1)}), bf16[1024,1024]{1,0:T(8,128)(2,1)}) %all-gather.13.cloned.1.call-update) | async-done | bytes 2097168 | tf_op jit(solution)/shard_map/all_gather | solution.py:908
  220.7 4.7 multiply_convert_fusion
  245.2 16.5 %reduce-scatter.6.cloned.1.call-done = bf16[256,1024]{1,0:T(8,128)(2,1)} async-done(((bf16[1024,1024]{1,0:T(8,128)(2,1)}), bf16[256,1024]{1,0:T(8,128)(2,1)}) %reduce-scatter.6.cloned.1.call-update) | async-done | bytes 524304 | tf_op jit(solution)/shard_map/reduce_scatter | solution.py:891
  268.7 10.2 %swap.14 = bf16[8,256,128]{2,1,0:T(8,128)(2,1)} custom-call(bf16[8,256,128]{2,1,0:T(8,128)(2,1)} %fusion.16.refs_0_), custom_call_target="tpu_custom_call" | custom-call | bytes 524288 | tf_op jit(solution)/shard_map/swap/pallas_call | solution.py:828
  278.8 11.8 %cross_backward.1 = (bf16[2048,128]{1,0:T(8,128)(2,1)}, bf16[512,256]{1,0:T(8,128)(2,1)}) custom-call(s32[2,8]{1,0:T(2,128)} %pad_add_fusion.2.lim_ref, s32[8,2048]{1,0:T(8,128)} %add_add_fusion.2.rows_ref, bf16[2048,128]{1,0:T(8,128)(2,1)} %bitcast.186, bf16[512,256]{1,0:T(8,128)(2,1)} %bitcast.195, bf16[2048,128]{1,0:T(8,128)(2,1)} %bitcast.187, ...), custom_call_target="tpu_custom_call" | custom-call | bytes 2441280 | tf_op jit(solution)/shard_map/cross_backward/pallas_call | solution.py:251
  290.7 11.9 %swap.15 = (bf16[8,256,128]{2,1,0:T(8,128)(2,1)}, bf16[8,64,256]{2,1,0:T(8,128)(2,1)}) custom-call(bf16[8,256,128]{2,1,0:T(8,128)(2,1)} %bitcast.197, bf16[8,64,256]{2,1,0:T(8,128)(2,1)} %bitcast.203), custom_call_target="tpu_custom_call" | custom-call | bytes 786432 | tf_op jit(solution)/shard_map/swap/pallas_call | solution.py:828
  302.6 8.5 %cross_to_self_out.1 = (f32[256,1024]{1,0:T(8,128)}, bf16[256,1024]{1,0:T(8,128)(2,1)}, bf16[8,256,128]{2,1,0:T(8,128)(2,1)}, f32[1,1024]{1,0:T(1,128)}, bf16[64...) custom-call(bf16[8,256,128]{2,1,0:T(8,128)(2,1)} %get-tuple-element.119.dq_ref, ...), custom_call_target="tpu_custom_call" | custom-call | bytes 8388608 | tf_op jit(solution)/shard_map/cross_to_self_out/pallas_call | solution.py:418
  321.9 9.6 %swap.16 = bf16[8,256,128]{2,1,0:T(8,128)(2,1)} custom-call(bf16[8,256,128]{2,1,0:T(8,128)(2,1)} %get-tuple-element.126.refs_0_), custom_call_target="tpu_custom_call" | custom-call | bytes 524288 | tf_op jit(solution)/shard_map/swap/pallas_call | solution.py:828
  331.6 23.4 %self_backward.1 = (bf16[2048,384]{1,0:T(8,128)(2,1)}, f32[2,1536]{1,0:T(2,128)}) custom-call(s32[2,8]{1,0:T(2,128)} %pad_add_fusion.1.lim_ref, s32[8,2048]{1,0:T(8,128)} %broadcast_in_dim.102.rows_ref, f32[2,1536]{1,0:T(2,128)} %maximum_maximum_fusion.ext_ref, bf16[2048,384]{1,0:T(8,128)(2,1)} %bitcast.179, bf16[2048,128]{1,0:T(8,128)(2,1)} %bitcast.188, ...), custom_call_target="tpu_custom_call" | custom-call | bytes 3240000 | tf_op jit(solution)/shard_map/self_backward/pallas_call | solution.py:251
  354.9 21.3 %swap.17 = bf16[8,256,384]{2,1,0:T(8,128)(2,1)} custom-call(bf16[8,256,384]{2,1,0:T(8,128)(2,1)} %bitcast.189), custom_call_target="tpu_custom_call" | custom-call | bytes 1572864 | tf_op jit(solution)/shard_map/swap/pallas_call | solution.py:828
  378.0 4.6 convolution_convert_fusion
  382.7 4.9 fusion.18
  388.5 6.9 %collective-permute-start.3 = (bf16[320,1024]{1,0:T(8,128)(2,1)S(1)}, bf16[320,1024]{1,0:T(8,128)(2,1)S(1)}, u32[]{:S(2)}, u32[]{:S(2)}) collective-permute-start(bf16[320,1024]{1,0:T(8,128)(2,1)S(1)} %pad_maximum_fusion.5), channel_id=1, source_target_pairs={{0,0},{1,16},{2,2},{3,18},{4,4},{5,20},{6,6},{7,22},{8,8},{9,24},{... | collective-permute-start | bytes 1966088 | tf_op jit(solution)/shard_map/ppermute | solution.py:869
  396.4 14.1 %collective-permute-done.3 = bf16[320,1024]{1,0:T(8,128)(2,1)S(1)} collective-permute-done((bf16[320,1024]{1,0:T(8,128)(2,1)S(1)}, bf16[320,1024]{1,0:T(8,128)(2,1)S(1)}, u32[]{:S(2)}, u32[]{:S(2)}) %collective-permute-start.3) | collective-permute-done | bytes 655392 | tf_op jit(solution)/shard_map/ppermute | solution.py:869
  412.0 100.7 %units_total.1 = (bf16[5632,256]{1,0:T(8,128)(2,1)}, bf16[704,1024]{1,0:T(8,128)(2,1)}, f32[256,1024]{1,0:T(8,128)}, f32[8,1024]{1,0:T(8,128)}) custom-call(bf16[2112,1024]{1,0:T(8,128)(2,1)} %bitcast.175, bf16[1024,1024]{1,0:T(8,128)(2,1)} %convolution_convert_fusion.5.part_ref, bf16[32,1024]{1,0:T(8,128)(2,1)} %pad_bitcast_fusion.few_ref), custom_call_target="tpu_custom_call" | custom-call | bytes 389283840 | tf_op jit(solution)/shard_map/units_total/pallas_call | solution.py:545
  515.5 83.7 %ring_total.1 = (bf16[256,1024]{1,0:T(8,128)(2,1)}, bf16[256,1024]{1,0:T(8,128)(2,1)}, bf16[256,3072]{1,0:T(8,128)(2,1)}, bf16[256,3072]{1,0:T(8,128)(2,1)}, bf1...) custom-call(bf16[256,1024]{1,0:T(8,128)(2,1)} %reduce-scatter.8.cloned.1.call-done.refs_0_, ...), custom_call_target="tpu_custom_call" | custom-call | bytes 425656320 | tf_op jit(solution)/shard_map/ring_total/pallas_call | solution.py:545
  601.3 11.4 %collective-permute-start.4 = (bf16[256,1024]{1,0:T(8,128)(2,1)S(1)}, bf16[256,1024]{1,0:T(8,128)(2,1)}, u32[]{:S(2)}, u32[]{:S(2)}) collective-permute-start(bf16[256,1024]{1,0:T(8,128)(2,1)S(1)} %add_convert_fusion.1), channel_id=1, source_target_pairs={{0,0},{1,16},{2,2},{3,18},{4,4},{5,20},{6,6},{7,22},{8,8},{9,24},{... | collective-permute-start | bytes 1572872 | tf_op jit(solution)/shard_map/ppermute | solution.py:869
  (244 shorter events, 102.4 us)
Async XLA Ops:
  7.2 183.3 %copy-start = (bf16[704,1024]{1,0:T(8,128)(2,1)S(1)}, bf16[704,1024]{1,0:T(8,128)(2,1)}, u32[]{:S(2)}) copy-start(bf16[704,1024]{1,0:T(8,128)(2,1)} %param.32) | copy-start | bytes 4325380
  7.2 52.1 %all-gather.7.cloned.1.call-start = ((), (), s32[]{:S(2)}) async-start(), calls=%async_computation.5 | async-start | bytes 7864320 | tf_op jit(solution)/shard_map/all_gather | solution.py:908
  8.0 124.4 %all-gather.9.cloned.1.call-start = ((), (), s32[]{:S(2)}) async-start(), calls=%async_computation.6 | async-start | bytes 10485760 | tf_op jit(solution)/shard_map/all_gather | solution.py:920
  8.8 7.1 %copy-start.30 = (bf16[256,1024]{1,0:T(8,128)(2,1)S(1)}, bf16[256,1024]{1,0:T(8,128)(2,1)}, u32[]{:S(2)}) copy-start(bf16[256,1024]{1,0:T(8,128)(2,1)} %param.27) | copy-start | bytes 1572868
  8.8 7.1 %copy-start.31 = (bf16[256,1024]{1,0:T(8,128)(2,1)S(1)}, bf16[256,1024]{1,0:T(8,128)(2,1)}, u32[]{:S(2)}) copy-start(bf16[256,1024]{1,0:T(8,128)(2,1)} %param.24) | copy-start | bytes 1572868
  17.6 7.4 %copy-start.27 = (bf16[1,256,1024]{2,1,0:T(8,128)(2,1)S(1)}, bf16[1,256,1024]{2,1,0:T(8,128)(2,1)}, u32[]{:S(2)}) copy-start(bf16[1,256,1024]{2,1,0:T(8,128)(2,1)} %param.33) | copy-start | bytes 1572868
  17.6 7.4 %copy-start.33 = (bf16[1,64,1024]{2,1,0:T(8,128)(2,1)S(1)}, bf16[1,64,1024]{2,1,0:T(8,128)(2,1)}, u32[]{:S(2)}) copy-start(bf16[1,64,1024]{2,1,0:T(8,128)(2,1)} %param.18) | copy-start | bytes 393220
  17.6 12.3 %copy-start.39 = (s32[2048]{0:T(1024)S(1)}, s32[2048]{0:T(1024)}, u32[]{:S(2)}) copy-start(s32[2048]{0:T(1024)} %param.21) | copy-start | bytes 24580
  17.6 168.2 %all-gather.11.cloned.1.call-start = ((), (), s32[]{:S(2)}) async-start(), calls=%async_computation.7 | async-start | bytes 5242880 | tf_op jit(solution)/shard_map/all_gather | solution.py:971
  18.3 17.8 %collective-permute-start.1 = (s32[8,128]{1,0:T(8,128)S(1)}, s32[8,128]{1,0:T(8,128)S(1)}, u32[]{:S(2)}, u32[]{:S(2)}) collective-permute-start(s32[8,128]{1,0:T(8,128)S(1)} %pad_bitcast_fusion.1), channel_id=1, source_target_pairs={{0,0},{1,16},{2,2},{3,18},{4,4},{5,20},{6,6},{7,22},{8,8},{9,24},{... | collective-permute-start | bytes 12296 | tf_op jit(solution)/shard_map/ppermute | solution.py:869
  23.0 31.3 %collective-permute-start = (bf16[256,1024]{1,0:T(8,128)(2,1)}, bf16[256,1024]{1,0:T(8,128)(2,1)S(1)}, u32[]{:S(2)}, u32[]{:S(2)}) collective-permute-start(bf16[256,1024]{1,0:T(8,128)(2,1)} %bitcast), channel_id=1, source_target_pairs={{0,0},{1,16},{2,2},{3,18},{4,4},{5,20},{6,6},{7,22},{8,8},{9,24},{... | collective-permute-start | bytes 1572872 | tf_op jit(solution)/shard_map/ppermute | solution.py:869
  25.0 29.3 %collective-permute-start.2 = (bf16[320,1024]{1,0:T(8,128)(2,1)S(1)}, bf16[320,1024]{1,0:T(8,128)(2,1)S(1)}, u32[]{:S(2)}, u32[]{:S(2)}) collective-permute-start(bf16[320,1024]{1,0:T(8,128)(2,1)S(1)} %pad_maximum_fusion.4), channel_id=1, source_target_pairs={{0,0},{1,16},{2,2},{3,18},{4,4},{5,20},{6,6},{7,22},{8,8},{9,24},{... | collective-permute-start | bytes 1966088 | tf_op jit(solution)/shard_map/ppermute | solution.py:869
  54.3 45.8 %copy-start.22 = (bf16[320,1024]{1,0:T(8,128)(2,1)}, bf16[320,1024]{1,0:T(8,128)(2,1)S(1)}, u32[]{:S(2)}) copy-start(bf16[320,1024]{1,0:T(8,128)(2,1)S(1)} %collective-permute-done.2) | copy-start | bytes 1966084
  54.3 11.7 %copy-start.7 = (bf16[256,1024]{1,0:T(8,128)(2,1)}, bf16[256,1024]{1,0:T(8,128)(2,1)S(1)}, u32[]{:S(2)}) copy-start(bf16[256,1024]{1,0:T(8,128)(2,1)S(1)} %collective-permute-done.home_ref) | copy-start | bytes 1572868
  60.2 5.9 copy-start.36
  99.4 117.3 %all-gather.13.cloned.1.call-start = ((), (), s32[]{:S(2)}) async-start(), calls=%async_computation.8 | async-start | bytes 2621440 | tf_op jit(solution)/shard_map/all_gather | solution.py:908
  189.1 74.1 %copy-start.2 = (f32[256,1024]{1,0:T(8,128)}, f32[256,1024]{1,0:T(8,128)S(1)}, u32[]{:S(2)}) copy-start(f32[256,1024]{1,0:T(8,128)S(1)} %get-tuple-element.256) | copy-start | bytes 3145732
  190.2 71.6 %reduce-scatter.6.cloned.1.call-start = ((), (), s32[]{:S(2)}) async-start(), calls=%async_computation.9 | async-start | bytes 2621440 | tf_op jit(solution)/shard_map/reduce_scatter | solution.py:891
  230.6 179.9 %reduce-scatter.8.cloned.1.call-start = ((), (), s32[]{:S(2)}) async-start(), calls=%async_computation.10 | async-start | bytes 2621440 | tf_op jit(solution)/shard_map/reduce_scatter | solution.py:891
  266.7 143.8 %reduce-scatter.10.cloned.1.call-start = ((), (), s32[]{:S(2)}) async-start(), calls=%async_computation.11 | async-start | bytes 7864320 | tf_op jit(solution)/shard_map/reduce_scatter | solution.py:891
  302.6 8.5 %copy-start.28 = (bf16[256,1024]{1,0:T(8,128)(2,1)S(1)}, bf16[256,1024]{1,0:T(8,128)(2,1)}, u32[]{:S(2)}) copy-start(bf16[256,1024]{1,0:T(8,128)(2,1)} %get-tuple-element.123) | copy-start | bytes 1572868
  318.4 197.1 %reduce-scatter.12.cloned.1.call-start = ((), (), s32[]{:S(2)}) async-start(), calls=%async_computation.12 | async-start | bytes 2621440 | tf_op jit(solution)/shard_map/reduce_scatter | solution.py:891
  321.7 193.8 %reduce-scatter.14.cloned.1.call-start = ((), (), s32[]{:S(2)}) async-start(), calls=%async_computation.13 | async-start | bytes 7864320 | tf_op jit(solution)/shard_map/reduce_scatter | solution.py:891
  382.7 4.9 copy-start.37
  382.7 4.9 copy-start.21
  387.6 8.0 %copy-start.46 = (f32[2,1536]{1,0:T(2,128)S(1)}, f32[2,1536]{1,0:T(2,128)}, u32[]{:S(2)}) copy-start(f32[2,1536]{1,0:T(2,128)} %get-tuple-element.133) | copy-start | bytes 36868
  387.6 8.7 %copy-start.38 = (f32[1,1024]{1,0:T(1,128)S(1)}, f32[1,1024]{1,0:T(1,128)}, u32[]{:S(2)}) copy-start(f32[1,1024]{1,0:T(1,128)} %get-tuple-element.132) | copy-start | bytes 12292
  388.5 21.9 %collective-permute-start.3 = (bf16[320,1024]{1,0:T(8,128)(2,1)S(1)}, bf16[320,1024]{1,0:T(8,128)(2,1)S(1)}, u32[]{:S(2)}, u32[]{:S(2)}) collective-permute-start(bf16[320,1024]{1,0:T(8,128)(2,1)S(1)} %pad_maximum_fusion.5), channel_id=1, source_target_pairs={{0,0},{1,16},{2,2},{3,18},{4,4},{5,20},{6,6},{7,22},{8,8},{9,24},{... | collective-permute-start | bytes 1966088 | tf_op jit(solution)/shard_map/ppermute | solution.py:869
  412.0 102.1 %copy-start.3 = (f32[256,1024]{1,0:T(8,128)S(1)}, f32[256,1024]{1,0:T(8,128)}, u32[]{:S(2)}) copy-start(f32[256,1024]{1,0:T(8,128)} %copy-done.2) | copy-start | bytes 3145732
  601.0 13.5 %copy-start.10 = (bf16[256,3072]{1,0:T(8,128)(2,1)S(1)}, bf16[256,3072]{1,0:T(8,128)(2,1)}, u32[]{:S(2)}) copy-start(bf16[256,3072]{1,0:T(8,128)(2,1)} %get-tuple-element.158) | copy-start | bytes 4718596
  601.3 28.9 %collective-permute-start.4 = (bf16[256,1024]{1,0:T(8,128)(2,1)S(1)}, bf16[256,1024]{1,0:T(8,128)(2,1)}, u32[]{:S(2)}, u32[]{:S(2)}) collective-permute-start(bf16[256,1024]{1,0:T(8,128)(2,1)S(1)} %add_convert_fusion.1), channel_id=1, source_target_pairs={{0,0},{1,16},{2,2},{3,18},{4,4},{5,20},{6,6},{7,22},{8,8},{9,24},{... | collective-permute-start | bytes 1572872 | tf_op jit(solution)/shard_map/ppermute | solution.py:869
  625.4 6.6 %copy-start.1 = (bf16[704,1024]{1,0:T(8,128)(2,1)S(1)}, bf16[704,1024]{1,0:T(8,128)(2,1)}, u32[]{:S(2)}) copy-start(bf16[704,1024]{1,0:T(8,128)(2,1)} %param.32) | copy-start | bytes 4325380
  (34 other events, 78.0 us)
Sparse Core Ops, SparseCore 0:
  9.6 49.7 all-gather.6
  61.5 70.7 all-gather.8
  134.5 41.2 all-gather.10
  190.3 26.3 all-gather.12
  230.7 31.0 reduce-scatter.5
  266.8 31.3 reduce-scatter.7
  318.5 60.8 reduce-scatter.9
  382.7 31.4 reduce-scatter.11
  416.7 65.9 reduce-scatter.13
